TPU v7x, 256 devices: a whole 4x4x8 slice. The times are simulated.
256 devices in a mesh: group: 4 (over y), row: 16 (over x, z_lo), col: 4 (over z_hi, core).
Axes of the slice: x: 4, y: 4, z: 8 (z_hi: 2, z_lo: 4; z = z_hi * 4 + z_lo), core: 2. Of those that a mesh axis runs over, the one named last changes fastest.
Arguments:
- fronts: bfloat16 [8, 12288, 12288], P('group', 'row', 'col'), may hold values from -0.0546875 to 0.0546875
- samples: bfloat16 [256, 8, 12288], P('row', 'group', 'col'), may hold values from -6 to 6
- second_samples: bfloat16 [256, 8, 12288], P('col', 'group', 'row'), may hold values from -6 to 6
- front_sizes: int32 [8], replicated, may hold values from 1536 to 12288, as said below
- parent_ids: int32 [8], replicated, may hold values from 1 to 8, as said below
- block_maps: int32 [8, 16], replicated, may hold values from 0 to 16, as said below
Outputs:
- sampled: bfloat16 [256, 8, 12288], P('col', 'group', 'row')
- projected: bfloat16 [256, 8, 12288], P('row', 'group', 'col')
Inputs may be any that keep to these rules, and one draw needn't show every extreme that they name: `front_sizes`: every front has at least 1536 rows and some front has exactly 12288. `parent_ids`: a front's parent has a larger index; 8 marks a root; the last front is a root. `block_maps`: for a front f with a parent p, entry b with b * 768 < front_sizes[f] names a parent block q with q * 768 < front_sizes[p]; all other entries are 16; several child blocks may name one parent block.
All inputs are finite; a program needn't handle non-finite values.
Results may differ from a plain program's by a relative error of at most 0.009.
Values may be sent and summed in bfloat16 or wider, within the bound.
No kernel may reach another device: no remote copies, remote signals or barrier semaphores. Data moves between devices by JAX's collectives and lax.ppermute only.
A program may use at most 64 MiB of HBM per device.

v0:
```python
import jax
import jax.numpy as jnp
from jax import lax
from jax.experimental import pallas as pl
from jax.experimental.pallas import tpu as pltpu
from jax.sharding import Mesh
from jax.sharding import PartitionSpec as P

DEVICES = ("group", "x", "z", "h", "c")
ROW = ("x", "z")
COL = ("h", "c")
F32 = jnp.float32
BF16 = jnp.bfloat16


def shift(value, axis, by):
    n = lax.axis_size(axis)
    return lax.ppermute(value, axis, [(i, (i + by) % n) for i in range(n)])


def pick(value, index):
    return lax.dynamic_index_in_dim(value, index, 0, keepdims=False)


def rolled(value, start):
    twice = jnp.concatenate([value, value], axis=0)
    return lax.dynamic_slice_in_dim(twice, start, value.shape[0], 0)


def ring_copies(mine):
    half = mine.shape[0] // 2
    left = shift(mine, "x", 1)
    right = shift(mine, "x", -1)
    over_left = shift(left[:half], "x", 1)
    over_right = shift(right[half:], "x", -1)
    return jnp.concatenate([mine, over_left, over_right, left, right], axis=0)


def gather_rows(samples):
    columns = []
    for f in range(samples.shape[1]):
        mine = samples[:, f, :]
        columns.append(jnp.concatenate([mine] + [shift(mine, "z", -k) for k in (1, 2, 3)], axis=0))
    return [ring_copies(column) for column in columns]


def mask_kernel(sizes_ref, origin_ref, fronts_ref, out_ref):
    tile = fronts_ref[...]
    size = sizes_ref[pl.program_id(0)]
    rows = origin_ref[0] + pl.program_id(1) * tile.shape[1] + lax.broadcasted_iota(jnp.int32, tile.shape, 1)
    cols = origin_ref[1] + lax.broadcasted_iota(jnp.int32, tile.shape, 2)
    out_ref[...] = jnp.where(jnp.maximum(rows, cols) < size, tile, jnp.zeros((), tile.dtype))


def masked_fronts(fronts, sizes, origin):
    local, rows, cols = fronts.shape
    step = 64
    spec = pl.BlockSpec((1, step, cols), lambda f, i: (f, i, 0))
    scalars = pl.BlockSpec(memory_space=pltpu.SMEM)
    return pl.pallas_call(
        mask_kernel,
        grid=(local, rows // step),
        in_specs=[scalars, scalars, spec],
        out_specs=spec,
        out_shape=jax.ShapeDtypeStruct(fronts.shape, fronts.dtype),
        compiler_params=pltpu.CompilerParams(vmem_limit_bytes=4 << 20),
    )(sizes, origin, fronts)


def reduce_cols(partial, x, h, c):
    odd = (x - c) & 1
    received = shift(pick(partial, 1 - odd), "c", 1)
    pair = pick(partial, odd).astype(F32) + received.astype(F32)
    kept = h ^ (((x - odd) & 3) >> 1)
    received = shift(pick(pair, 1 - kept).astype(BF16), "h", 1)
    return pick(pair, kept) + received.astype(F32)


def scatter_rows(product):
    block = product.shape[0] // 4
    half = block // 2
    to_right = shift(product[block + half : 2 * block + half], "x", 1)
    to_left = shift(product[2 * block + half : 3 * block + half], "x", -1)
    over_right = product[block : block + half].astype(F32) + to_right[half:].astype(F32)
    over_left = product[3 * block + half :].astype(F32) + to_left[:half].astype(F32)
    over_right = shift(over_right.astype(BF16), "x", 1)
    over_left = shift(over_left.astype(BF16), "x", -1)
    top = product[:half].astype(F32) + to_left[half:].astype(F32) + over_right.astype(F32)
    low = product[half:block].astype(F32) + to_right[:half].astype(F32) + over_left.astype(F32)
    own = jnp.concatenate([top, low], axis=0)
    rows = block // 4
    total = own[:rows]
    for k in (1, 2, 3):
        piece = own[k * rows : (k + 1) * rows].astype(BF16)
        total = total + shift(piece, "z", k).astype(F32)
    return total


def shards(fronts, samples, second_samples, front_sizes, parent_ids, block_maps):
    local, tile_rows, tile_cols = fronts.shape
    own_rows = samples.shape[0]
    slab = second_samples.shape[0]
    group, x, z, h, c = (lax.axis_index(axis) for axis in DEVICES)
    row = lax.axis_index(ROW)
    col = lax.axis_index(COL)
    count = parent_ids.shape[0]
    blocks = block_maps.shape[1]

    sizes = lax.dynamic_slice_in_dim(front_sizes, group * local, local, 0)
    masked = masked_fronts(fronts, sizes, jnp.stack([row * tile_rows, col * tile_cols]))

    slabs = []
    for f, gathered in enumerate(gather_rows(samples)):
        partial = jnp.einsum("sk,mk->sm", gathered, masked[f], preferred_element_type=F32)
        total = reduce_cols(partial.astype(BF16).reshape(2, 2, slab, tile_rows), x, h, c)
        total = total.astype(BF16).reshape(-1, own_rows, tile_rows)
        slabs.append(rolled(total, (4 - z) & 3).reshape(slab, tile_rows))
    sampled = jnp.stack(slabs, axis=1)

    spread = ("group",) + ROW
    arrived = lax.all_to_all(sampled, spread, split_axis=0, concat_axis=0, tiled=True)
    front_of = jnp.arange(count, dtype=jnp.int32)
    parent_match = parent_ids[:, None] == front_of[None, :]
    block_match = block_maps[:, :, None] == jnp.arange(blocks, dtype=jnp.int32)[None, None, :]
    weight = parent_match[:, None, :, None] & block_match[:, :, None, :]
    groups = count // local
    weight = weight.reshape(groups, local, blocks, groups, local, blocks)
    weight = weight.transpose(3, 5, 4, 0, 2, 1).reshape(count * blocks, count * blocks).astype(BF16)
    arrived = arrived.reshape(-1, tile_rows)
    extension = jnp.einsum("ij,jk->ik", weight, arrived, preferred_element_type=F32).astype(BF16)
    extension = extension.reshape(slab, local, tile_rows)
    extension = lax.all_to_all(extension, spread, split_axis=0, concat_axis=0, tiled=True)
    combined = (second_samples.astype(F32) + extension.astype(F32)).astype(BF16)

    mine = []
    for f in range(local):
        blocked = combined[:, f, :].reshape(-1, own_rows, tile_rows)
        mine.append(rolled(blocked, z).reshape(slab, tile_rows))
    everyone = lax.all_gather(jnp.concatenate(mine, axis=1), COL, axis=0, tiled=True)
    outs = []
    for f in range(local):
        ordered = everyone[:, f * tile_rows : (f + 1) * tile_rows].reshape(-1, slab, tile_rows)
        ordered = rolled(ordered, x).reshape(-1, tile_rows)
        product = jnp.einsum("sm,mk->sk", ordered, masked[f], preferred_element_type=F32)
        outs.append(scatter_rows(product.astype(BF16)).astype(BF16))
    return sampled, jnp.stack(outs, axis=1)


def solution(mesh):
    torus = Mesh(mesh.devices.reshape(mesh.shape["group"], 4, 4, 2, 2), DEVICES)
    in_specs = (P("group", ROW, COL), P(ROW, "group", COL), P(COL, "group", ROW), P(), P(), P())
    out_specs = (P(COL, "group", ROW), P(ROW, "group", COL))
    return jax.shard_map(
        shards, mesh=torus, in_specs=in_specs, out_specs=out_specs, check_vma=False
    )
```

profile of v0, /device:TPU:32, one launch (start us, length us, event | category | flops | bytes accessed | tf_op | source)
XLA Modules:
  0.0 178.4 jit_solution(10946465382415141928)
XLA Ops:
  0.7 1.4 fusion.32
  2.1 2.0 %collective-permute-start.2 = (bf16[16,3072]{1,0:T(8,128)(2,1)S(1)}, bf16[16,3072]{1,0:T(8,128)(2,1)S(1)}, u32[]{:S(2)}, u32[]{:S(2)}) collective-permute-start(bf16[16,3072]{1,0:T(8,128)(2,1)S(1)} %get-tuple-element.11), channel_id=1, source_target_pairs={{0,4},{4,8},{8,12},{12,0},{1,5},{5,9},{9,13},{13,1},{2,6},{6,10},{... | collective-permute-start | bytes 294920 | tf_op jit(solution)/shard_map/ppermute | solution.py:18
  4.1 2.3 %collective-permute-start.1 = (bf16[16,3072]{1,0:T(8,128)(2,1)S(1)}, bf16[16,3072]{1,0:T(8,128)(2,1)S(1)}, u32[]{:S(2)}, u32[]{:S(2)}) collective-permute-start(bf16[16,3072]{1,0:T(8,128)(2,1)S(1)} %get-tuple-element.11), channel_id=1, source_target_pairs={{0,8},{4,12},{8,0},{12,4},{1,9},{5,13},{9,1},{13,5},{2,10},{6,14},... | collective-permute-start | bytes 294920 | tf_op jit(solution)/shard_map/ppermute | solution.py:18
  6.4 1.1 collective-permute-start
  7.5 0.7 constant_dynamic-update-slice_fusion.15
  8.1 0.9 collective-permute-start.11
  9.1 2.4 %collective-permute-start.10 = (bf16[16,3072]{1,0:T(8,128)(2,1)S(1)}, bf16[16,3072]{1,0:T(8,128)(2,1)S(1)}, u32[]{:S(2)}, u32[]{:S(2)}) collective-permute-start(bf16[16,3072]{1,0:T(8,128)(2,1)S(1)} %get-tuple-element.13), channel_id=1, source_target_pairs={{0,8},{4,12},{8,0},{12,4},{1,9},{5,13},{9,1},{13,5},{2,10},{6,14},... | collective-permute-start | bytes 294920 | tf_op jit(solution)/shard_map/ppermute | solution.py:18
  11.6 0.1 copy.28
  11.9 3.7 %copy-done = bf16[2,768,3072]{2,1,0:T(8,128)(2,1)S(1)} copy-done((bf16[2,768,3072]{2,1,0:T(8,128)(2,1)S(1)}, bf16[2,768,3072]{2,1,0:T(8,128)(2,1)}, u32[]{:S(2)}) %copy-start) | copy-done | bytes 9437208
  15.6 3.5 %shard_map.77 = bf16[2,768,3072]{2,1,0:T(8,128)(2,1)S(1)} custom-call(s32[2]{0:T(128)S(1)} %dynamic_slice.47.sizes_ref, s32[2]{0:T(128)S(1)} %pad_add_fusion.origin_ref, bf16[2,768,3072]{2,1,0:T(8,128)(2,1)S(1)} %copy-done), custom_call_target="tpu_custom_call" | custom-call | tf_op jit(solution)/shard_map/pallas_call | solution.py:60
  19.3 2.8 %collective-permute-start.5 = (bf16[64,3072]{1,0:T(8,128)(2,1)S(1)}, bf16[64,3072]{1,0:T(8,128)(2,1)S(1)}, u32[]{:S(2)}, u32[]{:S(2)}) collective-permute-start(bf16[64,3072]{1,0:T(8,128)(2,1)S(1)} %pad_maximum_fusion), channel_id=1, source_target_pairs={{0,48},{16,0},{32,16},{48,32},{1,49},{17,1},{33,17},{49,33},{2,50}... | collective-permute-start | bytes 1179656 | tf_op jit(solution)/shard_map/ppermute | solution.py:18
  22.1 1.7 collective-permute-done.9
  23.9 2.8 %collective-permute-start.14 = (bf16[64,3072]{1,0:T(8,128)(2,1)S(1)}, bf16[64,3072]{1,0:T(8,128)(2,1)S(1)}, u32[]{:S(2)}, u32[]{:S(2)}) collective-permute-start(bf16[64,3072]{1,0:T(8,128)(2,1)S(1)} %pad_maximum_fusion.1), channel_id=1, source_target_pairs={{0,48},{16,0},{32,16},{48,32},{1,49},{17,1},{33,17},{49,33},{2,50}... | collective-permute-start | bytes 1179656 | tf_op jit(solution)/shard_map/ppermute | solution.py:18
  26.8 8.6 %collective-permute-done.3 = bf16[64,3072]{1,0:T(8,128)(2,1)S(1)} collective-permute-done((bf16[64,3072]{1,0:T(8,128)(2,1)S(1)}, bf16[64,3072]{1,0:T(8,128)(2,1)S(1)}, u32[]{:S(2)}, u32[]{:S(2)}) %collective-permute-start.3) | collective-permute-done | bytes 393248 | tf_op jit(solution)/shard_map/ppermute | solution.py:18
  35.4 0.1 collective-permute-start.4
  35.6 3.3 %collective-permute-start.6 = (bf16[32,3072]{1,0:T(8,128)(2,1)S(1)}, bf16[32,3072]{1,0:T(8,128)(2,1)S(1)}, u32[]{:S(2)}, u32[]{:S(2)}) collective-permute-start(bf16[32,3072]{1,0:T(8,128)(2,1)S(1)} %slice.169), channel_id=1, source_target_pairs={{0,48},{16,0},{32,16},{48,32},{1,49},{17,1},{33,17},{49,33},{2,50}... | collective-permute-start | bytes 589832 | tf_op jit(solution)/shard_map/ppermute | solution.py:18
  38.8 1.3 collective-permute-done.14
  40.1 3.8 %collective-permute-start.15 = (bf16[32,3072]{1,0:T(8,128)(2,1)S(1)}, bf16[32,3072]{1,0:T(8,128)(2,1)S(1)}, u32[]{:S(2)}, u32[]{:S(2)}) collective-permute-start(bf16[32,3072]{1,0:T(8,128)(2,1)S(1)} %slice.172), channel_id=1, source_target_pairs={{0,48},{16,0},{32,16},{48,32},{1,49},{17,1},{33,17},{49,33},{2,50}... | collective-permute-start | bytes 589832 | tf_op jit(solution)/shard_map/ppermute | solution.py:18
  43.9 0.3 collective-permute-start.13
  44.2 3.4 %collective-permute-done.4 = bf16[32,3072]{1,0:T(8,128)(2,1)S(1)} collective-permute-done((bf16[32,3072]{1,0:T(8,128)(2,1)S(1)}, bf16[32,3072]{1,0:T(8,128)(2,1)S(1)}, u32[]{:S(2)}, u32[]{:S(2)}) %collective-permute-start.4) | collective-permute-done | bytes 196640 | tf_op jit(solution)/shard_map/ppermute | solution.py:18
  47.7 1.4 fusion.7
  49.2 0.1 collective-permute-start.7
  49.3 1.8 collective-permute-done.13
  51.2 1.4 fusion.6
  52.7 0.1 collective-permute-start.16
  52.9 5.8 %collective-permute-start.8 = (bf16[64,768]{1,0:T(8,128)(2,1)S(1)}, bf16[64,768]{1,0:T(8,128)(2,1)S(1)}, u32[]{:S(2)}, u32[]{:S(2)}) collective-permute-start(bf16[64,768]{1,0:T(8,128)(2,1)S(1)} %fusion.18), channel_id=1, source_target_pairs={{0,2},{2,0},{1,3},{3,1},{4,6},{6,4},{5,7},{7,5},{8,10},{10,8},{9,1... | collective-permute-start | bytes 294920 | tf_op jit(solution)/shard_map/ppermute | solution.py:18
  58.7 1.3 collective-permute-start.17
  60.1 5.0 %collective-permute-done.8 = bf16[64,768]{1,0:T(8,128)(2,1)S(1)} collective-permute-done((bf16[64,768]{1,0:T(8,128)(2,1)S(1)}, bf16[64,768]{1,0:T(8,128)(2,1)S(1)}, u32[]{:S(2)}, u32[]{:S(2)}) %collective-permute-start.8) | collective-permute-done | bytes 98336 | tf_op jit(solution)/shard_map/ppermute | solution.py:18
  65.1 4.6 %collective-permute-done.17 = bf16[64,768]{1,0:T(8,128)(2,1)S(1)} collective-permute-done((bf16[64,768]{1,0:T(8,128)(2,1)S(1)}, bf16[64,768]{1,0:T(8,128)(2,1)S(1)}, u32[]{:S(2)}, u32[]{:S(2)}) %collective-permute-start.17) | collective-permute-done | bytes 98336 | tf_op jit(solution)/shard_map/ppermute | solution.py:18
  69.7 0.1 fusion.22
  69.9 0.9 copy.31
  70.7 7.3 %all-to-all-start = ((bf16[64,2,768]{2,1,0:T(2,128)(2,1)}), bf16[64,2,768]{2,1,0:T(2,128)(2,1)S(1)}, u32[]{:S(2)}, u32[]{:S(2)}) async-start(bf16[64,2,768]{2,1,0:T(2,128)(2,1)} %copy.31), calls=%async_computation | async-start | bytes 393216 | tf_op jit(solution)/shard_map/all_to_all | solution.py:121
  78.1 0.6 broadcast_and_fusion
  78.8 3.1 %and.46 = pred[128,128]{1,0:T(32,128)(4,1)S(1)} reshape(pred[4,16,2,4,16,2]{5,4,3,2,1,0:T(8,128)(4,1)S(1)} %broadcast_and_fusion) | data formatting | bytes 32768 | tf_op jit(solution)/shard_map/and | solution.py:125
  81.9 6.2 %all-to-all-done = bf16[64,2,768]{2,1,0:T(2,128)(2,1)S(1)} async-done(((bf16[64,2,768]{2,1,0:T(2,128)(2,1)}), bf16[64,2,768]{2,1,0:T(2,128)(2,1)S(1)}, u32[]{:S(2)}, u32[]{:S(2)}) %all-to-all-start) | async-done | bytes 196640 | tf_op jit(solution)/shard_map/all_to_all | solution.py:121
  88.2 0.2 convolution_convert_fusion
  88.4 0.8 reshape.91
  89.2 5.8 %all-to-all-start.1 = ((bf16[64,2,768]{2,1,0:T(2,128)(2,1)}), bf16[64,2,768]{2,1,0:T(2,128)(2,1)S(1)}, u32[]{:S(2)}, u32[]{:S(2)}) async-start(bf16[64,2,768]{2,1,0:T(2,128)(2,1)} %reshape.91), calls=%async_computation.1 | async-start | bytes 393216 | tf_op jit(solution)/shard_map/all_to_all | solution.py:132
  95.0 10.1 %all-to-all-done.1 = bf16[64,2,768]{2,1,0:T(2,128)(2,1)S(1)} async-done(((bf16[64,2,768]{2,1,0:T(2,128)(2,1)}), bf16[64,2,768]{2,1,0:T(2,128)(2,1)S(1)}, u32[]{:S(2)}, u32[]{:S(2)}) %all-to-all-start.1) | async-done | bytes 196640 | tf_op jit(solution)/shard_map/all_to_all | solution.py:132
  105.3 16.5 %all_gather.3 = bf16[256,1536]{1,0:T(8,128)(2,1)S(1)} all-gather(bf16[64,1536]{1,0:T(8,128)(2,1)S(1)} %pad_maximum_fusion.3), channel_id=1, replica_groups=mesh['group'=4,'x'=4,'z'=4,'h'=2,'c'=2] {'h','c'}, dimensions={0}, use_global_device_ids=true | all-gather | bytes 983040 | tf_op jit(solution)/shard_map/all_gather | solution.py:139
  121.9 0.2 fusion.9
  122.0 0.2 fusion.8
  122.2 3.8 %fusion.4 = bf16[256,3072]{1,0:T(8,128)(2,1)S(1)} fusion(bf16[256,768]{1,0:T(8,128)(2,1)S(1)} %bitcast.86, bf16[2,768,3072]{2,1,0:T(8,128)(2,1)} %copy-done.1), kind=kOutput, calls=%fused_computation.6 | convolution fusion | flops 1208745984 | bytes 6684672 | tf_op jit(solution)/shard_map/sm,mk->sk/dot_general | solution.py:144
  126.0 3.8 %fusion.5 = bf16[256,3072]{1,0:T(8,128)(2,1)S(1)} fusion(bf16[256,768]{1,0:T(8,128)(2,1)S(1)} %bitcast.85, bf16[2,768,3072]{2,1,0:T(8,128)(2,1)} %copy-done.1), kind=kOutput, calls=%fused_computation.7 | convolution fusion | flops 1208745984 | bytes 6684672 | tf_op jit(solution)/shard_map/sm,mk->sk/dot_general | solution.py:144
  129.8 0.7 collective-permute-start.19
  130.5 2.7 %collective-permute-start.18 = (bf16[64,3072]{1,0:T(8,128)(2,1)S(1)}, bf16[64,3072]{1,0:T(8,128)(2,1)S(1)}, u32[]{:S(2)}, u32[]{:S(2)}) collective-permute-start(bf16[64,3072]{1,0:T(8,128)(2,1)S(1)} %get-tuple-element.19), channel_id=1, source_target_pairs={{0,48},{16,0},{32,16},{48,32},{1,49},{17,1},{33,17},{49,33},{2,50}... | collective-permute-start | bytes 1179656 | tf_op jit(solution)/shard_map/ppermute | solution.py:18
  133.2 0.1 collective-permute-start.26
  133.3 3.2 %collective-permute-start.25 = (bf16[64,3072]{1,0:T(8,128)(2,1)S(1)}, bf16[64,3072]{1,0:T(8,128)(2,1)S(1)}, u32[]{:S(2)}, u32[]{:S(2)}) collective-permute-start(bf16[64,3072]{1,0:T(8,128)(2,1)S(1)} %get-tuple-element.21), channel_id=1, source_target_pairs={{0,48},{16,0},{32,16},{48,32},{1,49},{17,1},{33,17},{49,33},{2,50}... | collective-permute-start | bytes 1179656 | tf_op jit(solution)/shard_map/ppermute | solution.py:18
  136.5 6.5 %collective-permute-done.19 = bf16[64,3072]{1,0:T(8,128)(2,1)S(1)} collective-permute-done((bf16[64,3072]{1,0:T(8,128)(2,1)S(1)}, bf16[64,3072]{1,0:T(8,128)(2,1)S(1)}, u32[]{:S(2)}, u32[]{:S(2)}) %collective-permute-start.19) | collective-permute-done | bytes 393248 | tf_op jit(solution)/shard_map/ppermute | solution.py:18
  143.1 0.1 collective-permute-start.20
  143.2 8.3 %collective-permute-done.26 = bf16[64,3072]{1,0:T(8,128)(2,1)S(1)} collective-permute-done((bf16[64,3072]{1,0:T(8,128)(2,1)S(1)}, bf16[64,3072]{1,0:T(8,128)(2,1)S(1)}, u32[]{:S(2)}, u32[]{:S(2)}) %collective-permute-start.26) | collective-permute-done | bytes 393248 | tf_op jit(solution)/shard_map/ppermute | solution.py:18
  151.6 4.1 %collective-permute-done.20 = bf16[32,3072]{1,0:T(8,128)(2,1)S(1)} collective-permute-done((bf16[32,3072]{1,0:T(8,128)(2,1)S(1)}, bf16[32,3072]{1,0:T(8,128)(2,1)S(1)}, u32[]{:S(2)}, u32[]{:S(2)}) %collective-permute-start.20) | collective-permute-done | bytes 196640 | tf_op jit(solution)/shard_map/ppermute | solution.py:18
  155.7 0.1 convert_add_fusion.3
  155.9 0.1 collective-permute-start.22
  156.0 3.3 %collective-permute-done.27 = bf16[32,3072]{1,0:T(8,128)(2,1)S(1)} collective-permute-done((bf16[32,3072]{1,0:T(8,128)(2,1)S(1)}, bf16[32,3072]{1,0:T(8,128)(2,1)S(1)}, u32[]{:S(2)}, u32[]{:S(2)}) %collective-permute-start.27) | collective-permute-done | bytes 196640 | tf_op jit(solution)/shard_map/ppermute | solution.py:18
  159.3 0.1 convert_add_fusion.2
  159.6 0.1 collective-permute-start.29
  159.6 2.8 %collective-permute-done.22 = bf16[32,3072]{1,0:T(8,128)(2,1)S(1)} collective-permute-done((bf16[32,3072]{1,0:T(8,128)(2,1)S(1)}, bf16[32,3072]{1,0:T(8,128)(2,1)S(1)}, u32[]{:S(2)}, u32[]{:S(2)}) %collective-permute-start.22) | collective-permute-done | bytes 196640 | tf_op jit(solution)/shard_map/ppermute | solution.py:18
  162.6 3.9 %collective-permute-start.23 = (bf16[16,3072]{1,0:T(8,128)(2,1)S(1)}, bf16[16,3072]{1,0:T(8,128)(2,1)S(1)}, u32[]{:S(2)}, u32[]{:S(2)}) collective-permute-start(bf16[16,3072]{1,0:T(8,128)(2,1)S(1)} %get-tuple-element.24), channel_id=1, source_target_pairs={{0,8},{4,12},{8,0},{12,4},{1,9},{5,13},{9,1},{13,5},{2,10},{6,14},... | collective-permute-start | bytes 294920 | tf_op jit(solution)/shard_map/ppermute | solution.py:18
  166.6 3.2 %collective-permute-start.30 = (bf16[16,3072]{1,0:T(8,128)(2,1)S(1)}, bf16[16,3072]{1,0:T(8,128)(2,1)S(1)}, u32[]{:S(2)}, u32[]{:S(2)}) collective-permute-start(bf16[16,3072]{1,0:T(8,128)(2,1)S(1)} %get-tuple-element.26), channel_id=1, source_target_pairs={{0,8},{4,12},{8,0},{12,4},{1,9},{5,13},{9,1},{13,5},{2,10},{6,14},... | collective-permute-start | bytes 294920 | tf_op jit(solution)/shard_map/ppermute | solution.py:18
  169.8 0.4 collective-permute-start.31
  170.2 4.9 %collective-permute-done.24 = bf16[16,3072]{1,0:T(8,128)(2,1)S(1)} collective-permute-done((bf16[16,3072]{1,0:T(8,128)(2,1)S(1)}, bf16[16,3072]{1,0:T(8,128)(2,1)S(1)}, u32[]{:S(2)}, u32[]{:S(2)}) %collective-permute-start.24) | collective-permute-done | bytes 98336 | tf_op jit(solution)/shard_map/ppermute | solution.py:18
  175.2 2.3 %collective-permute-done.31 = bf16[16,3072]{1,0:T(8,128)(2,1)S(1)} collective-permute-done((bf16[16,3072]{1,0:T(8,128)(2,1)S(1)}, bf16[16,3072]{1,0:T(8,128)(2,1)S(1)}, u32[]{:S(2)}, u32[]{:S(2)}) %collective-permute-start.31) | collective-permute-done | bytes 98336 | tf_op jit(solution)/shard_map/ppermute | solution.py:18
  177.6 0.9 copy.32
  (94 shorter events, 2.2 us)
Async XLA Ops:
  0.6 10.9 %copy-start.5 = (s32[8]{0:T(128)S(1)}, s32[8]{0:T(128)}, u32[]{:S(2)}) copy-start(s32[8]{0:T(128)} %param.10) | copy-start | bytes 100
  0.6 11.0 %copy-start.4 = (s32[8,16]{1,0:T(8,128)S(1)}, s32[8,16]{1,0:T(8,128)}, u32[]{:S(2)}) copy-start(s32[8,16]{1,0:T(8,128)} %param.11) | copy-start | bytes 1540
  0.7 11.2 %copy-start.6 = (s32[8]{0:T(128)S(1)}, s32[8]{0:T(128)}, u32[]{:S(2)}) copy-start(s32[8]{0:T(128)} %param.9) | copy-start | bytes 100
  2.1 17.0 %collective-permute-start.2 = (bf16[16,3072]{1,0:T(8,128)(2,1)S(1)}, bf16[16,3072]{1,0:T(8,128)(2,1)S(1)}, u32[]{:S(2)}, u32[]{:S(2)}) collective-permute-start(bf16[16,3072]{1,0:T(8,128)(2,1)S(1)} %get-tuple-element.11), channel_id=1, source_target_pairs={{0,4},{4,8},{8,12},{12,0},{1,5},{5,9},{9,13},{13,1},{2,6},{6,10},{... | collective-permute-start | bytes 294920 | tf_op jit(solution)/shard_map/ppermute | solution.py:18
  4.1 15.2 %collective-permute-start.1 = (bf16[16,3072]{1,0:T(8,128)(2,1)S(1)}, bf16[16,3072]{1,0:T(8,128)(2,1)S(1)}, u32[]{:S(2)}, u32[]{:S(2)}) collective-permute-start(bf16[16,3072]{1,0:T(8,128)(2,1)S(1)} %get-tuple-element.11), channel_id=1, source_target_pairs={{0,8},{4,12},{8,0},{12,4},{1,9},{5,13},{9,1},{13,5},{2,10},{6,14},... | collective-permute-start | bytes 294920 | tf_op jit(solution)/shard_map/ppermute | solution.py:18
  6.4 12.9 %collective-permute-start = (bf16[16,3072]{1,0:T(8,128)(2,1)S(1)}, bf16[16,3072]{1,0:T(8,128)(2,1)S(1)}, u32[]{:S(2)}, u32[]{:S(2)}) collective-permute-start(bf16[16,3072]{1,0:T(8,128)(2,1)S(1)} %get-tuple-element.11), channel_id=1, source_target_pairs={{0,12},{4,0},{8,4},{12,8},{1,13},{5,1},{9,5},{13,9},{2,14},{6,2},{... | collective-permute-start | bytes 294920 | tf_op jit(solution)/shard_map/ppermute | solution.py:18
  8.1 14.0 %collective-permute-start.11 = (bf16[16,3072]{1,0:T(8,128)(2,1)S(1)}, bf16[16,3072]{1,0:T(8,128)(2,1)S(1)}, u32[]{:S(2)}, u32[]{:S(2)}) collective-permute-start(bf16[16,3072]{1,0:T(8,128)(2,1)S(1)} %get-tuple-element.13), channel_id=1, source_target_pairs={{0,4},{4,8},{8,12},{12,0},{1,5},{5,9},{9,13},{13,1},{2,6},{6,10},{... | collective-permute-start | bytes 294920 | tf_op jit(solution)/shard_map/ppermute | solution.py:18
  9.1 13.1 %collective-permute-start.10 = (bf16[16,3072]{1,0:T(8,128)(2,1)S(1)}, bf16[16,3072]{1,0:T(8,128)(2,1)S(1)}, u32[]{:S(2)}, u32[]{:S(2)}) collective-permute-start(bf16[16,3072]{1,0:T(8,128)(2,1)S(1)} %get-tuple-element.13), channel_id=1, source_target_pairs={{0,8},{4,12},{8,0},{12,4},{1,9},{5,13},{9,1},{13,5},{2,10},{6,14},... | collective-permute-start | bytes 294920 | tf_op jit(solution)/shard_map/ppermute | solution.py:18
  11.9 3.7 %copy-start = (bf16[2,768,3072]{2,1,0:T(8,128)(2,1)S(1)}, bf16[2,768,3072]{2,1,0:T(8,128)(2,1)}, u32[]{:S(2)}) copy-start(bf16[2,768,3072]{2,1,0:T(8,128)(2,1)} %fronts_ref.1) | copy-start | bytes 28311556
  19.1 32.1 %copy-start.1 = (bf16[2,768,3072]{2,1,0:T(8,128)(2,1)}, bf16[2,768,3072]{2,1,0:T(8,128)(2,1)S(1)}, u32[]{:S(2)}) copy-start(bf16[2,768,3072]{2,1,0:T(8,128)(2,1)S(1)} %shard_map.77) | copy-start | bytes 28311556
  19.1 7.6 %copy-start.3 = (bf16[256,3072]{1,0:T(8,128)(2,1)S(1)}, bf16[256,3072]{1,0:T(8,128)(2,1)}, u32[]{:S(2)}) copy-start(bf16[256,3072]{1,0:T(8,128)(2,1)} %get-tuple-element.12) | copy-start | bytes 4718596
  19.1 4.7 %collective-permute-start.9 = (bf16[16,3072]{1,0:T(8,128)(2,1)S(1)}, bf16[16,3072]{1,0:T(8,128)(2,1)S(1)}, u32[]{:S(2)}, u32[]{:S(2)}) collective-permute-start(bf16[16,3072]{1,0:T(8,128)(2,1)S(1)} %get-tuple-element.13), channel_id=1, source_target_pairs={{0,12},{4,0},{8,4},{12,8},{1,13},{5,1},{9,5},{13,9},{2,14},{6,2},{... | collective-permute-start | bytes 294920 | tf_op jit(solution)/shard_map/ppermute | solution.py:18
  19.3 16.2 %collective-permute-start.5 = (bf16[64,3072]{1,0:T(8,128)(2,1)S(1)}, bf16[64,3072]{1,0:T(8,128)(2,1)S(1)}, u32[]{:S(2)}, u32[]{:S(2)}) collective-permute-start(bf16[64,3072]{1,0:T(8,128)(2,1)S(1)} %pad_maximum_fusion), channel_id=1, source_target_pairs={{0,48},{16,0},{32,16},{48,32},{1,49},{17,1},{33,17},{49,33},{2,50}... | collective-permute-start | bytes 1179656 | tf_op jit(solution)/shard_map/ppermute | solution.py:18
  22.1 13.3 %collective-permute-start.3 = (bf16[64,3072]{1,0:T(8,128)(2,1)S(1)}, bf16[64,3072]{1,0:T(8,128)(2,1)S(1)}, u32[]{:S(2)}, u32[]{:S(2)}) collective-permute-start(bf16[64,3072]{1,0:T(8,128)(2,1)S(1)} %pad_maximum_fusion), channel_id=1, source_target_pairs={{0,16},{16,32},{32,48},{48,0},{1,17},{17,33},{33,49},{49,1},{2,18}... | collective-permute-start | bytes 1179656 | tf_op jit(solution)/shard_map/ppermute | solution.py:18
  23.9 16.2 %collective-permute-start.14 = (bf16[64,3072]{1,0:T(8,128)(2,1)S(1)}, bf16[64,3072]{1,0:T(8,128)(2,1)S(1)}, u32[]{:S(2)}, u32[]{:S(2)}) collective-permute-start(bf16[64,3072]{1,0:T(8,128)(2,1)S(1)} %pad_maximum_fusion.1), channel_id=1, source_target_pairs={{0,48},{16,0},{32,16},{48,32},{1,49},{17,1},{33,17},{49,33},{2,50}... | collective-permute-start | bytes 1179656 | tf_op jit(solution)/shard_map/ppermute | solution.py:18
  26.7 17.2 %collective-permute-start.12 = (bf16[64,3072]{1,0:T(8,128)(2,1)S(1)}, bf16[64,3072]{1,0:T(8,128)(2,1)S(1)}, u32[]{:S(2)}, u32[]{:S(2)}) collective-permute-start(bf16[64,3072]{1,0:T(8,128)(2,1)S(1)} %pad_maximum_fusion.1), channel_id=1, source_target_pairs={{0,16},{16,32},{32,48},{48,0},{1,17},{17,33},{33,49},{49,1},{2,18}... | collective-permute-start | bytes 1179656 | tf_op jit(solution)/shard_map/ppermute | solution.py:18
  35.4 12.2 %collective-permute-start.4 = (bf16[32,3072]{1,0:T(8,128)(2,1)S(1)}, bf16[32,3072]{1,0:T(8,128)(2,1)S(1)}, u32[]{:S(2)}, u32[]{:S(2)}) collective-permute-start(bf16[32,3072]{1,0:T(8,128)(2,1)S(1)} %slice.168), channel_id=1, source_target_pairs={{0,16},{16,32},{32,48},{48,0},{1,17},{17,33},{33,49},{49,1},{2,18}... | collective-permute-start | bytes 589832 | tf_op jit(solution)/shard_map/ppermute | solution.py:18
  35.6 12.1 %collective-permute-start.6 = (bf16[32,3072]{1,0:T(8,128)(2,1)S(1)}, bf16[32,3072]{1,0:T(8,128)(2,1)S(1)}, u32[]{:S(2)}, u32[]{:S(2)}) collective-permute-start(bf16[32,3072]{1,0:T(8,128)(2,1)S(1)} %slice.169), channel_id=1, source_target_pairs={{0,48},{16,0},{32,16},{48,32},{1,49},{17,1},{33,17},{49,33},{2,50}... | collective-permute-start | bytes 589832 | tf_op jit(solution)/shard_map/ppermute | solution.py:18
  40.1 10.9 %collective-permute-start.15 = (bf16[32,3072]{1,0:T(8,128)(2,1)S(1)}, bf16[32,3072]{1,0:T(8,128)(2,1)S(1)}, u32[]{:S(2)}, u32[]{:S(2)}) collective-permute-start(bf16[32,3072]{1,0:T(8,128)(2,1)S(1)} %slice.172), channel_id=1, source_target_pairs={{0,48},{16,0},{32,16},{48,32},{1,49},{17,1},{33,17},{49,33},{2,50}... | collective-permute-start | bytes 589832 | tf_op jit(solution)/shard_map/ppermute | solution.py:18
  43.9 7.1 %collective-permute-start.13 = (bf16[32,3072]{1,0:T(8,128)(2,1)S(1)}, bf16[32,3072]{1,0:T(8,128)(2,1)S(1)}, u32[]{:S(2)}, u32[]{:S(2)}) collective-permute-start(bf16[32,3072]{1,0:T(8,128)(2,1)S(1)} %slice.171), channel_id=1, source_target_pairs={{0,16},{16,32},{32,48},{48,0},{1,17},{17,33},{33,49},{49,1},{2,18}... | collective-permute-start | bytes 589832 | tf_op jit(solution)/shard_map/ppermute | solution.py:18
  49.2 3.6 %collective-permute-start.7 = (bf16[2,64,768]{2,1,0:T(8,128)(2,1)S(1)}, bf16[2,64,768]{2,1,0:T(8,128)(2,1)S(1)}, u32[]{:S(2)}, u32[]{:S(2)}) collective-permute-start(bf16[2,64,768]{2,1,0:T(8,128)(2,1)S(1)} %dynamic-slice_bitcast_fusion.1), channel_id=1, source_target_pairs={{0,1},{1,0},{2,3},{3,2},{4,5},{5,4},{6,7},{7,6},{8,9},{9,8},{10,11... | collective-permute-start | bytes 589832 | tf_op jit(solution)/shard_map/ppermute | solution.py:18
  52.7 6.0 %collective-permute-start.16 = (bf16[2,64,768]{2,1,0:T(8,128)(2,1)S(1)}, bf16[2,64,768]{2,1,0:T(8,128)(2,1)S(1)}, u32[]{:S(2)}, u32[]{:S(2)}) collective-permute-start(bf16[2,64,768]{2,1,0:T(8,128)(2,1)S(1)} %dynamic-slice_bitcast_fusion), channel_id=1, source_target_pairs={{0,1},{1,0},{2,3},{3,2},{4,5},{5,4},{6,7},{7,6},{8,9},{9,8},{10,11... | collective-permute-start | bytes 589832 | tf_op jit(solution)/shard_map/ppermute | solution.py:18
  52.9 12.2 %collective-permute-start.8 = (bf16[64,768]{1,0:T(8,128)(2,1)S(1)}, bf16[64,768]{1,0:T(8,128)(2,1)S(1)}, u32[]{:S(2)}, u32[]{:S(2)}) collective-permute-start(bf16[64,768]{1,0:T(8,128)(2,1)S(1)} %fusion.18), channel_id=1, source_target_pairs={{0,2},{2,0},{1,3},{3,1},{4,6},{6,4},{5,7},{7,5},{8,10},{10,8},{9,1... | collective-permute-start | bytes 294920 | tf_op jit(solution)/shard_map/ppermute | solution.py:18
  58.7 11.0 %collective-permute-start.17 = (bf16[64,768]{1,0:T(8,128)(2,1)S(1)}, bf16[64,768]{1,0:T(8,128)(2,1)S(1)}, u32[]{:S(2)}, u32[]{:S(2)}) collective-permute-start(bf16[64,768]{1,0:T(8,128)(2,1)S(1)} %fusion.19), channel_id=1, source_target_pairs={{0,2},{2,0},{1,3},{3,1},{4,6},{6,4},{5,7},{7,5},{8,10},{10,8},{9,1... | collective-permute-start | bytes 294920 | tf_op jit(solution)/shard_map/ppermute | solution.py:18
  70.7 17.4 %all-to-all-start = ((bf16[64,2,768]{2,1,0:T(2,128)(2,1)}), bf16[64,2,768]{2,1,0:T(2,128)(2,1)S(1)}, u32[]{:S(2)}, u32[]{:S(2)}) async-start(bf16[64,2,768]{2,1,0:T(2,128)(2,1)} %copy.31), calls=%async_computation | async-start | bytes 393216 | tf_op jit(solution)/shard_map/all_to_all | solution.py:121
  78.8 26.3 %copy-start.2 = (bf16[64,2,768]{2,1,0:T(2,128)(2,1)S(1)}, bf16[64,2,768]{2,1,0:T(2,128)(2,1)}, u32[]{:S(2)}) copy-start(bf16[64,2,768]{2,1,0:T(2,128)(2,1)} %param.8) | copy-start | bytes 589828
  89.2 15.9 %all-to-all-start.1 = ((bf16[64,2,768]{2,1,0:T(2,128)(2,1)}), bf16[64,2,768]{2,1,0:T(2,128)(2,1)S(1)}, u32[]{:S(2)}, u32[]{:S(2)}) async-start(bf16[64,2,768]{2,1,0:T(2,128)(2,1)} %reshape.91), calls=%async_computation.1 | async-start | bytes 393216 | tf_op jit(solution)/shard_map/all_to_all | solution.py:132
  129.8 13.2 %collective-permute-start.19 = (bf16[64,3072]{1,0:T(8,128)(2,1)S(1)}, bf16[64,3072]{1,0:T(8,128)(2,1)S(1)}, u32[]{:S(2)}, u32[]{:S(2)}) collective-permute-start(bf16[64,3072]{1,0:T(8,128)(2,1)S(1)} %get-tuple-element.18), channel_id=1, source_target_pairs={{0,16},{16,32},{32,48},{48,0},{1,17},{17,33},{33,49},{49,1},{2,18}... | collective-permute-start | bytes 1179656 | tf_op jit(solution)/shard_map/ppermute | solution.py:18
  130.5 21.1 %collective-permute-start.18 = (bf16[64,3072]{1,0:T(8,128)(2,1)S(1)}, bf16[64,3072]{1,0:T(8,128)(2,1)S(1)}, u32[]{:S(2)}, u32[]{:S(2)}) collective-permute-start(bf16[64,3072]{1,0:T(8,128)(2,1)S(1)} %get-tuple-element.19), channel_id=1, source_target_pairs={{0,48},{16,0},{32,16},{48,32},{1,49},{17,1},{33,17},{49,33},{2,50}... | collective-permute-start | bytes 1179656 | tf_op jit(solution)/shard_map/ppermute | solution.py:18
  133.2 18.3 %collective-permute-start.26 = (bf16[64,3072]{1,0:T(8,128)(2,1)S(1)}, bf16[64,3072]{1,0:T(8,128)(2,1)S(1)}, u32[]{:S(2)}, u32[]{:S(2)}) collective-permute-start(bf16[64,3072]{1,0:T(8,128)(2,1)S(1)} %get-tuple-element.20), channel_id=1, source_target_pairs={{0,16},{16,32},{32,48},{48,0},{1,17},{17,33},{33,49},{49,1},{2,18}... | collective-permute-start | bytes 1179656 | tf_op jit(solution)/shard_map/ppermute | solution.py:18
  133.3 22.7 %collective-permute-start.25 = (bf16[64,3072]{1,0:T(8,128)(2,1)S(1)}, bf16[64,3072]{1,0:T(8,128)(2,1)S(1)}, u32[]{:S(2)}, u32[]{:S(2)}) collective-permute-start(bf16[64,3072]{1,0:T(8,128)(2,1)S(1)} %get-tuple-element.21), channel_id=1, source_target_pairs={{0,48},{16,0},{32,16},{48,32},{1,49},{17,1},{33,17},{49,33},{2,50}... | collective-permute-start | bytes 1179656 | tf_op jit(solution)/shard_map/ppermute | solution.py:18
  143.1 12.6 %collective-permute-start.20 = (bf16[32,3072]{1,0:T(8,128)(2,1)S(1)}, bf16[32,3072]{1,0:T(8,128)(2,1)S(1)}, u32[]{:S(2)}, u32[]{:S(2)}) collective-permute-start(bf16[32,3072]{1,0:T(8,128)(2,1)S(1)} %add_convert_fusion.5), channel_id=1, source_target_pairs={{0,16},{16,32},{32,48},{48,0},{1,17},{17,33},{33,49},{49,1},{2,18}... | collective-permute-start | bytes 589832 | tf_op jit(solution)/shard_map/ppermute | solution.py:18
  151.5 7.8 %collective-permute-start.27 = (bf16[32,3072]{1,0:T(8,128)(2,1)S(1)}, bf16[32,3072]{1,0:T(8,128)(2,1)S(1)}, u32[]{:S(2)}, u32[]{:S(2)}) collective-permute-start(bf16[32,3072]{1,0:T(8,128)(2,1)S(1)} %add_convert_fusion.2), channel_id=1, source_target_pairs={{0,16},{16,32},{32,48},{48,0},{1,17},{17,33},{33,49},{49,1},{2,18}... | collective-permute-start | bytes 589832 | tf_op jit(solution)/shard_map/ppermute | solution.py:18
  155.8 14.0 %collective-permute-start.21 = (bf16[16,3072]{1,0:T(8,128)(2,1)S(1)}, bf16[16,3072]{1,0:T(8,128)(2,1)S(1)}, u32[]{:S(2)}, u32[]{:S(2)}) collective-permute-start(bf16[16,3072]{1,0:T(8,128)(2,1)S(1)} %slice.257), channel_id=1, source_target_pairs={{0,4},{4,8},{8,12},{12,0},{1,5},{5,9},{9,13},{13,1},{2,6},{6,10},{... | collective-permute-start | bytes 294920 | tf_op jit(solution)/shard_map/ppermute | solution.py:18
  155.9 6.5 %collective-permute-start.22 = (bf16[32,3072]{1,0:T(8,128)(2,1)S(1)}, bf16[32,3072]{1,0:T(8,128)(2,1)S(1)}, u32[]{:S(2)}, u32[]{:S(2)}) collective-permute-start(bf16[32,3072]{1,0:T(8,128)(2,1)S(1)} %get-tuple-element.15), channel_id=1, source_target_pairs={{0,48},{16,0},{32,16},{48,32},{1,49},{17,1},{33,17},{49,33},{2,50}... | collective-permute-start | bytes 589832 | tf_op jit(solution)/shard_map/ppermute | solution.py:18
  159.5 15.7 %collective-permute-start.28 = (bf16[16,3072]{1,0:T(8,128)(2,1)S(1)}, bf16[16,3072]{1,0:T(8,128)(2,1)S(1)}, u32[]{:S(2)}, u32[]{:S(2)}) collective-permute-start(bf16[16,3072]{1,0:T(8,128)(2,1)S(1)} %slice.256), channel_id=1, source_target_pairs={{0,4},{4,8},{8,12},{12,0},{1,5},{5,9},{9,13},{13,1},{2,6},{6,10},{... | collective-permute-start | bytes 294920 | tf_op jit(solution)/shard_map/ppermute | solution.py:18
  159.6 6.9 %collective-permute-start.29 = (bf16[32,3072]{1,0:T(8,128)(2,1)S(1)}, bf16[32,3072]{1,0:T(8,128)(2,1)S(1)}, u32[]{:S(2)}, u32[]{:S(2)}) collective-permute-start(bf16[32,3072]{1,0:T(8,128)(2,1)S(1)} %get-tuple-element.17), channel_id=1, source_target_pairs={{0,48},{16,0},{32,16},{48,32},{1,49},{17,1},{33,17},{49,33},{2,50}... | collective-permute-start | bytes 589832 | tf_op jit(solution)/shard_map/ppermute | solution.py:18
  162.6 7.6 %collective-permute-start.23 = (bf16[16,3072]{1,0:T(8,128)(2,1)S(1)}, bf16[16,3072]{1,0:T(8,128)(2,1)S(1)}, u32[]{:S(2)}, u32[]{:S(2)}) collective-permute-start(bf16[16,3072]{1,0:T(8,128)(2,1)S(1)} %get-tuple-element.24), channel_id=1, source_target_pairs={{0,8},{4,12},{8,0},{12,4},{1,9},{5,13},{9,1},{13,5},{2,10},{6,14},... | collective-permute-start | bytes 294920 | tf_op jit(solution)/shard_map/ppermute | solution.py:18
  166.5 8.6 %collective-permute-start.24 = (bf16[16,3072]{1,0:T(8,128)(2,1)S(1)}, bf16[16,3072]{1,0:T(8,128)(2,1)S(1)}, u32[]{:S(2)}, u32[]{:S(2)}) collective-permute-start(bf16[16,3072]{1,0:T(8,128)(2,1)S(1)} %get-tuple-element.25), channel_id=1, source_target_pairs={{0,12},{4,0},{8,4},{12,8},{1,13},{5,1},{9,5},{13,9},{2,14},{6,2},{... | collective-permute-start | bytes 294920 | tf_op jit(solution)/shard_map/ppermute | solution.py:18
  166.6 8.6 %collective-permute-start.30 = (bf16[16,3072]{1,0:T(8,128)(2,1)S(1)}, bf16[16,3072]{1,0:T(8,128)(2,1)S(1)}, u32[]{:S(2)}, u32[]{:S(2)}) collective-permute-start(bf16[16,3072]{1,0:T(8,128)(2,1)S(1)} %get-tuple-element.26), channel_id=1, source_target_pairs={{0,8},{4,12},{8,0},{12,4},{1,9},{5,13},{9,1},{13,5},{2,10},{6,14},... | collective-permute-start | bytes 294920 | tf_op jit(solution)/shard_map/ppermute | solution.py:18
  169.8 7.7 %collective-permute-start.31 = (bf16[16,3072]{1,0:T(8,128)(2,1)S(1)}, bf16[16,3072]{1,0:T(8,128)(2,1)S(1)}, u32[]{:S(2)}, u32[]{:S(2)}) collective-permute-start(bf16[16,3072]{1,0:T(8,128)(2,1)S(1)} %get-tuple-element.27), channel_id=1, source_target_pairs={{0,12},{4,0},{8,4},{12,8},{1,13},{5,1},{9,5},{13,9},{2,14},{6,2},{... | collective-permute-start | bytes 294920 | tf_op jit(solution)/shard_map/ppermute | solution.py:18
where the time goes:
time: 179 us; the launch traced here: 178 us
  waiting for transfers between devices  74.9 us (42%)
  starting transfers between devices  57 us (32%)
  blocking collectives  16.5 us (9%)
  local copies, waits for them, and re-layouts  12.4 us (7%)
  matrix products  10.6 us (6%)
  Pallas kernels  3.47 us (2%)
  other arithmetic  2.24 us (1%)
    ppermute x32, waiting for transfers between devices, shift(): return lax.ppermute(value, axis, [(i, (i + by) % n) for i in range(n)])  58.7 us
    ppermute x32, starting transfers between devices, shift(): return lax.ppermute(value, axis, [(i, (i + by) % n) for i in range(n)])  43.8 us
    all_gather x1, blocking collectives, shards(): lax.all_gather(jnp.concatenate(mine, axis=1), COL, axis=0, tiled=True)  16.5 us
    all_to_all x1, waiting for transfers between devices, shards(): lax.all_to_all(extension, spread, split_axis=0, concat_axis=0, tiled=True)  10.1 us
    dot_general x2, matrix products, shards(): jnp.einsum('sm,mk->sk', ordered, masked[f], preferred_element_type=F32)  7.53 us
    all_to_all x1, starting transfers between devices, shards(): lax.all_to_all(sampled, spread, split_axis=0, concat_axis=0, tiled=True)  7.32 us
    unnamed x30, local copies, waits for them, and re-layouts  6.34 us
    all_to_all x1, waiting for transfers between devices, shards(): lax.all_to_all(sampled, spread, split_axis=0, concat_axis=0, tiled=True)  6.22 us
  transfers between devices with their start and end apart: 34, of which 16 were waited for; matrix products, arithmetic and copies ran while one was open for 5% of the time, Pallas kernels for 2%

commit v1 on v0

v1 whole, which is shorter than its diff:
```python
import jax
import jax.numpy as jnp
from jax import lax
from jax.experimental import pallas as pl
from jax.experimental.pallas import tpu as pltpu
from jax.sharding import Mesh
from jax.sharding import PartitionSpec as P

DEVICES = ("group", "x", "z", "h", "c")
ROW = ("x", "z")
COL = ("h", "c")
F32 = jnp.float32
BF16 = jnp.bfloat16


def shift(value, axis, by):
    n = lax.axis_size(axis)
    return lax.ppermute(value, axis, [(i, (i + by) % n) for i in range(n)])


def pick(value, index):
    return lax.dynamic_index_in_dim(value, index, 0, keepdims=False)


def rolled(value, starts):
    sizes = value.shape
    for axis in range(len(starts)):
        value = jnp.concatenate([value, value], axis=axis)
    starts = tuple(starts) + (0,) * (len(sizes) - len(starts))
    return lax.dynamic_slice(value, starts, sizes)


def gather_rows(columns):
    left = shift(columns, "x", 1)
    right = shift(columns, "x", -1)
    over = (shift(left[0], "x", 1), shift(right[1], "x", -1))
    return [jnp.concatenate([columns[f], over[f], left[f], right[f]], axis=0) for f in range(2)]


def mask_kernel(sizes_ref, origin_ref, fronts_ref, out_ref):
    tile = fronts_ref[...]
    size = sizes_ref[pl.program_id(0)]
    rows = origin_ref[0] + pl.program_id(1) * tile.shape[1] + lax.broadcasted_iota(jnp.int32, tile.shape, 1)
    cols = origin_ref[1] + lax.broadcasted_iota(jnp.int32, tile.shape, 2)
    out_ref[...] = jnp.where(jnp.maximum(rows, cols) < size, tile, jnp.zeros((), tile.dtype))


def masked_fronts(fronts, sizes, origin):
    local, rows, cols = fronts.shape
    step = 64
    spec = pl.BlockSpec((1, step, cols), lambda f, i: (f, i, 0))
    scalars = pl.BlockSpec(memory_space=pltpu.SMEM)
    return pl.pallas_call(
        mask_kernel,
        grid=(local, rows // step),
        in_specs=[scalars, scalars, spec],
        out_specs=spec,
        out_shape=jax.ShapeDtypeStruct(fronts.shape, fronts.dtype),
        compiler_params=pltpu.CompilerParams(vmem_limit_bytes=4 << 20),
    )(sizes, origin, fronts)


def reduce_core(partial, x, c):
    odd = (x - c) & 1
    received = shift(pick(partial, 1 - odd), "c", 1)
    total = pick(partial, odd).astype(F32) + received.astype(F32)
    return rolled(total, (((x - odd) & 3) >> 1,))


def first_pieces(product):
    block = product.shape[0] // 4
    half = block // 2
    to_right = product[block + half : 2 * block + half]
    to_left = jnp.concatenate([product[block : block + half], product[3 * block + half :]], axis=0)
    return to_right, to_left


def scatter_rows(products, pieces):
    block = products[0].shape[0] // 4
    half = block // 2
    rows = block // 4
    near = []
    for to_right, to_left in pieces:
        near.append(lax.optimization_barrier((shift(to_right, "x", 1), shift(to_left, "x", -1))))
    far = []
    for product, (from_left, from_right) in zip(products, near):
        over_right = product[2 * block + half : 3 * block].astype(F32) + from_left[:half].astype(F32)
        over_left = product[3 * block : 3 * block + half].astype(F32) + from_right[:half].astype(F32)
        over_right = shift(over_right.astype(BF16), "x", 1)
        over_left = shift(over_left.astype(BF16), "x", -1)
        far.append(lax.optimization_barrier((over_right, over_left)))
    totals = []
    for product, (from_left, from_right), (over_right, over_left) in zip(products, near, far):
        top = product[:half].astype(F32) + from_left[half:].astype(F32) + over_left.astype(F32)
        low = product[half:block].astype(F32) + from_right[half:].astype(F32) + over_right.astype(F32)
        own = jnp.concatenate([top, low], axis=0)
        total = own[:rows]
        for k in (1, 2, 3):
            piece = own[k * rows : (k + 1) * rows].astype(BF16)
            total = total + shift(piece, "z", k).astype(F32)
        totals.append(total)
    return totals


def route_weight(parent_ids, block_maps, local):
    count, blocks = block_maps.shape
    order = (count // local, local, blocks)
    parent = jnp.broadcast_to(parent_ids[:, None], block_maps.shape).reshape(order)
    parent = parent.transpose(0, 2, 1).reshape(1, -1)
    block = block_maps.reshape(order).transpose(0, 2, 1).reshape(1, -1)
    index = lax.broadcasted_iota(jnp.int32, (count * blocks, 1), 0)
    to_parent = index // (blocks * local) * local + index % local
    to_block = index // local % blocks
    return ((parent == to_parent) & (block == to_block)).astype(BF16)


def shards(fronts, samples, second_samples, front_sizes, parent_ids, block_maps):
    local, tile_rows, tile_cols = fronts.shape
    own_rows = samples.shape[0]
    slab = second_samples.shape[0]
    group, x, z, h, c = (lax.axis_index(axis) for axis in DEVICES)
    row = lax.axis_index(ROW)
    col = lax.axis_index(COL)

    mine = jnp.stack([samples[:, f, :] for f in range(local)])
    columns = lax.all_gather(mine, "z", axis=1, tiled=True)
    gathered = gather_rows(columns)
    sizes = lax.dynamic_slice_in_dim(front_sizes, group * local, local, 0)
    second, sizes, columns = lax.optimization_barrier((second_samples, sizes, columns))
    second_of_pair = shift(second, "h", 1)
    masked = masked_fronts(fronts, sizes, jnp.stack([row * tile_rows, col * tile_cols]))
    weight = route_weight(parent_ids, block_maps, local)
    gathered[0], second_of_pair, weight = lax.optimization_barrier((gathered[0], second_of_pair, weight))
    second = rolled(jnp.stack([second, second_of_pair]), (h,))

    halves = []
    for f in range(local):
        partial = jnp.einsum("sk,mk->sm", gathered[f], masked[f], preferred_element_type=F32)
        halves.append(reduce_core(partial.astype(BF16).reshape(2, 2, slab, tile_rows), x, c))

    spread = ("h", "group") + ROW
    outgoing = jnp.stack([half.astype(BF16).reshape(2 * slab, tile_rows) for half in halves], axis=1)
    arrived = lax.all_to_all(outgoing, spread, split_axis=0, concat_axis=0, tiled=True)
    arrived = arrived[:slab].astype(F32) + arrived[slab:].astype(F32)
    arrived = arrived.astype(BF16).reshape(-1, tile_rows)
    extension = jnp.einsum("ij,jk->ik", weight, arrived, preferred_element_type=F32).astype(BF16)
    extension = extension.reshape(slab, local, tile_rows)
    extension = jnp.concatenate([extension, extension], axis=0)
    extension = lax.all_to_all(extension, spread, split_axis=0, concat_axis=0, tiled=True)
    combined = second.reshape(extension.shape).astype(F32) + extension.astype(F32)
    combined = combined.astype(BF16)

    nearer = ((x + ((c - x) & 1)) & 3) >> 1
    ordered = []
    for f in range(local):
        mine = combined[:, f, :].reshape(2, -1, own_rows, tile_rows)
        ordered.append(rolled(mine, (nearer, z)).reshape(2 * slab, tile_rows))
    everyone = lax.all_gather(jnp.stack(ordered), "c", axis=0)
    ordered = [rolled(everyone[:, f], (x & 1,)).reshape(4 * slab, tile_rows) for f in range(local)]
    products, pieces = [], []
    for f in range(local):
        if f > 0:
            ordered[f], pieces[0] = lax.optimization_barrier((ordered[f], pieces[0]))
        product = jnp.einsum("sm,mk->sk", ordered[f], masked[f], preferred_element_type=F32)
        products.append(product.astype(BF16))
        pieces.append(first_pieces(products[f]))

    away = jnp.stack([pick(half, 1 - h).astype(BF16) for half in halves])
    away, products[-1] = lax.optimization_barrier((away, products[-1]))
    received = shift(away, "h", 1)
    totals = scatter_rows(products, pieces)
    received, totals[0] = lax.optimization_barrier((received, totals[0]))
    slabs = [pick(half, h) + received[f].astype(F32) for f, half in enumerate(halves)]
    sampled = jnp.stack([total.astype(BF16) for total in slabs], axis=1)

    outs = [total.astype(BF16) for total in totals]
    return sampled, jnp.stack(outs, axis=1)


def solution(mesh):
    torus = Mesh(mesh.devices.reshape(mesh.shape["group"], 4, 4, 2, 2), DEVICES)
    in_specs = (P("group", ROW, COL), P(ROW, "group", COL), P(COL, "group", ROW), P(), P(), P())
    out_specs = (P(COL, "group", ROW), P(ROW, "group", COL))
    return jax.shard_map(
        shards, mesh=torus, in_specs=in_specs, out_specs=out_specs, check_vma=False
    )
```

time: 179 us -> 181 us (1.011)
  blocking collectives: 16.5 us -> 50.2 us
  waiting for transfers between devices: 74.9 us -> 49.1 us
  starting transfers between devices: 57 us -> 43.8 us
  other arithmetic: 2.24 us -> 12 us
  matrix products: 10.6 us -> 8.45 us
    all_to_all x0 -> x1, blocking collectives: none -> 29.1 us  [shards(): lax.all_to_all(outgoing, spread, split_axis=0, concat_axis=0, tiled=True)]
    ppermute x32 -> x22, waiting for transfers between devices: 58.7 us -> 32.7 us  [shift(): return lax.ppermute(value, axis, [(i, (i + by) % n) for i in range(n)])]
    all_to_all x1 -> x0, starting transfers between devices: 7.32 us -> none  [shards(): lax.all_to_all(sampled, spread, split_axis=0, concat_axis=0, tiled=True)]
    ppermute x32 -> x22, starting transfers between devices: 43.8 us -> 37.4 us  [shift(): return lax.ppermute(value, axis, [(i, (i + by) % n) for i in range(n)])]
    all_to_all x1, waiting for transfers between devices: 10.1 us -> 16.4 us  [shards(): lax.all_to_all(extension, spread, split_axis=0, concat_axis=0, tiled=True)]
    all_to_all x1 -> x0, waiting for transfers between devices: 6.22 us -> none  [shards(): lax.all_to_all(sampled, spread, split_axis=0, concat_axis=0, tiled=True)]
    all_gather x1 -> x2, blocking collectives: 16.5 us -> 21.1 us  [the longest x1 18.6 us: shards(): columns = lax.all_gather(mine, 'z', axis=1, tiled=True)]
    convert_element_type x5 -> x11, other arithmetic: 0.18 us -> 3.91 us  [the longest x2 2.89 us: scatter_rows(): over_left = shift(over_left.astype(BF16), 'x', -1)]
  transfers between devices with their start and end apart: 34 -> 23, of which waited for: 16 -> 12; matrix products, arithmetic and copies ran while one was open for 5% -> 7% of each run, Pallas kernels for 2% -> 2%
where the time goes in v1:
time: 181 us; the launch traced here: 180 us
  blocking collectives  50.2 us (28%)
  waiting for transfers between devices  49.1 us (27%)
  starting transfers between devices  43.8 us (24%)
  other arithmetic  12 us (7%)
  local copies, waits for them, and re-layouts  11.9 us (7%)
  matrix products  8.45 us (5%)
  Pallas kernels  3.47 us (2%)
    ppermute x22, starting transfers between devices, shift(): return lax.ppermute(value, axis, [(i, (i + by) % n) for i in range(n)])  37.4 us
    ppermute x22, waiting for transfers between devices, shift(): return lax.ppermute(value, axis, [(i, (i + by) % n) for i in range(n)])  32.7 us
    all_to_all x1, blocking collectives, shards(): lax.all_to_all(outgoing, spread, split_axis=0, concat_axis=0, tiled=True)  29.1 us
    all_gather x1, blocking collectives, shards(): columns = lax.all_gather(mine, 'z', axis=1, tiled=True)  18.6 us
    all_to_all x1, waiting for transfers between devices, shards(): lax.all_to_all(extension, spread, split_axis=0, concat_axis=0, tiled=True)  16.4 us
    all_to_all x1, starting transfers between devices, shards(): lax.all_to_all(extension, spread, split_axis=0, concat_axis=0, tiled=True)  6.41 us
    unnamed x18, local copies, waits for them, and re-layouts  5.47 us
    dot_general x2, matrix products, shards(): jnp.einsum('sm,mk->sk', ordered[f], masked[f], preferred_element_type=F32)  5.34 us
  transfers between devices with their start and end apart: 23, of which 12 were waited for; matrix products, arithmetic and copies ran while one was open for 7% of the time, Pallas kernels for 2%

profile of v1, /device:TPU:32, one launch (start us, length us, event | category | flops | bytes accessed | tf_op | source)
XLA Modules:
  0.0 180.1 jit_solution(9213479256628537609)
XLA Ops:
  0.7 1.4 fusion.61
  2.1 18.6 %all_gather.9 = bf16[2,64,3072]{2,1,0:T(8,128)(2,1)S(1)} all-gather(bf16[2,16,3072]{2,1,0:T(8,128)(2,1)S(1)} %pad_maximum_fusion.6), channel_id=1, replica_groups=mesh['group'=4,'x'=4,'z'=4,'h'=2,'c'=2] {'z'}, dimensions={1}, use_global_device_ids=true | all-gather | bytes 983040 | tf_op jit(solution)/shard_map/all_gather | solution.py:126
  20.7 1.6 collective-permute-start
  22.3 1.7 collective-permute-start.2
  24.0 0.7 dynamic_slice.58.sizes_ref
  24.7 0.9 copy.59
  25.7 4.8 %collective-permute-start.3 = (bf16[64,2,768]{2,0,1:T(8,128)(2,1)S(1)}, bf16[64,2,768]{2,0,1:T(8,128)(2,1)S(1)}, u32[]{:S(2)}, u32[]{:S(2)}) collective-permute-start(bf16[64,2,768]{2,0,1:T(8,128)(2,1)S(1)} %copy.59), channel_id=1, source_target_pairs={{0,2},{2,0},{1,3},{3,1},{4,6},{6,4},{5,7},{7,5},{8,10},{10,8},{9,1... | collective-permute-start | bytes 589832 | tf_op jit(solution)/shard_map/ppermute | solution.py:18
  31.2 3.7 %copy-done = bf16[2,768,3072]{2,1,0:T(8,128)(2,1)S(1)} copy-done((bf16[2,768,3072]{2,1,0:T(8,128)(2,1)S(1)}, bf16[2,768,3072]{2,1,0:T(8,128)(2,1)}, u32[]{:S(2)}) %copy-start) | copy-done | bytes 9437208
  34.9 3.5 %shard_map.77 = bf16[2,768,3072]{2,1,0:T(8,128)(2,1)S(1)} custom-call(s32[2]{0:T(128)S(1)} %dynamic_slice.58.sizes_ref, s32[2]{0:T(128)S(1)} %pad_add_fusion.origin_ref, bf16[2,768,3072]{2,1,0:T(8,128)(2,1)S(1)} %copy-done), custom_call_target="tpu_custom_call" | custom-call | tf_op jit(solution)/shard_map/pallas_call | solution.py:53
  38.4 1.3 collective-permute-done
  39.7 0.3 collective-permute-start.1
  40.0 3.1 %collective-permute-start.5 = (bf16[64,3072]{1,0:T(8,128)(2,1)S(1)}, bf16[64,3072]{1,0:T(8,128)(2,1)S(1)}, u32[]{:S(2)}, u32[]{:S(2)}) collective-permute-start(bf16[64,3072]{1,0:T(8,128)(2,1)S(1)} %get-tuple-element.71), channel_id=1, source_target_pairs={{0,48},{16,0},{32,16},{48,32},{1,49},{17,1},{33,17},{49,33},{2,50}... | collective-permute-start | bytes 1179656 | tf_op jit(solution)/shard_map/ppermute | solution.py:18
  43.2 6.2 %collective-permute-done.1 = bf16[64,3072]{1,0:T(8,128)(2,1)S(1)} collective-permute-done((bf16[64,3072]{1,0:T(8,128)(2,1)S(1)}, bf16[64,3072]{1,0:T(8,128)(2,1)S(1)}, u32[]{:S(2)}, u32[]{:S(2)}) %collective-permute-start.1) | collective-permute-done | bytes 393248 | tf_op jit(solution)/shard_map/ppermute | solution.py:18
  49.5 1.5 fusion.16
  51.1 1.4 fusion.13
  52.6 0.6 collective-permute-start.6
  53.3 0.3 copy.47
  53.6 0.6 collective-permute-done.6
  54.4 0.3 copy.48
  54.7 0.9 pad_maximum_fusion.1
  55.6 29.1 %all_to_all.10 = bf16[128,2,768]{2,1,0:T(2,128)(2,1)S(1)} all-to-all(bf16[128,2,768]{2,1,0:T(2,128)(2,1)S(1)} %pad_maximum_fusion.1), channel_id=1, replica_groups=mesh['group'=4,'x'=4,'z'=4,'h'=2,'c'=2] {'h','group','x','z'}, dimensions={0} | all-to-all | bytes 786432 | tf_op jit(solution)/shard_map/all_to_all | solution.py:143
  84.7 0.2 add_convert_fusion.6
  85.0 0.2 convolution_convert_fusion
  85.3 1.3 pad_maximum_fusion.2
  86.5 6.4 %all-to-all-start.1 = ((bf16[128,2,768]{2,1,0:T(2,128)(2,1)}), bf16[128,2,768]{2,1,0:T(2,128)(2,1)S(1)}, u32[]{:S(2)}, u32[]{:S(2)}) async-start(bf16[128,2,768]{2,1,0:T(2,128)(2,1)} %pad_maximum_fusion.2), calls=%async_computation.1 | async-start | bytes 786432 | tf_op jit(solution)/shard_map/all_to_all | solution.py:149
  93.0 0.3 fusion.23
  93.4 16.4 %all-to-all-done.1 = bf16[128,2,768]{2,1,0:T(2,128)(2,1)S(1)} async-done(((bf16[128,2,768]{2,1,0:T(2,128)(2,1)}), bf16[128,2,768]{2,1,0:T(2,128)(2,1)S(1)}, u32[]{:S(2)}, u32[]{:S(2)}) %all-to-all-start.1) | async-done | bytes 393248 | tf_op jit(solution)/shard_map/all_to_all | solution.py:149
  109.9 0.2 fusion.32
  110.1 0.2 fusion.29
  110.3 2.5 %all-gather = bf16[4,128,768]{2,1,0:T(8,128)(2,1)S(1)} all-gather(bf16[2,128,768]{2,1,0:T(8,128)(2,1)S(1)} %pad_maximum_fusion.3), channel_id=2, replica_groups=mesh['group'=4,'x'=4,'z'=4,'h'=2,'c'=2] {'c'}, dimensions={0}, use_global_device_ids=true | all-gather | bytes 1179648 | tf_op jit(solution)/shard_map/all_gather | solution.py:158
  112.9 0.2 fusion.18
  113.0 3.9 %fusion.5 = bf16[256,3072]{1,0:T(8,128)(2,1)S(1)} fusion(bf16[256,768]{1,0:T(8,128)(2,1)S(1)} %bitcast.100, bf16[2,768,3072]{2,1,0:T(8,128)(2,1)} %copy-done.1), kind=kOutput, calls=%fused_computation.7 | convolution fusion | flops 1208745984 | bytes 6684672 | tf_op jit(solution)/shard_map/sm,mk->sk/dot_general | solution.py:164
  117.0 0.9 slice.216
  118.0 0.8 pad_maximum_fusion.4
  118.8 1.4 fusion.4
  120.3 0.8 slice.227
  121.1 0.8 pad_maximum_fusion.5
  121.9 1.1 collective-permute-start.16
  123.0 0.9 collective-permute-start.15
  124.0 0.7 pad_maximum_fusion.7
  124.7 0.2 collective-permute-start.8
  124.9 3.0 %collective-permute-start.9 = (bf16[64,3072]{1,0:T(8,128)(2,1)}, bf16[64,3072]{1,0:T(8,128)(2,1)}, u32[]{:S(2)}, u32[]{:S(2)}) collective-permute-start(bf16[64,3072]{1,0:T(8,128)(2,1)} %pad_maximum_fusion.4), channel_id=1, source_target_pairs={{0,48},{16,0},{32,16},{48,32},{1,49},{17,1},{33,17},{49,33},{2,50}... | collective-permute-start | bytes 1179656 | tf_op jit(solution)/shard_map/ppermute | solution.py:18
  127.9 6.1 %collective-permute-done.16 = bf16[64,3072]{1,0:T(8,128)(2,1)S(1)} collective-permute-done((bf16[64,3072]{1,0:T(8,128)(2,1)}, bf16[64,3072]{1,0:T(8,128)(2,1)S(1)}, u32[]{:S(2)}, u32[]{:S(2)}) %collective-permute-start.16) | collective-permute-done | bytes 393248 | tf_op jit(solution)/shard_map/ppermute | solution.py:18
  134.1 2.4 %collective-permute-done.15 = bf16[64,3072]{1,0:T(8,128)(2,1)S(1)} collective-permute-done((bf16[64,3072]{1,0:T(8,128)(2,1)}, bf16[64,3072]{1,0:T(8,128)(2,1)S(1)}, u32[]{:S(2)}, u32[]{:S(2)}) %collective-permute-start.15) | collective-permute-done | bytes 393248 | tf_op jit(solution)/shard_map/ppermute | solution.py:18
  136.4 0.8 add_convert_fusion.1
  137.3 3.2 %collective-permute-start.18 = (bf16[32,3072]{1,0:T(8,128)(2,1)}, bf16[32,3072]{1,0:T(8,128)(2,1)}, u32[]{:S(2)}, u32[]{:S(2)}) collective-permute-start(bf16[32,3072]{1,0:T(8,128)(2,1)} %get-tuple-element.54), channel_id=1, source_target_pairs={{0,48},{16,0},{32,16},{48,32},{1,49},{17,1},{33,17},{49,33},{2,50}... | collective-permute-start | bytes 589832 | tf_op jit(solution)/shard_map/ppermute | solution.py:18
  140.5 4.5 %collective-permute-done.8 = bf16[64,3072]{1,0:T(8,128)(2,1)} collective-permute-done((bf16[64,3072]{1,0:T(8,128)(2,1)}, bf16[64,3072]{1,0:T(8,128)(2,1)}, u32[]{:S(2)}, u32[]{:S(2)}) %collective-permute-start.8) | collective-permute-done | bytes 393248 | tf_op jit(solution)/shard_map/ppermute | solution.py:18
  145.0 2.1 %add_convert_fusion.4 = (bf16[32,3072]{1,0:T(8,128)(2,1)}, bf16[32,3072]{1,0:T(8,128)(2,1)}) fusion(bf16[256,3072]{1,0:T(8,128)(2,1)} %copy-done.2, bf16[64,3072]{1,0:T(8,128)(2,1)} %collective-permute-done.9, bf16[64,3072]{1,0:T(8,128)(2,1)} %collective-permute-done.8), kind=kLoop, calls=%fused_computation.80 | loop fusion | flops 786432 | bytes 1179648 | tf_op jit(solution)/shard_map/convert_element_type | solution.py:90
  147.0 3.2 %collective-permute-start.11 = (bf16[32,3072]{1,0:T(8,128)(2,1)}, bf16[32,3072]{1,0:T(8,128)(2,1)}, u32[]{:S(2)}, u32[]{:S(2)}) collective-permute-start(bf16[32,3072]{1,0:T(8,128)(2,1)} %get-tuple-element.60), channel_id=1, source_target_pairs={{0,48},{16,0},{32,16},{48,32},{1,49},{17,1},{33,17},{49,33},{2,50}... | collective-permute-start | bytes 589832 | tf_op jit(solution)/shard_map/ppermute | solution.py:18
  150.3 1.7 collective-permute-start.7
  152.0 2.2 %collective-permute-done.10 = bf16[32,3072]{1,0:T(8,128)(2,1)} collective-permute-done((bf16[32,3072]{1,0:T(8,128)(2,1)}, bf16[32,3072]{1,0:T(8,128)(2,1)}, u32[]{:S(2)}, u32[]{:S(2)}) %collective-permute-start.10) | collective-permute-done | bytes 196640 | tf_op jit(solution)/shard_map/ppermute | solution.py:18
  154.2 1.5 add_convert_fusion.3
  155.7 1.1 collective-permute-start.13
  156.8 1.3 collective-permute-start.14
  158.2 0.8 collective-permute-start.12
  159.0 1.1 convert_add_fusion.2
  160.1 3.8 %collective-permute-start.20 = (bf16[16,3072]{1,0:T(8,128)(2,1)S(1)}, bf16[16,3072]{1,0:T(8,128)(2,1)S(1)}, u32[]{:S(2)}, u32[]{:S(2)}) collective-permute-start(bf16[16,3072]{1,0:T(8,128)(2,1)S(1)} %get-tuple-element.74), channel_id=1, source_target_pairs={{0,8},{4,12},{8,0},{12,4},{1,9},{5,13},{9,1},{13,5},{2,10},{6,14},... | collective-permute-start | bytes 294920 | tf_op jit(solution)/shard_map/ppermute | solution.py:18
  163.9 2.6 %collective-permute-done.13 = bf16[16,3072]{1,0:T(8,128)(2,1)S(1)} collective-permute-done((bf16[16,3072]{1,0:T(8,128)(2,1)S(1)}, bf16[16,3072]{1,0:T(8,128)(2,1)S(1)}, u32[]{:S(2)}, u32[]{:S(2)}) %collective-permute-start.13) | collective-permute-done | bytes 98336 | tf_op jit(solution)/shard_map/ppermute | solution.py:18
  166.5 4.9 %collective-permute-start.21 = (bf16[16,3072]{1,0:T(8,128)(2,1)S(1)}, bf16[16,3072]{1,0:T(8,128)(2,1)S(1)}, u32[]{:S(2)}, u32[]{:S(2)}) collective-permute-start(bf16[16,3072]{1,0:T(8,128)(2,1)S(1)} %get-tuple-element.75), channel_id=1, source_target_pairs={{0,12},{4,0},{8,4},{12,8},{1,13},{5,1},{9,5},{13,9},{2,14},{6,2},{... | collective-permute-start | bytes 294920 | tf_op jit(solution)/shard_map/ppermute | solution.py:18
  171.3 0.6 collective-permute-done.14
  172.1 1.8 %collective-permute-done.20 = bf16[16,3072]{1,0:T(8,128)(2,1)S(1)} collective-permute-done((bf16[16,3072]{1,0:T(8,128)(2,1)S(1)}, bf16[16,3072]{1,0:T(8,128)(2,1)S(1)}, u32[]{:S(2)}, u32[]{:S(2)}) %collective-permute-start.20) | collective-permute-done | bytes 98336 | tf_op jit(solution)/shard_map/ppermute | solution.py:18
  173.9 4.3 %collective-permute-done.21 = bf16[16,3072]{1,0:T(8,128)(2,1)S(1)} collective-permute-done((bf16[16,3072]{1,0:T(8,128)(2,1)S(1)}, bf16[16,3072]{1,0:T(8,128)(2,1)S(1)}, u32[]{:S(2)}, u32[]{:S(2)}) %collective-permute-start.21) | collective-permute-done | bytes 98336 | tf_op jit(solution)/shard_map/ppermute | solution.py:18
  178.2 0.9 copy.51
  179.2 0.9 copy.50
  (72 shorter events, 2.4 us)
Async XLA Ops:
  0.6 29.8 %copy-start.4 = (s32[8]{0:T(128)S(1)}, s32[8]{0:T(128)}, u32[]{:S(2)}) copy-start(s32[8]{0:T(128)} %param.10) | copy-start | bytes 100
  0.6 30.1 %copy-start.3 = (s32[8,16]{1,0:T(8,128)S(1)}, s32[8,16]{1,0:T(8,128)}, u32[]{:S(2)}) copy-start(s32[8,16]{1,0:T(8,128)} %param.11) | copy-start | bytes 1540
  20.7 18.9 %collective-permute-start = (bf16[2,64,3072]{2,1,0:T(8,128)(2,1)S(1)}, bf16[2,64,3072]{2,1,0:T(8,128)(2,1)S(1)}, u32[]{:S(2)}, u32[]{:S(2)}) collective-permute-start(bf16[2,64,3072]{2,1,0:T(8,128)(2,1)S(1)} %all_gather.9), channel_id=1, source_target_pairs={{0,16},{16,32},{32,48},{48,0},{1,17},{17,33},{33,49},{49,1},{2,18}... | collective-permute-start | bytes 2359304 | tf_op jit(solution)/shard_map/ppermute | solution.py:18
  22.3 17.7 %collective-permute-start.2 = (bf16[2,64,3072]{2,1,0:T(8,128)(2,1)S(1)}, bf16[2,64,3072]{2,1,0:T(8,128)(2,1)S(1)}, u32[]{:S(2)}, u32[]{:S(2)}) collective-permute-start(bf16[2,64,3072]{2,1,0:T(8,128)(2,1)S(1)} %all_gather.9), channel_id=1, source_target_pairs={{0,48},{16,0},{32,16},{48,32},{1,49},{17,1},{33,17},{49,33},{2,50}... | collective-permute-start | bytes 2359304 | tf_op jit(solution)/shard_map/ppermute | solution.py:18
  25.7 23.8 %collective-permute-start.3 = (bf16[64,2,768]{2,0,1:T(8,128)(2,1)S(1)}, bf16[64,2,768]{2,0,1:T(8,128)(2,1)S(1)}, u32[]{:S(2)}, u32[]{:S(2)}) collective-permute-start(bf16[64,2,768]{2,0,1:T(8,128)(2,1)S(1)} %copy.59), channel_id=1, source_target_pairs={{0,2},{2,0},{1,3},{3,1},{4,6},{6,4},{5,7},{7,5},{8,10},{10,8},{9,1... | collective-permute-start | bytes 589832 | tf_op jit(solution)/shard_map/ppermute | solution.py:18
  31.2 3.7 %copy-start = (bf16[2,768,3072]{2,1,0:T(8,128)(2,1)S(1)}, bf16[2,768,3072]{2,1,0:T(8,128)(2,1)}, u32[]{:S(2)}) copy-start(bf16[2,768,3072]{2,1,0:T(8,128)(2,1)} %fronts_ref.1) | copy-start | bytes 28311556
  38.4 12.7 %copy-start.1 = (bf16[2,768,3072]{2,1,0:T(8,128)(2,1)}, bf16[2,768,3072]{2,1,0:T(8,128)(2,1)S(1)}, u32[]{:S(2)}) copy-start(bf16[2,768,3072]{2,1,0:T(8,128)(2,1)S(1)} %shard_map.77) | copy-start | bytes 28311556
  39.7 9.6 %collective-permute-start.1 = (bf16[64,3072]{1,0:T(8,128)(2,1)S(1)}, bf16[64,3072]{1,0:T(8,128)(2,1)S(1)}, u32[]{:S(2)}, u32[]{:S(2)}) collective-permute-start(bf16[64,3072]{1,0:T(8,128)(2,1)S(1)} %get-tuple-element.68), channel_id=1, source_target_pairs={{0,16},{16,32},{32,48},{48,0},{1,17},{17,33},{33,49},{49,1},{2,18}... | collective-permute-start | bytes 1179656 | tf_op jit(solution)/shard_map/ppermute | solution.py:18
  40.0 11.1 %collective-permute-start.5 = (bf16[64,3072]{1,0:T(8,128)(2,1)S(1)}, bf16[64,3072]{1,0:T(8,128)(2,1)S(1)}, u32[]{:S(2)}, u32[]{:S(2)}) collective-permute-start(bf16[64,3072]{1,0:T(8,128)(2,1)S(1)} %get-tuple-element.71), channel_id=1, source_target_pairs={{0,48},{16,0},{32,16},{48,32},{1,49},{17,1},{33,17},{49,33},{2,50}... | collective-permute-start | bytes 1179656 | tf_op jit(solution)/shard_map/ppermute | solution.py:18
  51.0 2.2 %collective-permute-start.4 = (bf16[2,64,768]{2,1,0:T(8,128)(2,1)S(1)}, bf16[2,64,768]{2,1,0:T(8,128)(2,1)S(1)}, u32[]{:S(2)}, u32[]{:S(2)}) collective-permute-start(bf16[2,64,768]{2,1,0:T(8,128)(2,1)S(1)} %dynamic-slice_bitcast_fusion.1), channel_id=1, source_target_pairs={{0,1},{1,0},{2,3},{3,2},{4,5},{5,4},{6,7},{7,6},{8,9},{9,8},{10,11... | collective-permute-start | bytes 589832 | tf_op jit(solution)/shard_map/ppermute | solution.py:18
  52.6 1.6 collective-permute-start.6
  86.5 23.2 %all-to-all-start.1 = ((bf16[128,2,768]{2,1,0:T(2,128)(2,1)}), bf16[128,2,768]{2,1,0:T(2,128)(2,1)S(1)}, u32[]{:S(2)}, u32[]{:S(2)}) async-start(bf16[128,2,768]{2,1,0:T(2,128)(2,1)} %pad_maximum_fusion.2), calls=%async_computation.1 | async-start | bytes 786432 | tf_op jit(solution)/shard_map/all_to_all | solution.py:149
  92.9 25.9 %slice-start = ((s8[9437184]{0:T(1024)(128)(4,1)}), s8[1048576]{0:T(1024)(128)(4,1)S(1)}, s32[]{:S(2)}) async-start(s8[9437184]{0:T(1024)(128)(4,1)} %bitcast.84), calls=%async_computation.2 | async-start | bytes 2097152
  110.3 8.5 %slice-start.1 = ((s8[9437184]{0:T(1024)(128)(4,1)}), s8[4194304]{0:T(1024)(128)(4,1)S(1)}, s32[]{:S(2)}) async-start(s8[9437184]{0:T(1024)(128)(4,1)} %bitcast.84), calls=%async_computation.3 | async-start | bytes 8388608
  113.0 5.8 %slice-start.2 = ((s8[9437184]{0:T(1024)(128)(4,1)}), s8[4194304]{0:T(1024)(128)(4,1)S(1)}, s32[]{:S(2)}) async-start(s8[9437184]{0:T(1024)(128)(4,1)} %bitcast.84), calls=%async_computation.4 | async-start | bytes 8388608
  117.0 3.3 %copy-start.2 = (bf16[256,3072]{1,0:T(8,128)(2,1)}, bf16[256,3072]{1,0:T(8,128)(2,1)S(1)}, u32[]{:S(2)}) copy-start(bf16[256,3072]{1,0:T(8,128)(2,1)S(1)} %fusion.5) | copy-start | bytes 4718596
  121.9 12.2 %collective-permute-start.16 = (bf16[64,3072]{1,0:T(8,128)(2,1)}, bf16[64,3072]{1,0:T(8,128)(2,1)S(1)}, u32[]{:S(2)}, u32[]{:S(2)}) collective-permute-start(bf16[64,3072]{1,0:T(8,128)(2,1)} %pad_maximum_fusion.5), channel_id=1, source_target_pairs={{0,48},{16,0},{32,16},{48,32},{1,49},{17,1},{33,17},{49,33},{2,50}... | collective-permute-start | bytes 1179656 | tf_op jit(solution)/shard_map/ppermute | solution.py:18
  123.0 13.4 %collective-permute-start.15 = (bf16[64,3072]{1,0:T(8,128)(2,1)}, bf16[64,3072]{1,0:T(8,128)(2,1)S(1)}, u32[]{:S(2)}, u32[]{:S(2)}) collective-permute-start(bf16[64,3072]{1,0:T(8,128)(2,1)} %slice.227), channel_id=1, source_target_pairs={{0,16},{16,32},{32,48},{48,0},{1,17},{17,33},{33,49},{49,1},{2,18}... | collective-permute-start | bytes 1179656 | tf_op jit(solution)/shard_map/ppermute | solution.py:18
  124.7 20.2 %collective-permute-start.8 = (bf16[64,3072]{1,0:T(8,128)(2,1)}, bf16[64,3072]{1,0:T(8,128)(2,1)}, u32[]{:S(2)}, u32[]{:S(2)}) collective-permute-start(bf16[64,3072]{1,0:T(8,128)(2,1)} %slice.216), channel_id=1, source_target_pairs={{0,16},{16,32},{32,48},{48,0},{1,17},{17,33},{33,49},{49,1},{2,18}... | collective-permute-start | bytes 1179656 | tf_op jit(solution)/shard_map/ppermute | solution.py:18
  124.9 20.0 %collective-permute-start.9 = (bf16[64,3072]{1,0:T(8,128)(2,1)}, bf16[64,3072]{1,0:T(8,128)(2,1)}, u32[]{:S(2)}, u32[]{:S(2)}) collective-permute-start(bf16[64,3072]{1,0:T(8,128)(2,1)} %pad_maximum_fusion.4), channel_id=1, source_target_pairs={{0,48},{16,0},{32,16},{48,32},{1,49},{17,1},{33,17},{49,33},{2,50}... | collective-permute-start | bytes 1179656 | tf_op jit(solution)/shard_map/ppermute | solution.py:18
  137.3 14.7 %collective-permute-start.17 = (bf16[32,3072]{1,0:T(8,128)(2,1)}, bf16[32,3072]{1,0:T(8,128)(2,1)S(1)}, u32[]{:S(2)}, u32[]{:S(2)}) collective-permute-start(bf16[32,3072]{1,0:T(8,128)(2,1)} %get-tuple-element.55), channel_id=1, source_target_pairs={{0,16},{16,32},{32,48},{48,0},{1,17},{17,33},{33,49},{49,1},{2,18}... | collective-permute-start | bytes 589832 | tf_op jit(solution)/shard_map/ppermute | solution.py:18
  137.3 14.7 %collective-permute-start.18 = (bf16[32,3072]{1,0:T(8,128)(2,1)}, bf16[32,3072]{1,0:T(8,128)(2,1)}, u32[]{:S(2)}, u32[]{:S(2)}) collective-permute-start(bf16[32,3072]{1,0:T(8,128)(2,1)} %get-tuple-element.54), channel_id=1, source_target_pairs={{0,48},{16,0},{32,16},{48,32},{1,49},{17,1},{33,17},{49,33},{2,50}... | collective-permute-start | bytes 589832 | tf_op jit(solution)/shard_map/ppermute | solution.py:18
  147.0 7.2 %collective-permute-start.10 = (bf16[32,3072]{1,0:T(8,128)(2,1)}, bf16[32,3072]{1,0:T(8,128)(2,1)}, u32[]{:S(2)}, u32[]{:S(2)}) collective-permute-start(bf16[32,3072]{1,0:T(8,128)(2,1)} %get-tuple-element.61), channel_id=1, source_target_pairs={{0,16},{16,32},{32,48},{48,0},{1,17},{17,33},{33,49},{49,1},{2,18}... | collective-permute-start | bytes 589832 | tf_op jit(solution)/shard_map/ppermute | solution.py:18
  147.0 7.2 %collective-permute-start.11 = (bf16[32,3072]{1,0:T(8,128)(2,1)}, bf16[32,3072]{1,0:T(8,128)(2,1)}, u32[]{:S(2)}, u32[]{:S(2)}) collective-permute-start(bf16[32,3072]{1,0:T(8,128)(2,1)} %get-tuple-element.60), channel_id=1, source_target_pairs={{0,48},{16,0},{32,16},{48,32},{1,49},{17,1},{33,17},{49,33},{2,50}... | collective-permute-start | bytes 589832 | tf_op jit(solution)/shard_map/ppermute | solution.py:18
  150.3 21.8 %collective-permute-start.7 = (bf16[2,64,768]{2,1,0:T(8,128)(2,1)}, bf16[2,64,768]{2,1,0:T(8,128)(2,1)S(1)}, u32[]{:S(2)}, u32[]{:S(2)}) collective-permute-start(bf16[2,64,768]{2,1,0:T(8,128)(2,1)} %pad_maximum_fusion.7), channel_id=1, source_target_pairs={{0,2},{2,0},{1,3},{3,1},{4,6},{6,4},{5,7},{7,5},{8,10},{10,8},{9,1... | collective-permute-start | bytes 589832 | tf_op jit(solution)/shard_map/ppermute | solution.py:18
  155.7 10.8 %collective-permute-start.13 = (bf16[16,3072]{1,0:T(8,128)(2,1)S(1)}, bf16[16,3072]{1,0:T(8,128)(2,1)S(1)}, u32[]{:S(2)}, u32[]{:S(2)}) collective-permute-start(bf16[16,3072]{1,0:T(8,128)(2,1)S(1)} %get-tuple-element.78), channel_id=1, source_target_pairs={{0,8},{4,12},{8,0},{12,4},{1,9},{5,13},{9,1},{13,5},{2,10},{6,14},... | collective-permute-start | bytes 294920 | tf_op jit(solution)/shard_map/ppermute | solution.py:18
  156.8 15.1 %collective-permute-start.14 = (bf16[16,3072]{1,0:T(8,128)(2,1)S(1)}, bf16[16,3072]{1,0:T(8,128)(2,1)S(1)}, u32[]{:S(2)}, u32[]{:S(2)}) collective-permute-start(bf16[16,3072]{1,0:T(8,128)(2,1)S(1)} %get-tuple-element.79), channel_id=1, source_target_pairs={{0,12},{4,0},{8,4},{12,8},{1,13},{5,1},{9,5},{13,9},{2,14},{6,2},{... | collective-permute-start | bytes 294920 | tf_op jit(solution)/shard_map/ppermute | solution.py:18
  158.2 13.8 %collective-permute-start.12 = (bf16[16,3072]{1,0:T(8,128)(2,1)S(1)}, bf16[16,3072]{1,0:T(8,128)(2,1)S(1)}, u32[]{:S(2)}, u32[]{:S(2)}) collective-permute-start(bf16[16,3072]{1,0:T(8,128)(2,1)S(1)} %slice.297), channel_id=1, source_target_pairs={{0,4},{4,8},{8,12},{12,0},{1,5},{5,9},{9,13},{13,1},{2,6},{6,10},{... | collective-permute-start | bytes 294920 | tf_op jit(solution)/shard_map/ppermute | solution.py:18
  160.1 13.8 %collective-permute-start.20 = (bf16[16,3072]{1,0:T(8,128)(2,1)S(1)}, bf16[16,3072]{1,0:T(8,128)(2,1)S(1)}, u32[]{:S(2)}, u32[]{:S(2)}) collective-permute-start(bf16[16,3072]{1,0:T(8,128)(2,1)S(1)} %get-tuple-element.74), channel_id=1, source_target_pairs={{0,8},{4,12},{8,0},{12,4},{1,9},{5,13},{9,1},{13,5},{2,10},{6,14},... | collective-permute-start | bytes 294920 | tf_op jit(solution)/shard_map/ppermute | solution.py:18
  166.5 11.7 %collective-permute-start.21 = (bf16[16,3072]{1,0:T(8,128)(2,1)S(1)}, bf16[16,3072]{1,0:T(8,128)(2,1)S(1)}, u32[]{:S(2)}, u32[]{:S(2)}) collective-permute-start(bf16[16,3072]{1,0:T(8,128)(2,1)S(1)} %get-tuple-element.75), channel_id=1, source_target_pairs={{0,12},{4,0},{8,4},{12,8},{1,13},{5,1},{9,5},{13,9},{2,14},{6,2},{... | collective-permute-start | bytes 294920 | tf_op jit(solution)/shard_map/ppermute | solution.py:18
  172.0 6.2 %collective-permute-start.19 = (bf16[16,3072]{1,0:T(8,128)(2,1)S(1)}, bf16[16,3072]{1,0:T(8,128)(2,1)S(1)}, u32[]{:S(2)}, u32[]{:S(2)}) collective-permute-start(bf16[16,3072]{1,0:T(8,128)(2,1)S(1)} %slice.296), channel_id=1, source_target_pairs={{0,4},{4,8},{8,12},{12,0},{1,5},{5,9},{9,13},{13,1},{2,6},{6,10},{... | collective-permute-start | bytes 294920 | tf_op jit(solution)/shard_map/ppermute | solution.py:18

commit v2 on v1

--- a/solution.py
+++ b/solution.py
@@ -75,31 +75,35 @@
     return to_right, to_left
 
 
-def scatter_rows(products, pieces):
-    block = products[0].shape[0] // 4
+def first_step(pieces):
+    to_right, to_left = pieces
+    return lax.optimization_barrier((shift(to_right, "x", 1), shift(to_left, "x", -1)))
+
+
+def second_step(product, near):
+    block = product.shape[0] // 4
+    half = block // 2
+    from_left, from_right = near
+    over_right = product[2 * block + half : 3 * block].astype(F32) + from_left[:half].astype(F32)
+    over_left = product[3 * block : 3 * block + half].astype(F32) + from_right[:half].astype(F32)
+    over_right = shift(over_right.astype(BF16), "x", 1)
+    over_left = shift(over_left.astype(BF16), "x", -1)
+    return lax.optimization_barrier((over_right, over_left))
+
+
+def last_step(product, near, far):
+    block = product.shape[0] // 4
     half = block // 2
     rows = block // 4
-    near = []
-    for to_right, to_left in pieces:
-        near.append(lax.optimization_barrier((shift(to_right, "x", 1), shift(to_left, "x", -1))))
-    far = []
-    for product, (from_left, from_right) in zip(products, near):
-        over_right = product[2 * block + half : 3 * block].astype(F32) + from_left[:half].astype(F32)
-        over_left = product[3 * block : 3 * block + half].astype(F32) + from_right[:half].astype(F32)
-        over_right = shift(over_right.astype(BF16), "x", 1)
-        over_left = shift(over_left.astype(BF16), "x", -1)
-        far.append(lax.optimization_barrier((over_right, over_left)))
-    totals = []
-    for product, (from_left, from_right), (over_right, over_left) in zip(products, near, far):
-        top = product[:half].astype(F32) + from_left[half:].astype(F32) + over_left.astype(F32)
-        low = product[half:block].astype(F32) + from_right[half:].astype(F32) + over_right.astype(F32)
-        own = jnp.concatenate([top, low], axis=0)
-        total = own[:rows]
-        for k in (1, 2, 3):
-            piece = own[k * rows : (k + 1) * rows].astype(BF16)
-            total = total + shift(piece, "z", k).astype(F32)
-        totals.append(total)
-    return totals
+    (from_left, from_right), (over_right, over_left) = near, far
+    top = product[:half].astype(F32) + from_left[half:].astype(F32) + over_left.astype(F32)
+    low = product[half:block].astype(F32) + from_right[half:].astype(F32) + over_right.astype(F32)
+    own = jnp.concatenate([top, low], axis=0)
+    total = own[:rows]
+    for k in (1, 2, 3):
+        piece = own[k * rows : (k + 1) * rows].astype(BF16)
+        total = total + shift(piece, "z", k).astype(F32)
+    return total
 
 
 def route_weight(parent_ids, block_maps, local):
@@ -157,23 +161,28 @@
         ordered.append(rolled(mine, (nearer, z)).reshape(2 * slab, tile_rows))
     everyone = lax.all_gather(jnp.stack(ordered), "c", axis=0)
     ordered = [rolled(everyone[:, f], (x & 1,)).reshape(4 * slab, tile_rows) for f in range(local)]
-    products, pieces = [], []
-    for f in range(local):
-        if f > 0:
-            ordered[f], pieces[0] = lax.optimization_barrier((ordered[f], pieces[0]))
+
+    def multiplied(f):
         product = jnp.einsum("sm,mk->sk", ordered[f], masked[f], preferred_element_type=F32)
-        products.append(product.astype(BF16))
-        pieces.append(first_pieces(products[f]))
+        return product.astype(BF16)
 
+    product_0 = multiplied(0)
+    near_0 = first_step(first_pieces(product_0))
+    product_1 = multiplied(1)
+    pieces_1 = first_pieces(product_1)
+    near_0, product_1, pieces_1 = lax.optimization_barrier((near_0, product_1, pieces_1))
+    far_0 = second_step(product_0, near_0)
+    near_1 = first_step(pieces_1)
     away = jnp.stack([pick(half, 1 - h).astype(BF16) for half in halves])
-    away, products[-1] = lax.optimization_barrier((away, products[-1]))
+    away, far_0 = lax.optimization_barrier((away, far_0))
     received = shift(away, "h", 1)
-    totals = scatter_rows(products, pieces)
-    received, totals[0] = lax.optimization_barrier((received, totals[0]))
+    total_0 = last_step(product_0, near_0, far_0)
+    far_1 = second_step(product_1, near_1)
+    received, far_1 = lax.optimization_barrier((received, far_1))
     slabs = [pick(half, h) + received[f].astype(F32) for f, half in enumerate(halves)]
     sampled = jnp.stack([total.astype(BF16) for total in slabs], axis=1)
-
-    outs = [total.astype(BF16) for total in totals]
+    total_1 = last_step(product_1, near_1, far_1)
+    outs = [total_0.astype(BF16), total_1.astype(BF16)]
     return sampled, jnp.stack(outs, axis=1)
 
 

time: 181 us -> 174 us (0.961)
  waiting for transfers between devices: 49.1 us -> 59.3 us
  starting transfers between devices: 43.8 us -> 36 us
  other arithmetic: 12 us -> 4.89 us
    ppermute x22, waiting for transfers between devices: 32.7 us -> 43.2 us  [shift(): return lax.ppermute(value, axis, [(i, (i + by) % n) for i in range(n)])]
    ppermute x22, starting transfers between devices: 37.4 us -> 29.5 us  [shift(): return lax.ppermute(value, axis, [(i, (i + by) % n) for i in range(n)])]
    convert_element_type x2, other arithmetic: 2.89 us -> 0.19 us  [second_step(): over_left = shift(over_left.astype(BF16), 'x', -1)]
    unnamed x18 -> x16, local copies, waits for them, and re-layouts: 5.47 us -> 5.47 us
  transfers between devices with their start and end apart: 23 -> 23, of which waited for: 12 -> 16; matrix products, arithmetic and copies ran while one was open for 7% -> 5% of each run, Pallas kernels for 2% -> 2%
where the time goes in v2:
time: 174 us
  waiting for transfers between devices  59.3 us (34%)
  blocking collectives  50.5 us (29%)
  starting transfers between devices  36 us (21%)
  local copies, waits for them, and re-layouts  10.3 us (6%)
  matrix products  8.46 us (5%)
  other arithmetic  4.89 us (3%)
  Pallas kernels  3.47 us (2%)
    ppermute x22, waiting for transfers between devices, shift(): return lax.ppermute(value, axis, [(i, (i + by) % n) for i in range(n)])  43.2 us
    ppermute x22, starting transfers between devices, shift(): return lax.ppermute(value, axis, [(i, (i + by) % n) for i in range(n)])  29.5 us
    all_to_all x1, blocking collectives, shards(): lax.all_to_all(outgoing, spread, split_axis=0, concat_axis=0, tiled=True)  29.4 us
    all_gather x1, blocking collectives, shards(): columns = lax.all_gather(mine, 'z', axis=1, tiled=True)  18.6 us
    all_to_all x1, waiting for transfers between devices, shards(): lax.all_to_all(extension, spread, split_axis=0, concat_axis=0, tiled=True)  16.1 us
    all_to_all x1, starting transfers between devices, shards(): lax.all_to_all(extension, spread, split_axis=0, concat_axis=0, tiled=True)  6.53 us
    unnamed x16, local copies, waits for them, and re-layouts  5.47 us
    dot_general x2, matrix products, multiplied(): jnp.einsum('sm,mk->sk', ordered[f], masked[f], preferred_element_type=F32)  5.34 us
  transfers between devices with their start and end apart: 23, of which 16 were waited for; matrix products, arithmetic and copies ran while one was open for 5% of the time, Pallas kernels for 2%

profile of v2, /device:TPU:32, one launch (start us, length us, event | category | flops | bytes accessed | tf_op | source)
XLA Modules:
  0.0 174.2 jit_solution(14917214080439292732)
XLA Ops:
  0.7 1.4 fusion.63
  2.1 18.6 %all_gather.9 = bf16[2,64,3072]{2,1,0:T(8,128)(2,1)S(1)} all-gather(bf16[2,16,3072]{2,1,0:T(8,128)(2,1)S(1)} %pad_maximum_fusion.6), channel_id=1, replica_groups=mesh['group'=4,'x'=4,'z'=4,'h'=2,'c'=2] {'z'}, dimensions={1}, use_global_device_ids=true | all-gather | bytes 983040 | tf_op jit(solution)/shard_map/all_gather | solution.py:130
  20.7 2.8 %collective-permute-start.2 = (bf16[2,64,3072]{2,1,0:T(8,128)(2,1)S(1)}, bf16[2,64,3072]{2,1,0:T(8,128)(2,1)S(1)}, u32[]{:S(2)}, u32[]{:S(2)}) collective-permute-start(bf16[2,64,3072]{2,1,0:T(8,128)(2,1)S(1)} %all_gather.9), channel_id=1, source_target_pairs={{0,48},{16,0},{32,16},{48,32},{1,49},{17,1},{33,17},{49,33},{2,50}... | collective-permute-start | bytes 2359304 | tf_op jit(solution)/shard_map/ppermute | solution.py:18
  23.6 0.7 dynamic_slice.58.sizes_ref
  24.3 0.9 copy.59
  25.3 4.7 %collective-permute-start.3 = (bf16[64,2,768]{2,0,1:T(8,128)(2,1)S(1)}, bf16[64,2,768]{2,0,1:T(8,128)(2,1)S(1)}, u32[]{:S(2)}, u32[]{:S(2)}) collective-permute-start(bf16[64,2,768]{2,0,1:T(8,128)(2,1)S(1)} %copy.59), channel_id=1, source_target_pairs={{0,2},{2,0},{1,3},{3,1},{4,6},{6,4},{5,7},{7,5},{8,10},{10,8},{9,1... | collective-permute-start | bytes 589832 | tf_op jit(solution)/shard_map/ppermute | solution.py:18
  30.1 0.1 eq.33
  30.2 0.1 copy.44
  30.3 0.1 eq.37
  30.7 3.7 %copy-done = bf16[2,768,3072]{2,1,0:T(8,128)(2,1)S(1)} copy-done((bf16[2,768,3072]{2,1,0:T(8,128)(2,1)S(1)}, bf16[2,768,3072]{2,1,0:T(8,128)(2,1)}, u32[]{:S(2)}) %copy-start) | copy-done | bytes 9437208
  34.4 3.5 %shard_map.77 = bf16[2,768,3072]{2,1,0:T(8,128)(2,1)S(1)} custom-call(s32[2]{0:T(128)S(1)} %dynamic_slice.58.sizes_ref, s32[2]{0:T(128)S(1)} %pad_add_fusion.origin_ref, bf16[2,768,3072]{2,1,0:T(8,128)(2,1)S(1)} %copy-done), custom_call_target="tpu_custom_call" | custom-call | tf_op jit(solution)/shard_map/pallas_call | solution.py:53
  37.9 4.1 %collective-permute-done = bf16[2,64,3072]{2,1,0:T(8,128)(2,1)S(1)} collective-permute-done((bf16[2,64,3072]{2,1,0:T(8,128)(2,1)S(1)}, bf16[2,64,3072]{2,1,0:T(8,128)(2,1)S(1)}, u32[]{:S(2)}, u32[]{:S(2)}) %collective-permute-start) | collective-permute-done | bytes 786464 | tf_op jit(solution)/shard_map/ppermute | solution.py:18
  42.3 3.3 %collective-permute-start.5 = (bf16[64,3072]{1,0:T(8,128)(2,1)S(1)}, bf16[64,3072]{1,0:T(8,128)(2,1)S(1)}, u32[]{:S(2)}, u32[]{:S(2)}) collective-permute-start(bf16[64,3072]{1,0:T(8,128)(2,1)S(1)} %get-tuple-element.79), channel_id=1, source_target_pairs={{0,48},{16,0},{32,16},{48,32},{1,49},{17,1},{33,17},{49,33},{2,50}... | collective-permute-start | bytes 1179656 | tf_op jit(solution)/shard_map/ppermute | solution.py:18
  45.5 5.7 %collective-permute-done.1 = bf16[64,3072]{1,0:T(8,128)(2,1)S(1)} collective-permute-done((bf16[64,3072]{1,0:T(8,128)(2,1)S(1)}, bf16[64,3072]{1,0:T(8,128)(2,1)S(1)}, u32[]{:S(2)}, u32[]{:S(2)}) %collective-permute-start.1) | collective-permute-done | bytes 393248 | tf_op jit(solution)/shard_map/ppermute | solution.py:18
  51.3 0.1 pad_maximum_fusion
  51.4 1.5 fusion.16
  53.0 1.4 fusion.13
  54.5 0.6 collective-permute-start.6
  55.2 0.3 copy.47
  55.5 0.6 collective-permute-done.6
  56.3 0.3 copy.48
  56.6 0.9 pad_maximum_fusion.1
  57.5 29.4 %all_to_all.10 = bf16[128,2,768]{2,1,0:T(2,128)(2,1)S(1)} all-to-all(bf16[128,2,768]{2,1,0:T(2,128)(2,1)S(1)} %pad_maximum_fusion.1), channel_id=1, replica_groups=mesh['group'=4,'x'=4,'z'=4,'h'=2,'c'=2] {'h','group','x','z'}, dimensions={0} | all-to-all | bytes 786432 | tf_op jit(solution)/shard_map/all_to_all | solution.py:147
  86.9 0.2 add_convert_fusion.6
  87.2 0.2 convolution_convert_fusion
  87.5 1.3 pad_maximum_fusion.2
  88.8 6.5 %all-to-all-start.1 = ((bf16[128,2,768]{2,1,0:T(2,128)(2,1)}), bf16[128,2,768]{2,1,0:T(2,128)(2,1)S(1)}, u32[]{:S(2)}, u32[]{:S(2)}) async-start(bf16[128,2,768]{2,1,0:T(2,128)(2,1)} %pad_maximum_fusion.2), calls=%async_computation.1 | async-start | bytes 786432 | tf_op jit(solution)/shard_map/all_to_all | solution.py:153
  95.3 0.3 fusion.23
  95.8 16.1 %all-to-all-done.1 = bf16[128,2,768]{2,1,0:T(2,128)(2,1)S(1)} async-done(((bf16[128,2,768]{2,1,0:T(2,128)(2,1)}), bf16[128,2,768]{2,1,0:T(2,128)(2,1)S(1)}, u32[]{:S(2)}, u32[]{:S(2)}) %all-to-all-start.1) | async-done | bytes 393248 | tf_op jit(solution)/shard_map/all_to_all | solution.py:153
  111.9 0.2 fusion.32
  112.1 0.2 fusion.29
  112.4 2.5 %all-gather = bf16[4,128,768]{2,1,0:T(8,128)(2,1)S(1)} all-gather(bf16[2,128,768]{2,1,0:T(8,128)(2,1)S(1)} %pad_maximum_fusion.3), channel_id=2, replica_groups=mesh['group'=4,'x'=4,'z'=4,'h'=2,'c'=2] {'c'}, dimensions={0}, use_global_device_ids=true | all-gather | bytes 1179648 | tf_op jit(solution)/shard_map/all_gather | solution.py:162
  114.9 0.2 fusion.19
  115.1 3.9 %fusion.5 = bf16[256,3072]{1,0:T(8,128)(2,1)S(1)} fusion(bf16[256,768]{1,0:T(8,128)(2,1)S(1)} %bitcast.98, bf16[2,768,3072]{2,1,0:T(8,128)(2,1)} %copy-done.1), kind=kOutput, calls=%fused_computation.7 | convolution fusion | flops 1208745984 | bytes 6684672 | tf_op jit(solution)/shard_map/sm,mk->sk/dot_general | solution.py:166
  119.1 0.2 fusion.18
  119.3 1.4 fusion.4
  120.8 1.2 collective-permute-start.8
  122.0 0.9 collective-permute-start.7
  123.0 9.0 %collective-permute-done.8 = bf16[64,3072]{1,0:T(8,128)(2,1)S(1)} collective-permute-done((bf16[64,3072]{1,0:T(8,128)(2,1)S(1)}, bf16[64,3072]{1,0:T(8,128)(2,1)S(1)}, u32[]{:S(2)}, u32[]{:S(2)}) %collective-permute-start.8) | collective-permute-done | bytes 393248 | tf_op jit(solution)/shard_map/ppermute | solution.py:18
  132.0 2.0 %collective-permute-done.7 = bf16[64,3072]{1,0:T(8,128)(2,1)S(1)} collective-permute-done((bf16[64,3072]{1,0:T(8,128)(2,1)S(1)}, bf16[64,3072]{1,0:T(8,128)(2,1)S(1)}, u32[]{:S(2)}, u32[]{:S(2)}) %collective-permute-start.7) | collective-permute-done | bytes 393248 | tf_op jit(solution)/shard_map/ppermute | solution.py:18
  134.1 0.4 collective-permute-start.10
  134.5 1.7 %collective-permute-start.9 = (bf16[32,3072]{1,0:T(8,128)(2,1)S(1)}, bf16[32,3072]{1,0:T(8,128)(2,1)S(1)}, u32[]{:S(2)}, u32[]{:S(2)}) collective-permute-start(bf16[32,3072]{1,0:T(8,128)(2,1)S(1)} %get-tuple-element.67), channel_id=1, source_target_pairs={{0,16},{16,32},{32,48},{48,0},{1,17},{17,33},{33,49},{49,1},{2,18}... | collective-permute-start | bytes 589832 | tf_op jit(solution)/shard_map/ppermute | solution.py:18
  136.4 3.2 %collective-permute-start.13 = (bf16[64,3072]{1,0:T(8,128)(2,1)S(1)}, bf16[64,3072]{1,0:T(8,128)(2,1)S(1)}, u32[]{:S(2)}, u32[]{:S(2)}) collective-permute-start(bf16[64,3072]{1,0:T(8,128)(2,1)S(1)} %pad_maximum_fusion.5), channel_id=1, source_target_pairs={{0,48},{16,0},{32,16},{48,32},{1,49},{17,1},{33,17},{49,33},{2,50}... | collective-permute-start | bytes 1179656 | tf_op jit(solution)/shard_map/ppermute | solution.py:18
  139.6 2.4 %collective-permute-done.10 = bf16[32,3072]{1,0:T(8,128)(2,1)S(1)} collective-permute-done((bf16[32,3072]{1,0:T(8,128)(2,1)S(1)}, bf16[32,3072]{1,0:T(8,128)(2,1)S(1)}, u32[]{:S(2)}, u32[]{:S(2)}) %collective-permute-start.10) | collective-permute-done | bytes 196640 | tf_op jit(solution)/shard_map/ppermute | solution.py:18
  142.0 1.5 collective-permute-done.9
  143.5 0.1 convert_add_fusion.3
  143.7 1.0 collective-permute-start.16
  144.7 3.0 %collective-permute-start.17 = (bf16[16,3072]{1,0:T(8,128)(2,1)S(1)}, bf16[16,3072]{1,0:T(8,128)(2,1)S(1)}, u32[]{:S(2)}, u32[]{:S(2)}) collective-permute-start(bf16[16,3072]{1,0:T(8,128)(2,1)S(1)} %get-tuple-element.82), channel_id=1, source_target_pairs={{0,8},{4,12},{8,0},{12,4},{1,9},{5,13},{9,1},{13,5},{2,10},{6,14},... | collective-permute-start | bytes 294920 | tf_op jit(solution)/shard_map/ppermute | solution.py:18
  147.8 2.2 %collective-permute-done.12 = bf16[64,3072]{1,0:T(8,128)(2,1)S(1)} collective-permute-done((bf16[64,3072]{1,0:T(8,128)(2,1)S(1)}, bf16[64,3072]{1,0:T(8,128)(2,1)S(1)}, u32[]{:S(2)}, u32[]{:S(2)}) %collective-permute-start.12) | collective-permute-done | bytes 393248 | tf_op jit(solution)/shard_map/ppermute | solution.py:18
  149.9 1.7 %collective-permute-start.11 = (bf16[2,64,768]{2,1,0:T(8,128)(2,1)S(1)}, bf16[2,64,768]{2,1,0:T(8,128)(2,1)S(1)}, u32[]{:S(2)}, u32[]{:S(2)}) collective-permute-start(bf16[2,64,768]{2,1,0:T(8,128)(2,1)S(1)} %pad_maximum_fusion.7), channel_id=1, source_target_pairs={{0,2},{2,0},{1,3},{3,1},{4,6},{6,4},{5,7},{7,5},{8,10},{10,8},{9,1... | collective-permute-start | bytes 589832 | tf_op jit(solution)/shard_map/ppermute | solution.py:18
  151.9 2.0 %collective-permute-start.14 = (bf16[32,3072]{1,0:T(8,128)(2,1)S(1)}, bf16[32,3072]{1,0:T(8,128)(2,1)S(1)}, u32[]{:S(2)}, u32[]{:S(2)}) collective-permute-start(bf16[32,3072]{1,0:T(8,128)(2,1)S(1)} %get-tuple-element.65), channel_id=1, source_target_pairs={{0,16},{16,32},{32,48},{48,0},{1,17},{17,33},{33,49},{49,1},{2,18}... | collective-permute-start | bytes 589832 | tf_op jit(solution)/shard_map/ppermute | solution.py:18
  153.9 3.0 %collective-permute-done.17 = bf16[16,3072]{1,0:T(8,128)(2,1)S(1)} collective-permute-done((bf16[16,3072]{1,0:T(8,128)(2,1)S(1)}, bf16[16,3072]{1,0:T(8,128)(2,1)S(1)}, u32[]{:S(2)}, u32[]{:S(2)}) %collective-permute-start.17) | collective-permute-done | bytes 98336 | tf_op jit(solution)/shard_map/ppermute | solution.py:18
  156.9 1.8 %collective-permute-done.18 = bf16[16,3072]{1,0:T(8,128)(2,1)S(1)} collective-permute-done((bf16[16,3072]{1,0:T(8,128)(2,1)S(1)}, bf16[16,3072]{1,0:T(8,128)(2,1)S(1)}, u32[]{:S(2)}, u32[]{:S(2)}) %collective-permute-start.18) | collective-permute-done | bytes 98336 | tf_op jit(solution)/shard_map/ppermute | solution.py:18
  158.7 0.2 collective-permute-done.14
  158.8 4.2 %collective-permute-done.11 = bf16[2,64,768]{2,1,0:T(8,128)(2,1)S(1)} collective-permute-done((bf16[2,64,768]{2,1,0:T(8,128)(2,1)S(1)}, bf16[2,64,768]{2,1,0:T(8,128)(2,1)S(1)}, u32[]{:S(2)}, u32[]{:S(2)}) %collective-permute-start.11) | collective-permute-done | bytes 196640 | tf_op jit(solution)/shard_map/ppermute | solution.py:18
  163.0 0.1 convert_add_fusion.2
  163.2 1.0 collective-permute-start.19
  164.2 1.2 collective-permute-start.20
  165.4 0.3 collective-permute-start.21
  165.9 0.9 copy.50
  166.8 2.2 %collective-permute-done.19 = bf16[16,3072]{1,0:T(8,128)(2,1)S(1)} collective-permute-done((bf16[16,3072]{1,0:T(8,128)(2,1)S(1)}, bf16[16,3072]{1,0:T(8,128)(2,1)S(1)}, u32[]{:S(2)}, u32[]{:S(2)}) %collective-permute-start.19) | collective-permute-done | bytes 98336 | tf_op jit(solution)/shard_map/ppermute | solution.py:18
  169.0 2.2 %collective-permute-done.20 = bf16[16,3072]{1,0:T(8,128)(2,1)S(1)} collective-permute-done((bf16[16,3072]{1,0:T(8,128)(2,1)S(1)}, bf16[16,3072]{1,0:T(8,128)(2,1)S(1)}, u32[]{:S(2)}, u32[]{:S(2)}) %collective-permute-start.20) | collective-permute-done | bytes 98336 | tf_op jit(solution)/shard_map/ppermute | solution.py:18
  171.2 2.0 %collective-permute-done.21 = bf16[16,3072]{1,0:T(8,128)(2,1)S(1)} collective-permute-done((bf16[16,3072]{1,0:T(8,128)(2,1)S(1)}, bf16[16,3072]{1,0:T(8,128)(2,1)S(1)}, u32[]{:S(2)}, u32[]{:S(2)}) %collective-permute-start.21) | collective-permute-done | bytes 98336 | tf_op jit(solution)/shard_map/ppermute | solution.py:18
  173.3 0.9 copy.51
  (70 shorter events, 2.3 us)
Async XLA Ops:
  0.6 29.4 %copy-start.3 = (s32[8]{0:T(128)S(1)}, s32[8]{0:T(128)}, u32[]{:S(2)}) copy-start(s32[8]{0:T(128)} %param.10) | copy-start | bytes 100
  0.6 29.6 %copy-start.2 = (s32[8,16]{1,0:T(8,128)S(1)}, s32[8,16]{1,0:T(8,128)}, u32[]{:S(2)}) copy-start(s32[8,16]{1,0:T(8,128)} %param.11) | copy-start | bytes 1540
  20.7 21.4 %collective-permute-start.2 = (bf16[2,64,3072]{2,1,0:T(8,128)(2,1)S(1)}, bf16[2,64,3072]{2,1,0:T(8,128)(2,1)S(1)}, u32[]{:S(2)}, u32[]{:S(2)}) collective-permute-start(bf16[2,64,3072]{2,1,0:T(8,128)(2,1)S(1)} %all_gather.9), channel_id=1, source_target_pairs={{0,48},{16,0},{32,16},{48,32},{1,49},{17,1},{33,17},{49,33},{2,50}... | collective-permute-start | bytes 2359304 | tf_op jit(solution)/shard_map/ppermute | solution.py:18
  23.6 18.5 %collective-permute-start = (bf16[2,64,3072]{2,1,0:T(8,128)(2,1)S(1)}, bf16[2,64,3072]{2,1,0:T(8,128)(2,1)S(1)}, u32[]{:S(2)}, u32[]{:S(2)}) collective-permute-start(bf16[2,64,3072]{2,1,0:T(8,128)(2,1)S(1)} %all_gather.9), channel_id=1, source_target_pairs={{0,16},{16,32},{32,48},{48,0},{1,17},{17,33},{33,49},{49,1},{2,18}... | collective-permute-start | bytes 2359304 | tf_op jit(solution)/shard_map/ppermute | solution.py:18
  25.3 26.1 %collective-permute-start.3 = (bf16[64,2,768]{2,0,1:T(8,128)(2,1)S(1)}, bf16[64,2,768]{2,0,1:T(8,128)(2,1)S(1)}, u32[]{:S(2)}, u32[]{:S(2)}) collective-permute-start(bf16[64,2,768]{2,0,1:T(8,128)(2,1)S(1)} %copy.59), channel_id=1, source_target_pairs={{0,2},{2,0},{1,3},{3,1},{4,6},{6,4},{5,7},{7,5},{8,10},{10,8},{9,1... | collective-permute-start | bytes 589832 | tf_op jit(solution)/shard_map/ppermute | solution.py:18
  30.7 3.7 %copy-start = (bf16[2,768,3072]{2,1,0:T(8,128)(2,1)S(1)}, bf16[2,768,3072]{2,1,0:T(8,128)(2,1)}, u32[]{:S(2)}) copy-start(bf16[2,768,3072]{2,1,0:T(8,128)(2,1)} %fronts_ref.1) | copy-start | bytes 28311556
  37.9 15.2 %copy-start.1 = (bf16[2,768,3072]{2,1,0:T(8,128)(2,1)}, bf16[2,768,3072]{2,1,0:T(8,128)(2,1)S(1)}, u32[]{:S(2)}) copy-start(bf16[2,768,3072]{2,1,0:T(8,128)(2,1)S(1)} %shard_map.77) | copy-start | bytes 28311556
  42.1 9.2 %collective-permute-start.1 = (bf16[64,3072]{1,0:T(8,128)(2,1)S(1)}, bf16[64,3072]{1,0:T(8,128)(2,1)S(1)}, u32[]{:S(2)}, u32[]{:S(2)}) collective-permute-start(bf16[64,3072]{1,0:T(8,128)(2,1)S(1)} %get-tuple-element.76), channel_id=1, source_target_pairs={{0,16},{16,32},{32,48},{48,0},{1,17},{17,33},{33,49},{49,1},{2,18}... | collective-permute-start | bytes 1179656 | tf_op jit(solution)/shard_map/ppermute | solution.py:18
  42.3 10.8 %collective-permute-start.5 = (bf16[64,3072]{1,0:T(8,128)(2,1)S(1)}, bf16[64,3072]{1,0:T(8,128)(2,1)S(1)}, u32[]{:S(2)}, u32[]{:S(2)}) collective-permute-start(bf16[64,3072]{1,0:T(8,128)(2,1)S(1)} %get-tuple-element.79), channel_id=1, source_target_pairs={{0,48},{16,0},{32,16},{48,32},{1,49},{17,1},{33,17},{49,33},{2,50}... | collective-permute-start | bytes 1179656 | tf_op jit(solution)/shard_map/ppermute | solution.py:18
  52.9 2.2 %collective-permute-start.4 = (bf16[2,64,768]{2,1,0:T(8,128)(2,1)S(1)}, bf16[2,64,768]{2,1,0:T(8,128)(2,1)S(1)}, u32[]{:S(2)}, u32[]{:S(2)}) collective-permute-start(bf16[2,64,768]{2,1,0:T(8,128)(2,1)S(1)} %dynamic-slice_bitcast_fusion.1), channel_id=1, source_target_pairs={{0,1},{1,0},{2,3},{3,2},{4,5},{5,4},{6,7},{7,6},{8,9},{9,8},{10,11... | collective-permute-start | bytes 589832 | tf_op jit(solution)/shard_map/ppermute | solution.py:18
  54.5 1.6 collective-permute-start.6
  88.8 30.5 %slice-start = ((s8[9437184]{0:T(1024)(128)(4,1)}), s8[1048576]{0:T(1024)(128)(4,1)S(1)}, s32[]{:S(2)}) async-start(s8[9437184]{0:T(1024)(128)(4,1)} %bitcast.83), calls=%async_computation.2 | async-start | bytes 2097152
  88.8 23.1 %all-to-all-start.1 = ((bf16[128,2,768]{2,1,0:T(2,128)(2,1)}), bf16[128,2,768]{2,1,0:T(2,128)(2,1)S(1)}, u32[]{:S(2)}, u32[]{:S(2)}) async-start(bf16[128,2,768]{2,1,0:T(2,128)(2,1)} %pad_maximum_fusion.2), calls=%async_computation.1 | async-start | bytes 786432 | tf_op jit(solution)/shard_map/all_to_all | solution.py:153
  112.3 7.0 %slice-start.1 = ((s8[9437184]{0:T(1024)(128)(4,1)}), s8[4194304]{0:T(1024)(128)(4,1)S(1)}, s32[]{:S(2)}) async-start(s8[9437184]{0:T(1024)(128)(4,1)} %bitcast.83), calls=%async_computation.3 | async-start | bytes 8388608
  115.1 4.2 %slice-start.2 = ((s8[9437184]{0:T(1024)(128)(4,1)}), s8[4194304]{0:T(1024)(128)(4,1)S(1)}, s32[]{:S(2)}) async-start(s8[9437184]{0:T(1024)(128)(4,1)} %bitcast.83), calls=%async_computation.4 | async-start | bytes 8388608
  120.8 11.2 %collective-permute-start.8 = (bf16[64,3072]{1,0:T(8,128)(2,1)S(1)}, bf16[64,3072]{1,0:T(8,128)(2,1)S(1)}, u32[]{:S(2)}, u32[]{:S(2)}) collective-permute-start(bf16[64,3072]{1,0:T(8,128)(2,1)S(1)} %pad_maximum_fusion.4), channel_id=1, source_target_pairs={{0,48},{16,0},{32,16},{48,32},{1,49},{17,1},{33,17},{49,33},{2,50}... | collective-permute-start | bytes 1179656 | tf_op jit(solution)/shard_map/ppermute | solution.py:18
  122.0 12.1 %collective-permute-start.7 = (bf16[64,3072]{1,0:T(8,128)(2,1)S(1)}, bf16[64,3072]{1,0:T(8,128)(2,1)S(1)}, u32[]{:S(2)}, u32[]{:S(2)}) collective-permute-start(bf16[64,3072]{1,0:T(8,128)(2,1)S(1)} %slice.216), channel_id=1, source_target_pairs={{0,16},{16,32},{32,48},{48,0},{1,17},{17,33},{33,49},{49,1},{2,18}... | collective-permute-start | bytes 1179656 | tf_op jit(solution)/shard_map/ppermute | solution.py:18
  134.1 7.9 %collective-permute-start.10 = (bf16[32,3072]{1,0:T(8,128)(2,1)S(1)}, bf16[32,3072]{1,0:T(8,128)(2,1)S(1)}, u32[]{:S(2)}, u32[]{:S(2)}) collective-permute-start(bf16[32,3072]{1,0:T(8,128)(2,1)S(1)} %get-tuple-element.66), channel_id=1, source_target_pairs={{0,48},{16,0},{32,16},{48,32},{1,49},{17,1},{33,17},{49,33},{2,50}... | collective-permute-start | bytes 589832 | tf_op jit(solution)/shard_map/ppermute | solution.py:18
  134.5 9.0 %collective-permute-start.9 = (bf16[32,3072]{1,0:T(8,128)(2,1)S(1)}, bf16[32,3072]{1,0:T(8,128)(2,1)S(1)}, u32[]{:S(2)}, u32[]{:S(2)}) collective-permute-start(bf16[32,3072]{1,0:T(8,128)(2,1)S(1)} %get-tuple-element.67), channel_id=1, source_target_pairs={{0,16},{16,32},{32,48},{48,0},{1,17},{17,33},{33,49},{49,1},{2,18}... | collective-permute-start | bytes 589832 | tf_op jit(solution)/shard_map/ppermute | solution.py:18
  136.3 13.6 %collective-permute-start.12 = (bf16[64,3072]{1,0:T(8,128)(2,1)S(1)}, bf16[64,3072]{1,0:T(8,128)(2,1)S(1)}, u32[]{:S(2)}, u32[]{:S(2)}) collective-permute-start(bf16[64,3072]{1,0:T(8,128)(2,1)S(1)} %slice.220), channel_id=1, source_target_pairs={{0,16},{16,32},{32,48},{48,0},{1,17},{17,33},{33,49},{49,1},{2,18}... | collective-permute-start | bytes 1179656 | tf_op jit(solution)/shard_map/ppermute | solution.py:18
  136.4 15.3 %collective-permute-start.13 = (bf16[64,3072]{1,0:T(8,128)(2,1)S(1)}, bf16[64,3072]{1,0:T(8,128)(2,1)S(1)}, u32[]{:S(2)}, u32[]{:S(2)}) collective-permute-start(bf16[64,3072]{1,0:T(8,128)(2,1)S(1)} %pad_maximum_fusion.5), channel_id=1, source_target_pairs={{0,48},{16,0},{32,16},{48,32},{1,49},{17,1},{33,17},{49,33},{2,50}... | collective-permute-start | bytes 1179656 | tf_op jit(solution)/shard_map/ppermute | solution.py:18
  143.7 8.2 %collective-permute-start.16 = (bf16[16,3072]{1,0:T(8,128)(2,1)S(1)}, bf16[16,3072]{1,0:T(8,128)(2,1)S(1)}, u32[]{:S(2)}, u32[]{:S(2)}) collective-permute-start(bf16[16,3072]{1,0:T(8,128)(2,1)S(1)} %slice.301), channel_id=1, source_target_pairs={{0,4},{4,8},{8,12},{12,0},{1,5},{5,9},{9,13},{13,1},{2,6},{6,10},{... | collective-permute-start | bytes 294920 | tf_op jit(solution)/shard_map/ppermute | solution.py:18
  144.7 12.2 %collective-permute-start.17 = (bf16[16,3072]{1,0:T(8,128)(2,1)S(1)}, bf16[16,3072]{1,0:T(8,128)(2,1)S(1)}, u32[]{:S(2)}, u32[]{:S(2)}) collective-permute-start(bf16[16,3072]{1,0:T(8,128)(2,1)S(1)} %get-tuple-element.82), channel_id=1, source_target_pairs={{0,8},{4,12},{8,0},{12,4},{1,9},{5,13},{9,1},{13,5},{2,10},{6,14},... | collective-permute-start | bytes 294920 | tf_op jit(solution)/shard_map/ppermute | solution.py:18
  147.8 10.9 %collective-permute-start.18 = (bf16[16,3072]{1,0:T(8,128)(2,1)S(1)}, bf16[16,3072]{1,0:T(8,128)(2,1)S(1)}, u32[]{:S(2)}, u32[]{:S(2)}) collective-permute-start(bf16[16,3072]{1,0:T(8,128)(2,1)S(1)} %get-tuple-element.83), channel_id=1, source_target_pairs={{0,12},{4,0},{8,4},{12,8},{1,13},{5,1},{9,5},{13,9},{2,14},{6,2},{... | collective-permute-start | bytes 294920 | tf_op jit(solution)/shard_map/ppermute | solution.py:18
  149.9 13.1 %collective-permute-start.11 = (bf16[2,64,768]{2,1,0:T(8,128)(2,1)S(1)}, bf16[2,64,768]{2,1,0:T(8,128)(2,1)S(1)}, u32[]{:S(2)}, u32[]{:S(2)}) collective-permute-start(bf16[2,64,768]{2,1,0:T(8,128)(2,1)S(1)} %pad_maximum_fusion.7), channel_id=1, source_target_pairs={{0,2},{2,0},{1,3},{3,1},{4,6},{6,4},{5,7},{7,5},{8,10},{10,8},{9,1... | collective-permute-start | bytes 589832 | tf_op jit(solution)/shard_map/ppermute | solution.py:18
  151.8 6.9 %collective-permute-start.15 = (bf16[32,3072]{1,0:T(8,128)(2,1)S(1)}, bf16[32,3072]{1,0:T(8,128)(2,1)S(1)}, u32[]{:S(2)}, u32[]{:S(2)}) collective-permute-start(bf16[32,3072]{1,0:T(8,128)(2,1)S(1)} %get-tuple-element.64), channel_id=1, source_target_pairs={{0,48},{16,0},{32,16},{48,32},{1,49},{17,1},{33,17},{49,33},{2,50}... | collective-permute-start | bytes 589832 | tf_op jit(solution)/shard_map/ppermute | solution.py:18
  151.9 7.0 %collective-permute-start.14 = (bf16[32,3072]{1,0:T(8,128)(2,1)S(1)}, bf16[32,3072]{1,0:T(8,128)(2,1)S(1)}, u32[]{:S(2)}, u32[]{:S(2)}) collective-permute-start(bf16[32,3072]{1,0:T(8,128)(2,1)S(1)} %get-tuple-element.65), channel_id=1, source_target_pairs={{0,16},{16,32},{32,48},{48,0},{1,17},{17,33},{33,49},{49,1},{2,18}... | collective-permute-start | bytes 589832 | tf_op jit(solution)/shard_map/ppermute | solution.py:18
  163.2 5.8 %collective-permute-start.19 = (bf16[16,3072]{1,0:T(8,128)(2,1)S(1)}, bf16[16,3072]{1,0:T(8,128)(2,1)S(1)}, u32[]{:S(2)}, u32[]{:S(2)}) collective-permute-start(bf16[16,3072]{1,0:T(8,128)(2,1)S(1)} %slice.300), channel_id=1, source_target_pairs={{0,4},{4,8},{8,12},{12,0},{1,5},{5,9},{9,13},{13,1},{2,6},{6,10},{... | collective-permute-start | bytes 294920 | tf_op jit(solution)/shard_map/ppermute | solution.py:18
  164.2 7.0 %collective-permute-start.20 = (bf16[16,3072]{1,0:T(8,128)(2,1)S(1)}, bf16[16,3072]{1,0:T(8,128)(2,1)S(1)}, u32[]{:S(2)}, u32[]{:S(2)}) collective-permute-start(bf16[16,3072]{1,0:T(8,128)(2,1)S(1)} %get-tuple-element.84), channel_id=1, source_target_pairs={{0,8},{4,12},{8,0},{12,4},{1,9},{5,13},{9,1},{13,5},{2,10},{6,14},... | collective-permute-start | bytes 294920 | tf_op jit(solution)/shard_map/ppermute | solution.py:18
  165.4 7.8 %collective-permute-start.21 = (bf16[16,3072]{1,0:T(8,128)(2,1)S(1)}, bf16[16,3072]{1,0:T(8,128)(2,1)S(1)}, u32[]{:S(2)}, u32[]{:S(2)}) collective-permute-start(bf16[16,3072]{1,0:T(8,128)(2,1)S(1)} %get-tuple-element.85), channel_id=1, source_target_pairs={{0,12},{4,0},{8,4},{12,8},{1,13},{5,1},{9,5},{13,9},{2,14},{6,2},{... | collective-permute-start | bytes 294920 | tf_op jit(solution)/shard_map/ppermute | solution.py:18

commit v3 on v2

--- a/solution.py
+++ b/solution.py
@@ -150,7 +150,10 @@
     extension = jnp.einsum("ij,jk->ik", weight, arrived, preferred_element_type=F32).astype(BF16)
     extension = extension.reshape(slab, local, tile_rows)
     extension = jnp.concatenate([extension, extension], axis=0)
+    away = jnp.stack([pick(half, 1 - h).astype(BF16) for half in halves])
+    away, extension = lax.optimization_barrier((away, extension))
     extension = lax.all_to_all(extension, spread, split_axis=0, concat_axis=0, tiled=True)
+    received, extension = lax.optimization_barrier((shift(away, "h", 1), extension))
     combined = second.reshape(extension.shape).astype(F32) + extension.astype(F32)
     combined = combined.astype(BF16)
 
@@ -173,9 +176,6 @@
     near_0, product_1, pieces_1 = lax.optimization_barrier((near_0, product_1, pieces_1))
     far_0 = second_step(product_0, near_0)
     near_1 = first_step(pieces_1)
-    away = jnp.stack([pick(half, 1 - h).astype(BF16) for half in halves])
-    away, far_0 = lax.optimization_barrier((away, far_0))
-    received = shift(away, "h", 1)
     total_0 = last_step(product_0, near_0, far_0)
     far_1 = second_step(product_1, near_1)
     received, far_1 = lax.optimization_barrier((received, far_1))

time: 174 us -> 176 us (1.011)
  blocking collectives: 50.5 us -> 21.1 us
  starting transfers between devices: 36 us -> 53.8 us
  waiting for transfers between devices: 59.3 us -> 67.6 us
  other arithmetic: 4.89 us -> 8.29 us
    all_to_all x1 -> x0, blocking collectives: 29.4 us -> none  [shards(): lax.all_to_all(outgoing, spread, split_axis=0, concat_axis=0, tiled=True)]
    all_to_all x0 -> x1, waiting for transfers between devices: none -> 17.5 us  [shards(): lax.all_to_all(outgoing, spread, split_axis=0, concat_axis=0, tiled=True)]
    all_to_all x1, waiting for transfers between devices: 16.1 us -> 0.07 us  [shards(): lax.all_to_all(extension, spread, split_axis=0, concat_axis=0, tiled=True)]
    all_to_all x0 -> x1, starting transfers between devices: none -> 12 us  [shards(): lax.all_to_all(outgoing, spread, split_axis=0, concat_axis=0, tiled=True)]
    ppermute x22, waiting for transfers between devices: 43.2 us -> 50 us  [shift(): return lax.ppermute(value, axis, [(i, (i + by) % n) for i in range(n)])]
    ppermute x22, starting transfers between devices: 29.5 us -> 35.4 us  [shift(): return lax.ppermute(value, axis, [(i, (i + by) % n) for i in range(n)])]
    unnamed x16 -> x26, local copies, waits for them, and re-layouts: 5.47 us -> 5.49 us
  transfers between devices with their start and end apart: 23 -> 24, of which waited for: 16 -> 18; matrix products, arithmetic and copies ran while one was open for 5% -> 6% of each run, Pallas kernels for 2% -> 2%
where the time goes in v3:
time: 176 us; the launch traced here: 175 us
  waiting for transfers between devices  67.6 us (38%)
  starting transfers between devices  53.8 us (31%)
  blocking collectives  21.1 us (12%)
  local copies, waits for them, and re-layouts  11.1 us (6%)
  matrix products  8.45 us (5%)
  other arithmetic  8.29 us (5%)
  Pallas kernels  3.47 us (2%)
    ppermute x22, waiting for transfers between devices, shift(): return lax.ppermute(value, axis, [(i, (i + by) % n) for i in range(n)])  50 us
    ppermute x22, starting transfers between devices, shift(): return lax.ppermute(value, axis, [(i, (i + by) % n) for i in range(n)])  35.4 us
    all_gather x1, blocking collectives, shards(): columns = lax.all_gather(mine, 'z', axis=1, tiled=True)  18.6 us
    all_to_all x1, waiting for transfers between devices, shards(): lax.all_to_all(outgoing, spread, split_axis=0, concat_axis=0, tiled=True)  17.5 us
    all_to_all x1, starting transfers between devices, shards(): lax.all_to_all(outgoing, spread, split_axis=0, concat_axis=0, tiled=True)  12 us
    all_to_all x1, starting transfers between devices, shards(): lax.all_to_all(extension, spread, split_axis=0, concat_axis=0, tiled=True)  6.53 us
    unnamed x26, local copies, waits for them, and re-layouts  5.49 us
    dot_general x2, matrix products, multiplied(): jnp.einsum('sm,mk->sk', ordered[f], masked[f], preferred_element_type=F32)  5.34 us
  transfers between devices with their start and end apart: 24, of which 18 were waited for; matrix products, arithmetic and copies ran while one was open for 6% of the time, Pallas kernels for 2%

profile of v3, /device:TPU:32, one launch (start us, length us, event | category | flops | bytes accessed | tf_op | source)
XLA Modules:
  0.0 175.1 jit_solution(3166216132089550545)
XLA Ops:
  0.7 1.4 fusion.63
  2.1 18.6 %all_gather.9 = bf16[2,64,3072]{2,1,0:T(8,128)(2,1)S(1)} all-gather(bf16[2,16,3072]{2,1,0:T(8,128)(2,1)S(1)} %pad_maximum_fusion.6), channel_id=1, replica_groups=mesh['group'=4,'x'=4,'z'=4,'h'=2,'c'=2] {'z'}, dimensions={1}, use_global_device_ids=true | all-gather | bytes 983040 | tf_op jit(solution)/shard_map/all_gather | solution.py:130
  20.7 2.8 %collective-permute-start.2 = (bf16[2,64,3072]{2,1,0:T(8,128)(2,1)S(1)}, bf16[2,64,3072]{2,1,0:T(8,128)(2,1)S(1)}, u32[]{:S(2)}, u32[]{:S(2)}) collective-permute-start(bf16[2,64,3072]{2,1,0:T(8,128)(2,1)S(1)} %all_gather.9), channel_id=1, source_target_pairs={{0,48},{16,0},{32,16},{48,32},{1,49},{17,1},{33,17},{49,33},{2,50}... | collective-permute-start | bytes 2359304 | tf_op jit(solution)/shard_map/ppermute | solution.py:18
  23.6 0.7 dynamic_slice.58.sizes_ref
  24.3 0.9 copy.59
  25.3 4.7 %collective-permute-start.3 = (bf16[64,2,768]{2,0,1:T(8,128)(2,1)S(1)}, bf16[64,2,768]{2,0,1:T(8,128)(2,1)S(1)}, u32[]{:S(2)}, u32[]{:S(2)}) collective-permute-start(bf16[64,2,768]{2,0,1:T(8,128)(2,1)S(1)} %copy.59), channel_id=1, source_target_pairs={{0,2},{2,0},{1,3},{3,1},{4,6},{6,4},{5,7},{7,5},{8,10},{10,8},{9,1... | collective-permute-start | bytes 589832 | tf_op jit(solution)/shard_map/ppermute | solution.py:18
  30.1 0.1 eq.33
  30.7 3.7 %copy-done = bf16[2,768,3072]{2,1,0:T(8,128)(2,1)S(1)} copy-done((bf16[2,768,3072]{2,1,0:T(8,128)(2,1)S(1)}, bf16[2,768,3072]{2,1,0:T(8,128)(2,1)}, u32[]{:S(2)}) %copy-start) | copy-done | bytes 9437208
  34.4 3.5 %shard_map.77 = bf16[2,768,3072]{2,1,0:T(8,128)(2,1)S(1)} custom-call(s32[2]{0:T(128)S(1)} %dynamic_slice.58.sizes_ref, s32[2]{0:T(128)S(1)} %pad_add_fusion.origin_ref, bf16[2,768,3072]{2,1,0:T(8,128)(2,1)S(1)} %copy-done), custom_call_target="tpu_custom_call" | custom-call | tf_op jit(solution)/shard_map/pallas_call | solution.py:53
  37.9 4.1 %collective-permute-done = bf16[2,64,3072]{2,1,0:T(8,128)(2,1)S(1)} collective-permute-done((bf16[2,64,3072]{2,1,0:T(8,128)(2,1)S(1)}, bf16[2,64,3072]{2,1,0:T(8,128)(2,1)S(1)}, u32[]{:S(2)}, u32[]{:S(2)}) %collective-permute-start) | collective-permute-done | bytes 786464 | tf_op jit(solution)/shard_map/ppermute | solution.py:18
  42.3 3.3 %collective-permute-start.5 = (bf16[64,3072]{1,0:T(8,128)(2,1)S(1)}, bf16[64,3072]{1,0:T(8,128)(2,1)S(1)}, u32[]{:S(2)}, u32[]{:S(2)}) collective-permute-start(bf16[64,3072]{1,0:T(8,128)(2,1)S(1)} %get-tuple-element.81), channel_id=1, source_target_pairs={{0,48},{16,0},{32,16},{48,32},{1,49},{17,1},{33,17},{49,33},{2,50}... | collective-permute-start | bytes 1179656 | tf_op jit(solution)/shard_map/ppermute | solution.py:18
  45.5 5.7 %collective-permute-done.1 = bf16[64,3072]{1,0:T(8,128)(2,1)S(1)} collective-permute-done((bf16[64,3072]{1,0:T(8,128)(2,1)S(1)}, bf16[64,3072]{1,0:T(8,128)(2,1)S(1)}, u32[]{:S(2)}, u32[]{:S(2)}) %collective-permute-start.1) | collective-permute-done | bytes 393248 | tf_op jit(solution)/shard_map/ppermute | solution.py:18
  51.4 1.5 fusion.16
  53.1 1.4 fusion.13
  54.5 0.6 collective-permute-start.6
  55.2 0.3 copy.45
  55.6 0.6 collective-permute-done.6
  56.3 0.3 copy.46
  56.6 1.7 pad_maximum_fusion.1
  58.3 12.0 %all-to-all-start = ((bf16[128,2,768]{2,1,0:T(2,128)(2,1)}), bf16[128,2,768]{2,1,0:T(2,128)(2,1)S(1)}, u32[]{:S(2)}, u32[]{:S(2)}) async-start(bf16[128,2,768]{2,1,0:T(2,128)(2,1)} %pad_maximum_fusion.1), calls=%async_computation | async-start | bytes 786432 | tf_op jit(solution)/shard_map/all_to_all | solution.py:147
  70.4 17.5 %all-to-all-done = bf16[128,2,768]{2,1,0:T(2,128)(2,1)S(1)} async-done(((bf16[128,2,768]{2,1,0:T(2,128)(2,1)}), bf16[128,2,768]{2,1,0:T(2,128)(2,1)S(1)}, u32[]{:S(2)}, u32[]{:S(2)}) %all-to-all-start) | async-done | bytes 393248 | tf_op jit(solution)/shard_map/all_to_all | solution.py:147
  87.9 0.2 add_convert_fusion.6
  88.2 0.2 convolution_convert_fusion
  88.5 1.3 pad_maximum_fusion.2
  89.8 6.5 %all-to-all-start.1 = ((bf16[128,2,768]{2,1,0:T(2,128)(2,1)}), bf16[128,2,768]{2,1,0:T(2,128)(2,1)S(1)}, u32[]{:S(2)}, u32[]{:S(2)}) async-start(bf16[128,2,768]{2,1,0:T(2,128)(2,1)} %pad_maximum_fusion.2), calls=%async_computation.1 | async-start | bytes 786432 | tf_op jit(solution)/shard_map/all_to_all | solution.py:155
  96.3 5.0 %collective-permute-start.7 = (bf16[2,64,768]{2,1,0:T(8,128)(2,1)S(1)}, bf16[2,64,768]{2,1,0:T(8,128)(2,1)S(1)}, u32[]{:S(2)}, u32[]{:S(2)}) collective-permute-start(bf16[2,64,768]{2,1,0:T(8,128)(2,1)S(1)} %pad_maximum_fusion.7), channel_id=1, source_target_pairs={{0,2},{2,0},{1,3},{3,1},{4,6},{6,4},{5,7},{7,5},{8,10},{10,8},{9,1... | collective-permute-start | bytes 589832 | tf_op jit(solution)/shard_map/ppermute | solution.py:18
  101.3 0.3 fusion.23
  101.7 14.9 %collective-permute-done.7 = bf16[2,64,768]{2,1,0:T(8,128)(2,1)S(1)} collective-permute-done((bf16[2,64,768]{2,1,0:T(8,128)(2,1)S(1)}, bf16[2,64,768]{2,1,0:T(8,128)(2,1)S(1)}, u32[]{:S(2)}, u32[]{:S(2)}) %collective-permute-start.7) | collective-permute-done | bytes 196640 | tf_op jit(solution)/shard_map/ppermute | solution.py:18
  116.8 0.2 fusion.32
  117.0 0.2 fusion.29
  117.2 2.5 %all-gather = bf16[4,128,768]{2,1,0:T(8,128)(2,1)S(1)} all-gather(bf16[2,128,768]{2,1,0:T(8,128)(2,1)S(1)} %pad_maximum_fusion.3), channel_id=2, replica_groups=mesh['group'=4,'x'=4,'z'=4,'h'=2,'c'=2] {'c'}, dimensions={0}, use_global_device_ids=true | all-gather | bytes 1179648 | tf_op jit(solution)/shard_map/all_gather | solution.py:165
  119.8 0.2 fusion.19
  120.0 3.9 %fusion.5 = bf16[256,3072]{1,0:T(8,128)(2,1)S(1)} fusion(bf16[256,768]{1,0:T(8,128)(2,1)S(1)} %bitcast.98, bf16[2,768,3072]{2,1,0:T(8,128)(2,1)} %copy-done.1), kind=kOutput, calls=%fused_computation.7 | convolution fusion | flops 1208745984 | bytes 6684672 | tf_op jit(solution)/shard_map/sm,mk->sk/dot_general | solution.py:169
  124.0 0.2 fusion.18
  124.2 1.4 fusion.4
  125.7 2.8 %collective-permute-start.9 = (bf16[64,3072]{1,0:T(8,128)(2,1)S(1)}, bf16[64,3072]{1,0:T(8,128)(2,1)S(1)}, u32[]{:S(2)}, u32[]{:S(2)}) collective-permute-start(bf16[64,3072]{1,0:T(8,128)(2,1)S(1)} %pad_maximum_fusion.4), channel_id=1, source_target_pairs={{0,48},{16,0},{32,16},{48,32},{1,49},{17,1},{33,17},{49,33},{2,50}... | collective-permute-start | bytes 1179656 | tf_op jit(solution)/shard_map/ppermute | solution.py:18
  128.5 0.8 slice.219
  129.3 0.8 pad_maximum_fusion.5
  130.1 7.0 %collective-permute-done.9 = bf16[64,3072]{1,0:T(8,128)(2,1)S(1)} collective-permute-done((bf16[64,3072]{1,0:T(8,128)(2,1)S(1)}, bf16[64,3072]{1,0:T(8,128)(2,1)S(1)}, u32[]{:S(2)}, u32[]{:S(2)}) %collective-permute-start.9) | collective-permute-done | bytes 393248 | tf_op jit(solution)/shard_map/ppermute | solution.py:18
  137.1 3.4 %collective-permute-done.8 = bf16[64,3072]{1,0:T(8,128)(2,1)S(1)} collective-permute-done((bf16[64,3072]{1,0:T(8,128)(2,1)S(1)}, bf16[64,3072]{1,0:T(8,128)(2,1)S(1)}, u32[]{:S(2)}, u32[]{:S(2)}) %collective-permute-start.8) | collective-permute-done | bytes 393248 | tf_op jit(solution)/shard_map/ppermute | solution.py:18
  140.5 0.8 add_convert_fusion.2
  141.3 0.3 collective-permute-start.15
  141.6 1.7 collective-permute-start.14
  143.4 3.2 %collective-permute-start.11 = (bf16[64,3072]{1,0:T(8,128)(2,1)}, bf16[64,3072]{1,0:T(8,128)(2,1)S(1)}, u32[]{:S(2)}, u32[]{:S(2)}) collective-permute-start(bf16[64,3072]{1,0:T(8,128)(2,1)} %pad_maximum_fusion.5), channel_id=1, source_target_pairs={{0,48},{16,0},{32,16},{48,32},{1,49},{17,1},{33,17},{49,33},{2,50}... | collective-permute-start | bytes 1179656 | tf_op jit(solution)/shard_map/ppermute | solution.py:18
  146.6 2.8 %collective-permute-done.15 = bf16[32,3072]{1,0:T(8,128)(2,1)S(1)} collective-permute-done((bf16[32,3072]{1,0:T(8,128)(2,1)}, bf16[32,3072]{1,0:T(8,128)(2,1)S(1)}, u32[]{:S(2)}, u32[]{:S(2)}) %collective-permute-start.15) | collective-permute-done | bytes 196640 | tf_op jit(solution)/shard_map/ppermute | solution.py:18
  149.4 1.6 collective-permute-done.14
  151.0 1.3 convert_add_fusion.3
  152.3 2.5 %collective-permute-start.16 = (bf16[16,3072]{1,0:T(8,128)(2,1)S(1)}, bf16[16,3072]{1,0:T(8,128)(2,1)S(1)}, u32[]{:S(2)}, u32[]{:S(2)}) collective-permute-start(bf16[16,3072]{1,0:T(8,128)(2,1)S(1)} %slice.301), channel_id=1, source_target_pairs={{0,4},{4,8},{8,12},{12,0},{1,5},{5,9},{9,13},{13,1},{2,6},{6,10},{... | collective-permute-start | bytes 294920 | tf_op jit(solution)/shard_map/ppermute | solution.py:18
  154.7 1.3 collective-permute-start.17
  156.1 0.6 collective-permute-start.18
  156.6 0.6 collective-permute-done.10
  157.4 0.4 collective-permute-start.13
  157.7 1.8 collective-permute-start.12
  159.5 1.0 collective-permute-done.17
  160.4 1.2 collective-permute-done.18
  161.7 1.4 collective-permute-done.13
  163.1 1.5 collective-permute-done.12
  164.8 2.5 %collective-permute-start.19 = (bf16[16,3072]{1,0:T(8,128)(2,1)S(1)}, bf16[16,3072]{1,0:T(8,128)(2,1)S(1)}, u32[]{:S(2)}, u32[]{:S(2)}) collective-permute-start(bf16[16,3072]{1,0:T(8,128)(2,1)S(1)} %slice.300), channel_id=1, source_target_pairs={{0,4},{4,8},{8,12},{12,0},{1,5},{5,9},{9,13},{13,1},{2,6},{6,10},{... | collective-permute-start | bytes 294920 | tf_op jit(solution)/shard_map/ppermute | solution.py:18
  167.3 1.7 collective-permute-start.20
  169.2 0.9 copy.50
  170.1 1.0 collective-permute-done.19
  171.0 1.7 collective-permute-done.20
  172.8 1.3 collective-permute-done.21
  174.2 0.9 copy.51
  (81 shorter events, 2.7 us)
Async XLA Ops:
  0.6 29.4 %copy-start.8 = (s32[8]{0:T(128)S(1)}, s32[8]{0:T(128)}, u32[]{:S(2)}) copy-start(s32[8]{0:T(128)} %param.10) | copy-start | bytes 100
  0.6 29.6 %copy-start.7 = (s32[8,16]{1,0:T(8,128)S(1)}, s32[8,16]{1,0:T(8,128)}, u32[]{:S(2)}) copy-start(s32[8,16]{1,0:T(8,128)} %param.11) | copy-start | bytes 1540
  20.7 21.4 %collective-permute-start.2 = (bf16[2,64,3072]{2,1,0:T(8,128)(2,1)S(1)}, bf16[2,64,3072]{2,1,0:T(8,128)(2,1)S(1)}, u32[]{:S(2)}, u32[]{:S(2)}) collective-permute-start(bf16[2,64,3072]{2,1,0:T(8,128)(2,1)S(1)} %all_gather.9), channel_id=1, source_target_pairs={{0,48},{16,0},{32,16},{48,32},{1,49},{17,1},{33,17},{49,33},{2,50}... | collective-permute-start | bytes 2359304 | tf_op jit(solution)/shard_map/ppermute | solution.py:18
  23.6 18.5 %collective-permute-start = (bf16[2,64,3072]{2,1,0:T(8,128)(2,1)S(1)}, bf16[2,64,3072]{2,1,0:T(8,128)(2,1)S(1)}, u32[]{:S(2)}, u32[]{:S(2)}) collective-permute-start(bf16[2,64,3072]{2,1,0:T(8,128)(2,1)S(1)} %all_gather.9), channel_id=1, source_target_pairs={{0,16},{16,32},{32,48},{48,0},{1,17},{17,33},{33,49},{49,1},{2,18}... | collective-permute-start | bytes 2359304 | tf_op jit(solution)/shard_map/ppermute | solution.py:18
  25.3 26.1 %collective-permute-start.3 = (bf16[64,2,768]{2,0,1:T(8,128)(2,1)S(1)}, bf16[64,2,768]{2,0,1:T(8,128)(2,1)S(1)}, u32[]{:S(2)}, u32[]{:S(2)}) collective-permute-start(bf16[64,2,768]{2,0,1:T(8,128)(2,1)S(1)} %copy.59), channel_id=1, source_target_pairs={{0,2},{2,0},{1,3},{3,1},{4,6},{6,4},{5,7},{7,5},{8,10},{10,8},{9,1... | collective-permute-start | bytes 589832 | tf_op jit(solution)/shard_map/ppermute | solution.py:18
  30.7 3.7 %copy-start = (bf16[2,768,3072]{2,1,0:T(8,128)(2,1)S(1)}, bf16[2,768,3072]{2,1,0:T(8,128)(2,1)}, u32[]{:S(2)}) copy-start(bf16[2,768,3072]{2,1,0:T(8,128)(2,1)} %fronts_ref.1) | copy-start | bytes 28311556
  37.9 15.2 %copy-start.1 = (bf16[2,768,3072]{2,1,0:T(8,128)(2,1)}, bf16[2,768,3072]{2,1,0:T(8,128)(2,1)S(1)}, u32[]{:S(2)}) copy-start(bf16[2,768,3072]{2,1,0:T(8,128)(2,1)S(1)} %shard_map.77) | copy-start | bytes 28311556
  42.1 9.2 %collective-permute-start.1 = (bf16[64,3072]{1,0:T(8,128)(2,1)S(1)}, bf16[64,3072]{1,0:T(8,128)(2,1)S(1)}, u32[]{:S(2)}, u32[]{:S(2)}) collective-permute-start(bf16[64,3072]{1,0:T(8,128)(2,1)S(1)} %get-tuple-element.78), channel_id=1, source_target_pairs={{0,16},{16,32},{32,48},{48,0},{1,17},{17,33},{33,49},{49,1},{2,18}... | collective-permute-start | bytes 1179656 | tf_op jit(solution)/shard_map/ppermute | solution.py:18
  42.3 10.8 %collective-permute-start.5 = (bf16[64,3072]{1,0:T(8,128)(2,1)S(1)}, bf16[64,3072]{1,0:T(8,128)(2,1)S(1)}, u32[]{:S(2)}, u32[]{:S(2)}) collective-permute-start(bf16[64,3072]{1,0:T(8,128)(2,1)S(1)} %get-tuple-element.81), channel_id=1, source_target_pairs={{0,48},{16,0},{32,16},{48,32},{1,49},{17,1},{33,17},{49,33},{2,50}... | collective-permute-start | bytes 1179656 | tf_op jit(solution)/shard_map/ppermute | solution.py:18
  51.4 1.5 copy-start.5
  52.9 2.2 %collective-permute-start.4 = (bf16[2,64,768]{2,1,0:T(8,128)(2,1)S(1)}, bf16[2,64,768]{2,1,0:T(8,128)(2,1)S(1)}, u32[]{:S(2)}, u32[]{:S(2)}) collective-permute-start(bf16[2,64,768]{2,1,0:T(8,128)(2,1)S(1)} %dynamic-slice_bitcast_fusion.1), channel_id=1, source_target_pairs={{0,1},{1,0},{2,3},{3,2},{4,5},{5,4},{6,7},{7,6},{8,9},{9,8},{10,11... | collective-permute-start | bytes 589832 | tf_op jit(solution)/shard_map/ppermute | solution.py:18
  54.5 1.6 collective-permute-start.6
  56.6 44.7 %copy-start.6 = (bf16[64,2,768]{2,0,1:T(8,128)(2,1)S(1)}, bf16[64,2,768]{2,0,1:T(8,128)(2,1)}, u32[]{:S(2)}) copy-start(bf16[64,2,768]{2,0,1:T(8,128)(2,1)} %copy-done.5) | copy-start | bytes 589828
  58.3 29.6 %all-to-all-start = ((bf16[128,2,768]{2,1,0:T(2,128)(2,1)}), bf16[128,2,768]{2,1,0:T(2,128)(2,1)S(1)}, u32[]{:S(2)}, u32[]{:S(2)}) async-start(bf16[128,2,768]{2,1,0:T(2,128)(2,1)} %pad_maximum_fusion.1), calls=%async_computation | async-start | bytes 786432 | tf_op jit(solution)/shard_map/all_to_all | solution.py:147
  89.8 34.4 %slice-start = ((s8[9437184]{0:T(1024)(128)(4,1)}), s8[1048576]{0:T(1024)(128)(4,1)S(1)}, s32[]{:S(2)}) async-start(s8[9437184]{0:T(1024)(128)(4,1)} %bitcast.83), calls=%async_computation.2 | async-start | bytes 2097152
  89.8 26.9 %all-to-all-start.1 = ((bf16[128,2,768]{2,1,0:T(2,128)(2,1)}), bf16[128,2,768]{2,1,0:T(2,128)(2,1)S(1)}, u32[]{:S(2)}, u32[]{:S(2)}) async-start(bf16[128,2,768]{2,1,0:T(2,128)(2,1)} %pad_maximum_fusion.2), calls=%async_computation.1 | async-start | bytes 786432 | tf_op jit(solution)/shard_map/all_to_all | solution.py:155
  96.3 20.3 %collective-permute-start.7 = (bf16[2,64,768]{2,1,0:T(8,128)(2,1)S(1)}, bf16[2,64,768]{2,1,0:T(8,128)(2,1)S(1)}, u32[]{:S(2)}, u32[]{:S(2)}) collective-permute-start(bf16[2,64,768]{2,1,0:T(8,128)(2,1)S(1)} %pad_maximum_fusion.7), channel_id=1, source_target_pairs={{0,2},{2,0},{1,3},{3,1},{4,6},{6,4},{5,7},{7,5},{8,10},{10,8},{9,1... | collective-permute-start | bytes 589832 | tf_op jit(solution)/shard_map/ppermute | solution.py:18
  116.6 3.2 %copy-start.3 = (bf16[2,64,768]{2,1,0:T(8,128)(2,1)}, bf16[2,64,768]{2,1,0:T(8,128)(2,1)S(1)}, u32[]{:S(2)}) copy-start(bf16[2,64,768]{2,1,0:T(8,128)(2,1)S(1)} %collective-permute-done.7) | copy-start | bytes 589828
  117.2 7.0 %slice-start.1 = ((s8[9437184]{0:T(1024)(128)(4,1)}), s8[4194304]{0:T(1024)(128)(4,1)S(1)}, s32[]{:S(2)}) async-start(s8[9437184]{0:T(1024)(128)(4,1)} %bitcast.83), calls=%async_computation.3 | async-start | bytes 8388608
  120.0 4.2 %slice-start.2 = ((s8[9437184]{0:T(1024)(128)(4,1)}), s8[4194304]{0:T(1024)(128)(4,1)S(1)}, s32[]{:S(2)}) async-start(s8[9437184]{0:T(1024)(128)(4,1)} %bitcast.83), calls=%async_computation.4 | async-start | bytes 8388608
  123.9 16.6 %copy-start.2 = (bf16[256,3072]{1,0:T(8,128)(2,1)}, bf16[256,3072]{1,0:T(8,128)(2,1)S(1)}, u32[]{:S(2)}) copy-start(bf16[256,3072]{1,0:T(8,128)(2,1)S(1)} %fusion.5) | copy-start | bytes 4718596
  125.7 11.4 %collective-permute-start.9 = (bf16[64,3072]{1,0:T(8,128)(2,1)S(1)}, bf16[64,3072]{1,0:T(8,128)(2,1)S(1)}, u32[]{:S(2)}, u32[]{:S(2)}) collective-permute-start(bf16[64,3072]{1,0:T(8,128)(2,1)S(1)} %pad_maximum_fusion.4), channel_id=1, source_target_pairs={{0,48},{16,0},{32,16},{48,32},{1,49},{17,1},{33,17},{49,33},{2,50}... | collective-permute-start | bytes 1179656 | tf_op jit(solution)/shard_map/ppermute | solution.py:18
  128.4 12.1 %collective-permute-start.8 = (bf16[64,3072]{1,0:T(8,128)(2,1)S(1)}, bf16[64,3072]{1,0:T(8,128)(2,1)S(1)}, u32[]{:S(2)}, u32[]{:S(2)}) collective-permute-start(bf16[64,3072]{1,0:T(8,128)(2,1)S(1)} %slice.215), channel_id=1, source_target_pairs={{0,16},{16,32},{32,48},{48,0},{1,17},{17,33},{33,49},{49,1},{2,18}... | collective-permute-start | bytes 1179656 | tf_op jit(solution)/shard_map/ppermute | solution.py:18
  141.3 8.0 %collective-permute-start.15 = (bf16[32,3072]{1,0:T(8,128)(2,1)}, bf16[32,3072]{1,0:T(8,128)(2,1)S(1)}, u32[]{:S(2)}, u32[]{:S(2)}) collective-permute-start(bf16[32,3072]{1,0:T(8,128)(2,1)} %get-tuple-element.64), channel_id=1, source_target_pairs={{0,48},{16,0},{32,16},{48,32},{1,49},{17,1},{33,17},{49,33},{2,50}... | collective-permute-start | bytes 589832 | tf_op jit(solution)/shard_map/ppermute | solution.py:18
  141.6 9.4 %collective-permute-start.14 = (bf16[32,3072]{1,0:T(8,128)(2,1)}, bf16[32,3072]{1,0:T(8,128)(2,1)}, u32[]{:S(2)}, u32[]{:S(2)}) collective-permute-start(bf16[32,3072]{1,0:T(8,128)(2,1)} %get-tuple-element.65), channel_id=1, source_target_pairs={{0,16},{16,32},{32,48},{48,0},{1,17},{17,33},{33,49},{49,1},{2,18}... | collective-permute-start | bytes 589832 | tf_op jit(solution)/shard_map/ppermute | solution.py:18
  143.4 25.7 %copy-start.4 = (bf16[2,64,768]{2,1,0:T(8,128)(2,1)S(1)}, bf16[2,64,768]{2,1,0:T(8,128)(2,1)}, u32[]{:S(2)}) copy-start(bf16[2,64,768]{2,1,0:T(8,128)(2,1)} %copy-done.3) | copy-start | bytes 589828
  143.4 13.9 %collective-permute-start.10 = (bf16[64,3072]{1,0:T(8,128)(2,1)}, bf16[64,3072]{1,0:T(8,128)(2,1)S(1)}, u32[]{:S(2)}, u32[]{:S(2)}) collective-permute-start(bf16[64,3072]{1,0:T(8,128)(2,1)} %slice.219), channel_id=1, source_target_pairs={{0,16},{16,32},{32,48},{48,0},{1,17},{17,33},{33,49},{49,1},{2,18}... | collective-permute-start | bytes 1179656 | tf_op jit(solution)/shard_map/ppermute | solution.py:18
  143.4 13.9 %collective-permute-start.11 = (bf16[64,3072]{1,0:T(8,128)(2,1)}, bf16[64,3072]{1,0:T(8,128)(2,1)S(1)}, u32[]{:S(2)}, u32[]{:S(2)}) collective-permute-start(bf16[64,3072]{1,0:T(8,128)(2,1)} %pad_maximum_fusion.5), channel_id=1, source_target_pairs={{0,48},{16,0},{32,16},{48,32},{1,49},{17,1},{33,17},{49,33},{2,50}... | collective-permute-start | bytes 1179656 | tf_op jit(solution)/shard_map/ppermute | solution.py:18
  152.3 7.2 %collective-permute-start.16 = (bf16[16,3072]{1,0:T(8,128)(2,1)S(1)}, bf16[16,3072]{1,0:T(8,128)(2,1)S(1)}, u32[]{:S(2)}, u32[]{:S(2)}) collective-permute-start(bf16[16,3072]{1,0:T(8,128)(2,1)S(1)} %slice.301), channel_id=1, source_target_pairs={{0,4},{4,8},{8,12},{12,0},{1,5},{5,9},{9,13},{13,1},{2,6},{6,10},{... | collective-permute-start | bytes 294920 | tf_op jit(solution)/shard_map/ppermute | solution.py:18
  154.7 5.7 %collective-permute-start.17 = (bf16[16,3072]{1,0:T(8,128)(2,1)S(1)}, bf16[16,3072]{1,0:T(8,128)(2,1)S(1)}, u32[]{:S(2)}, u32[]{:S(2)}) collective-permute-start(bf16[16,3072]{1,0:T(8,128)(2,1)S(1)} %get-tuple-element.84), channel_id=1, source_target_pairs={{0,8},{4,12},{8,0},{12,4},{1,9},{5,13},{9,1},{13,5},{2,10},{6,14},... | collective-permute-start | bytes 294920 | tf_op jit(solution)/shard_map/ppermute | solution.py:18
  156.1 5.6 %collective-permute-start.18 = (bf16[16,3072]{1,0:T(8,128)(2,1)S(1)}, bf16[16,3072]{1,0:T(8,128)(2,1)S(1)}, u32[]{:S(2)}, u32[]{:S(2)}) collective-permute-start(bf16[16,3072]{1,0:T(8,128)(2,1)S(1)} %get-tuple-element.85), channel_id=1, source_target_pairs={{0,12},{4,0},{8,4},{12,8},{1,13},{5,1},{9,5},{13,9},{2,14},{6,2},{... | collective-permute-start | bytes 294920 | tf_op jit(solution)/shard_map/ppermute | solution.py:18
  157.4 5.7 %collective-permute-start.13 = (bf16[32,3072]{1,0:T(8,128)(2,1)S(1)}, bf16[32,3072]{1,0:T(8,128)(2,1)S(1)}, u32[]{:S(2)}, u32[]{:S(2)}) collective-permute-start(bf16[32,3072]{1,0:T(8,128)(2,1)S(1)} %get-tuple-element.68), channel_id=1, source_target_pairs={{0,48},{16,0},{32,16},{48,32},{1,49},{17,1},{33,17},{49,33},{2,50}... | collective-permute-start | bytes 589832 | tf_op jit(solution)/shard_map/ppermute | solution.py:18
  157.7 6.9 %collective-permute-start.12 = (bf16[32,3072]{1,0:T(8,128)(2,1)S(1)}, bf16[32,3072]{1,0:T(8,128)(2,1)S(1)}, u32[]{:S(2)}, u32[]{:S(2)}) collective-permute-start(bf16[32,3072]{1,0:T(8,128)(2,1)S(1)} %get-tuple-element.69), channel_id=1, source_target_pairs={{0,16},{16,32},{32,48},{48,0},{1,17},{17,33},{33,49},{49,1},{2,18}... | collective-permute-start | bytes 589832 | tf_op jit(solution)/shard_map/ppermute | solution.py:18
  164.8 6.2 %collective-permute-start.19 = (bf16[16,3072]{1,0:T(8,128)(2,1)S(1)}, bf16[16,3072]{1,0:T(8,128)(2,1)S(1)}, u32[]{:S(2)}, u32[]{:S(2)}) collective-permute-start(bf16[16,3072]{1,0:T(8,128)(2,1)S(1)} %slice.300), channel_id=1, source_target_pairs={{0,4},{4,8},{8,12},{12,0},{1,5},{5,9},{9,13},{13,1},{2,6},{6,10},{... | collective-permute-start | bytes 294920 | tf_op jit(solution)/shard_map/ppermute | solution.py:18
  167.3 5.5 %collective-permute-start.20 = (bf16[16,3072]{1,0:T(8,128)(2,1)S(1)}, bf16[16,3072]{1,0:T(8,128)(2,1)S(1)}, u32[]{:S(2)}, u32[]{:S(2)}) collective-permute-start(bf16[16,3072]{1,0:T(8,128)(2,1)S(1)} %get-tuple-element.86), channel_id=1, source_target_pairs={{0,8},{4,12},{8,0},{12,4},{1,9},{5,13},{9,1},{13,5},{2,10},{6,14},... | collective-permute-start | bytes 294920 | tf_op jit(solution)/shard_map/ppermute | solution.py:18
  169.0 5.1 %collective-permute-start.21 = (bf16[16,3072]{1,0:T(8,128)(2,1)S(1)}, bf16[16,3072]{1,0:T(8,128)(2,1)S(1)}, u32[]{:S(2)}, u32[]{:S(2)}) collective-permute-start(bf16[16,3072]{1,0:T(8,128)(2,1)S(1)} %get-tuple-element.87), channel_id=1, source_target_pairs={{0,12},{4,0},{8,4},{12,8},{1,13},{5,1},{9,5},{13,9},{2,14},{6,2},{... | collective-permute-start | bytes 294920 | tf_op jit(solution)/shard_map/ppermute | solution.py:18

commit v4 on v3

--- a/solution.py
+++ b/solution.py
@@ -150,10 +150,7 @@
     extension = jnp.einsum("ij,jk->ik", weight, arrived, preferred_element_type=F32).astype(BF16)
     extension = extension.reshape(slab, local, tile_rows)
     extension = jnp.concatenate([extension, extension], axis=0)
-    away = jnp.stack([pick(half, 1 - h).astype(BF16) for half in halves])
-    away, extension = lax.optimization_barrier((away, extension))
     extension = lax.all_to_all(extension, spread, split_axis=0, concat_axis=0, tiled=True)
-    received, extension = lax.optimization_barrier((shift(away, "h", 1), extension))
     combined = second.reshape(extension.shape).astype(F32) + extension.astype(F32)
     combined = combined.astype(BF16)
 
@@ -170,10 +167,14 @@
         return product.astype(BF16)
 
     product_0 = multiplied(0)
+    product_0, *halves = lax.optimization_barrier((product_0, *halves))
     near_0 = first_step(first_pieces(product_0))
     product_1 = multiplied(1)
     pieces_1 = first_pieces(product_1)
-    near_0, product_1, pieces_1 = lax.optimization_barrier((near_0, product_1, pieces_1))
+    away = jnp.stack([pick(half, 1 - h).astype(BF16) for half in halves])
+    away, pieces_1 = lax.optimization_barrier((away, pieces_1))
+    received = shift(away, "h", 1)
+    near_0, product_1, pieces_1, received = lax.optimization_barrier((near_0, product_1, pieces_1, received))
     far_0 = second_step(product_0, near_0)
     near_1 = first_step(pieces_1)
     total_0 = last_step(product_0, near_0, far_0)

time: 176 us -> 175 us (level)
  blocking collectives: 21.1 us -> 50.5 us
  starting transfers between devices: 53.8 us -> 35.3 us
  waiting for transfers between devices: 67.6 us -> 57.5 us
    all_to_all x0 -> x1, blocking collectives: none -> 29.4 us  [shards(): lax.all_to_all(outgoing, spread, split_axis=0, concat_axis=0, tiled=True)]
    all_to_all x1 -> x0, waiting for transfers between devices: 17.5 us -> none  [shards(): lax.all_to_all(outgoing, spread, split_axis=0, concat_axis=0, tiled=True)]
    all_to_all x1, waiting for transfers between devices: 0.07 us -> 16.1 us  [shards(): lax.all_to_all(extension, spread, split_axis=0, concat_axis=0, tiled=True)]
    all_to_all x1 -> x0, starting transfers between devices: 12 us -> none  [shards(): lax.all_to_all(outgoing, spread, split_axis=0, concat_axis=0, tiled=True)]
    ppermute x22, waiting for transfers between devices: 50 us -> 41.4 us  [shift(): return lax.ppermute(value, axis, [(i, (i + by) % n) for i in range(n)])]
    ppermute x22, starting transfers between devices: 35.4 us -> 28.7 us  [shift(): return lax.ppermute(value, axis, [(i, (i + by) % n) for i in range(n)])]
  transfers between devices with their start and end apart: 24 -> 23, of which waited for: 18 -> 16; matrix products, arithmetic and copies ran while one was open for 6% -> 5% of each run, Pallas kernels for 2% -> 2%
where the time goes in v4:
time: 175 us
  waiting for transfers between devices  57.5 us (33%)
  blocking collectives  50.5 us (29%)
  starting transfers between devices  35.3 us (20%)
  local copies, waits for them, and re-layouts  11.1 us (6%)
  matrix products  8.41 us (5%)
  other arithmetic  7.44 us (4%)
  Pallas kernels  3.47 us (2%)
    ppermute x22, waiting for transfers between devices, shift(): return lax.ppermute(value, axis, [(i, (i + by) % n) for i in range(n)])  41.4 us
    all_to_all x1, blocking collectives, shards(): lax.all_to_all(outgoing, spread, split_axis=0, concat_axis=0, tiled=True)  29.4 us
    ppermute x22, starting transfers between devices, shift(): return lax.ppermute(value, axis, [(i, (i + by) % n) for i in range(n)])  28.7 us
    all_gather x1, blocking collectives, shards(): columns = lax.all_gather(mine, 'z', axis=1, tiled=True)  18.6 us
    all_to_all x1, waiting for transfers between devices, shards(): lax.all_to_all(extension, spread, split_axis=0, concat_axis=0, tiled=True)  16.1 us
    all_to_all x1, starting transfers between devices, shards(): lax.all_to_all(extension, spread, split_axis=0, concat_axis=0, tiled=True)  6.53 us
    unnamed x26, local copies, waits for them, and re-layouts  5.49 us
    dot_general x2, matrix products, multiplied(): jnp.einsum('sm,mk->sk', ordered[f], masked[f], preferred_element_type=F32)  5.3 us
  transfers between devices with their start and end apart: 23, of which 16 were waited for; matrix products, arithmetic and copies ran while one was open for 5% of the time, Pallas kernels for 2%

profile of v4, /device:TPU:32, one launch (start us, length us, event | category | flops | bytes accessed | tf_op | source)
XLA Modules:
  0.0 174.9 jit_solution(11763966824401882920)
XLA Ops:
  0.7 1.4 fusion.56
  2.1 18.6 %all_gather.9 = bf16[2,64,3072]{2,1,0:T(8,128)(2,1)S(1)} all-gather(bf16[2,16,3072]{2,1,0:T(8,128)(2,1)S(1)} %pad_maximum_fusion.6), channel_id=1, replica_groups=mesh['group'=4,'x'=4,'z'=4,'h'=2,'c'=2] {'z'}, dimensions={1}, use_global_device_ids=true | all-gather | bytes 983040 | tf_op jit(solution)/shard_map/all_gather | solution.py:130
  20.7 2.8 %collective-permute-start.2 = (bf16[2,64,3072]{2,1,0:T(8,128)(2,1)S(1)}, bf16[2,64,3072]{2,1,0:T(8,128)(2,1)S(1)}, u32[]{:S(2)}, u32[]{:S(2)}) collective-permute-start(bf16[2,64,3072]{2,1,0:T(8,128)(2,1)S(1)} %all_gather.9), channel_id=1, source_target_pairs={{0,48},{16,0},{32,16},{48,32},{1,49},{17,1},{33,17},{49,33},{2,50}... | collective-permute-start | bytes 2359304 | tf_op jit(solution)/shard_map/ppermute | solution.py:18
  23.6 0.7 dynamic_slice.50.sizes_ref
  24.3 0.9 copy.59
  25.3 4.7 %collective-permute-start.3 = (bf16[64,2,768]{2,0,1:T(8,128)(2,1)S(1)}, bf16[64,2,768]{2,0,1:T(8,128)(2,1)S(1)}, u32[]{:S(2)}, u32[]{:S(2)}) collective-permute-start(bf16[64,2,768]{2,0,1:T(8,128)(2,1)S(1)} %copy.59), channel_id=1, source_target_pairs={{0,2},{2,0},{1,3},{3,1},{4,6},{6,4},{5,7},{7,5},{8,10},{10,8},{9,1... | collective-permute-start | bytes 589832 | tf_op jit(solution)/shard_map/ppermute | solution.py:18
  30.1 0.1 eq.33
  30.7 3.7 %copy-done = bf16[2,768,3072]{2,1,0:T(8,128)(2,1)S(1)} copy-done((bf16[2,768,3072]{2,1,0:T(8,128)(2,1)S(1)}, bf16[2,768,3072]{2,1,0:T(8,128)(2,1)}, u32[]{:S(2)}) %copy-start) | copy-done | bytes 9437208
  34.4 3.5 %shard_map.77 = bf16[2,768,3072]{2,1,0:T(8,128)(2,1)S(1)} custom-call(s32[2]{0:T(128)S(1)} %dynamic_slice.50.sizes_ref, s32[2]{0:T(128)S(1)} %pad_add_fusion.origin_ref, bf16[2,768,3072]{2,1,0:T(8,128)(2,1)S(1)} %copy-done), custom_call_target="tpu_custom_call" | custom-call | tf_op jit(solution)/shard_map/pallas_call | solution.py:53
  37.9 4.1 %collective-permute-done = bf16[2,64,3072]{2,1,0:T(8,128)(2,1)S(1)} collective-permute-done((bf16[2,64,3072]{2,1,0:T(8,128)(2,1)S(1)}, bf16[2,64,3072]{2,1,0:T(8,128)(2,1)S(1)}, u32[]{:S(2)}, u32[]{:S(2)}) %collective-permute-start) | collective-permute-done | bytes 786464 | tf_op jit(solution)/shard_map/ppermute | solution.py:18
  42.3 3.3 %collective-permute-start.5 = (bf16[64,3072]{1,0:T(8,128)(2,1)S(1)}, bf16[64,3072]{1,0:T(8,128)(2,1)S(1)}, u32[]{:S(2)}, u32[]{:S(2)}) collective-permute-start(bf16[64,3072]{1,0:T(8,128)(2,1)S(1)} %get-tuple-element.90), channel_id=1, source_target_pairs={{0,48},{16,0},{32,16},{48,32},{1,49},{17,1},{33,17},{49,33},{2,50}... | collective-permute-start | bytes 1179656 | tf_op jit(solution)/shard_map/ppermute | solution.py:18
  45.5 5.7 %collective-permute-done.1 = bf16[64,3072]{1,0:T(8,128)(2,1)S(1)} collective-permute-done((bf16[64,3072]{1,0:T(8,128)(2,1)S(1)}, bf16[64,3072]{1,0:T(8,128)(2,1)S(1)}, u32[]{:S(2)}, u32[]{:S(2)}) %collective-permute-start.1) | collective-permute-done | bytes 393248 | tf_op jit(solution)/shard_map/ppermute | solution.py:18
  51.4 1.5 fusion.16
  53.1 1.4 fusion.13
  54.5 0.6 collective-permute-start.6
  55.3 0.3 copy.47
  55.6 0.6 collective-permute-done.6
  56.3 0.3 copy.48
  56.7 0.9 pad_maximum_fusion.1
  57.6 29.4 %all_to_all.10 = bf16[128,2,768]{2,1,0:T(2,128)(2,1)S(1)} all-to-all(bf16[128,2,768]{2,1,0:T(2,128)(2,1)S(1)} %pad_maximum_fusion.1), channel_id=1, replica_groups=mesh['group'=4,'x'=4,'z'=4,'h'=2,'c'=2] {'h','group','x','z'}, dimensions={0} | all-to-all | bytes 786432 | tf_op jit(solution)/shard_map/all_to_all | solution.py:147
  86.9 0.2 add_convert_fusion.6
  87.2 0.2 convolution_convert_fusion
  87.5 1.3 pad_maximum_fusion.2
  88.8 6.5 %all-to-all-start.1 = ((bf16[128,2,768]{2,1,0:T(2,128)(2,1)}), bf16[128,2,768]{2,1,0:T(2,128)(2,1)S(1)}, u32[]{:S(2)}, u32[]{:S(2)}) async-start(bf16[128,2,768]{2,1,0:T(2,128)(2,1)} %pad_maximum_fusion.2), calls=%async_computation.1 | async-start | bytes 786432 | tf_op jit(solution)/shard_map/all_to_all | solution.py:153
  95.4 0.3 fusion.25
  95.7 16.1 %all-to-all-done.1 = bf16[128,2,768]{2,1,0:T(2,128)(2,1)S(1)} async-done(((bf16[128,2,768]{2,1,0:T(2,128)(2,1)}), bf16[128,2,768]{2,1,0:T(2,128)(2,1)S(1)}, u32[]{:S(2)}, u32[]{:S(2)}) %all-to-all-start.1) | async-done | bytes 393248 | tf_op jit(solution)/shard_map/all_to_all | solution.py:153
  112.0 0.2 fusion.30
  112.2 0.2 fusion.27
  112.4 2.5 %all-gather = bf16[4,128,768]{2,1,0:T(8,128)(2,1)S(1)} all-gather(bf16[2,128,768]{2,1,0:T(8,128)(2,1)S(1)} %pad_maximum_fusion.3), channel_id=2, replica_groups=mesh['group'=4,'x'=4,'z'=4,'h'=2,'c'=2] {'c'}, dimensions={0}, use_global_device_ids=true | all-gather | bytes 1179648 | tf_op jit(solution)/shard_map/all_gather | solution.py:162
  115.0 0.2 fusion.19
  115.1 3.9 %fusion.5 = bf16[256,3072]{1,0:T(8,128)(2,1)S(1)} fusion(bf16[256,768]{1,0:T(8,128)(2,1)S(1)} %bitcast.97, bf16[2,768,3072]{2,1,0:T(8,128)(2,1)} %copy-done.1), kind=kOutput, calls=%fused_computation.7 | convolution fusion | flops 1208745984 | bytes 6684672 | tf_op jit(solution)/shard_map/sm,mk->sk/dot_general | solution.py:166
  119.1 0.2 fusion.18
  119.3 1.4 fusion.4
  120.7 0.8 slice.216
  121.6 1.2 collective-permute-start.8
  122.8 0.9 collective-permute-start.7
  123.7 0.8 pad_maximum_fusion.5
  124.6 1.1 collective-permute-start.9
  125.7 7.2 %collective-permute-done.8 = bf16[64,3072]{1,0:T(8,128)(2,1)S(1)} collective-permute-done((bf16[64,3072]{1,0:T(8,128)(2,1)S(1)}, bf16[64,3072]{1,0:T(8,128)(2,1)S(1)}, u32[]{:S(2)}, u32[]{:S(2)}) %collective-permute-start.8) | collective-permute-done | bytes 393248 | tf_op jit(solution)/shard_map/ppermute | solution.py:18
  132.8 2.0 %collective-permute-done.7 = bf16[64,3072]{1,0:T(8,128)(2,1)S(1)} collective-permute-done((bf16[64,3072]{1,0:T(8,128)(2,1)S(1)}, bf16[64,3072]{1,0:T(8,128)(2,1)S(1)}, u32[]{:S(2)}, u32[]{:S(2)}) %collective-permute-start.7) | collective-permute-done | bytes 393248 | tf_op jit(solution)/shard_map/ppermute | solution.py:18
  134.9 3.5 %collective-permute-done.9 = bf16[2,64,768]{2,1,0:T(8,128)(2,1)S(1)} collective-permute-done((bf16[2,64,768]{2,1,0:T(8,128)(2,1)S(1)}, bf16[2,64,768]{2,1,0:T(8,128)(2,1)S(1)}, u32[]{:S(2)}, u32[]{:S(2)}) %collective-permute-start.9) | collective-permute-done | bytes 196640 | tf_op jit(solution)/shard_map/ppermute | solution.py:18
  138.3 0.9 add_convert_fusion.2
  139.2 3.1 %collective-permute-start.15 = (bf16[32,3072]{1,0:T(8,128)(2,1)}, bf16[32,3072]{1,0:T(8,128)(2,1)S(1)}, u32[]{:S(2)}, u32[]{:S(2)}) collective-permute-start(bf16[32,3072]{1,0:T(8,128)(2,1)} %get-tuple-element.74), channel_id=1, source_target_pairs={{0,48},{16,0},{32,16},{48,32},{1,49},{17,1},{33,17},{49,33},{2,50}... | collective-permute-start | bytes 589832 | tf_op jit(solution)/shard_map/ppermute | solution.py:18
  142.3 3.3 %collective-permute-start.11 = (bf16[64,3072]{1,0:T(8,128)(2,1)}, bf16[64,3072]{1,0:T(8,128)(2,1)S(1)}, u32[]{:S(2)}, u32[]{:S(2)}) collective-permute-start(bf16[64,3072]{1,0:T(8,128)(2,1)} %pad_maximum_fusion.5), channel_id=1, source_target_pairs={{0,48},{16,0},{32,16},{48,32},{1,49},{17,1},{33,17},{49,33},{2,50}... | collective-permute-start | bytes 1179656 | tf_op jit(solution)/shard_map/ppermute | solution.py:18
  145.6 2.1 %collective-permute-done.15 = bf16[32,3072]{1,0:T(8,128)(2,1)S(1)} collective-permute-done((bf16[32,3072]{1,0:T(8,128)(2,1)}, bf16[32,3072]{1,0:T(8,128)(2,1)S(1)}, u32[]{:S(2)}, u32[]{:S(2)}) %collective-permute-start.15) | collective-permute-done | bytes 196640 | tf_op jit(solution)/shard_map/ppermute | solution.py:18
  147.7 4.0 %collective-permute-done.14 = bf16[32,3072]{1,0:T(8,128)(2,1)} collective-permute-done((bf16[32,3072]{1,0:T(8,128)(2,1)}, bf16[32,3072]{1,0:T(8,128)(2,1)}, u32[]{:S(2)}, u32[]{:S(2)}) %collective-permute-start.14) | collective-permute-done | bytes 196640 | tf_op jit(solution)/shard_map/ppermute | solution.py:18
  151.7 1.3 convert_add_fusion.3
  153.0 0.9 collective-permute-start.16
  153.9 0.8 collective-permute-start.17
  154.8 0.9 collective-permute-start.18
  155.6 2.3 %collective-permute-done.10 = bf16[64,3072]{1,0:T(8,128)(2,1)S(1)} collective-permute-done((bf16[64,3072]{1,0:T(8,128)(2,1)}, bf16[64,3072]{1,0:T(8,128)(2,1)S(1)}, u32[]{:S(2)}, u32[]{:S(2)}) %collective-permute-start.10) | collective-permute-done | bytes 393248 | tf_op jit(solution)/shard_map/ppermute | solution.py:18
  158.0 0.4 collective-permute-start.13
  158.3 1.8 %collective-permute-start.12 = (bf16[32,3072]{1,0:T(8,128)(2,1)S(1)}, bf16[32,3072]{1,0:T(8,128)(2,1)S(1)}, u32[]{:S(2)}, u32[]{:S(2)}) collective-permute-start(bf16[32,3072]{1,0:T(8,128)(2,1)S(1)} %get-tuple-element.79), channel_id=1, source_target_pairs={{0,16},{16,32},{32,48},{48,0},{1,17},{17,33},{33,49},{49,1},{2,18}... | collective-permute-start | bytes 589832 | tf_op jit(solution)/shard_map/ppermute | solution.py:18
  160.1 1.2 collective-permute-done.18
  161.4 2.3 %collective-permute-done.13 = bf16[32,3072]{1,0:T(8,128)(2,1)S(1)} collective-permute-done((bf16[32,3072]{1,0:T(8,128)(2,1)S(1)}, bf16[32,3072]{1,0:T(8,128)(2,1)S(1)}, u32[]{:S(2)}, u32[]{:S(2)}) %collective-permute-start.13) | collective-permute-done | bytes 196640 | tf_op jit(solution)/shard_map/ppermute | solution.py:18
  163.7 1.5 collective-permute-done.12
  165.2 0.1 convert_add_fusion.2
  165.4 0.5 collective-permute-start.19
  165.9 2.3 %collective-permute-start.20 = (bf16[16,3072]{1,0:T(8,128)(2,1)S(1)}, bf16[16,3072]{1,0:T(8,128)(2,1)S(1)}, u32[]{:S(2)}, u32[]{:S(2)}) collective-permute-start(bf16[16,3072]{1,0:T(8,128)(2,1)S(1)} %get-tuple-element.96), channel_id=1, source_target_pairs={{0,8},{4,12},{8,0},{12,4},{1,9},{5,13},{9,1},{13,5},{2,10},{6,14},... | collective-permute-start | bytes 294920 | tf_op jit(solution)/shard_map/ppermute | solution.py:18
  168.3 0.9 copy.50
  169.1 1.0 collective-permute-done.19
  170.1 2.2 %collective-permute-done.20 = bf16[16,3072]{1,0:T(8,128)(2,1)S(1)} collective-permute-done((bf16[16,3072]{1,0:T(8,128)(2,1)S(1)}, bf16[16,3072]{1,0:T(8,128)(2,1)S(1)}, u32[]{:S(2)}, u32[]{:S(2)}) %collective-permute-start.20) | collective-permute-done | bytes 98336 | tf_op jit(solution)/shard_map/ppermute | solution.py:18
  172.3 1.6 collective-permute-done.21
  174.0 0.9 copy.51
  (80 shorter events, 2.3 us)
Async XLA Ops:
  0.6 29.4 %copy-start.8 = (s32[8]{0:T(128)S(1)}, s32[8]{0:T(128)}, u32[]{:S(2)}) copy-start(s32[8]{0:T(128)} %param.10) | copy-start | bytes 100
  0.6 29.6 %copy-start.7 = (s32[8,16]{1,0:T(8,128)S(1)}, s32[8,16]{1,0:T(8,128)}, u32[]{:S(2)}) copy-start(s32[8,16]{1,0:T(8,128)} %param.11) | copy-start | bytes 1540
  20.7 21.4 %collective-permute-start.2 = (bf16[2,64,3072]{2,1,0:T(8,128)(2,1)S(1)}, bf16[2,64,3072]{2,1,0:T(8,128)(2,1)S(1)}, u32[]{:S(2)}, u32[]{:S(2)}) collective-permute-start(bf16[2,64,3072]{2,1,0:T(8,128)(2,1)S(1)} %all_gather.9), channel_id=1, source_target_pairs={{0,48},{16,0},{32,16},{48,32},{1,49},{17,1},{33,17},{49,33},{2,50}... | collective-permute-start | bytes 2359304 | tf_op jit(solution)/shard_map/ppermute | solution.py:18
  23.6 18.5 %collective-permute-start = (bf16[2,64,3072]{2,1,0:T(8,128)(2,1)S(1)}, bf16[2,64,3072]{2,1,0:T(8,128)(2,1)S(1)}, u32[]{:S(2)}, u32[]{:S(2)}) collective-permute-start(bf16[2,64,3072]{2,1,0:T(8,128)(2,1)S(1)} %all_gather.9), channel_id=1, source_target_pairs={{0,16},{16,32},{32,48},{48,0},{1,17},{17,33},{33,49},{49,1},{2,18}... | collective-permute-start | bytes 2359304 | tf_op jit(solution)/shard_map/ppermute | solution.py:18
  25.3 26.1 %collective-permute-start.3 = (bf16[64,2,768]{2,0,1:T(8,128)(2,1)S(1)}, bf16[64,2,768]{2,0,1:T(8,128)(2,1)S(1)}, u32[]{:S(2)}, u32[]{:S(2)}) collective-permute-start(bf16[64,2,768]{2,0,1:T(8,128)(2,1)S(1)} %copy.59), channel_id=1, source_target_pairs={{0,2},{2,0},{1,3},{3,1},{4,6},{6,4},{5,7},{7,5},{8,10},{10,8},{9,1... | collective-permute-start | bytes 589832 | tf_op jit(solution)/shard_map/ppermute | solution.py:18
  30.7 3.7 %copy-start = (bf16[2,768,3072]{2,1,0:T(8,128)(2,1)S(1)}, bf16[2,768,3072]{2,1,0:T(8,128)(2,1)}, u32[]{:S(2)}) copy-start(bf16[2,768,3072]{2,1,0:T(8,128)(2,1)} %fronts_ref.1) | copy-start | bytes 28311556
  37.9 15.2 %copy-start.1 = (bf16[2,768,3072]{2,1,0:T(8,128)(2,1)}, bf16[2,768,3072]{2,1,0:T(8,128)(2,1)S(1)}, u32[]{:S(2)}) copy-start(bf16[2,768,3072]{2,1,0:T(8,128)(2,1)S(1)} %shard_map.77) | copy-start | bytes 28311556
  42.1 9.2 %collective-permute-start.1 = (bf16[64,3072]{1,0:T(8,128)(2,1)S(1)}, bf16[64,3072]{1,0:T(8,128)(2,1)S(1)}, u32[]{:S(2)}, u32[]{:S(2)}) collective-permute-start(bf16[64,3072]{1,0:T(8,128)(2,1)S(1)} %get-tuple-element.89), channel_id=1, source_target_pairs={{0,16},{16,32},{32,48},{48,0},{1,17},{17,33},{33,49},{49,1},{2,18}... | collective-permute-start | bytes 1179656 | tf_op jit(solution)/shard_map/ppermute | solution.py:18
  42.3 10.8 %collective-permute-start.5 = (bf16[64,3072]{1,0:T(8,128)(2,1)S(1)}, bf16[64,3072]{1,0:T(8,128)(2,1)S(1)}, u32[]{:S(2)}, u32[]{:S(2)}) collective-permute-start(bf16[64,3072]{1,0:T(8,128)(2,1)S(1)} %get-tuple-element.90), channel_id=1, source_target_pairs={{0,48},{16,0},{32,16},{48,32},{1,49},{17,1},{33,17},{49,33},{2,50}... | collective-permute-start | bytes 1179656 | tf_op jit(solution)/shard_map/ppermute | solution.py:18
  51.4 1.5 copy-start.5
  52.9 2.2 %collective-permute-start.4 = (bf16[2,64,768]{2,1,0:T(8,128)(2,1)S(1)}, bf16[2,64,768]{2,1,0:T(8,128)(2,1)S(1)}, u32[]{:S(2)}, u32[]{:S(2)}) collective-permute-start(bf16[2,64,768]{2,1,0:T(8,128)(2,1)S(1)} %dynamic-slice_bitcast_fusion.1), channel_id=1, source_target_pairs={{0,1},{1,0},{2,3},{3,2},{4,5},{5,4},{6,7},{7,6},{8,9},{9,8},{10,11... | collective-permute-start | bytes 589832 | tf_op jit(solution)/shard_map/ppermute | solution.py:18
  54.5 1.6 collective-permute-start.6
  56.2 39.1 %copy-start.6 = (bf16[64,2,768]{2,0,1:T(8,128)(2,1)S(1)}, bf16[64,2,768]{2,0,1:T(8,128)(2,1)}, u32[]{:S(2)}) copy-start(bf16[64,2,768]{2,0,1:T(8,128)(2,1)} %copy-done.5) | copy-start | bytes 589828
  88.8 30.5 %slice-start = ((s8[9437184]{0:T(1024)(128)(4,1)}), s8[1048576]{0:T(1024)(128)(4,1)S(1)}, s32[]{:S(2)}) async-start(s8[9437184]{0:T(1024)(128)(4,1)} %bitcast.82), calls=%async_computation.2 | async-start | bytes 2097152
  88.8 23.1 %all-to-all-start.1 = ((bf16[128,2,768]{2,1,0:T(2,128)(2,1)}), bf16[128,2,768]{2,1,0:T(2,128)(2,1)S(1)}, u32[]{:S(2)}, u32[]{:S(2)}) async-start(bf16[128,2,768]{2,1,0:T(2,128)(2,1)} %pad_maximum_fusion.2), calls=%async_computation.1 | async-start | bytes 786432 | tf_op jit(solution)/shard_map/all_to_all | solution.py:153
  112.3 6.9 %slice-start.1 = ((s8[9437184]{0:T(1024)(128)(4,1)}), s8[4194304]{0:T(1024)(128)(4,1)S(1)}, s32[]{:S(2)}) async-start(s8[9437184]{0:T(1024)(128)(4,1)} %bitcast.82), calls=%async_computation.3 | async-start | bytes 8388608
  115.1 4.2 %slice-start.2 = ((s8[9437184]{0:T(1024)(128)(4,1)}), s8[4194304]{0:T(1024)(128)(4,1)S(1)}, s32[]{:S(2)}) async-start(s8[9437184]{0:T(1024)(128)(4,1)} %bitcast.82), calls=%async_computation.4 | async-start | bytes 8388608
  119.0 19.3 %copy-start.2 = (bf16[256,3072]{1,0:T(8,128)(2,1)}, bf16[256,3072]{1,0:T(8,128)(2,1)S(1)}, u32[]{:S(2)}) copy-start(bf16[256,3072]{1,0:T(8,128)(2,1)S(1)} %fusion.5) | copy-start | bytes 4718596
  121.6 11.2 %collective-permute-start.8 = (bf16[64,3072]{1,0:T(8,128)(2,1)S(1)}, bf16[64,3072]{1,0:T(8,128)(2,1)S(1)}, u32[]{:S(2)}, u32[]{:S(2)}) collective-permute-start(bf16[64,3072]{1,0:T(8,128)(2,1)S(1)} %pad_maximum_fusion.4), channel_id=1, source_target_pairs={{0,48},{16,0},{32,16},{48,32},{1,49},{17,1},{33,17},{49,33},{2,50}... | collective-permute-start | bytes 1179656 | tf_op jit(solution)/shard_map/ppermute | solution.py:18
  122.8 12.1 %collective-permute-start.7 = (bf16[64,3072]{1,0:T(8,128)(2,1)S(1)}, bf16[64,3072]{1,0:T(8,128)(2,1)S(1)}, u32[]{:S(2)}, u32[]{:S(2)}) collective-permute-start(bf16[64,3072]{1,0:T(8,128)(2,1)S(1)} %slice.169), channel_id=1, source_target_pairs={{0,16},{16,32},{32,48},{48,0},{1,17},{17,33},{33,49},{49,1},{2,18}... | collective-permute-start | bytes 1179656 | tf_op jit(solution)/shard_map/ppermute | solution.py:18
  124.6 13.8 %collective-permute-start.9 = (bf16[2,64,768]{2,1,0:T(8,128)(2,1)S(1)}, bf16[2,64,768]{2,1,0:T(8,128)(2,1)S(1)}, u32[]{:S(2)}, u32[]{:S(2)}) collective-permute-start(bf16[2,64,768]{2,1,0:T(8,128)(2,1)S(1)} %pad_maximum_fusion.7), channel_id=1, source_target_pairs={{0,2},{2,0},{1,3},{3,1},{4,6},{6,4},{5,7},{7,5},{8,10},{10,8},{9,1... | collective-permute-start | bytes 589832 | tf_op jit(solution)/shard_map/ppermute | solution.py:18
  138.3 0.9 copy-start.3
  139.2 8.5 %collective-permute-start.15 = (bf16[32,3072]{1,0:T(8,128)(2,1)}, bf16[32,3072]{1,0:T(8,128)(2,1)S(1)}, u32[]{:S(2)}, u32[]{:S(2)}) collective-permute-start(bf16[32,3072]{1,0:T(8,128)(2,1)} %get-tuple-element.74), channel_id=1, source_target_pairs={{0,48},{16,0},{32,16},{48,32},{1,49},{17,1},{33,17},{49,33},{2,50}... | collective-permute-start | bytes 589832 | tf_op jit(solution)/shard_map/ppermute | solution.py:18
  142.3 9.4 %collective-permute-start.14 = (bf16[32,3072]{1,0:T(8,128)(2,1)}, bf16[32,3072]{1,0:T(8,128)(2,1)}, u32[]{:S(2)}, u32[]{:S(2)}) collective-permute-start(bf16[32,3072]{1,0:T(8,128)(2,1)} %get-tuple-element.75), channel_id=1, source_target_pairs={{0,16},{16,32},{32,48},{48,0},{1,17},{17,33},{33,49},{49,1},{2,18}... | collective-permute-start | bytes 589832 | tf_op jit(solution)/shard_map/ppermute | solution.py:18
  142.3 25.9 %copy-start.4 = (bf16[2,64,768]{2,1,0:T(8,128)(2,1)S(1)}, bf16[2,64,768]{2,1,0:T(8,128)(2,1)}, u32[]{:S(2)}) copy-start(bf16[2,64,768]{2,1,0:T(8,128)(2,1)} %copy-done.3) | copy-start | bytes 589828
  142.3 15.6 %collective-permute-start.10 = (bf16[64,3072]{1,0:T(8,128)(2,1)}, bf16[64,3072]{1,0:T(8,128)(2,1)S(1)}, u32[]{:S(2)}, u32[]{:S(2)}) collective-permute-start(bf16[64,3072]{1,0:T(8,128)(2,1)} %slice.216), channel_id=1, source_target_pairs={{0,16},{16,32},{32,48},{48,0},{1,17},{17,33},{33,49},{49,1},{2,18}... | collective-permute-start | bytes 1179656 | tf_op jit(solution)/shard_map/ppermute | solution.py:18
  142.3 15.6 %collective-permute-start.11 = (bf16[64,3072]{1,0:T(8,128)(2,1)}, bf16[64,3072]{1,0:T(8,128)(2,1)S(1)}, u32[]{:S(2)}, u32[]{:S(2)}) collective-permute-start(bf16[64,3072]{1,0:T(8,128)(2,1)} %pad_maximum_fusion.5), channel_id=1, source_target_pairs={{0,48},{16,0},{32,16},{48,32},{1,49},{17,1},{33,17},{49,33},{2,50}... | collective-permute-start | bytes 1179656 | tf_op jit(solution)/shard_map/ppermute | solution.py:18
  153.0 7.1 %collective-permute-start.16 = (bf16[16,3072]{1,0:T(8,128)(2,1)S(1)}, bf16[16,3072]{1,0:T(8,128)(2,1)S(1)}, u32[]{:S(2)}, u32[]{:S(2)}) collective-permute-start(bf16[16,3072]{1,0:T(8,128)(2,1)S(1)} %slice.290), channel_id=1, source_target_pairs={{0,4},{4,8},{8,12},{12,0},{1,5},{5,9},{9,13},{13,1},{2,6},{6,10},{... | collective-permute-start | bytes 294920 | tf_op jit(solution)/shard_map/ppermute | solution.py:18
  153.9 6.2 %collective-permute-start.17 = (bf16[16,3072]{1,0:T(8,128)(2,1)S(1)}, bf16[16,3072]{1,0:T(8,128)(2,1)S(1)}, u32[]{:S(2)}, u32[]{:S(2)}) collective-permute-start(bf16[16,3072]{1,0:T(8,128)(2,1)S(1)} %get-tuple-element.94), channel_id=1, source_target_pairs={{0,8},{4,12},{8,0},{12,4},{1,9},{5,13},{9,1},{13,5},{2,10},{6,14},... | collective-permute-start | bytes 294920 | tf_op jit(solution)/shard_map/ppermute | solution.py:18
  154.8 6.6 %collective-permute-start.18 = (bf16[16,3072]{1,0:T(8,128)(2,1)S(1)}, bf16[16,3072]{1,0:T(8,128)(2,1)S(1)}, u32[]{:S(2)}, u32[]{:S(2)}) collective-permute-start(bf16[16,3072]{1,0:T(8,128)(2,1)S(1)} %get-tuple-element.95), channel_id=1, source_target_pairs={{0,12},{4,0},{8,4},{12,8},{1,13},{5,1},{9,5},{13,9},{2,14},{6,2},{... | collective-permute-start | bytes 294920 | tf_op jit(solution)/shard_map/ppermute | solution.py:18
  158.0 5.7 %collective-permute-start.13 = (bf16[32,3072]{1,0:T(8,128)(2,1)S(1)}, bf16[32,3072]{1,0:T(8,128)(2,1)S(1)}, u32[]{:S(2)}, u32[]{:S(2)}) collective-permute-start(bf16[32,3072]{1,0:T(8,128)(2,1)S(1)} %get-tuple-element.78), channel_id=1, source_target_pairs={{0,48},{16,0},{32,16},{48,32},{1,49},{17,1},{33,17},{49,33},{2,50}... | collective-permute-start | bytes 589832 | tf_op jit(solution)/shard_map/ppermute | solution.py:18
  158.3 6.9 %collective-permute-start.12 = (bf16[32,3072]{1,0:T(8,128)(2,1)S(1)}, bf16[32,3072]{1,0:T(8,128)(2,1)S(1)}, u32[]{:S(2)}, u32[]{:S(2)}) collective-permute-start(bf16[32,3072]{1,0:T(8,128)(2,1)S(1)} %get-tuple-element.79), channel_id=1, source_target_pairs={{0,16},{16,32},{32,48},{48,0},{1,17},{17,33},{33,49},{49,1},{2,18}... | collective-permute-start | bytes 589832 | tf_op jit(solution)/shard_map/ppermute | solution.py:18
  165.4 4.7 %collective-permute-start.19 = (bf16[16,3072]{1,0:T(8,128)(2,1)S(1)}, bf16[16,3072]{1,0:T(8,128)(2,1)S(1)}, u32[]{:S(2)}, u32[]{:S(2)}) collective-permute-start(bf16[16,3072]{1,0:T(8,128)(2,1)S(1)} %slice.289), channel_id=1, source_target_pairs={{0,4},{4,8},{8,12},{12,0},{1,5},{5,9},{9,13},{13,1},{2,6},{6,10},{... | collective-permute-start | bytes 294920 | tf_op jit(solution)/shard_map/ppermute | solution.py:18
  165.9 6.4 %collective-permute-start.20 = (bf16[16,3072]{1,0:T(8,128)(2,1)S(1)}, bf16[16,3072]{1,0:T(8,128)(2,1)S(1)}, u32[]{:S(2)}, u32[]{:S(2)}) collective-permute-start(bf16[16,3072]{1,0:T(8,128)(2,1)S(1)} %get-tuple-element.96), channel_id=1, source_target_pairs={{0,8},{4,12},{8,0},{12,4},{1,9},{5,13},{9,1},{13,5},{2,10},{6,14},... | collective-permute-start | bytes 294920 | tf_op jit(solution)/shard_map/ppermute | solution.py:18
  168.2 5.8 %collective-permute-start.21 = (bf16[16,3072]{1,0:T(8,128)(2,1)S(1)}, bf16[16,3072]{1,0:T(8,128)(2,1)S(1)}, u32[]{:S(2)}, u32[]{:S(2)}) collective-permute-start(bf16[16,3072]{1,0:T(8,128)(2,1)S(1)} %get-tuple-element.97), channel_id=1, source_target_pairs={{0,12},{4,0},{8,4},{12,8},{1,13},{5,1},{9,5},{13,9},{2,14},{6,2},{... | collective-permute-start | bytes 294920 | tf_op jit(solution)/shard_map/ppermute | solution.py:18

commit v5 on v3

--- a/solution.py
+++ b/solution.py
@@ -80,15 +80,18 @@
     return lax.optimization_barrier((shift(to_right, "x", 1), shift(to_left, "x", -1)))
 
 
-def second_step(product, near):
+def second_pieces(product, near):
     block = product.shape[0] // 4
     half = block // 2
     from_left, from_right = near
     over_right = product[2 * block + half : 3 * block].astype(F32) + from_left[:half].astype(F32)
     over_left = product[3 * block : 3 * block + half].astype(F32) + from_right[:half].astype(F32)
-    over_right = shift(over_right.astype(BF16), "x", 1)
-    over_left = shift(over_left.astype(BF16), "x", -1)
-    return lax.optimization_barrier((over_right, over_left))
+    return over_right.astype(BF16), over_left.astype(BF16)
+
+
+def second_step(pieces):
+    over_right, over_left = pieces
+    return lax.optimization_barrier((shift(over_right, "x", 1), shift(over_left, "x", -1)))
 
 
 def last_step(product, near, far):
@@ -142,18 +145,17 @@
         partial = jnp.einsum("sk,mk->sm", gathered[f], masked[f], preferred_element_type=F32)
         halves.append(reduce_core(partial.astype(BF16).reshape(2, 2, slab, tile_rows), x, c))
 
-    spread = ("h", "group") + ROW
-    outgoing = jnp.stack([half.astype(BF16).reshape(2 * slab, tile_rows) for half in halves], axis=1)
-    arrived = lax.all_to_all(outgoing, spread, split_axis=0, concat_axis=0, tiled=True)
-    arrived = arrived[:slab].astype(F32) + arrived[slab:].astype(F32)
-    arrived = arrived.astype(BF16).reshape(-1, tile_rows)
+    away = jnp.stack([pick(half, 1 - h).astype(BF16) for half in halves])
+    received = shift(away, "h", 1)
+    slabs = [pick(half, h) + received[f].astype(F32) for f, half in enumerate(halves)]
+    sampled = jnp.stack([total.astype(BF16) for total in slabs], axis=1)
+    spread = ("group",) + ROW
+    arrived = lax.all_to_all(sampled, spread, split_axis=0, concat_axis=0, tiled=True)
+    arrived = arrived.reshape(-1, tile_rows)
     extension = jnp.einsum("ij,jk->ik", weight, arrived, preferred_element_type=F32).astype(BF16)
     extension = extension.reshape(slab, local, tile_rows)
     extension = jnp.concatenate([extension, extension], axis=0)
-    away = jnp.stack([pick(half, 1 - h).astype(BF16) for half in halves])
-    away, extension = lax.optimization_barrier((away, extension))
-    extension = lax.all_to_all(extension, spread, split_axis=0, concat_axis=0, tiled=True)
-    received, extension = lax.optimization_barrier((shift(away, "h", 1), extension))
+    extension = lax.all_to_all(extension, ("h",) + spread, split_axis=0, concat_axis=0, tiled=True)
     combined = second.reshape(extension.shape).astype(F32) + extension.astype(F32)
     combined = combined.astype(BF16)
 
@@ -174,13 +176,10 @@
     product_1 = multiplied(1)
     pieces_1 = first_pieces(product_1)
     near_0, product_1, pieces_1 = lax.optimization_barrier((near_0, product_1, pieces_1))
-    far_0 = second_step(product_0, near_0)
+    far_0 = second_step(second_pieces(product_0, near_0))
     near_1 = first_step(pieces_1)
     total_0 = last_step(product_0, near_0, far_0)
-    far_1 = second_step(product_1, near_1)
-    received, far_1 = lax.optimization_barrier((received, far_1))
-    slabs = [pick(half, h) + received[f].astype(F32) for f, half in enumerate(halves)]
-    sampled = jnp.stack([total.astype(BF16) for total in slabs], axis=1)
+    far_1 = second_step(second_pieces(product_1, near_1))
     total_1 = last_step(product_1, near_1, far_1)
     outs = [total_0.astype(BF16), total_1.astype(BF16)]
     return sampled, jnp.stack(outs, axis=1)

time: 176 us -> 178 us (1.011)
  blocking collectives: 21.1 us -> 43.3 us
  starting transfers between devices: 53.8 us -> 42.8 us
  other arithmetic: 8.29 us -> 3.64 us
  local copies, waits for them, and re-layouts: 11.1 us -> 9.04 us
    all_to_all x0 -> x1, blocking collectives: none -> 22.2 us  [shards(): lax.all_to_all(sampled, spread, split_axis=0, concat_axis=0, tiled=True)]
    all_to_all x2 -> x1, starting transfers between devices: 18.5 us -> 9.06 us  [shards(): lax.all_to_all(extension, ('h',) + spread, split_axis=0, concat_axis=0, t...]
    all_to_all x2 -> x1, waiting for transfers between devices: 17.5 us -> 15.4 us  [shards(): lax.all_to_all(extension, ('h',) + spread, split_axis=0, concat_axis=0, t...]
    unnamed x26 -> x18, local copies, waits for them, and re-layouts: 5.49 us -> 4.8 us
  transfers between devices with their start and end apart: 24 -> 23, of which waited for: 18 -> 15; matrix products, arithmetic and copies ran while one was open for 6% -> 4% of each run, Pallas kernels for 2% -> 2%
where the time goes in v5:
time: 178 us
  waiting for transfers between devices  65.9 us (37%)
  blocking collectives  43.3 us (24%)
  starting transfers between devices  42.8 us (24%)
  local copies, waits for them, and re-layouts  9.04 us (5%)
  matrix products  8.46 us (5%)
  other arithmetic  3.64 us (2%)
  Pallas kernels  3.47 us (2%)
    ppermute x22, waiting for transfers between devices, shift(): return lax.ppermute(value, axis, [(i, (i + by) % n) for i in range(n)])  50.5 us
    ppermute x22, starting transfers between devices, shift(): return lax.ppermute(value, axis, [(i, (i + by) % n) for i in range(n)])  33.7 us
    all_to_all x1, blocking collectives, shards(): lax.all_to_all(sampled, spread, split_axis=0, concat_axis=0, tiled=True)  22.2 us
    all_gather x1, blocking collectives, shards(): columns = lax.all_gather(mine, 'z', axis=1, tiled=True)  18.6 us
    all_to_all x1, waiting for transfers between devices, shards(): lax.all_to_all(extension, ('h',) + spread, split_axis=0, concat_axis=0, t...  15.4 us
    all_to_all x1, starting transfers between devices, shards(): lax.all_to_all(extension, ('h',) + spread, split_axis=0, concat_axis=0, t...  9.06 us
    dot_general x2, matrix products, multiplied(): jnp.einsum('sm,mk->sk', ordered[f], masked[f], preferred_element_type=F32)  5.35 us
    unnamed x18, local copies, waits for them, and re-layouts  4.8 us
  transfers between devices with their start and end apart: 23, of which 15 were waited for; matrix products, arithmetic and copies ran while one was open for 4% of the time, Pallas kernels for 2%

profile of v5, /device:TPU:32, one launch (start us, length us, event | category | flops | bytes accessed | tf_op | source)
XLA Modules:
  0.0 177.7 jit_solution(8329587618075610791)
XLA Ops:
  0.7 1.4 fusion.59
  2.1 18.6 %all_gather.9 = bf16[2,64,3072]{2,1,0:T(8,128)(2,1)S(1)} all-gather(bf16[2,16,3072]{2,1,0:T(8,128)(2,1)S(1)} %pad_maximum_fusion.5), channel_id=1, replica_groups=mesh['group'=4,'x'=4,'z'=4,'h'=2,'c'=2] {'z'}, dimensions={1}, use_global_device_ids=true | all-gather | bytes 983040 | tf_op jit(solution)/shard_map/all_gather | solution.py:133
  20.7 2.8 %collective-permute-start.2 = (bf16[2,64,3072]{2,1,0:T(8,128)(2,1)S(1)}, bf16[2,64,3072]{2,1,0:T(8,128)(2,1)S(1)}, u32[]{:S(2)}, u32[]{:S(2)}) collective-permute-start(bf16[2,64,3072]{2,1,0:T(8,128)(2,1)S(1)} %all_gather.9), channel_id=1, source_target_pairs={{0,48},{16,0},{32,16},{48,32},{1,49},{17,1},{33,17},{49,33},{2,50}... | collective-permute-start | bytes 2359304 | tf_op jit(solution)/shard_map/ppermute | solution.py:18
  23.6 0.7 dynamic_slice.54.sizes_ref
  24.3 0.9 copy.63
  25.3 4.7 %collective-permute-start.3 = (bf16[64,2,768]{2,0,1:T(8,128)(2,1)S(1)}, bf16[64,2,768]{2,0,1:T(8,128)(2,1)S(1)}, u32[]{:S(2)}, u32[]{:S(2)}) collective-permute-start(bf16[64,2,768]{2,0,1:T(8,128)(2,1)S(1)} %copy.63), channel_id=1, source_target_pairs={{0,2},{2,0},{1,3},{3,1},{4,6},{6,4},{5,7},{7,5},{8,10},{10,8},{9,1... | collective-permute-start | bytes 589832 | tf_op jit(solution)/shard_map/ppermute | solution.py:18
  30.1 0.1 eq.33
  30.2 0.1 copy.49
  30.3 0.1 eq.37
  30.5 0.1 and_convert_fusion
  30.7 3.7 %copy-done = bf16[2,768,3072]{2,1,0:T(8,128)(2,1)S(1)} copy-done((bf16[2,768,3072]{2,1,0:T(8,128)(2,1)S(1)}, bf16[2,768,3072]{2,1,0:T(8,128)(2,1)}, u32[]{:S(2)}) %copy-start) | copy-done | bytes 9437208
  34.4 3.5 %shard_map.77 = bf16[2,768,3072]{2,1,0:T(8,128)(2,1)S(1)} custom-call(s32[2]{0:T(128)S(1)} %dynamic_slice.54.sizes_ref, s32[2]{0:T(128)S(1)} %pad_add_fusion.origin_ref, bf16[2,768,3072]{2,1,0:T(8,128)(2,1)S(1)} %copy-done), custom_call_target="tpu_custom_call" | custom-call | tf_op jit(solution)/shard_map/pallas_call | solution.py:53
  37.9 4.1 %collective-permute-done = bf16[2,64,3072]{2,1,0:T(8,128)(2,1)S(1)} collective-permute-done((bf16[2,64,3072]{2,1,0:T(8,128)(2,1)S(1)}, bf16[2,64,3072]{2,1,0:T(8,128)(2,1)S(1)}, u32[]{:S(2)}, u32[]{:S(2)}) %collective-permute-start) | collective-permute-done | bytes 786464 | tf_op jit(solution)/shard_map/ppermute | solution.py:18
  42.1 0.1 collective-permute-start.1
  42.3 3.3 %collective-permute-start.5 = (bf16[64,3072]{1,0:T(8,128)(2,1)S(1)}, bf16[64,3072]{1,0:T(8,128)(2,1)S(1)}, u32[]{:S(2)}, u32[]{:S(2)}) collective-permute-start(bf16[64,3072]{1,0:T(8,128)(2,1)S(1)} %get-tuple-element.69), channel_id=1, source_target_pairs={{0,48},{16,0},{32,16},{48,32},{1,49},{17,1},{33,17},{49,33},{2,50}... | collective-permute-start | bytes 1179656 | tf_op jit(solution)/shard_map/ppermute | solution.py:18
  45.5 5.7 %collective-permute-done.1 = bf16[64,3072]{1,0:T(8,128)(2,1)S(1)} collective-permute-done((bf16[64,3072]{1,0:T(8,128)(2,1)S(1)}, bf16[64,3072]{1,0:T(8,128)(2,1)S(1)}, u32[]{:S(2)}, u32[]{:S(2)}) %collective-permute-start.1) | collective-permute-done | bytes 393248 | tf_op jit(solution)/shard_map/ppermute | solution.py:18
  51.3 0.1 pad_maximum_fusion
  51.4 1.5 fusion.16
  52.9 0.1 collective-permute-start.4
  53.0 1.4 fusion.13
  54.5 0.6 collective-permute-start.6
  55.2 1.0 collective-permute-done.6
  56.3 4.4 %collective-permute-start.7 = (bf16[2,64,768]{2,1,0:T(8,128)(2,1)S(1)}, bf16[2,64,768]{2,1,0:T(8,128)(2,1)S(1)}, u32[]{:S(2)}, u32[]{:S(2)}) collective-permute-start(bf16[2,64,768]{2,1,0:T(8,128)(2,1)S(1)} %pad_maximum_fusion.6), channel_id=1, source_target_pairs={{0,2},{2,0},{1,3},{3,1},{4,6},{6,4},{5,7},{7,5},{8,10},{10,8},{9,1... | collective-permute-start | bytes 589832 | tf_op jit(solution)/shard_map/ppermute | solution.py:18
  60.7 8.2 %collective-permute-done.7 = bf16[2,64,768]{2,1,0:T(8,128)(2,1)S(1)} collective-permute-done((bf16[2,64,768]{2,1,0:T(8,128)(2,1)S(1)}, bf16[2,64,768]{2,1,0:T(8,128)(2,1)S(1)}, u32[]{:S(2)}, u32[]{:S(2)}) %collective-permute-start.7) | collective-permute-done | bytes 196640 | tf_op jit(solution)/shard_map/ppermute | solution.py:18
  69.0 0.2 copy.54
  69.2 22.2 %all_to_all.10 = bf16[64,2,768]{2,1,0:T(2,128)(2,1)S(1)} all-to-all(bf16[64,2,768]{2,1,0:T(2,128)(2,1)S(1)} %copy.54), channel_id=1, replica_groups=mesh['group'=4,'x'=4,'z'=4,'h'=2,'c'=2] {'group','x','z'}, dimensions={0} | all-to-all | bytes 393216 | tf_op jit(solution)/shard_map/all_to_all | solution.py:153
  91.5 0.2 convolution_convert_fusion
  91.8 1.3 pad_maximum_fusion.1
  93.0 9.1 %all-to-all-start.1 = ((bf16[128,2,768]{2,1,0:T(2,128)(2,1)}), bf16[128,2,768]{2,1,0:T(2,128)(2,1)S(1)}, u32[]{:S(2)}, u32[]{:S(2)}) async-start(bf16[128,2,768]{2,1,0:T(2,128)(2,1)} %pad_maximum_fusion.1), calls=%async_computation.1 | async-start | bytes 786432 | tf_op jit(solution)/shard_map/all_to_all | solution.py:158
  102.1 0.3 fusion.23
  102.5 15.4 %all-to-all-done.1 = bf16[128,2,768]{2,1,0:T(2,128)(2,1)S(1)} async-done(((bf16[128,2,768]{2,1,0:T(2,128)(2,1)}), bf16[128,2,768]{2,1,0:T(2,128)(2,1)S(1)}, u32[]{:S(2)}, u32[]{:S(2)}) %all-to-all-start.1) | async-done | bytes 393248 | tf_op jit(solution)/shard_map/all_to_all | solution.py:158
  118.0 0.2 fusion.28
  118.2 0.2 fusion.25
  118.4 2.5 %all-gather = bf16[4,128,768]{2,1,0:T(8,128)(2,1)S(1)} all-gather(bf16[2,128,768]{2,1,0:T(8,128)(2,1)S(1)} %pad_maximum_fusion.2), channel_id=2, replica_groups=mesh['group'=4,'x'=4,'z'=4,'h'=2,'c'=2] {'c'}, dimensions={0}, use_global_device_ids=true | all-gather | bytes 1179648 | tf_op jit(solution)/shard_map/all_gather | solution.py:167
  121.0 0.2 fusion.19
  121.2 3.9 %fusion.5 = bf16[256,3072]{1,0:T(8,128)(2,1)S(1)} fusion(bf16[256,768]{1,0:T(8,128)(2,1)S(1)} %bitcast.94, bf16[2,768,3072]{2,1,0:T(8,128)(2,1)} %copy-done.1), kind=kOutput, calls=%fused_computation.7 | convolution fusion | flops 1208745984 | bytes 6684672 | tf_op jit(solution)/shard_map/sm,mk->sk/dot_general | solution.py:171
  125.2 0.2 fusion.18
  125.4 1.4 fusion.4
  126.8 1.2 collective-permute-start.9
  128.0 0.9 collective-permute-start.8
  129.0 9.0 %collective-permute-done.9 = bf16[64,3072]{1,0:T(8,128)(2,1)S(1)} collective-permute-done((bf16[64,3072]{1,0:T(8,128)(2,1)S(1)}, bf16[64,3072]{1,0:T(8,128)(2,1)S(1)}, u32[]{:S(2)}, u32[]{:S(2)}) %collective-permute-start.9) | collective-permute-done | bytes 393248 | tf_op jit(solution)/shard_map/ppermute | solution.py:18
  138.1 2.0 %collective-permute-done.8 = bf16[64,3072]{1,0:T(8,128)(2,1)S(1)} collective-permute-done((bf16[64,3072]{1,0:T(8,128)(2,1)S(1)}, bf16[64,3072]{1,0:T(8,128)(2,1)S(1)}, u32[]{:S(2)}, u32[]{:S(2)}) %collective-permute-start.8) | collective-permute-done | bytes 393248 | tf_op jit(solution)/shard_map/ppermute | solution.py:18
  140.1 0.1 add_convert_fusion.4
  140.2 0.4 collective-permute-start.11
  140.6 1.7 collective-permute-start.10
  142.3 3.2 %collective-permute-start.16 = (bf16[64,3072]{1,0:T(8,128)(2,1)S(1)}, bf16[64,3072]{1,0:T(8,128)(2,1)S(1)}, u32[]{:S(2)}, u32[]{:S(2)}) collective-permute-start(bf16[64,3072]{1,0:T(8,128)(2,1)S(1)} %pad_maximum_fusion.4), channel_id=1, source_target_pairs={{0,48},{16,0},{32,16},{48,32},{1,49},{17,1},{33,17},{49,33},{2,50}... | collective-permute-start | bytes 1179656 | tf_op jit(solution)/shard_map/ppermute | solution.py:18
  145.5 2.6 %collective-permute-done.11 = bf16[32,3072]{1,0:T(8,128)(2,1)S(1)} collective-permute-done((bf16[32,3072]{1,0:T(8,128)(2,1)S(1)}, bf16[32,3072]{1,0:T(8,128)(2,1)S(1)}, u32[]{:S(2)}, u32[]{:S(2)}) %collective-permute-start.11) | collective-permute-done | bytes 196640 | tf_op jit(solution)/shard_map/ppermute | solution.py:18
  148.1 1.5 collective-permute-done.10
  149.6 0.1 convert_add_fusion.3
  149.8 6.3 %collective-permute-done.15 = bf16[64,3072]{1,0:T(8,128)(2,1)S(1)} collective-permute-done((bf16[64,3072]{1,0:T(8,128)(2,1)S(1)}, bf16[64,3072]{1,0:T(8,128)(2,1)S(1)}, u32[]{:S(2)}, u32[]{:S(2)}) %collective-permute-start.15) | collective-permute-done | bytes 393248 | tf_op jit(solution)/shard_map/ppermute | solution.py:18
  156.0 0.1 add_convert_fusion.1
  156.1 0.4 collective-permute-start.18
  156.5 1.8 collective-permute-start.17
  158.3 1.2 collective-permute-start.12
  159.5 3.0 %collective-permute-start.13 = (bf16[16,3072]{1,0:T(8,128)(2,1)S(1)}, bf16[16,3072]{1,0:T(8,128)(2,1)S(1)}, u32[]{:S(2)}, u32[]{:S(2)}) collective-permute-start(bf16[16,3072]{1,0:T(8,128)(2,1)S(1)} %get-tuple-element.72), channel_id=1, source_target_pairs={{0,8},{4,12},{8,0},{12,4},{1,9},{5,13},{9,1},{13,5},{2,10},{6,14},... | collective-permute-start | bytes 294920 | tf_op jit(solution)/shard_map/ppermute | solution.py:18
  162.5 0.9 collective-permute-done.17
  163.4 0.1 convert_add_fusion.2
  163.6 1.2 collective-permute-start.19
  164.8 2.8 %collective-permute-start.20 = (bf16[16,3072]{1,0:T(8,128)(2,1)S(1)}, bf16[16,3072]{1,0:T(8,128)(2,1)S(1)}, u32[]{:S(2)}, u32[]{:S(2)}) collective-permute-start(bf16[16,3072]{1,0:T(8,128)(2,1)S(1)} %get-tuple-element.74), channel_id=1, source_target_pairs={{0,8},{4,12},{8,0},{12,4},{1,9},{5,13},{9,1},{13,5},{2,10},{6,14},... | collective-permute-start | bytes 294920 | tf_op jit(solution)/shard_map/ppermute | solution.py:18
  167.5 4.4 %collective-permute-done.13 = bf16[16,3072]{1,0:T(8,128)(2,1)S(1)} collective-permute-done((bf16[16,3072]{1,0:T(8,128)(2,1)S(1)}, bf16[16,3072]{1,0:T(8,128)(2,1)S(1)}, u32[]{:S(2)}, u32[]{:S(2)}) %collective-permute-start.13) | collective-permute-done | bytes 98336 | tf_op jit(solution)/shard_map/ppermute | solution.py:18
  172.0 2.2 %collective-permute-done.14 = bf16[16,3072]{1,0:T(8,128)(2,1)S(1)} collective-permute-done((bf16[16,3072]{1,0:T(8,128)(2,1)S(1)}, bf16[16,3072]{1,0:T(8,128)(2,1)S(1)}, u32[]{:S(2)}, u32[]{:S(2)}) %collective-permute-start.14) | collective-permute-done | bytes 98336 | tf_op jit(solution)/shard_map/ppermute | solution.py:18
  174.3 0.3 collective-permute-done.20
  174.6 2.2 %collective-permute-done.21 = bf16[16,3072]{1,0:T(8,128)(2,1)S(1)} collective-permute-done((bf16[16,3072]{1,0:T(8,128)(2,1)S(1)}, bf16[16,3072]{1,0:T(8,128)(2,1)S(1)}, u32[]{:S(2)}, u32[]{:S(2)}) %collective-permute-start.21) | collective-permute-done | bytes 98336 | tf_op jit(solution)/shard_map/ppermute | solution.py:18
  176.9 0.9 copy.55
  (66 shorter events, 1.6 us)
Async XLA Ops:
  0.6 29.4 %copy-start.4 = (s32[8]{0:T(128)S(1)}, s32[8]{0:T(128)}, u32[]{:S(2)}) copy-start(s32[8]{0:T(128)} %param.10) | copy-start | bytes 100
  0.6 29.6 %copy-start.3 = (s32[8,16]{1,0:T(8,128)S(1)}, s32[8,16]{1,0:T(8,128)}, u32[]{:S(2)}) copy-start(s32[8,16]{1,0:T(8,128)} %param.11) | copy-start | bytes 1540
  20.7 21.4 %collective-permute-start.2 = (bf16[2,64,3072]{2,1,0:T(8,128)(2,1)S(1)}, bf16[2,64,3072]{2,1,0:T(8,128)(2,1)S(1)}, u32[]{:S(2)}, u32[]{:S(2)}) collective-permute-start(bf16[2,64,3072]{2,1,0:T(8,128)(2,1)S(1)} %all_gather.9), channel_id=1, source_target_pairs={{0,48},{16,0},{32,16},{48,32},{1,49},{17,1},{33,17},{49,33},{2,50}... | collective-permute-start | bytes 2359304 | tf_op jit(solution)/shard_map/ppermute | solution.py:18
  23.6 18.5 %collective-permute-start = (bf16[2,64,3072]{2,1,0:T(8,128)(2,1)S(1)}, bf16[2,64,3072]{2,1,0:T(8,128)(2,1)S(1)}, u32[]{:S(2)}, u32[]{:S(2)}) collective-permute-start(bf16[2,64,3072]{2,1,0:T(8,128)(2,1)S(1)} %all_gather.9), channel_id=1, source_target_pairs={{0,16},{16,32},{32,48},{48,0},{1,17},{17,33},{33,49},{49,1},{2,18}... | collective-permute-start | bytes 2359304 | tf_op jit(solution)/shard_map/ppermute | solution.py:18
  25.3 26.1 %collective-permute-start.3 = (bf16[64,2,768]{2,0,1:T(8,128)(2,1)S(1)}, bf16[64,2,768]{2,0,1:T(8,128)(2,1)S(1)}, u32[]{:S(2)}, u32[]{:S(2)}) collective-permute-start(bf16[64,2,768]{2,0,1:T(8,128)(2,1)S(1)} %copy.63), channel_id=1, source_target_pairs={{0,2},{2,0},{1,3},{3,1},{4,6},{6,4},{5,7},{7,5},{8,10},{10,8},{9,1... | collective-permute-start | bytes 589832 | tf_op jit(solution)/shard_map/ppermute | solution.py:18
  30.7 3.7 %copy-start = (bf16[2,768,3072]{2,1,0:T(8,128)(2,1)S(1)}, bf16[2,768,3072]{2,1,0:T(8,128)(2,1)}, u32[]{:S(2)}) copy-start(bf16[2,768,3072]{2,1,0:T(8,128)(2,1)} %fronts_ref.1) | copy-start | bytes 28311556
  37.9 15.1 %copy-start.1 = (bf16[2,768,3072]{2,1,0:T(8,128)(2,1)}, bf16[2,768,3072]{2,1,0:T(8,128)(2,1)S(1)}, u32[]{:S(2)}) copy-start(bf16[2,768,3072]{2,1,0:T(8,128)(2,1)S(1)} %shard_map.77) | copy-start | bytes 28311556
  42.1 9.2 %collective-permute-start.1 = (bf16[64,3072]{1,0:T(8,128)(2,1)S(1)}, bf16[64,3072]{1,0:T(8,128)(2,1)S(1)}, u32[]{:S(2)}, u32[]{:S(2)}) collective-permute-start(bf16[64,3072]{1,0:T(8,128)(2,1)S(1)} %get-tuple-element.66), channel_id=1, source_target_pairs={{0,16},{16,32},{32,48},{48,0},{1,17},{17,33},{33,49},{49,1},{2,18}... | collective-permute-start | bytes 1179656 | tf_op jit(solution)/shard_map/ppermute | solution.py:18
  42.3 10.8 %collective-permute-start.5 = (bf16[64,3072]{1,0:T(8,128)(2,1)S(1)}, bf16[64,3072]{1,0:T(8,128)(2,1)S(1)}, u32[]{:S(2)}, u32[]{:S(2)}) collective-permute-start(bf16[64,3072]{1,0:T(8,128)(2,1)S(1)} %get-tuple-element.69), channel_id=1, source_target_pairs={{0,48},{16,0},{32,16},{48,32},{1,49},{17,1},{33,17},{49,33},{2,50}... | collective-permute-start | bytes 1179656 | tf_op jit(solution)/shard_map/ppermute | solution.py:18
  52.9 2.2 %collective-permute-start.4 = (bf16[2,64,768]{2,1,0:T(8,128)(2,1)S(1)}, bf16[2,64,768]{2,1,0:T(8,128)(2,1)S(1)}, u32[]{:S(2)}, u32[]{:S(2)}) collective-permute-start(bf16[2,64,768]{2,1,0:T(8,128)(2,1)S(1)} %dynamic-slice_bitcast_fusion.1), channel_id=1, source_target_pairs={{0,1},{1,0},{2,3},{3,2},{4,5},{5,4},{6,7},{7,6},{8,9},{9,8},{10,11... | collective-permute-start | bytes 589832 | tf_op jit(solution)/shard_map/ppermute | solution.py:18
  54.5 1.6 collective-permute-start.6
  56.3 12.6 %collective-permute-start.7 = (bf16[2,64,768]{2,1,0:T(8,128)(2,1)S(1)}, bf16[2,64,768]{2,1,0:T(8,128)(2,1)S(1)}, u32[]{:S(2)}, u32[]{:S(2)}) collective-permute-start(bf16[2,64,768]{2,1,0:T(8,128)(2,1)S(1)} %pad_maximum_fusion.6), channel_id=1, source_target_pairs={{0,2},{2,0},{1,3},{3,1},{4,6},{6,4},{5,7},{7,5},{8,10},{10,8},{9,1... | collective-permute-start | bytes 589832 | tf_op jit(solution)/shard_map/ppermute | solution.py:18
  69.2 48.7 %copy-start.2 = (bf16[64,2,768]{2,1,0:T(2,128)(2,1)}, bf16[64,2,768]{2,1,0:T(2,128)(2,1)S(1)}, u32[]{:S(2)}) copy-start(bf16[64,2,768]{2,1,0:T(2,128)(2,1)S(1)} %copy.54) | copy-start | bytes 589828
  93.0 32.3 %slice-start = ((s8[9437184]{0:T(1024)(128)(4,1)}), s8[1048576]{0:T(1024)(128)(4,1)S(1)}, s32[]{:S(2)}) async-start(s8[9437184]{0:T(1024)(128)(4,1)} %bitcast.81), calls=%async_computation.2 | async-start | bytes 2097152
  93.0 24.8 %all-to-all-start.1 = ((bf16[128,2,768]{2,1,0:T(2,128)(2,1)}), bf16[128,2,768]{2,1,0:T(2,128)(2,1)S(1)}, u32[]{:S(2)}, u32[]{:S(2)}) async-start(bf16[128,2,768]{2,1,0:T(2,128)(2,1)} %pad_maximum_fusion.1), calls=%async_computation.1 | async-start | bytes 786432 | tf_op jit(solution)/shard_map/all_to_all | solution.py:158
  118.4 7.0 %slice-start.1 = ((s8[9437184]{0:T(1024)(128)(4,1)}), s8[4194304]{0:T(1024)(128)(4,1)S(1)}, s32[]{:S(2)}) async-start(s8[9437184]{0:T(1024)(128)(4,1)} %bitcast.81), calls=%async_computation.3 | async-start | bytes 8388608
  121.1 4.2 %slice-start.2 = ((s8[9437184]{0:T(1024)(128)(4,1)}), s8[4194304]{0:T(1024)(128)(4,1)S(1)}, s32[]{:S(2)}) async-start(s8[9437184]{0:T(1024)(128)(4,1)} %bitcast.81), calls=%async_computation.4 | async-start | bytes 8388608
  126.8 11.2 %collective-permute-start.9 = (bf16[64,3072]{1,0:T(8,128)(2,1)S(1)}, bf16[64,3072]{1,0:T(8,128)(2,1)S(1)}, u32[]{:S(2)}, u32[]{:S(2)}) collective-permute-start(bf16[64,3072]{1,0:T(8,128)(2,1)S(1)} %pad_maximum_fusion.3), channel_id=1, source_target_pairs={{0,48},{16,0},{32,16},{48,32},{1,49},{17,1},{33,17},{49,33},{2,50}... | collective-permute-start | bytes 1179656 | tf_op jit(solution)/shard_map/ppermute | solution.py:18
  128.0 12.1 %collective-permute-start.8 = (bf16[64,3072]{1,0:T(8,128)(2,1)S(1)}, bf16[64,3072]{1,0:T(8,128)(2,1)S(1)}, u32[]{:S(2)}, u32[]{:S(2)}) collective-permute-start(bf16[64,3072]{1,0:T(8,128)(2,1)S(1)} %slice.208), channel_id=1, source_target_pairs={{0,16},{16,32},{32,48},{48,0},{1,17},{17,33},{33,49},{49,1},{2,18}... | collective-permute-start | bytes 1179656 | tf_op jit(solution)/shard_map/ppermute | solution.py:18
  140.2 7.9 %collective-permute-start.11 = (bf16[32,3072]{1,0:T(8,128)(2,1)S(1)}, bf16[32,3072]{1,0:T(8,128)(2,1)S(1)}, u32[]{:S(2)}, u32[]{:S(2)}) collective-permute-start(bf16[32,3072]{1,0:T(8,128)(2,1)S(1)} %get-tuple-element.52), channel_id=1, source_target_pairs={{0,48},{16,0},{32,16},{48,32},{1,49},{17,1},{33,17},{49,33},{2,50}... | collective-permute-start | bytes 589832 | tf_op jit(solution)/shard_map/ppermute | solution.py:18
  140.6 9.0 %collective-permute-start.10 = (bf16[32,3072]{1,0:T(8,128)(2,1)S(1)}, bf16[32,3072]{1,0:T(8,128)(2,1)S(1)}, u32[]{:S(2)}, u32[]{:S(2)}) collective-permute-start(bf16[32,3072]{1,0:T(8,128)(2,1)S(1)} %get-tuple-element.53), channel_id=1, source_target_pairs={{0,16},{16,32},{32,48},{48,0},{1,17},{17,33},{33,49},{49,1},{2,18}... | collective-permute-start | bytes 589832 | tf_op jit(solution)/shard_map/ppermute | solution.py:18
  142.3 13.7 %collective-permute-start.15 = (bf16[64,3072]{1,0:T(8,128)(2,1)S(1)}, bf16[64,3072]{1,0:T(8,128)(2,1)S(1)}, u32[]{:S(2)}, u32[]{:S(2)}) collective-permute-start(bf16[64,3072]{1,0:T(8,128)(2,1)S(1)} %slice.212), channel_id=1, source_target_pairs={{0,16},{16,32},{32,48},{48,0},{1,17},{17,33},{33,49},{49,1},{2,18}... | collective-permute-start | bytes 1179656 | tf_op jit(solution)/shard_map/ppermute | solution.py:18
  142.3 13.7 %collective-permute-start.16 = (bf16[64,3072]{1,0:T(8,128)(2,1)S(1)}, bf16[64,3072]{1,0:T(8,128)(2,1)S(1)}, u32[]{:S(2)}, u32[]{:S(2)}) collective-permute-start(bf16[64,3072]{1,0:T(8,128)(2,1)S(1)} %pad_maximum_fusion.4), channel_id=1, source_target_pairs={{0,48},{16,0},{32,16},{48,32},{1,49},{17,1},{33,17},{49,33},{2,50}... | collective-permute-start | bytes 1179656 | tf_op jit(solution)/shard_map/ppermute | solution.py:18
  156.1 6.3 %collective-permute-start.18 = (bf16[32,3072]{1,0:T(8,128)(2,1)S(1)}, bf16[32,3072]{1,0:T(8,128)(2,1)S(1)}, u32[]{:S(2)}, u32[]{:S(2)}) collective-permute-start(bf16[32,3072]{1,0:T(8,128)(2,1)S(1)} %get-tuple-element.56), channel_id=1, source_target_pairs={{0,48},{16,0},{32,16},{48,32},{1,49},{17,1},{33,17},{49,33},{2,50}... | collective-permute-start | bytes 589832 | tf_op jit(solution)/shard_map/ppermute | solution.py:18
  156.5 6.9 %collective-permute-start.17 = (bf16[32,3072]{1,0:T(8,128)(2,1)S(1)}, bf16[32,3072]{1,0:T(8,128)(2,1)S(1)}, u32[]{:S(2)}, u32[]{:S(2)}) collective-permute-start(bf16[32,3072]{1,0:T(8,128)(2,1)S(1)} %get-tuple-element.57), channel_id=1, source_target_pairs={{0,16},{16,32},{32,48},{48,0},{1,17},{17,33},{33,49},{49,1},{2,18}... | collective-permute-start | bytes 589832 | tf_op jit(solution)/shard_map/ppermute | solution.py:18
  158.3 9.2 %collective-permute-start.12 = (bf16[16,3072]{1,0:T(8,128)(2,1)S(1)}, bf16[16,3072]{1,0:T(8,128)(2,1)S(1)}, u32[]{:S(2)}, u32[]{:S(2)}) collective-permute-start(bf16[16,3072]{1,0:T(8,128)(2,1)S(1)} %slice.291), channel_id=1, source_target_pairs={{0,4},{4,8},{8,12},{12,0},{1,5},{5,9},{9,13},{13,1},{2,6},{6,10},{... | collective-permute-start | bytes 294920 | tf_op jit(solution)/shard_map/ppermute | solution.py:18
  159.5 12.5 %collective-permute-start.13 = (bf16[16,3072]{1,0:T(8,128)(2,1)S(1)}, bf16[16,3072]{1,0:T(8,128)(2,1)S(1)}, u32[]{:S(2)}, u32[]{:S(2)}) collective-permute-start(bf16[16,3072]{1,0:T(8,128)(2,1)S(1)} %get-tuple-element.72), channel_id=1, source_target_pairs={{0,8},{4,12},{8,0},{12,4},{1,9},{5,13},{9,1},{13,5},{2,10},{6,14},... | collective-permute-start | bytes 294920 | tf_op jit(solution)/shard_map/ppermute | solution.py:18
  162.5 11.7 %collective-permute-start.14 = (bf16[16,3072]{1,0:T(8,128)(2,1)S(1)}, bf16[16,3072]{1,0:T(8,128)(2,1)S(1)}, u32[]{:S(2)}, u32[]{:S(2)}) collective-permute-start(bf16[16,3072]{1,0:T(8,128)(2,1)S(1)} %get-tuple-element.73), channel_id=1, source_target_pairs={{0,12},{4,0},{8,4},{12,8},{1,13},{5,1},{9,5},{13,9},{2,14},{6,2},{... | collective-permute-start | bytes 294920 | tf_op jit(solution)/shard_map/ppermute | solution.py:18
  163.6 10.7 %collective-permute-start.19 = (bf16[16,3072]{1,0:T(8,128)(2,1)S(1)}, bf16[16,3072]{1,0:T(8,128)(2,1)S(1)}, u32[]{:S(2)}, u32[]{:S(2)}) collective-permute-start(bf16[16,3072]{1,0:T(8,128)(2,1)S(1)} %slice.290), channel_id=1, source_target_pairs={{0,4},{4,8},{8,12},{12,0},{1,5},{5,9},{9,13},{13,1},{2,6},{6,10},{... | collective-permute-start | bytes 294920 | tf_op jit(solution)/shard_map/ppermute | solution.py:18
  164.8 9.8 %collective-permute-start.20 = (bf16[16,3072]{1,0:T(8,128)(2,1)S(1)}, bf16[16,3072]{1,0:T(8,128)(2,1)S(1)}, u32[]{:S(2)}, u32[]{:S(2)}) collective-permute-start(bf16[16,3072]{1,0:T(8,128)(2,1)S(1)} %get-tuple-element.74), channel_id=1, source_target_pairs={{0,8},{4,12},{8,0},{12,4},{1,9},{5,13},{9,1},{13,5},{2,10},{6,14},... | collective-permute-start | bytes 294920 | tf_op jit(solution)/shard_map/ppermute | solution.py:18
  167.5 9.2 %collective-permute-start.21 = (bf16[16,3072]{1,0:T(8,128)(2,1)S(1)}, bf16[16,3072]{1,0:T(8,128)(2,1)S(1)}, u32[]{:S(2)}, u32[]{:S(2)}) collective-permute-start(bf16[16,3072]{1,0:T(8,128)(2,1)S(1)} %get-tuple-element.75), channel_id=1, source_target_pairs={{0,12},{4,0},{8,4},{12,8},{1,13},{5,1},{9,5},{13,9},{2,14},{6,2},{... | collective-permute-start | bytes 294920 | tf_op jit(solution)/shard_map/ppermute | solution.py:18

commit v6 on v2

v6 whole, which is shorter than its diff:
```python
import jax
import jax.numpy as jnp
from jax import lax
from jax.experimental import pallas as pl
from jax.experimental.pallas import tpu as pltpu
from jax.sharding import Mesh
from jax.sharding import PartitionSpec as P

DEVICES = ("group", "x", "z", "h", "c")
ROW = ("x", "z")
COL = ("h", "c")
F32 = jnp.float32
BF16 = jnp.bfloat16


def shift(value, axis, by):
    n = lax.axis_size(axis)
    return lax.ppermute(value, axis, [(i, (i + by) % n) for i in range(n)])


def pick(value, index):
    return lax.dynamic_index_in_dim(value, index, 0, keepdims=False)


def rolled(value, starts):
    sizes = value.shape
    for axis in range(len(starts)):
        value = jnp.concatenate([value, value], axis=axis)
    starts = tuple(starts) + (0,) * (len(sizes) - len(starts))
    return lax.dynamic_slice(value, starts, sizes)


def gather_rows(columns):
    left = shift(columns, "x", 1)
    right = shift(columns, "x", -1)
    return left, right, (shift(left[0], "x", 1), shift(right[1], "x", -1))


def tile_of(cols):
    return min(cols, 512)


def sample_kernel(size_ref, place_ref, mine_ref, over_ref, left_ref, right_ref, front_ref, kept_ref, away_ref, total_ref):
    step = pl.program_id(0)
    rows = jnp.concatenate([mine_ref[0], over_ref[...], left_ref[0], right_ref[0]], axis=0)
    col = place_ref[1] + step * rows.shape[1] + lax.broadcasted_iota(jnp.int32, rows.shape, 1)
    rows = jnp.where(col < size_ref[0], rows, jnp.zeros((), BF16))
    part = lax.dot_general(rows, front_ref[0], (((1,), (1,)), ((), ())), preferred_element_type=F32)
    part = part.reshape(total_ref.shape)

    @pl.when(step == 0)
    def _():
        total_ref[...] = part

    @pl.when(step > 0)
    def _():
        total_ref[...] += part

    @pl.when(step == pl.num_programs(0) - 1)
    def _():
        row = place_ref[0] + lax.broadcasted_iota(jnp.int32, kept_ref.shape, 1)
        keep = row < size_ref[0]
        odd = place_ref[2]
        kept_ref[...] = jnp.where(keep, total_ref[odd], 0.0)
        away_ref[...] = jnp.where(keep, total_ref[1 - odd], 0.0).astype(BF16)


def sample_product(f, size, place, columns, over, left, right, fronts):
    _, rows, cols = fronts.shape
    count = columns.shape[1]
    tile = tile_of(cols)
    scalars = pl.BlockSpec(memory_space=pltpu.SMEM)
    of_front = pl.BlockSpec((1, count, tile), lambda j: (f, 0, j))
    half = pl.BlockSpec((2 * count, rows), lambda j: (0, 0))
    return pl.pallas_call(
        sample_kernel,
        grid=(cols // tile,),
        in_specs=[
            scalars,
            scalars,
            of_front,
            pl.BlockSpec((count, tile), lambda j: (0, j)),
            of_front,
            of_front,
            pl.BlockSpec((1, rows, tile), lambda j: (f, 0, j)),
        ],
        out_specs=[half, half],
        out_shape=[
            jax.ShapeDtypeStruct((2 * count, rows), F32),
            jax.ShapeDtypeStruct((2 * count, rows), BF16),
        ],
        scratch_shapes=[pltpu.VMEM((2, 2 * count, rows), F32)],
        compiler_params=pltpu.CompilerParams(vmem_limit_bytes=16 << 20),
    )(size, place, columns, over, left, right, pltpu.with_memory_space_constraint(fronts, pltpu.HBM))


def project_kernel(size_ref, place_ref, rows_ref, front_ref, right_ref, left_ref, rest_ref):
    first = place_ref[3]
    rows = jnp.concatenate([rows_ref[first, 0], rows_ref[1 - first, 0]], axis=0)
    product = jnp.dot(rows, front_ref[0], preferred_element_type=F32)
    col = place_ref[1] + pl.program_id(0) * product.shape[1] + lax.broadcasted_iota(jnp.int32, product.shape, 1)
    product = jnp.where(col < size_ref[0], product, 0.0).astype(BF16)
    half = right_ref.shape[0] // 2
    right_ref[...] = product[3 * half : 5 * half]
    left_ref[:half] = product[2 * half : 3 * half]
    left_ref[half:] = product[7 * half :]
    rest_ref[: 2 * half] = product[: 2 * half]
    rest_ref[2 * half :] = product[5 * half : 7 * half]


def project_product(f, size, place, everyone, fronts):
    _, rows, cols = fronts.shape
    count = everyone.shape[2]
    tile = tile_of(cols)
    scalars = pl.BlockSpec(memory_space=pltpu.SMEM)
    heights = (count // 2, count // 2, count)
    return pl.pallas_call(
        project_kernel,
        grid=(cols // tile,),
        in_specs=[
            scalars,
            scalars,
            pl.BlockSpec((2, 1, count, rows), lambda j: (0, f, 0, 0)),
            pl.BlockSpec((1, rows, tile), lambda j: (f, 0, j)),
        ],
        out_specs=[pl.BlockSpec((height, tile), lambda j: (0, j)) for height in heights],
        out_shape=[jax.ShapeDtypeStruct((height, cols), BF16) for height in heights],
        compiler_params=pltpu.CompilerParams(vmem_limit_bytes=16 << 20),
    )(size, place, everyone, pltpu.with_memory_space_constraint(fronts, pltpu.HBM))


def first_step(to_right, to_left):
    return lax.optimization_barrier((shift(to_right, "x", 1), shift(to_left, "x", -1)))


def second_pieces(rest, near):
    half = rest.shape[0] // 4
    from_left, from_right = near
    over_right = rest[2 * half : 3 * half].astype(F32) + from_left[:half].astype(F32)
    over_left = rest[3 * half :].astype(F32) + from_right[:half].astype(F32)
    return over_right.astype(BF16), over_left.astype(BF16)


def second_step(pieces):
    over_right, over_left = pieces
    return lax.optimization_barrier((shift(over_right, "x", 1), shift(over_left, "x", -1)))


def last_step(rest, near, far):
    half = rest.shape[0] // 4
    rows = half // 2
    (from_left, from_right), (over_right, over_left) = near, far
    top = rest[:half].astype(F32) + from_left[half:].astype(F32) + over_left.astype(F32)
    low = rest[half : 2 * half].astype(F32) + from_right[half:].astype(F32) + over_right.astype(F32)
    own = jnp.concatenate([top, low], axis=0)
    total = own[:rows]
    for k in (1, 2, 3):
        piece = own[k * rows : (k + 1) * rows].astype(BF16)
        total = total + shift(piece, "z", k).astype(F32)
    return total


def route_weight(parent_ids, block_maps, local):
    count, blocks = block_maps.shape
    order = (count // local, local, blocks)
    parent = jnp.broadcast_to(parent_ids[:, None], block_maps.shape).reshape(order)
    parent = parent.transpose(0, 2, 1).reshape(1, -1)
    block = block_maps.reshape(order).transpose(0, 2, 1).reshape(1, -1)
    index = lax.broadcasted_iota(jnp.int32, (count * blocks, 1), 0)
    to_parent = index // (blocks * local) * local + index % local
    to_block = index // local % blocks
    return ((parent == to_parent) & (block == to_block)).astype(BF16)


def shards(fronts, samples, second_samples, front_sizes, parent_ids, block_maps):
    local, tile_rows, tile_cols = fronts.shape
    own_rows = samples.shape[0]
    slab = second_samples.shape[0]
    group, x, z, h, c = (lax.axis_index(axis) for axis in DEVICES)
    row = lax.axis_index(ROW)
    col = lax.axis_index(COL)

    mine = jnp.stack([samples[:, f, :] for f in range(local)])
    columns = lax.all_gather(mine, "z", axis=1, tiled=True)
    left, right, over = gather_rows(columns)
    sizes = lax.dynamic_slice_in_dim(front_sizes, group * local, local, 0)
    second, _ = lax.optimization_barrier((second_samples, columns))
    second_of_pair = shift(second, "h", 1)
    odd = (x - c) & 1
    place = jnp.stack([row * tile_rows, col * tile_cols, odd, x & 1])
    weight = route_weight(parent_ids, block_maps, local)
    over_0, second_of_pair, weight = lax.optimization_barrier((over[0], second_of_pair, weight))
    over = (over_0, over[1])
    second = rolled(jnp.stack([second, second_of_pair]), (h,))

    halves = []
    for f in range(local):
        size = sizes[f : f + 1]
        kept, away = sample_product(f, size, place, columns, over[f], left, right, fronts)
        total = (kept + shift(away, "c", 1).astype(F32)).reshape(2, slab, tile_rows)
        halves.append(rolled(total, (((x - odd) & 3) >> 1,)))

    spread = ("h", "group") + ROW
    outgoing = jnp.stack([half.astype(BF16).reshape(2 * slab, tile_rows) for half in halves], axis=1)
    arrived = lax.all_to_all(outgoing, spread, split_axis=0, concat_axis=0, tiled=True)
    arrived = arrived[:slab].astype(F32) + arrived[slab:].astype(F32)
    arrived = arrived.astype(BF16).reshape(-1, tile_rows)
    extension = jnp.einsum("ij,jk->ik", weight, arrived, preferred_element_type=F32).astype(BF16)
    extension = extension.reshape(slab, local, tile_rows)
    extension = jnp.concatenate([extension, extension], axis=0)
    extension = lax.all_to_all(extension, spread, split_axis=0, concat_axis=0, tiled=True)
    combined = second.reshape(extension.shape).astype(F32) + extension.astype(F32)
    row_keep = row * tile_rows + lax.broadcasted_iota(jnp.int32, (local, tile_rows), 1) < sizes[:, None]
    combined = jnp.where(row_keep[None], combined, 0.0).astype(BF16)

    nearer = ((x + ((c - x) & 1)) & 3) >> 1
    ordered = []
    for f in range(local):
        mine = combined[:, f, :].reshape(2, -1, own_rows, tile_rows)
        ordered.append(rolled(mine, (nearer, z)).reshape(2 * slab, tile_rows))
    everyone = lax.all_gather(jnp.stack(ordered), "c", axis=0)
    right_0, left_0, rest_0 = project_product(0, sizes[:1], place, everyone, fronts)
    near_0 = first_step(right_0, left_0)
    everyone, right_0 = lax.optimization_barrier((everyone, right_0))
    right_1, left_1, rest_1 = project_product(1, sizes[1:], place, everyone, fronts)
    near_0, right_1, left_1 = lax.optimization_barrier((near_0, right_1, left_1))
    far_0 = second_step(second_pieces(rest_0, near_0))
    near_1 = first_step(right_1, left_1)
    away = jnp.stack([pick(half, 1 - h).astype(BF16) for half in halves])
    away, far_0 = lax.optimization_barrier((away, far_0))
    received = shift(away, "h", 1)
    total_0 = last_step(rest_0, near_0, far_0)
    far_1 = second_step(second_pieces(rest_1, near_1))
    received, far_1 = lax.optimization_barrier((received, far_1))
    slabs = [pick(half, h) + received[f].astype(F32) for f, half in enumerate(halves)]
    sampled = jnp.stack([total.astype(BF16) for total in slabs], axis=1)
    total_1 = last_step(rest_1, near_1, far_1)
    outs = [total_0.astype(BF16), total_1.astype(BF16)]
    return sampled, jnp.stack(outs, axis=1)


def solution(mesh):
    torus = Mesh(mesh.devices.reshape(mesh.shape["group"], 4, 4, 2, 2), DEVICES)
    in_specs = (P("group", ROW, COL), P(ROW, "group", COL), P(COL, "group", ROW), P(), P(), P())
    out_specs = (P(COL, "group", ROW), P(ROW, "group", COL))
    return jax.shard_map(
        shards, mesh=torus, in_specs=in_specs, out_specs=out_specs, check_vma=False
    )
```

time: 174 us -> 186 us (1.069)
  Pallas kernels: 3.47 us -> 24.2 us
  matrix products: 8.46 us -> 0.19 us
  waiting for transfers between devices: 59.3 us -> 51.8 us
  local copies, waits for them, and re-layouts: 10.3 us -> 12.5 us
  other arithmetic: 4.89 us -> 6.9 us
  blocking collectives: 50.5 us -> 52.5 us
    pallas_call x1 -> x4, Pallas kernels: 3.47 us -> 24.2 us  [the longest x2 12.5 us: sample_product(): pl.pallas_call(sample_kernel, grid=(cols // tile,), in_specs=[scalars, sc...]
    dot_general x4 -> x0, matrix products: 8.27 us -> none  [the longest x2 5.34 us: multiplied(): jnp.einsum('sm,mk->sk', ordered[f], masked[f], preferred_element_type=F32)]
    ppermute x22, waiting for transfers between devices: 43.2 us -> 35.5 us  [shift(): return lax.ppermute(value, axis, [(i, (i + by) % n) for i in range(n)])]
    unnamed x16 -> x6, local copies, waits for them, and re-layouts: 5.47 us -> 1.77 us
    all_to_all x1, blocking collectives: 29.4 us -> 31.5 us  [shards(): lax.all_to_all(outgoing, spread, split_axis=0, concat_axis=0, tiled=True)]
  transfers between devices with their start and end apart: 23 -> 23, of which waited for: 16 -> 14; matrix products, arithmetic and copies ran while one was open for 5% -> 7% of each run, Pallas kernels for 2% -> 10%
where the time goes in v6:
time: 186 us; the launch traced here: 185 us
  blocking collectives  52.5 us (28%)
  waiting for transfers between devices  51.8 us (28%)
  starting transfers between devices  36.3 us (20%)
  Pallas kernels  24.2 us (13%)
  local copies, waits for them, and re-layouts  12.5 us (7%)
  other arithmetic  6.9 us (4%)
    ppermute x22, waiting for transfers between devices, shift(): return lax.ppermute(value, axis, [(i, (i + by) % n) for i in range(n)])  35.5 us
    all_to_all x1, blocking collectives, shards(): lax.all_to_all(outgoing, spread, split_axis=0, concat_axis=0, tiled=True)  31.5 us
    ppermute x22, starting transfers between devices, shift(): return lax.ppermute(value, axis, [(i, (i + by) % n) for i in range(n)])  29.7 us
    all_gather x1, blocking collectives, shards(): columns = lax.all_gather(mine, 'z', axis=1, tiled=True)  18.6 us
    all_to_all x1, waiting for transfers between devices, shards(): lax.all_to_all(extension, spread, split_axis=0, concat_axis=0, tiled=True)  16.4 us
    pallas_call x2, Pallas kernels, sample_product(): pl.pallas_call(sample_kernel, grid=(cols // tile,), in_specs=[scalars, sc...  12.5 us
    pallas_call x2, Pallas kernels, project_product(): pl.pallas_call(project_kernel, grid=(cols // tile,), in_specs=[scalars, s...  11.7 us
    all_to_all x1, starting transfers between devices, shards(): lax.all_to_all(extension, spread, split_axis=0, concat_axis=0, tiled=True)  6.57 us
  transfers between devices with their start and end apart: 23, of which 14 were waited for; matrix products, arithmetic and copies ran while one was open for 7% of the time, Pallas kernels for 10%

profile of v6, /device:TPU:32, one launch (start us, length us, event | category | flops | bytes accessed | tf_op | source)
XLA Modules:
  0.0 185.4 jit_solution(1246712457722228847)
XLA Ops:
  0.6 1.4 fusion.42
  2.1 18.6 %all_gather.9.mine_ref = bf16[2,64,3072]{2,1,0:T(8,128)(2,1)S(1)} all-gather(bf16[2,16,3072]{2,1,0:T(8,128)(2,1)S(1)} %pad_maximum_fusion.3), channel_id=1, replica_groups=mesh['group'=4,'x'=4,'z'=4,'h'=2,'c'=2] {'z'}, dimensions={1}, use_global_device_ids=true | all-gather | bytes 983040 | tf_op jit(solution)/shard_map/all_gather | solution.py:184
  20.7 2.8 %collective-permute-start.3 = (bf16[2,64,3072]{2,1,0:T(8,128)(2,1)S(1)}, bf16[2,64,3072]{2,1,0:T(8,128)(2,1)S(1)}, u32[]{:S(2)}, u32[]{:S(2)}) collective-permute-start(bf16[2,64,3072]{2,1,0:T(8,128)(2,1)S(1)} %all_gather.9.mine_ref), channel_id=1, source_target_pairs={{0,48},{16,0},{32,16},{48,32},{1,49},{17,1},{33,17},{49,33},{2,50}... | collective-permute-start | bytes 2359304 | tf_op jit(solution)/shard_map/ppermute | solution.py:18
  23.5 0.9 copy.60
  24.5 4.7 %collective-permute-start.2 = (bf16[64,2,768]{2,0,1:T(8,128)(2,1)S(1)}, bf16[64,2,768]{2,0,1:T(8,128)(2,1)S(1)}, u32[]{:S(2)}, u32[]{:S(2)}) collective-permute-start(bf16[64,2,768]{2,0,1:T(8,128)(2,1)S(1)} %copy.60), channel_id=1, source_target_pairs={{0,2},{2,0},{1,3},{3,1},{4,6},{6,4},{5,7},{7,5},{8,10},{10,8},{9,1... | collective-permute-start | bytes 589832 | tf_op jit(solution)/shard_map/ppermute | solution.py:18
  29.2 0.6 and_select_fusion
  29.8 8.8 %collective-permute-done.3.right_ref = bf16[2,64,3072]{2,1,0:T(8,128)(2,1)S(1)} collective-permute-done((bf16[2,64,3072]{2,1,0:T(8,128)(2,1)S(1)}, bf16[2,64,3072]{2,1,0:T(8,128)(2,1)S(1)}, u32[]{:S(2)}, u32[]{:S(2)}) %collective-permute-start.3) | collective-permute-done | bytes 786464 | tf_op jit(solution)/shard_map/ppermute | solution.py:18
  38.6 0.8 slice_bitcast_fusion
  39.4 3.7 %collective-permute-start.5 = (bf16[64,3072]{1,0:T(8,128)(2,1)}, bf16[64,3072]{1,0:T(8,128)(2,1)S(1)}, u32[]{:S(2)}, u32[]{:S(2)}) collective-permute-start(bf16[64,3072]{1,0:T(8,128)(2,1)} %slice_bitcast_fusion), channel_id=1, source_target_pairs={{0,48},{16,0},{32,16},{48,32},{1,49},{17,1},{33,17},{49,33},{2,50}... | collective-permute-start | bytes 1179656 | tf_op jit(solution)/shard_map/ppermute | solution.py:18
  43.1 0.8 slice_bitcast_fusion.1
  43.9 0.7 broadcast_in_dim.20
  44.7 0.6 transpose.13
  45.3 0.9 eq.33
  46.2 1.4 copy.45
  47.6 0.9 eq.37
  48.5 0.7 dynamic_slice.39
  49.2 0.6 fusion.43
  49.8 6.3 %shard_map.78 = (f32[128,768]{1,0:T(8,128)S(1)}, bf16[128,768]{1,0:T(8,128)(2,1)S(1)}) custom-call(s32[1]{0:T(128)} %get-tuple-element.99.size_ref, s32[4]{0:T(128)S(1)} %pad_add_fusion.place_ref, bf16[2,64,3072]{2,1,0:T(8,128)(2,1)S(1)} %all_gather.9.mine_ref, bf16[64,3072]{1,0:T(8,128)(2,1)S(1)} %collective-permute-done.5.over_ref, ...), custom_call_target="tpu_custom_call" | custom-call | tf_op jit(solution)/shard_map/pallas_call | solution.py:75
  56.3 6.3 %shard_map.77 = (f32[128,768]{1,0:T(8,128)S(1)}, bf16[128,768]{1,0:T(8,128)(2,1)S(1)}) custom-call(s32[1]{0:T(128)} %get-tuple-element.98.size_ref, s32[4]{0:T(128)S(1)} %pad_add_fusion.place_ref, bf16[2,64,3072]{2,1,0:T(8,128)(2,1)S(1)} %all_gather.9.mine_ref, bf16[64,3072]{1,0:T(8,128)(2,1)S(1)} %collective-permute-done.1.over_ref, ...), custom_call_target="tpu_custom_call" | custom-call | tf_op jit(solution)/shard_map/pallas_call | solution.py:75
  62.6 0.6 collective-permute-start.4
  63.3 0.3 copy.49
  63.6 0.6 collective-permute-done.4
  64.4 0.3 copy.48
  64.7 0.9 pad_maximum_fusion
  65.6 31.5 %all_to_all.10 = bf16[128,2,768]{2,1,0:T(2,128)(2,1)S(1)} all-to-all(bf16[128,2,768]{2,1,0:T(2,128)(2,1)S(1)} %pad_maximum_fusion), channel_id=1, replica_groups=mesh['group'=4,'x'=4,'z'=4,'h'=2,'c'=2] {'h','group','x','z'}, dimensions={0} | all-to-all | bytes 786432 | tf_op jit(solution)/shard_map/all_to_all | solution.py:205
  97.1 0.2 add_convert_fusion.6
  97.4 0.2 convolution_convert_fusion
  97.7 1.3 pad_maximum_fusion.1
  98.9 6.6 %all-to-all-start.1 = ((bf16[128,2,768]{2,1,0:T(2,128)(2,1)}), bf16[128,2,768]{2,1,0:T(2,128)(2,1)S(1)}, u32[]{:S(2)}, u32[]{:S(2)}) async-start(bf16[128,2,768]{2,1,0:T(2,128)(2,1)} %pad_maximum_fusion.1), calls=%async_computation.1 | async-start | bytes 786432 | tf_op jit(solution)/shard_map/all_to_all | solution.py:211
  105.6 0.3 fusion.5
  106.0 16.4 %all-to-all-done.1 = bf16[128,2,768]{2,1,0:T(2,128)(2,1)S(1)} async-done(((bf16[128,2,768]{2,1,0:T(2,128)(2,1)}), bf16[128,2,768]{2,1,0:T(2,128)(2,1)S(1)}, u32[]{:S(2)}, u32[]{:S(2)}) %all-to-all-start.1) | async-done | bytes 393248 | tf_op jit(solution)/shard_map/all_to_all | solution.py:211
  122.5 0.2 fusion.14
  122.7 0.2 fusion.11
  122.9 2.4 %all-gather = bf16[4,128,768]{2,1,0:T(8,128)(2,1)S(1)} all-gather(bf16[2,128,768]{2,1,0:T(8,128)(2,1)S(1)} %pad_maximum_fusion.2), channel_id=2, replica_groups=mesh['group'=4,'x'=4,'z'=4,'h'=2,'c'=2] {'c'}, dimensions={0}, use_global_device_ids=true | all-gather | bytes 1179648 | tf_op jit(solution)/shard_map/all_gather | solution.py:221
  125.3 5.8 %shard_map.79 = (bf16[64,3072]{1,0:T(8,128)(2,1)S(1)}, bf16[64,3072]{1,0:T(8,128)(2,1)S(1)}, bf16[128,3072]{1,0:T(8,128)(2,1)S(1)}) custom-call(s32[1]{0:T(128)} %get-tuple-element.98.size_ref, s32[4]{0:T(128)S(1)} %pad_add_fusion.place_ref, bf16[2,2,128,768]{3,2,1,0:T(8,128)(2,1)S(1)} %bitcast.44, bf16[2,768,3072]{2,1,0:T(8,128)(2,1)} %front_ref.7), custom_call_target="tpu_custom_call" | custom-call | tf_op jit(solution)/shard_map/pallas_call | solution.py:117
  131.1 1.2 collective-permute-start.8
  132.3 0.9 collective-permute-start.7
  133.2 5.8 %shard_map.80 = (bf16[64,3072]{1,0:T(8,128)(2,1)S(1)}, bf16[64,3072]{1,0:T(8,128)(2,1)S(1)}, bf16[128,3072]{1,0:T(8,128)(2,1)S(1)}) custom-call(s32[1]{0:T(128)} %get-tuple-element.99.size_ref, s32[4]{0:T(128)S(1)} %pad_add_fusion.place_ref, bf16[2,2,128,768]{3,2,1,0:T(8,128)(2,1)S(1)} %bitcast.45, bf16[2,768,3072]{2,1,0:T(8,128)(2,1)} %front_ref.7), custom_call_target="tpu_custom_call" | custom-call | tf_op jit(solution)/shard_map/pallas_call | solution.py:117
  139.1 3.2 %collective-permute-done.8 = bf16[64,3072]{1,0:T(8,128)(2,1)S(1)} collective-permute-done((bf16[64,3072]{1,0:T(8,128)(2,1)S(1)}, bf16[64,3072]{1,0:T(8,128)(2,1)S(1)}, u32[]{:S(2)}, u32[]{:S(2)}) %collective-permute-start.8) | collective-permute-done | bytes 393248 | tf_op jit(solution)/shard_map/ppermute | solution.py:18
  142.3 2.1 %collective-permute-done.7 = bf16[64,3072]{1,0:T(8,128)(2,1)} collective-permute-done((bf16[64,3072]{1,0:T(8,128)(2,1)S(1)}, bf16[64,3072]{1,0:T(8,128)(2,1)}, u32[]{:S(2)}, u32[]{:S(2)}) %collective-permute-start.7) | collective-permute-done | bytes 393248 | tf_op jit(solution)/shard_map/ppermute | solution.py:18
  144.5 1.0 add_convert_fusion.4
  145.5 0.3 collective-permute-start.10
  145.8 1.8 collective-permute-start.9
  147.8 3.2 %collective-permute-start.13 = (bf16[64,3072]{1,0:T(8,128)(2,1)S(1)}, bf16[64,3072]{1,0:T(8,128)(2,1)S(1)}, u32[]{:S(2)}, u32[]{:S(2)}) collective-permute-start(bf16[64,3072]{1,0:T(8,128)(2,1)S(1)} %get-tuple-element.58), channel_id=1, source_target_pairs={{0,48},{16,0},{32,16},{48,32},{1,49},{17,1},{33,17},{49,33},{2,50}... | collective-permute-start | bytes 1179656 | tf_op jit(solution)/shard_map/ppermute | solution.py:18
  151.0 2.4 %collective-permute-done.10 = bf16[32,3072]{1,0:T(8,128)(2,1)S(1)} collective-permute-done((bf16[32,3072]{1,0:T(8,128)(2,1)S(1)}, bf16[32,3072]{1,0:T(8,128)(2,1)S(1)}, u32[]{:S(2)}, u32[]{:S(2)}) %collective-permute-start.10) | collective-permute-done | bytes 196640 | tf_op jit(solution)/shard_map/ppermute | solution.py:18
  153.4 1.4 collective-permute-done.9
  154.8 1.1 convert_add_fusion.1
  155.9 1.0 collective-permute-start.16
  156.9 3.0 %collective-permute-start.17 = (bf16[16,3072]{1,0:T(8,128)(2,1)S(1)}, bf16[16,3072]{1,0:T(8,128)(2,1)S(1)}, u32[]{:S(2)}, u32[]{:S(2)}) collective-permute-start(bf16[16,3072]{1,0:T(8,128)(2,1)S(1)} %get-tuple-element.88), channel_id=1, source_target_pairs={{0,8},{4,12},{8,0},{12,4},{1,9},{5,13},{9,1},{13,5},{2,10},{6,14},... | collective-permute-start | bytes 294920 | tf_op jit(solution)/shard_map/ppermute | solution.py:18
  160.0 1.3 collective-permute-done.12
  161.2 1.7 collective-permute-start.11
  163.1 2.0 %collective-permute-start.14 = (bf16[32,3072]{1,0:T(8,128)(2,1)S(1)}, bf16[32,3072]{1,0:T(8,128)(2,1)S(1)}, u32[]{:S(2)}, u32[]{:S(2)}) collective-permute-start(bf16[32,3072]{1,0:T(8,128)(2,1)S(1)} %get-tuple-element.83), channel_id=1, source_target_pairs={{0,16},{16,32},{32,48},{48,0},{1,17},{17,33},{33,49},{49,1},{2,18}... | collective-permute-start | bytes 589832 | tf_op jit(solution)/shard_map/ppermute | solution.py:18
  165.1 4.3 %collective-permute-done.17 = bf16[16,3072]{1,0:T(8,128)(2,1)S(1)} collective-permute-done((bf16[16,3072]{1,0:T(8,128)(2,1)S(1)}, bf16[16,3072]{1,0:T(8,128)(2,1)S(1)}, u32[]{:S(2)}, u32[]{:S(2)}) %collective-permute-start.17) | collective-permute-done | bytes 98336 | tf_op jit(solution)/shard_map/ppermute | solution.py:18
  169.5 1.7 collective-permute-done.18
  171.2 3.1 %collective-permute-done.11 = bf16[2,64,768]{2,1,0:T(8,128)(2,1)S(1)} collective-permute-done((bf16[2,64,768]{2,1,0:T(8,128)(2,1)S(1)}, bf16[2,64,768]{2,1,0:T(8,128)(2,1)S(1)}, u32[]{:S(2)}, u32[]{:S(2)}) %collective-permute-start.11) | collective-permute-done | bytes 196640 | tf_op jit(solution)/shard_map/ppermute | solution.py:18
  174.3 0.1 convert_add_fusion
  174.5 0.9 collective-permute-start.19
  175.4 1.2 collective-permute-start.20
  176.7 0.3 collective-permute-start.21
  177.1 0.9 copy.51
  178.0 2.2 %collective-permute-done.19 = bf16[16,3072]{1,0:T(8,128)(2,1)S(1)} collective-permute-done((bf16[16,3072]{1,0:T(8,128)(2,1)S(1)}, bf16[16,3072]{1,0:T(8,128)(2,1)S(1)}, u32[]{:S(2)}, u32[]{:S(2)}) %collective-permute-start.19) | collective-permute-done | bytes 98336 | tf_op jit(solution)/shard_map/ppermute | solution.py:18
  180.2 2.2 %collective-permute-done.20 = bf16[16,3072]{1,0:T(8,128)(2,1)S(1)} collective-permute-done((bf16[16,3072]{1,0:T(8,128)(2,1)S(1)}, bf16[16,3072]{1,0:T(8,128)(2,1)S(1)}, u32[]{:S(2)}, u32[]{:S(2)}) %collective-permute-start.20) | collective-permute-done | bytes 98336 | tf_op jit(solution)/shard_map/ppermute | solution.py:18
  182.4 2.0 %collective-permute-done.21 = bf16[16,3072]{1,0:T(8,128)(2,1)S(1)} collective-permute-done((bf16[16,3072]{1,0:T(8,128)(2,1)S(1)}, bf16[16,3072]{1,0:T(8,128)(2,1)S(1)}, u32[]{:S(2)}, u32[]{:S(2)}) %collective-permute-start.21) | collective-permute-done | bytes 98336 | tf_op jit(solution)/shard_map/ppermute | solution.py:18
  184.5 0.9 copy.52
  (48 shorter events, 1.7 us)
Async XLA Ops:
  20.7 17.9 %collective-permute-start.3 = (bf16[2,64,3072]{2,1,0:T(8,128)(2,1)S(1)}, bf16[2,64,3072]{2,1,0:T(8,128)(2,1)S(1)}, u32[]{:S(2)}, u32[]{:S(2)}) collective-permute-start(bf16[2,64,3072]{2,1,0:T(8,128)(2,1)S(1)} %all_gather.9.mine_ref), channel_id=1, source_target_pairs={{0,48},{16,0},{32,16},{48,32},{1,49},{17,1},{33,17},{49,33},{2,50}... | collective-permute-start | bytes 2359304 | tf_op jit(solution)/shard_map/ppermute | solution.py:18
  23.5 19.5 %collective-permute-start = (bf16[2,64,3072]{2,1,0:T(8,128)(2,1)S(1)}, bf16[2,64,3072]{2,1,0:T(8,128)(2,1)S(1)}, u32[]{:S(2)}, u32[]{:S(2)}) collective-permute-start(bf16[2,64,3072]{2,1,0:T(8,128)(2,1)S(1)} %all_gather.9.mine_ref), channel_id=1, source_target_pairs={{0,16},{16,32},{32,48},{48,0},{1,17},{17,33},{33,49},{49,1},{2,18}... | collective-permute-start | bytes 2359304 | tf_op jit(solution)/shard_map/ppermute | solution.py:18
  24.5 31.8 %collective-permute-start.2 = (bf16[64,2,768]{2,0,1:T(8,128)(2,1)S(1)}, bf16[64,2,768]{2,0,1:T(8,128)(2,1)S(1)}, u32[]{:S(2)}, u32[]{:S(2)}) collective-permute-start(bf16[64,2,768]{2,0,1:T(8,128)(2,1)S(1)} %copy.60), channel_id=1, source_target_pairs={{0,2},{2,0},{1,3},{3,1},{4,6},{6,4},{5,7},{7,5},{8,10},{10,8},{9,1... | collective-permute-start | bytes 589832 | tf_op jit(solution)/shard_map/ppermute | solution.py:18
  39.4 10.4 %collective-permute-start.5 = (bf16[64,3072]{1,0:T(8,128)(2,1)}, bf16[64,3072]{1,0:T(8,128)(2,1)S(1)}, u32[]{:S(2)}, u32[]{:S(2)}) collective-permute-start(bf16[64,3072]{1,0:T(8,128)(2,1)} %slice_bitcast_fusion), channel_id=1, source_target_pairs={{0,48},{16,0},{32,16},{48,32},{1,49},{17,1},{33,17},{49,33},{2,50}... | collective-permute-start | bytes 1179656 | tf_op jit(solution)/shard_map/ppermute | solution.py:18
  43.8 12.5 %collective-permute-start.1 = (bf16[64,3072]{1,0:T(8,128)(2,1)}, bf16[64,3072]{1,0:T(8,128)(2,1)S(1)}, u32[]{:S(2)}, u32[]{:S(2)}) collective-permute-start(bf16[64,3072]{1,0:T(8,128)(2,1)} %slice_bitcast_fusion.1), channel_id=1, source_target_pairs={{0,16},{16,32},{32,48},{48,0},{1,17},{17,33},{33,49},{49,1},{2,18}... | collective-permute-start | bytes 1179656 | tf_op jit(solution)/shard_map/ppermute | solution.py:18
  48.5 7.7 %copy-start = (s32[128]{0:T(128)S(1)}, s32[128]{0:T(128)}, u32[]{:S(2)}) copy-start(s32[128]{0:T(128)} %get-tuple-element.100) | copy-start | bytes 1540
  48.5 7.7 %copy-start.1 = (s32[128]{0:T(128)S(1)}, s32[128]{0:T(128)}, u32[]{:S(2)}) copy-start(s32[128]{0:T(128)} %get-tuple-element.101) | copy-start | bytes 1540
  56.1 7.1 %collective-permute-start.6 = (bf16[128,768]{1,0:T(8,128)(2,1)S(1)}, bf16[128,768]{1,0:T(8,128)(2,1)S(1)}, u32[]{:S(2)}, u32[]{:S(2)}) collective-permute-start(bf16[128,768]{1,0:T(8,128)(2,1)S(1)} %get-tuple-element.40), channel_id=1, source_target_pairs={{0,1},{1,0},{2,3},{3,2},{4,5},{5,4},{6,7},{7,6},{8,9},{9,8},{10,11... | collective-permute-start | bytes 589832 | tf_op jit(solution)/shard_map/ppermute | solution.py:18
  62.6 1.7 collective-permute-start.4
  98.9 23.4 %all-to-all-start.1 = ((bf16[128,2,768]{2,1,0:T(2,128)(2,1)}), bf16[128,2,768]{2,1,0:T(2,128)(2,1)S(1)}, u32[]{:S(2)}, u32[]{:S(2)}) async-start(bf16[128,2,768]{2,1,0:T(2,128)(2,1)} %pad_maximum_fusion.1), calls=%async_computation.1 | async-start | bytes 786432 | tf_op jit(solution)/shard_map/all_to_all | solution.py:211
  131.1 11.2 %collective-permute-start.8 = (bf16[64,3072]{1,0:T(8,128)(2,1)S(1)}, bf16[64,3072]{1,0:T(8,128)(2,1)S(1)}, u32[]{:S(2)}, u32[]{:S(2)}) collective-permute-start(bf16[64,3072]{1,0:T(8,128)(2,1)S(1)} %get-tuple-element.45), channel_id=1, source_target_pairs={{0,48},{16,0},{32,16},{48,32},{1,49},{17,1},{33,17},{49,33},{2,50}... | collective-permute-start | bytes 1179656 | tf_op jit(solution)/shard_map/ppermute | solution.py:18
  132.3 12.2 %collective-permute-start.7 = (bf16[64,3072]{1,0:T(8,128)(2,1)S(1)}, bf16[64,3072]{1,0:T(8,128)(2,1)}, u32[]{:S(2)}, u32[]{:S(2)}) collective-permute-start(bf16[64,3072]{1,0:T(8,128)(2,1)S(1)} %get-tuple-element.44), channel_id=1, source_target_pairs={{0,16},{16,32},{32,48},{48,0},{1,17},{17,33},{33,49},{49,1},{2,18}... | collective-permute-start | bytes 1179656 | tf_op jit(solution)/shard_map/ppermute | solution.py:18
  145.5 7.9 %collective-permute-start.10 = (bf16[32,3072]{1,0:T(8,128)(2,1)S(1)}, bf16[32,3072]{1,0:T(8,128)(2,1)S(1)}, u32[]{:S(2)}, u32[]{:S(2)}) collective-permute-start(bf16[32,3072]{1,0:T(8,128)(2,1)S(1)} %get-tuple-element.84), channel_id=1, source_target_pairs={{0,48},{16,0},{32,16},{48,32},{1,49},{17,1},{33,17},{49,33},{2,50}... | collective-permute-start | bytes 589832 | tf_op jit(solution)/shard_map/ppermute | solution.py:18
  145.8 9.0 %collective-permute-start.9 = (bf16[32,3072]{1,0:T(8,128)(2,1)S(1)}, bf16[32,3072]{1,0:T(8,128)(2,1)S(1)}, u32[]{:S(2)}, u32[]{:S(2)}) collective-permute-start(bf16[32,3072]{1,0:T(8,128)(2,1)S(1)} %get-tuple-element.85), channel_id=1, source_target_pairs={{0,16},{16,32},{32,48},{48,0},{1,17},{17,33},{33,49},{49,1},{2,18}... | collective-permute-start | bytes 589832 | tf_op jit(solution)/shard_map/ppermute | solution.py:18
  147.7 13.6 %collective-permute-start.12 = (bf16[64,3072]{1,0:T(8,128)(2,1)S(1)}, bf16[64,3072]{1,0:T(8,128)(2,1)S(1)}, u32[]{:S(2)}, u32[]{:S(2)}) collective-permute-start(bf16[64,3072]{1,0:T(8,128)(2,1)S(1)} %get-tuple-element.57), channel_id=1, source_target_pairs={{0,16},{16,32},{32,48},{48,0},{1,17},{17,33},{33,49},{49,1},{2,18}... | collective-permute-start | bytes 1179656 | tf_op jit(solution)/shard_map/ppermute | solution.py:18
  147.8 15.2 %collective-permute-start.13 = (bf16[64,3072]{1,0:T(8,128)(2,1)S(1)}, bf16[64,3072]{1,0:T(8,128)(2,1)S(1)}, u32[]{:S(2)}, u32[]{:S(2)}) collective-permute-start(bf16[64,3072]{1,0:T(8,128)(2,1)S(1)} %get-tuple-element.58), channel_id=1, source_target_pairs={{0,48},{16,0},{32,16},{48,32},{1,49},{17,1},{33,17},{49,33},{2,50}... | collective-permute-start | bytes 1179656 | tf_op jit(solution)/shard_map/ppermute | solution.py:18
  155.9 7.2 %collective-permute-start.16 = (bf16[16,3072]{1,0:T(8,128)(2,1)S(1)}, bf16[16,3072]{1,0:T(8,128)(2,1)S(1)}, u32[]{:S(2)}, u32[]{:S(2)}) collective-permute-start(bf16[16,3072]{1,0:T(8,128)(2,1)S(1)} %slice.213), channel_id=1, source_target_pairs={{0,4},{4,8},{8,12},{12,0},{1,5},{5,9},{9,13},{13,1},{2,6},{6,10},{... | collective-permute-start | bytes 294920 | tf_op jit(solution)/shard_map/ppermute | solution.py:18
  156.9 12.6 %collective-permute-start.17 = (bf16[16,3072]{1,0:T(8,128)(2,1)S(1)}, bf16[16,3072]{1,0:T(8,128)(2,1)S(1)}, u32[]{:S(2)}, u32[]{:S(2)}) collective-permute-start(bf16[16,3072]{1,0:T(8,128)(2,1)S(1)} %get-tuple-element.88), channel_id=1, source_target_pairs={{0,8},{4,12},{8,0},{12,4},{1,9},{5,13},{9,1},{13,5},{2,10},{6,14},... | collective-permute-start | bytes 294920 | tf_op jit(solution)/shard_map/ppermute | solution.py:18
  159.9 11.2 %collective-permute-start.18 = (bf16[16,3072]{1,0:T(8,128)(2,1)S(1)}, bf16[16,3072]{1,0:T(8,128)(2,1)S(1)}, u32[]{:S(2)}, u32[]{:S(2)}) collective-permute-start(bf16[16,3072]{1,0:T(8,128)(2,1)S(1)} %get-tuple-element.89), channel_id=1, source_target_pairs={{0,12},{4,0},{8,4},{12,8},{1,13},{5,1},{9,5},{13,9},{2,14},{6,2},{... | collective-permute-start | bytes 294920 | tf_op jit(solution)/shard_map/ppermute | solution.py:18
  161.2 13.1 %collective-permute-start.11 = (bf16[2,64,768]{2,1,0:T(8,128)(2,1)S(1)}, bf16[2,64,768]{2,1,0:T(8,128)(2,1)S(1)}, u32[]{:S(2)}, u32[]{:S(2)}) collective-permute-start(bf16[2,64,768]{2,1,0:T(8,128)(2,1)S(1)} %pad_maximum_fusion.4), channel_id=1, source_target_pairs={{0,2},{2,0},{1,3},{3,1},{4,6},{6,4},{5,7},{7,5},{8,10},{10,8},{9,1... | collective-permute-start | bytes 589832 | tf_op jit(solution)/shard_map/ppermute | solution.py:18
  163.0 8.2 %collective-permute-start.15 = (bf16[32,3072]{1,0:T(8,128)(2,1)S(1)}, bf16[32,3072]{1,0:T(8,128)(2,1)S(1)}, u32[]{:S(2)}, u32[]{:S(2)}) collective-permute-start(bf16[32,3072]{1,0:T(8,128)(2,1)S(1)} %get-tuple-element.82), channel_id=1, source_target_pairs={{0,48},{16,0},{32,16},{48,32},{1,49},{17,1},{33,17},{49,33},{2,50}... | collective-permute-start | bytes 589832 | tf_op jit(solution)/shard_map/ppermute | solution.py:18
  163.1 8.1 %collective-permute-start.14 = (bf16[32,3072]{1,0:T(8,128)(2,1)S(1)}, bf16[32,3072]{1,0:T(8,128)(2,1)S(1)}, u32[]{:S(2)}, u32[]{:S(2)}) collective-permute-start(bf16[32,3072]{1,0:T(8,128)(2,1)S(1)} %get-tuple-element.83), channel_id=1, source_target_pairs={{0,16},{16,32},{32,48},{48,0},{1,17},{17,33},{33,49},{49,1},{2,18}... | collective-permute-start | bytes 589832 | tf_op jit(solution)/shard_map/ppermute | solution.py:18
  174.5 5.7 %collective-permute-start.19 = (bf16[16,3072]{1,0:T(8,128)(2,1)S(1)}, bf16[16,3072]{1,0:T(8,128)(2,1)S(1)}, u32[]{:S(2)}, u32[]{:S(2)}) collective-permute-start(bf16[16,3072]{1,0:T(8,128)(2,1)S(1)} %slice.212), channel_id=1, source_target_pairs={{0,4},{4,8},{8,12},{12,0},{1,5},{5,9},{9,13},{13,1},{2,6},{6,10},{... | collective-permute-start | bytes 294920 | tf_op jit(solution)/shard_map/ppermute | solution.py:18
  175.4 7.0 %collective-permute-start.20 = (bf16[16,3072]{1,0:T(8,128)(2,1)S(1)}, bf16[16,3072]{1,0:T(8,128)(2,1)S(1)}, u32[]{:S(2)}, u32[]{:S(2)}) collective-permute-start(bf16[16,3072]{1,0:T(8,128)(2,1)S(1)} %get-tuple-element.90), channel_id=1, source_target_pairs={{0,8},{4,12},{8,0},{12,4},{1,9},{5,13},{9,1},{13,5},{2,10},{6,14},... | collective-permute-start | bytes 294920 | tf_op jit(solution)/shard_map/ppermute | solution.py:18
  176.7 7.8 %collective-permute-start.21 = (bf16[16,3072]{1,0:T(8,128)(2,1)S(1)}, bf16[16,3072]{1,0:T(8,128)(2,1)S(1)}, u32[]{:S(2)}, u32[]{:S(2)}) collective-permute-start(bf16[16,3072]{1,0:T(8,128)(2,1)S(1)} %get-tuple-element.91), channel_id=1, source_target_pairs={{0,12},{4,0},{8,4},{12,8},{1,13},{5,1},{9,5},{13,9},{2,14},{6,2},{... | collective-permute-start | bytes 294920 | tf_op jit(solution)/shard_map/ppermute | solution.py:18

commit v7 on v2

--- a/solution.py
+++ b/solution.py
@@ -75,35 +75,41 @@
     return to_right, to_left
 
 
-def first_step(pieces):
-    to_right, to_left = pieces
-    return lax.optimization_barrier((shift(to_right, "x", 1), shift(to_left, "x", -1)))
-
-
-def second_step(product, near):
+def first_step(products):
+    pieces = [first_pieces(product) for product in products]
+    to_right = jnp.concatenate([piece[0] for piece in pieces], axis=0)
+    to_left = jnp.concatenate([piece[1] for piece in pieces], axis=0)
+    return shift(to_right, "x", 1), shift(to_left, "x", -1)
+
+
+def second_pieces(product, near):
     block = product.shape[0] // 4
     half = block // 2
     from_left, from_right = near
     over_right = product[2 * block + half : 3 * block].astype(F32) + from_left[:half].astype(F32)
     over_left = product[3 * block : 3 * block + half].astype(F32) + from_right[:half].astype(F32)
-    over_right = shift(over_right.astype(BF16), "x", 1)
-    over_left = shift(over_left.astype(BF16), "x", -1)
-    return lax.optimization_barrier((over_right, over_left))
-
-
-def last_step(product, near, far):
+    return over_right.astype(BF16), over_left.astype(BF16)
+
+
+def second_step(pieces):
+    over_right, over_left = pieces
+    return lax.optimization_barrier((shift(over_right, "x", 1), shift(over_left, "x", -1)))
+
+
+def own_rows_of(product, near, far):
     block = product.shape[0] // 4
     half = block // 2
-    rows = block // 4
     (from_left, from_right), (over_right, over_left) = near, far
     top = product[:half].astype(F32) + from_left[half:].astype(F32) + over_left.astype(F32)
     low = product[half:block].astype(F32) + from_right[half:].astype(F32) + over_right.astype(F32)
-    own = jnp.concatenate([top, low], axis=0)
-    total = own[:rows]
-    for k in (1, 2, 3):
-        piece = own[k * rows : (k + 1) * rows].astype(BF16)
-        total = total + shift(piece, "z", k).astype(F32)
-    return total
+    own = jnp.concatenate([top, low], axis=0).reshape(4, -1, product.shape[1])
+    return own[0], [own[k].astype(BF16) for k in (1, 2, 3)]
+
+
+def last_step(own, pieces):
+    for k, piece in enumerate(pieces):
+        own = own + shift(piece, "z", k + 1).astype(F32)
+    return own
 
 
 def route_weight(parent_ids, block_maps, local):
@@ -134,7 +140,10 @@
     second_of_pair = shift(second, "h", 1)
     masked = masked_fronts(fronts, sizes, jnp.stack([row * tile_rows, col * tile_cols]))
     weight = route_weight(parent_ids, block_maps, local)
-    gathered[0], second_of_pair, weight = lax.optimization_barrier((gathered[0], second_of_pair, weight))
+    first = jnp.broadcast_to(h == 0, (1, tile_rows))
+    gathered[0], second_of_pair, weight, first = lax.optimization_barrier(
+        (gathered[0], second_of_pair, weight, first)
+    )
     second = rolled(jnp.stack([second, second_of_pair]), (h,))
 
     halves = []
@@ -166,22 +175,26 @@
         product = jnp.einsum("sm,mk->sk", ordered[f], masked[f], preferred_element_type=F32)
         return product.astype(BF16)
 
-    product_0 = multiplied(0)
-    near_0 = first_step(first_pieces(product_0))
-    product_1 = multiplied(1)
-    pieces_1 = first_pieces(product_1)
-    near_0, product_1, pieces_1 = lax.optimization_barrier((near_0, product_1, pieces_1))
-    far_0 = second_step(product_0, near_0)
-    near_1 = first_step(pieces_1)
-    away = jnp.stack([pick(half, 1 - h).astype(BF16) for half in halves])
-    away, far_0 = lax.optimization_barrier((away, far_0))
+    products = [multiplied(f) for f in range(local)]
+    products[0], *halves = lax.optimization_barrier((products[0], *halves))
+    from_left, from_right = first_step(products)
+    away = jnp.stack([jnp.where(first, half[1], half[0]).astype(BF16) for half in halves])
+    away, _ = lax.optimization_barrier((away, products[1]))
     received = shift(away, "h", 1)
-    total_0 = last_step(product_0, near_0, far_0)
-    far_1 = second_step(product_1, near_1)
-    received, far_1 = lax.optimization_barrier((received, far_1))
-    slabs = [pick(half, h) + received[f].astype(F32) for f, half in enumerate(halves)]
+    from_left, from_right, received = lax.optimization_barrier((from_left, from_right, received))
+    near = [(from_left[f * slab : (f + 1) * slab], from_right[f * slab : (f + 1) * slab]) for f in range(local)]
+    far_0 = second_step(second_pieces(products[0], near[0]))
+    passed_1 = second_pieces(products[1], near[1])
+    far_1 = second_step(passed_1)
+    far_0, _ = lax.optimization_barrier((far_0, passed_1))
+    own_0, pieces_0 = own_rows_of(products[0], near[0], far_0)
+    far_1, _ = lax.optimization_barrier((far_1, pieces_0))
+    own_1, pieces_1 = own_rows_of(products[1], near[1], far_1)
+    total_0 = last_step(own_0, pieces_0)
+    received, _ = lax.optimization_barrier((received, pieces_1))
+    slabs = [jnp.where(first, half[0], half[1]) + received[f].astype(F32) for f, half in enumerate(halves)]
     sampled = jnp.stack([total.astype(BF16) for total in slabs], axis=1)
-    total_1 = last_step(product_1, near_1, far_1)
+    total_1 = last_step(own_1, pieces_1)
     outs = [total_0.astype(BF16), total_1.astype(BF16)]
     return sampled, jnp.stack(outs, axis=1)
 

time: 174 us -> 176 us (1.011); the launches traced: 174 us -> 173 us
  other arithmetic: 4.89 us -> 8.95 us
  waiting for transfers between devices: 59.3 us -> 56.6 us
    ppermute x22 -> x20, waiting for transfers between devices: 43.2 us -> 40.5 us  [shift(): return lax.ppermute(value, axis, [(i, (i + by) % n) for i in range(n)])]
    another operation x1 -> x3, other arithmetic: 0.02 us -> 2.15 us  [shards(): away = jnp.stack([pick(half, 1 - h).astype(BF16) for half in halves])]
    concatenate x2, other arithmetic: 0.06 us -> 1.91 us  [the longest x1 0.96 us: first_step(): to_right = jnp.concatenate([piece[0] for piece in pieces], axis=0)]
    ppermute x22 -> x20, starting transfers between devices: 29.5 us -> 28.6 us  [shift(): return lax.ppermute(value, axis, [(i, (i + by) % n) for i in range(n)])]
    unnamed x16 -> x28, local copies, waits for them, and re-layouts: 5.47 us -> 5.9 us
  transfers between devices with their start and end apart: 23 -> 21, of which waited for: 16 -> 11; matrix products, arithmetic and copies ran while one was open for 5% -> 5% of each run, Pallas kernels for 2% -> 2%
where the time goes in v7:
time: 176 us; the launch traced here: 173 us
  waiting for transfers between devices  56.6 us (32%)
  blocking collectives  50.5 us (29%)
  starting transfers between devices  35.1 us (20%)
  local copies, waits for them, and re-layouts  8.99 us (5%)
  other arithmetic  8.95 us (5%)
  matrix products  8.48 us (5%)
  Pallas kernels  3.47 us (2%)
    ppermute x20, waiting for transfers between devices, shift(): return lax.ppermute(value, axis, [(i, (i + by) % n) for i in range(n)])  40.5 us
    all_to_all x1, blocking collectives, shards(): lax.all_to_all(outgoing, spread, split_axis=0, concat_axis=0, tiled=True)  29.4 us
    ppermute x20, starting transfers between devices, shift(): return lax.ppermute(value, axis, [(i, (i + by) % n) for i in range(n)])  28.6 us
    all_gather x1, blocking collectives, shards(): columns = lax.all_gather(mine, 'z', axis=1, tiled=True)  18.6 us
    all_to_all x1, waiting for transfers between devices, shards(): lax.all_to_all(extension, spread, split_axis=0, concat_axis=0, tiled=True)  16.1 us
    all_to_all x1, starting transfers between devices, shards(): lax.all_to_all(extension, spread, split_axis=0, concat_axis=0, tiled=True)  6.54 us
    unnamed x28, local copies, waits for them, and re-layouts  5.9 us
    dot_general x2, matrix products, multiplied(): jnp.einsum('sm,mk->sk', ordered[f], masked[f], preferred_element_type=F32)  5.35 us
  transfers between devices with their start and end apart: 21, of which 11 were waited for; matrix products, arithmetic and copies ran while one was open for 5% of the time, Pallas kernels for 2%

profile of v7, /device:TPU:32, one launch (start us, length us, event | category | flops | bytes accessed | tf_op | source)
XLA Modules:
  0.0 173.3 jit_solution(4784991132168220790)
XLA Ops:
  0.7 1.4 fusion.56
  2.2 18.6 %all_gather.9 = bf16[2,64,3072]{2,1,0:T(8,128)(2,1)S(1)} all-gather(bf16[2,16,3072]{2,1,0:T(8,128)(2,1)S(1)} %pad_maximum_fusion.6), channel_id=1, replica_groups=mesh['group'=4,'x'=4,'z'=4,'h'=2,'c'=2] {'z'}, dimensions={1}, use_global_device_ids=true | all-gather | bytes 983040 | tf_op jit(solution)/shard_map/all_gather | solution.py:136
  20.8 2.8 %collective-permute-start.2 = (bf16[2,64,3072]{2,1,0:T(8,128)(2,1)S(1)}, bf16[2,64,3072]{2,1,0:T(8,128)(2,1)S(1)}, u32[]{:S(2)}, u32[]{:S(2)}) collective-permute-start(bf16[2,64,3072]{2,1,0:T(8,128)(2,1)S(1)} %all_gather.9), channel_id=1, source_target_pairs={{0,48},{16,0},{32,16},{48,32},{1,49},{17,1},{33,17},{49,33},{2,50}... | collective-permute-start | bytes 2359304 | tf_op jit(solution)/shard_map/ppermute | solution.py:18
  23.7 4.7 %collective-permute-start.3 = (bf16[64,2,768]{2,0,1:T(8,128)(2,1)S(1)}, bf16[64,2,768]{2,0,1:T(8,128)(2,1)S(1)}, u32[]{:S(2)}, u32[]{:S(2)}) collective-permute-start(bf16[64,2,768]{2,0,1:T(8,128)(2,1)S(1)} %copy.66), channel_id=1, source_target_pairs={{0,2},{2,0},{1,3},{3,1},{4,6},{6,4},{5,7},{7,5},{8,10},{10,8},{9,1... | collective-permute-start | bytes 589832 | tf_op jit(solution)/shard_map/ppermute | solution.py:18
  28.5 0.1 broadcast_in_dim.28
  28.6 0.1 eq.36
  28.7 0.1 copy.52
  28.8 0.1 eq.40
  29.0 0.1 and_convert_fusion
  29.2 3.7 %copy-done = bf16[2,768,3072]{2,1,0:T(8,128)(2,1)S(1)} copy-done((bf16[2,768,3072]{2,1,0:T(8,128)(2,1)S(1)}, bf16[2,768,3072]{2,1,0:T(8,128)(2,1)}, u32[]{:S(2)}) %copy-start) | copy-done | bytes 9437208
  32.9 3.5 %shard_map.77 = bf16[2,768,3072]{2,1,0:T(8,128)(2,1)S(1)} custom-call(s32[2]{0:T(128)S(1)} %dynamic_slice.37.sizes_ref, s32[2]{0:T(128)S(1)} %pad_add_fusion.origin_ref, bf16[2,768,3072]{2,1,0:T(8,128)(2,1)S(1)} %copy-done), custom_call_target="tpu_custom_call" | custom-call | tf_op jit(solution)/shard_map/pallas_call | solution.py:53
  36.4 5.7 %collective-permute-done = bf16[2,64,3072]{2,1,0:T(8,128)(2,1)S(1)} collective-permute-done((bf16[2,64,3072]{2,1,0:T(8,128)(2,1)S(1)}, bf16[2,64,3072]{2,1,0:T(8,128)(2,1)S(1)}, u32[]{:S(2)}, u32[]{:S(2)}) %collective-permute-start) | collective-permute-done | bytes 786464 | tf_op jit(solution)/shard_map/ppermute | solution.py:18
  42.1 0.1 collective-permute-start.1
  42.3 3.3 %collective-permute-start.5 = (bf16[64,3072]{1,0:T(8,128)(2,1)S(1)}, bf16[64,3072]{1,0:T(8,128)(2,1)S(1)}, u32[]{:S(2)}, u32[]{:S(2)}) collective-permute-start(bf16[64,3072]{1,0:T(8,128)(2,1)S(1)} %get-tuple-element.82), channel_id=1, source_target_pairs={{0,48},{16,0},{32,16},{48,32},{1,49},{17,1},{33,17},{49,33},{2,50}... | collective-permute-start | bytes 1179656 | tf_op jit(solution)/shard_map/ppermute | solution.py:18
  45.6 5.7 %collective-permute-done.1 = bf16[64,3072]{1,0:T(8,128)(2,1)S(1)} collective-permute-done((bf16[64,3072]{1,0:T(8,128)(2,1)S(1)}, bf16[64,3072]{1,0:T(8,128)(2,1)S(1)}, u32[]{:S(2)}, u32[]{:S(2)}) %collective-permute-start.1) | collective-permute-done | bytes 393248 | tf_op jit(solution)/shard_map/ppermute | solution.py:18
  51.3 0.1 pad_maximum_fusion
  51.5 1.5 fusion.16
  53.0 0.1 collective-permute-start.4
  53.1 1.5 fusion.13
  54.6 0.6 collective-permute-start.6
  55.2 0.1 fusion.46
  55.3 0.9 collective-permute-done.6
  56.3 0.1 fusion.48
  56.4 0.4 copy.55
  56.9 29.4 %all_to_all.10 = bf16[128,2,768]{2,1,0:T(2,128)(2,1)S(1)} all-to-all(bf16[128,2,768]{2,1,0:T(2,128)(2,1)S(1)} %copy.55), channel_id=1, replica_groups=mesh['group'=4,'x'=4,'z'=4,'h'=2,'c'=2] {'h','group','x','z'}, dimensions={0} | all-to-all | bytes 786432 | tf_op jit(solution)/shard_map/all_to_all | solution.py:156
  86.2 0.2 add_convert_fusion.6
  86.5 0.2 convolution_convert_fusion
  86.8 1.3 pad_maximum_fusion.4
  88.1 6.5 %all-to-all-start.1 = ((bf16[128,2,768]{2,1,0:T(2,128)(2,1)}), bf16[128,2,768]{2,1,0:T(2,128)(2,1)S(1)}, u32[]{:S(2)}, u32[]{:S(2)}) async-start(bf16[128,2,768]{2,1,0:T(2,128)(2,1)} %pad_maximum_fusion.4), calls=%async_computation.1 | async-start | bytes 786432 | tf_op jit(solution)/shard_map/all_to_all | solution.py:162
  94.7 0.3 fusion.25
  95.1 16.1 %all-to-all-done.1 = bf16[128,2,768]{2,1,0:T(2,128)(2,1)S(1)} async-done(((bf16[128,2,768]{2,1,0:T(2,128)(2,1)}), bf16[128,2,768]{2,1,0:T(2,128)(2,1)S(1)}, u32[]{:S(2)}, u32[]{:S(2)}) %all-to-all-start.1) | async-done | bytes 393248 | tf_op jit(solution)/shard_map/all_to_all | solution.py:162
  111.3 0.2 fusion.30
  111.5 0.2 fusion.27
  111.7 2.5 %all-gather = bf16[4,128,768]{2,1,0:T(8,128)(2,1)S(1)} all-gather(bf16[2,128,768]{2,1,0:T(8,128)(2,1)S(1)} %pad_maximum_fusion.5), channel_id=2, replica_groups=mesh['group'=4,'x'=4,'z'=4,'h'=2,'c'=2] {'c'}, dimensions={0}, use_global_device_ids=true | all-gather | bytes 1179648 | tf_op jit(solution)/shard_map/all_gather | solution.py:171
  114.3 0.2 fusion.19
  114.4 3.9 %fusion.5 = bf16[256,3072]{1,0:T(8,128)(2,1)S(1)} fusion(bf16[256,768]{1,0:T(8,128)(2,1)S(1)} %bitcast.111, bf16[2,768,3072]{2,1,0:T(8,128)(2,1)} %copy-done.1), kind=kOutput, calls=%fused_computation.7 | convolution fusion | flops 1208745984 | bytes 6684672 | tf_op jit(solution)/shard_map/sm,mk->sk/dot_general | solution.py:175
  118.4 0.2 fusion.18
  118.6 1.4 fusion.4
  120.2 0.9 pad_maximum_fusion.2
  121.1 0.4 copy-done.2
  121.5 1.1 collective-permute-start.8
  122.6 1.0 pad_maximum_fusion.1
  123.6 0.9 collective-permute-start.7
  124.6 1.1 collective-permute-start.9
  125.7 12.7 %collective-permute-done.9 = bf16[2,64,768]{2,1,0:T(8,128)(2,1)S(1)} collective-permute-done((bf16[2,64,768]{2,1,0:T(8,128)(2,1)S(1)}, bf16[2,64,768]{2,1,0:T(8,128)(2,1)S(1)}, u32[]{:S(2)}, u32[]{:S(2)}) %collective-permute-start.9) | collective-permute-done | bytes 196640 | tf_op jit(solution)/shard_map/ppermute | solution.py:18
  138.4 3.0 %collective-permute-done.8 = bf16[128,3072]{1,0:T(8,128)(2,1)} collective-permute-done((bf16[128,3072]{1,0:T(8,128)(2,1)}, bf16[128,3072]{1,0:T(8,128)(2,1)}, u32[]{:S(2)}, u32[]{:S(2)}) %collective-permute-start.8) | collective-permute-done | bytes 786464 | tf_op jit(solution)/shard_map/ppermute | solution.py:18
  141.4 2.9 %collective-permute-done.7 = bf16[128,3072]{1,0:T(8,128)(2,1)S(1)} collective-permute-done((bf16[128,3072]{1,0:T(8,128)(2,1)}, bf16[128,3072]{1,0:T(8,128)(2,1)S(1)}, u32[]{:S(2)}, u32[]{:S(2)}) %collective-permute-start.7) | collective-permute-done | bytes 786464 | tf_op jit(solution)/shard_map/ppermute | solution.py:18
  144.3 1.4 add_convert_fusion.4
  145.7 0.1 collective-permute-start.12
  145.8 3.2 %collective-permute-start.13 = (bf16[32,3072]{1,0:T(8,128)(2,1)S(1)}, bf16[32,3072]{1,0:T(8,128)(2,1)S(1)}, u32[]{:S(2)}, u32[]{:S(2)}) collective-permute-start(bf16[32,3072]{1,0:T(8,128)(2,1)S(1)} %get-tuple-element.71), channel_id=1, source_target_pairs={{0,48},{16,0},{32,16},{48,32},{1,49},{17,1},{33,17},{49,33},{2,50}... | collective-permute-start | bytes 589832 | tf_op jit(solution)/shard_map/ppermute | solution.py:18
  149.1 2.0 %collective-permute-start.10 = (bf16[32,3072]{1,0:T(8,128)(2,1)S(1)}, bf16[32,3072]{1,0:T(8,128)(2,1)S(1)}, u32[]{:S(2)}, u32[]{:S(2)}) collective-permute-start(bf16[32,3072]{1,0:T(8,128)(2,1)S(1)} %get-tuple-element.69), channel_id=1, source_target_pairs={{0,16},{16,32},{32,48},{48,0},{1,17},{17,33},{33,49},{49,1},{2,18}... | collective-permute-start | bytes 589832 | tf_op jit(solution)/shard_map/ppermute | solution.py:18
  151.1 3.3 %collective-permute-done.12 = bf16[32,3072]{1,0:T(8,128)(2,1)S(1)} collective-permute-done((bf16[32,3072]{1,0:T(8,128)(2,1)S(1)}, bf16[32,3072]{1,0:T(8,128)(2,1)S(1)}, u32[]{:S(2)}, u32[]{:S(2)}) %collective-permute-start.12) | collective-permute-done | bytes 196640 | tf_op jit(solution)/shard_map/ppermute | solution.py:18
  154.4 1.1 add_convert_fusion.1
  155.5 1.0 collective-permute-start.14
  156.4 1.1 collective-permute-start.16
  157.6 1.9 %collective-permute-start.15 = (bf16[16,3072]{1,0:T(8,128)(2,1)S(1)}, bf16[16,3072]{1,0:T(8,128)(2,1)S(1)}, u32[]{:S(2)}, u32[]{:S(2)}) collective-permute-start(bf16[16,3072]{1,0:T(8,128)(2,1)S(1)} %get-tuple-element.91), channel_id=1, source_target_pairs={{0,8},{4,12},{8,0},{12,4},{1,9},{5,13},{9,1},{13,5},{2,10},{6,14},... | collective-permute-start | bytes 294920 | tf_op jit(solution)/shard_map/ppermute | solution.py:18
  159.4 1.1 add_convert_fusion
  160.6 3.0 %collective-permute-start.17 = (bf16[16,3072]{1,0:T(8,128)(2,1)S(1)}, bf16[16,3072]{1,0:T(8,128)(2,1)S(1)}, u32[]{:S(2)}, u32[]{:S(2)}) collective-permute-start(bf16[16,3072]{1,0:T(8,128)(2,1)S(1)} %slice.349), channel_id=1, source_target_pairs={{0,4},{4,8},{8,12},{12,0},{1,5},{5,9},{9,13},{13,1},{2,6},{6,10},{... | collective-permute-start | bytes 294920 | tf_op jit(solution)/shard_map/ppermute | solution.py:18
  163.6 0.9 copy.57
  164.5 1.6 collective-permute-start.18
  166.1 1.1 collective-permute-done.15
  167.2 3.3 %collective-permute-done.17 = bf16[16,3072]{1,0:T(8,128)(2,1)S(1)} collective-permute-done((bf16[16,3072]{1,0:T(8,128)(2,1)S(1)}, bf16[16,3072]{1,0:T(8,128)(2,1)S(1)}, u32[]{:S(2)}, u32[]{:S(2)}) %collective-permute-start.17) | collective-permute-done | bytes 98336 | tf_op jit(solution)/shard_map/ppermute | solution.py:18
  170.6 1.8 %collective-permute-done.19 = bf16[16,3072]{1,0:T(8,128)(2,1)S(1)} collective-permute-done((bf16[16,3072]{1,0:T(8,128)(2,1)S(1)}, bf16[16,3072]{1,0:T(8,128)(2,1)S(1)}, u32[]{:S(2)}, u32[]{:S(2)}) %collective-permute-start.19) | collective-permute-done | bytes 98336 | tf_op jit(solution)/shard_map/ppermute | solution.py:18
  172.4 0.9 copy.58
  (78 shorter events, 1.5 us)
Async XLA Ops:
  0.6 23.0 %copy-start.9 = (s32[8]{0:T(128)S(1)}, s32[8]{0:T(128)}, u32[]{:S(2)}) copy-start(s32[8]{0:T(128)} %param.9) | copy-start | bytes 100
  0.6 23.1 %copy-start.6 = (bf16[64,2,768]{2,1,0:T(2,128)(2,1)S(1)}, bf16[64,2,768]{2,1,0:T(2,128)(2,1)}, u32[]{:S(2)}) copy-start(bf16[64,2,768]{2,1,0:T(2,128)(2,1)} %param.8) | copy-start | bytes 589828
  0.7 27.8 %copy-start.8 = (s32[8]{0:T(128)S(1)}, s32[8]{0:T(128)}, u32[]{:S(2)}) copy-start(s32[8]{0:T(128)} %param.10) | copy-start | bytes 100
  0.7 28.0 %copy-start.7 = (s32[8,16]{1,0:T(8,128)S(1)}, s32[8,16]{1,0:T(8,128)}, u32[]{:S(2)}) copy-start(s32[8,16]{1,0:T(8,128)} %param.11) | copy-start | bytes 1540
  20.8 21.4 %collective-permute-start.2 = (bf16[2,64,3072]{2,1,0:T(8,128)(2,1)S(1)}, bf16[2,64,3072]{2,1,0:T(8,128)(2,1)S(1)}, u32[]{:S(2)}, u32[]{:S(2)}) collective-permute-start(bf16[2,64,3072]{2,1,0:T(8,128)(2,1)S(1)} %all_gather.9), channel_id=1, source_target_pairs={{0,48},{16,0},{32,16},{48,32},{1,49},{17,1},{33,17},{49,33},{2,50}... | collective-permute-start | bytes 2359304 | tf_op jit(solution)/shard_map/ppermute | solution.py:18
  23.6 18.5 %collective-permute-start = (bf16[2,64,3072]{2,1,0:T(8,128)(2,1)S(1)}, bf16[2,64,3072]{2,1,0:T(8,128)(2,1)S(1)}, u32[]{:S(2)}, u32[]{:S(2)}) collective-permute-start(bf16[2,64,3072]{2,1,0:T(8,128)(2,1)S(1)} %all_gather.9), channel_id=1, source_target_pairs={{0,16},{16,32},{32,48},{48,0},{1,17},{17,33},{33,49},{49,1},{2,18}... | collective-permute-start | bytes 2359304 | tf_op jit(solution)/shard_map/ppermute | solution.py:18
  23.7 27.7 %collective-permute-start.3 = (bf16[64,2,768]{2,0,1:T(8,128)(2,1)S(1)}, bf16[64,2,768]{2,0,1:T(8,128)(2,1)S(1)}, u32[]{:S(2)}, u32[]{:S(2)}) collective-permute-start(bf16[64,2,768]{2,0,1:T(8,128)(2,1)S(1)} %copy.66), channel_id=1, source_target_pairs={{0,2},{2,0},{1,3},{3,1},{4,6},{6,4},{5,7},{7,5},{8,10},{10,8},{9,1... | collective-permute-start | bytes 589832 | tf_op jit(solution)/shard_map/ppermute | solution.py:18
  29.2 3.7 %copy-start = (bf16[2,768,3072]{2,1,0:T(8,128)(2,1)S(1)}, bf16[2,768,3072]{2,1,0:T(8,128)(2,1)}, u32[]{:S(2)}) copy-start(bf16[2,768,3072]{2,1,0:T(8,128)(2,1)} %fronts_ref.1) | copy-start | bytes 28311556
  36.4 16.7 %copy-start.1 = (bf16[2,768,3072]{2,1,0:T(8,128)(2,1)}, bf16[2,768,3072]{2,1,0:T(8,128)(2,1)S(1)}, u32[]{:S(2)}) copy-start(bf16[2,768,3072]{2,1,0:T(8,128)(2,1)S(1)} %shard_map.77) | copy-start | bytes 28311556
  42.1 9.2 %collective-permute-start.1 = (bf16[64,3072]{1,0:T(8,128)(2,1)S(1)}, bf16[64,3072]{1,0:T(8,128)(2,1)S(1)}, u32[]{:S(2)}, u32[]{:S(2)}) collective-permute-start(bf16[64,3072]{1,0:T(8,128)(2,1)S(1)} %get-tuple-element.81), channel_id=1, source_target_pairs={{0,16},{16,32},{32,48},{48,0},{1,17},{17,33},{33,49},{49,1},{2,18}... | collective-permute-start | bytes 1179656 | tf_op jit(solution)/shard_map/ppermute | solution.py:18
  42.3 10.8 %collective-permute-start.5 = (bf16[64,3072]{1,0:T(8,128)(2,1)S(1)}, bf16[64,3072]{1,0:T(8,128)(2,1)S(1)}, u32[]{:S(2)}, u32[]{:S(2)}) collective-permute-start(bf16[64,3072]{1,0:T(8,128)(2,1)S(1)} %get-tuple-element.82), channel_id=1, source_target_pairs={{0,48},{16,0},{32,16},{48,32},{1,49},{17,1},{33,17},{49,33},{2,50}... | collective-permute-start | bytes 1179656 | tf_op jit(solution)/shard_map/ppermute | solution.py:18
  53.0 2.2 %collective-permute-start.4 = (bf16[2,64,768]{2,1,0:T(8,128)(2,1)S(1)}, bf16[2,64,768]{2,1,0:T(8,128)(2,1)S(1)}, u32[]{:S(2)}, u32[]{:S(2)}) collective-permute-start(bf16[2,64,768]{2,1,0:T(8,128)(2,1)S(1)} %dynamic-slice_bitcast_fusion.1), channel_id=1, source_target_pairs={{0,1},{1,0},{2,3},{3,2},{4,5},{5,4},{6,7},{7,6},{8,9},{9,8},{10,11... | collective-permute-start | bytes 589832 | tf_op jit(solution)/shard_map/ppermute | solution.py:18
  54.6 1.6 collective-permute-start.6
  88.1 30.5 %slice-start = ((s8[9437184]{0:T(1024)(128)(4,1)}), s8[1048576]{0:T(1024)(128)(4,1)S(1)}, s32[]{:S(2)}) async-start(s8[9437184]{0:T(1024)(128)(4,1)} %bitcast.96), calls=%async_computation.2 | async-start | bytes 2097152
  88.1 23.1 %all-to-all-start.1 = ((bf16[128,2,768]{2,1,0:T(2,128)(2,1)}), bf16[128,2,768]{2,1,0:T(2,128)(2,1)S(1)}, u32[]{:S(2)}, u32[]{:S(2)}) async-start(bf16[128,2,768]{2,1,0:T(2,128)(2,1)} %pad_maximum_fusion.4), calls=%async_computation.1 | async-start | bytes 786432 | tf_op jit(solution)/shard_map/all_to_all | solution.py:162
  111.7 6.9 %slice-start.1 = ((s8[9437184]{0:T(1024)(128)(4,1)}), s8[4194304]{0:T(1024)(128)(4,1)S(1)}, s32[]{:S(2)}) async-start(s8[9437184]{0:T(1024)(128)(4,1)} %bitcast.96), calls=%async_computation.3 | async-start | bytes 8388608
  114.4 4.2 %slice-start.2 = ((s8[9437184]{0:T(1024)(128)(4,1)}), s8[4194304]{0:T(1024)(128)(4,1)S(1)}, s32[]{:S(2)}) async-start(s8[9437184]{0:T(1024)(128)(4,1)} %bitcast.96), calls=%async_computation.4 | async-start | bytes 8388608
  118.4 1.7 copy-start.4
  120.1 1.4 copy-start.2
  120.1 2.5 %slice-start.3 = ((bf16[256,3072]{1,0:T(8,128)(2,1)}), bf16[64,3072]{1,0:T(8,128)(2,1)S(1)}, s32[]{:S(2)}) async-start(bf16[256,3072]{1,0:T(8,128)(2,1)} %copy-done.4), calls=%async_computation.5 | async-start | bytes 786432 | tf_op jit(solution)/shard_map/slice | solution.py:73
  121.5 19.9 %collective-permute-start.8 = (bf16[128,3072]{1,0:T(8,128)(2,1)}, bf16[128,3072]{1,0:T(8,128)(2,1)}, u32[]{:S(2)}, u32[]{:S(2)}) collective-permute-start(bf16[128,3072]{1,0:T(8,128)(2,1)} %pad_maximum_fusion.2), channel_id=1, source_target_pairs={{0,48},{16,0},{32,16},{48,32},{1,49},{17,1},{33,17},{49,33},{2,50}... | collective-permute-start | bytes 2359304 | tf_op jit(solution)/shard_map/ppermute | solution.py:18
  122.6 21.7 %copy-start.3 = (bf16[256,3072]{1,0:T(8,128)(2,1)S(1)}, bf16[256,3072]{1,0:T(8,128)(2,1)}, u32[]{:S(2)}) copy-start(bf16[256,3072]{1,0:T(8,128)(2,1)} %copy-done.2) | copy-start | bytes 4718596
  123.6 20.7 %collective-permute-start.7 = (bf16[128,3072]{1,0:T(8,128)(2,1)}, bf16[128,3072]{1,0:T(8,128)(2,1)S(1)}, u32[]{:S(2)}, u32[]{:S(2)}) collective-permute-start(bf16[128,3072]{1,0:T(8,128)(2,1)} %pad_maximum_fusion.1), channel_id=1, source_target_pairs={{0,16},{16,32},{32,48},{48,0},{1,17},{17,33},{33,49},{49,1},{2,18}... | collective-permute-start | bytes 2359304 | tf_op jit(solution)/shard_map/ppermute | solution.py:18
  124.5 29.8 %copy-start.5 = (bf16[256,3072]{1,0:T(8,128)(2,1)S(1)}, bf16[256,3072]{1,0:T(8,128)(2,1)}, u32[]{:S(2)}) copy-start(bf16[256,3072]{1,0:T(8,128)(2,1)} %copy-done.4) | copy-start | bytes 4718596
  124.6 13.8 %collective-permute-start.9 = (bf16[2,64,768]{2,1,0:T(8,128)(2,1)S(1)}, bf16[2,64,768]{2,1,0:T(8,128)(2,1)S(1)}, u32[]{:S(2)}, u32[]{:S(2)}) collective-permute-start(bf16[2,64,768]{2,1,0:T(8,128)(2,1)S(1)} %pad_maximum_fusion.7), channel_id=1, source_target_pairs={{0,2},{2,0},{1,3},{3,1},{4,6},{6,4},{5,7},{7,5},{8,10},{10,8},{9,1... | collective-permute-start | bytes 589832 | tf_op jit(solution)/shard_map/ppermute | solution.py:18
  145.7 8.6 %collective-permute-start.12 = (bf16[32,3072]{1,0:T(8,128)(2,1)S(1)}, bf16[32,3072]{1,0:T(8,128)(2,1)S(1)}, u32[]{:S(2)}, u32[]{:S(2)}) collective-permute-start(bf16[32,3072]{1,0:T(8,128)(2,1)S(1)} %get-tuple-element.70), channel_id=1, source_target_pairs={{0,16},{16,32},{32,48},{48,0},{1,17},{17,33},{33,49},{49,1},{2,18}... | collective-permute-start | bytes 589832 | tf_op jit(solution)/shard_map/ppermute | solution.py:18
  145.8 8.5 %collective-permute-start.13 = (bf16[32,3072]{1,0:T(8,128)(2,1)S(1)}, bf16[32,3072]{1,0:T(8,128)(2,1)S(1)}, u32[]{:S(2)}, u32[]{:S(2)}) collective-permute-start(bf16[32,3072]{1,0:T(8,128)(2,1)S(1)} %get-tuple-element.71), channel_id=1, source_target_pairs={{0,48},{16,0},{32,16},{48,32},{1,49},{17,1},{33,17},{49,33},{2,50}... | collective-permute-start | bytes 589832 | tf_op jit(solution)/shard_map/ppermute | solution.py:18
  149.0 10.4 %collective-permute-start.11 = (bf16[32,3072]{1,0:T(8,128)(2,1)S(1)}, bf16[32,3072]{1,0:T(8,128)(2,1)S(1)}, u32[]{:S(2)}, u32[]{:S(2)}) collective-permute-start(bf16[32,3072]{1,0:T(8,128)(2,1)S(1)} %get-tuple-element.68), channel_id=1, source_target_pairs={{0,48},{16,0},{32,16},{48,32},{1,49},{17,1},{33,17},{49,33},{2,50}... | collective-permute-start | bytes 589832 | tf_op jit(solution)/shard_map/ppermute | solution.py:18
  149.1 10.4 %collective-permute-start.10 = (bf16[32,3072]{1,0:T(8,128)(2,1)S(1)}, bf16[32,3072]{1,0:T(8,128)(2,1)S(1)}, u32[]{:S(2)}, u32[]{:S(2)}) collective-permute-start(bf16[32,3072]{1,0:T(8,128)(2,1)S(1)} %get-tuple-element.69), channel_id=1, source_target_pairs={{0,16},{16,32},{32,48},{48,0},{1,17},{17,33},{33,49},{49,1},{2,18}... | collective-permute-start | bytes 589832 | tf_op jit(solution)/shard_map/ppermute | solution.py:18
  155.5 9.1 %collective-permute-start.14 = (bf16[16,3072]{1,0:T(8,128)(2,1)S(1)}, bf16[16,3072]{1,0:T(8,128)(2,1)S(1)}, u32[]{:S(2)}, u32[]{:S(2)}) collective-permute-start(bf16[16,3072]{1,0:T(8,128)(2,1)S(1)} %slice.350), channel_id=1, source_target_pairs={{0,4},{4,8},{8,12},{12,0},{1,5},{5,9},{9,13},{13,1},{2,6},{6,10},{... | collective-permute-start | bytes 294920 | tf_op jit(solution)/shard_map/ppermute | solution.py:18
  156.4 9.6 %collective-permute-start.16 = (bf16[16,3072]{1,0:T(8,128)(2,1)S(1)}, bf16[16,3072]{1,0:T(8,128)(2,1)S(1)}, u32[]{:S(2)}, u32[]{:S(2)}) collective-permute-start(bf16[16,3072]{1,0:T(8,128)(2,1)S(1)} %get-tuple-element.90), channel_id=1, source_target_pairs={{0,12},{4,0},{8,4},{12,8},{1,13},{5,1},{9,5},{13,9},{2,14},{6,2},{... | collective-permute-start | bytes 294920 | tf_op jit(solution)/shard_map/ppermute | solution.py:18
  157.6 9.6 %collective-permute-start.15 = (bf16[16,3072]{1,0:T(8,128)(2,1)S(1)}, bf16[16,3072]{1,0:T(8,128)(2,1)S(1)}, u32[]{:S(2)}, u32[]{:S(2)}) collective-permute-start(bf16[16,3072]{1,0:T(8,128)(2,1)S(1)} %get-tuple-element.91), channel_id=1, source_target_pairs={{0,8},{4,12},{8,0},{12,4},{1,9},{5,13},{9,1},{13,5},{2,10},{6,14},... | collective-permute-start | bytes 294920 | tf_op jit(solution)/shard_map/ppermute | solution.py:18
  160.6 10.0 %collective-permute-start.17 = (bf16[16,3072]{1,0:T(8,128)(2,1)S(1)}, bf16[16,3072]{1,0:T(8,128)(2,1)S(1)}, u32[]{:S(2)}, u32[]{:S(2)}) collective-permute-start(bf16[16,3072]{1,0:T(8,128)(2,1)S(1)} %slice.349), channel_id=1, source_target_pairs={{0,4},{4,8},{8,12},{12,0},{1,5},{5,9},{9,13},{13,1},{2,6},{6,10},{... | collective-permute-start | bytes 294920 | tf_op jit(solution)/shard_map/ppermute | solution.py:18
  163.6 8.8 %collective-permute-start.19 = (bf16[16,3072]{1,0:T(8,128)(2,1)S(1)}, bf16[16,3072]{1,0:T(8,128)(2,1)S(1)}, u32[]{:S(2)}, u32[]{:S(2)}) collective-permute-start(bf16[16,3072]{1,0:T(8,128)(2,1)S(1)} %get-tuple-element.88), channel_id=1, source_target_pairs={{0,12},{4,0},{8,4},{12,8},{1,13},{5,1},{9,5},{13,9},{2,14},{6,2},{... | collective-permute-start | bytes 294920 | tf_op jit(solution)/shard_map/ppermute | solution.py:18
  164.5 7.8 %collective-permute-start.18 = (bf16[16,3072]{1,0:T(8,128)(2,1)S(1)}, bf16[16,3072]{1,0:T(8,128)(2,1)S(1)}, u32[]{:S(2)}, u32[]{:S(2)}) collective-permute-start(bf16[16,3072]{1,0:T(8,128)(2,1)S(1)} %get-tuple-element.89), channel_id=1, source_target_pairs={{0,8},{4,12},{8,0},{12,4},{1,9},{5,13},{9,1},{13,5},{2,10},{6,14},... | collective-permute-start | bytes 294920 | tf_op jit(solution)/shard_map/ppermute | solution.py:18

commit v8 on v5

--- a/solution.py
+++ b/solution.py
@@ -137,7 +137,10 @@
     second_of_pair = shift(second, "h", 1)
     masked = masked_fronts(fronts, sizes, jnp.stack([row * tile_rows, col * tile_cols]))
     weight = route_weight(parent_ids, block_maps, local)
-    gathered[0], second_of_pair, weight = lax.optimization_barrier((gathered[0], second_of_pair, weight))
+    first = jnp.broadcast_to(h == 0, (1, tile_rows))
+    gathered[0], second_of_pair, weight, first = lax.optimization_barrier(
+        (gathered[0], second_of_pair, weight, first)
+    )
     second = rolled(jnp.stack([second, second_of_pair]), (h,))
 
     halves = []
@@ -145,17 +148,15 @@
         partial = jnp.einsum("sk,mk->sm", gathered[f], masked[f], preferred_element_type=F32)
         halves.append(reduce_core(partial.astype(BF16).reshape(2, 2, slab, tile_rows), x, c))
 
-    away = jnp.stack([pick(half, 1 - h).astype(BF16) for half in halves])
-    received = shift(away, "h", 1)
-    slabs = [pick(half, h) + received[f].astype(F32) for f, half in enumerate(halves)]
-    sampled = jnp.stack([total.astype(BF16) for total in slabs], axis=1)
-    spread = ("group",) + ROW
-    arrived = lax.all_to_all(sampled, spread, split_axis=0, concat_axis=0, tiled=True)
-    arrived = arrived.reshape(-1, tile_rows)
+    spread = ("h", "group") + ROW
+    outgoing = jnp.stack([half.astype(BF16).reshape(2 * slab, tile_rows) for half in halves], axis=1)
+    arrived = lax.all_to_all(outgoing, spread, split_axis=0, concat_axis=0, tiled=True)
+    arrived = arrived[:slab].astype(F32) + arrived[slab:].astype(F32)
+    arrived = arrived.astype(BF16).reshape(-1, tile_rows)
     extension = jnp.einsum("ij,jk->ik", weight, arrived, preferred_element_type=F32).astype(BF16)
     extension = extension.reshape(slab, local, tile_rows)
     extension = jnp.concatenate([extension, extension], axis=0)
-    extension = lax.all_to_all(extension, ("h",) + spread, split_axis=0, concat_axis=0, tiled=True)
+    extension = lax.all_to_all(extension, spread, split_axis=0, concat_axis=0, tiled=True)
     combined = second.reshape(extension.shape).astype(F32) + extension.astype(F32)
     combined = combined.astype(BF16)
 
@@ -172,14 +173,29 @@
         return product.astype(BF16)
 
     product_0 = multiplied(0)
-    near_0 = first_step(first_pieces(product_0))
+    product_0, *halves = lax.optimization_barrier((product_0, *halves))
+    pieces_0 = first_pieces(product_0)
+    near_0 = first_step(pieces_0)
+    ordered[1], _ = lax.optimization_barrier((ordered[1], pieces_0))
     product_1 = multiplied(1)
     pieces_1 = first_pieces(product_1)
-    near_0, product_1, pieces_1 = lax.optimization_barrier((near_0, product_1, pieces_1))
+    away = [jnp.where(first, half[1], half[0]).astype(BF16) for half in halves]
+    away[0], _ = lax.optimization_barrier((away[0], pieces_0))
+    received_0 = shift(away[0], "h", 1)
+    near_0, product_1, pieces_1, received_0 = lax.optimization_barrier((near_0, product_1, pieces_1, received_0))
     far_0 = second_step(second_pieces(product_0, near_0))
     near_1 = first_step(pieces_1)
     total_0 = last_step(product_0, near_0, far_0)
-    far_1 = second_step(second_pieces(product_1, near_1))
+    passed_1 = second_pieces(product_1, near_1)
+    far_1 = second_step(passed_1)
+    away[1], _ = lax.optimization_barrier((away[1], passed_1))
+    received_1 = shift(away[1], "h", 1)
+    received_1, far_1 = lax.optimization_barrier((received_1, far_1))
+    slabs = [
+        jnp.where(first, half[0], half[1]) + received.astype(F32)
+        for half, received in zip(halves, (received_0, received_1))
+    ]
+    sampled = jnp.stack([total.astype(BF16) for total in slabs], axis=1)
     total_1 = last_step(product_1, near_1, far_1)
     outs = [total_0.astype(BF16), total_1.astype(BF16)]
     return sampled, jnp.stack(outs, axis=1)

time: 178 us -> 172 us (0.966)
  waiting for transfers between devices: 65.9 us -> 53.8 us
  blocking collectives: 43.3 us -> 50.5 us
  starting transfers between devices: 42.8 us -> 38.5 us
    ppermute x22 -> x23, waiting for transfers between devices: 50.5 us -> 37.7 us  [shift(): return lax.ppermute(value, axis, [(i, (i + by) % n) for i in range(n)])]
    all_to_all x1, blocking collectives: 22.2 us -> 29.4 us  [shards(): lax.all_to_all(outgoing, spread, split_axis=0, concat_axis=0, tiled=True)]
    all_to_all x1, starting transfers between devices: 9.06 us -> 6.4 us  [shards(): lax.all_to_all(extension, spread, split_axis=0, concat_axis=0, tiled=True)]
    ppermute x22 -> x23, starting transfers between devices: 33.7 us -> 32.1 us  [shift(): return lax.ppermute(value, axis, [(i, (i + by) % n) for i in range(n)])]
    unnamed x18 -> x16, local copies, waits for them, and re-layouts: 4.8 us -> 5.47 us
  transfers between devices with their start and end apart: 23 -> 24, of which waited for: 15 -> 16; matrix products, arithmetic and copies ran while one was open for 4% -> 5% of each run, Pallas kernels for 2% -> 2%
where the time goes in v8:
time: 172 us; the launch traced here: 171 us
  waiting for transfers between devices  53.8 us (31%)
  blocking collectives  50.5 us (29%)
  starting transfers between devices  38.5 us (22%)
  local copies, waits for them, and re-layouts  10.3 us (6%)
  matrix products  8.47 us (5%)
  other arithmetic  4.87 us (3%)
  Pallas kernels  3.47 us (2%)
    ppermute x23, waiting for transfers between devices, shift(): return lax.ppermute(value, axis, [(i, (i + by) % n) for i in range(n)])  37.7 us
    ppermute x23, starting transfers between devices, shift(): return lax.ppermute(value, axis, [(i, (i + by) % n) for i in range(n)])  32.1 us
    all_to_all x1, blocking collectives, shards(): lax.all_to_all(outgoing, spread, split_axis=0, concat_axis=0, tiled=True)  29.4 us
    all_gather x1, blocking collectives, shards(): columns = lax.all_gather(mine, 'z', axis=1, tiled=True)  18.6 us
    all_to_all x1, waiting for transfers between devices, shards(): lax.all_to_all(extension, spread, split_axis=0, concat_axis=0, tiled=True)  16.1 us
    all_to_all x1, starting transfers between devices, shards(): lax.all_to_all(extension, spread, split_axis=0, concat_axis=0, tiled=True)  6.4 us
    unnamed x16, local copies, waits for them, and re-layouts  5.47 us
    dot_general x2, matrix products, multiplied(): jnp.einsum('sm,mk->sk', ordered[f], masked[f], preferred_element_type=F32)  5.35 us
  transfers between devices with their start and end apart: 24, of which 16 were waited for; matrix products, arithmetic and copies ran while one was open for 5% of the time, Pallas kernels for 2%

profile of v8, /device:TPU:32, one launch (start us, length us, event | category | flops | bytes accessed | tf_op | source)
XLA Modules:
  0.0 171.0 jit_solution(10423795426306873359)
XLA Ops:
  0.7 1.4 fusion.62
  2.1 18.6 %all_gather.9 = bf16[2,64,3072]{2,1,0:T(8,128)(2,1)S(1)} all-gather(bf16[2,16,3072]{2,1,0:T(8,128)(2,1)S(1)} %pad_maximum_fusion.6), channel_id=1, replica_groups=mesh['group'=4,'x'=4,'z'=4,'h'=2,'c'=2] {'z'}, dimensions={1}, use_global_device_ids=true | all-gather | bytes 983040 | tf_op jit(solution)/shard_map/all_gather | solution.py:133
  20.7 2.8 %collective-permute-start.2 = (bf16[2,64,3072]{2,1,0:T(8,128)(2,1)S(1)}, bf16[2,64,3072]{2,1,0:T(8,128)(2,1)S(1)}, u32[]{:S(2)}, u32[]{:S(2)}) collective-permute-start(bf16[2,64,3072]{2,1,0:T(8,128)(2,1)S(1)} %all_gather.9), channel_id=1, source_target_pairs={{0,48},{16,0},{32,16},{48,32},{1,49},{17,1},{33,17},{49,33},{2,50}... | collective-permute-start | bytes 2359304 | tf_op jit(solution)/shard_map/ppermute | solution.py:18
  23.6 0.7 dynamic_slice.37.sizes_ref
  24.3 0.9 copy.59
  25.3 4.7 %collective-permute-start.3 = (bf16[64,2,768]{2,0,1:T(8,128)(2,1)S(1)}, bf16[64,2,768]{2,0,1:T(8,128)(2,1)S(1)}, u32[]{:S(2)}, u32[]{:S(2)}) collective-permute-start(bf16[64,2,768]{2,0,1:T(8,128)(2,1)S(1)} %copy.59), channel_id=1, source_target_pairs={{0,2},{2,0},{1,3},{3,1},{4,6},{6,4},{5,7},{7,5},{8,10},{10,8},{9,1... | collective-permute-start | bytes 589832 | tf_op jit(solution)/shard_map/ppermute | solution.py:18
  30.1 0.1 eq.36
  30.3 0.1 eq.40
  30.7 3.7 %copy-done = bf16[2,768,3072]{2,1,0:T(8,128)(2,1)S(1)} copy-done((bf16[2,768,3072]{2,1,0:T(8,128)(2,1)S(1)}, bf16[2,768,3072]{2,1,0:T(8,128)(2,1)}, u32[]{:S(2)}) %copy-start) | copy-done | bytes 9437208
  34.4 3.5 %shard_map.77 = bf16[2,768,3072]{2,1,0:T(8,128)(2,1)S(1)} custom-call(s32[2]{0:T(128)S(1)} %dynamic_slice.37.sizes_ref, s32[2]{0:T(128)S(1)} %pad_add_fusion.origin_ref, bf16[2,768,3072]{2,1,0:T(8,128)(2,1)S(1)} %copy-done), custom_call_target="tpu_custom_call" | custom-call | tf_op jit(solution)/shard_map/pallas_call | solution.py:53
  37.9 4.1 %collective-permute-done = bf16[2,64,3072]{2,1,0:T(8,128)(2,1)S(1)} collective-permute-done((bf16[2,64,3072]{2,1,0:T(8,128)(2,1)S(1)}, bf16[2,64,3072]{2,1,0:T(8,128)(2,1)S(1)}, u32[]{:S(2)}, u32[]{:S(2)}) %collective-permute-start) | collective-permute-done | bytes 786464 | tf_op jit(solution)/shard_map/ppermute | solution.py:18
  42.3 3.3 %collective-permute-start.5 = (bf16[64,3072]{1,0:T(8,128)(2,1)S(1)}, bf16[64,3072]{1,0:T(8,128)(2,1)S(1)}, u32[]{:S(2)}, u32[]{:S(2)}) collective-permute-start(bf16[64,3072]{1,0:T(8,128)(2,1)S(1)} %get-tuple-element.92), channel_id=1, source_target_pairs={{0,48},{16,0},{32,16},{48,32},{1,49},{17,1},{33,17},{49,33},{2,50}... | collective-permute-start | bytes 1179656 | tf_op jit(solution)/shard_map/ppermute | solution.py:18
  45.5 5.7 %collective-permute-done.1 = bf16[64,3072]{1,0:T(8,128)(2,1)S(1)} collective-permute-done((bf16[64,3072]{1,0:T(8,128)(2,1)S(1)}, bf16[64,3072]{1,0:T(8,128)(2,1)S(1)}, u32[]{:S(2)}, u32[]{:S(2)}) %collective-permute-start.1) | collective-permute-done | bytes 393248 | tf_op jit(solution)/shard_map/ppermute | solution.py:18
  51.3 0.1 pad_maximum_fusion
  51.4 1.5 fusion.16
  53.1 1.4 fusion.13
  54.5 0.6 collective-permute-start.6
  55.3 0.3 copy.47
  55.6 0.6 collective-permute-done.6
  56.3 0.3 copy.48
  56.6 0.9 pad_maximum_fusion.1
  57.5 29.4 %all_to_all.10 = bf16[128,2,768]{2,1,0:T(2,128)(2,1)S(1)} all-to-all(bf16[128,2,768]{2,1,0:T(2,128)(2,1)S(1)} %pad_maximum_fusion.1), channel_id=1, replica_groups=mesh['group'=4,'x'=4,'z'=4,'h'=2,'c'=2] {'h','group','x','z'}, dimensions={0} | all-to-all | bytes 786432 | tf_op jit(solution)/shard_map/all_to_all | solution.py:153
  86.9 0.2 add_convert_fusion.6
  87.2 0.2 convolution_convert_fusion
  87.5 1.3 pad_maximum_fusion.2
  88.8 6.4 %all-to-all-start.1 = ((bf16[128,2,768]{2,1,0:T(2,128)(2,1)}), bf16[128,2,768]{2,1,0:T(2,128)(2,1)S(1)}, u32[]{:S(2)}, u32[]{:S(2)}) async-start(bf16[128,2,768]{2,1,0:T(2,128)(2,1)} %pad_maximum_fusion.2), calls=%async_computation.1 | async-start | bytes 786432 | tf_op jit(solution)/shard_map/all_to_all | solution.py:159
  95.2 0.3 fusion.25
  95.6 16.1 %all-to-all-done.1 = bf16[128,2,768]{2,1,0:T(2,128)(2,1)S(1)} async-done(((bf16[128,2,768]{2,1,0:T(2,128)(2,1)}), bf16[128,2,768]{2,1,0:T(2,128)(2,1)S(1)}, u32[]{:S(2)}, u32[]{:S(2)}) %all-to-all-start.1) | async-done | bytes 393248 | tf_op jit(solution)/shard_map/all_to_all | solution.py:159
  111.8 0.2 fusion.30
  112.0 0.2 fusion.27
  112.2 2.5 %all-gather = bf16[4,128,768]{2,1,0:T(8,128)(2,1)S(1)} all-gather(bf16[2,128,768]{2,1,0:T(8,128)(2,1)S(1)} %pad_maximum_fusion.3), channel_id=2, replica_groups=mesh['group'=4,'x'=4,'z'=4,'h'=2,'c'=2] {'c'}, dimensions={0}, use_global_device_ids=true | all-gather | bytes 1179648 | tf_op jit(solution)/shard_map/all_gather | solution.py:168
  114.8 0.2 fusion.19
  115.0 3.9 %fusion.5 = bf16[256,3072]{1,0:T(8,128)(2,1)S(1)} fusion(bf16[256,768]{1,0:T(8,128)(2,1)S(1)} %bitcast.129, bf16[2,768,3072]{2,1,0:T(8,128)(2,1)} %copy-done.1), kind=kOutput, calls=%fused_computation.7 | convolution fusion | flops 1208745984 | bytes 6684672 | tf_op jit(solution)/shard_map/sm,mk->sk/dot_general | solution.py:172
  119.0 0.2 fusion.18
  119.2 1.2 collective-permute-start.8
  120.4 0.9 collective-permute-start.7
  121.4 1.4 fusion.4
  122.8 1.1 collective-permute-start.9
  124.0 6.4 %collective-permute-done.8 = bf16[64,3072]{1,0:T(8,128)(2,1)S(1)} collective-permute-done((bf16[64,3072]{1,0:T(8,128)(2,1)S(1)}, bf16[64,3072]{1,0:T(8,128)(2,1)S(1)}, u32[]{:S(2)}, u32[]{:S(2)}) %collective-permute-start.8) | collective-permute-done | bytes 393248 | tf_op jit(solution)/shard_map/ppermute | solution.py:18
  130.4 2.0 %collective-permute-done.7 = bf16[64,3072]{1,0:T(8,128)(2,1)S(1)} collective-permute-done((bf16[64,3072]{1,0:T(8,128)(2,1)S(1)}, bf16[64,3072]{1,0:T(8,128)(2,1)S(1)}, u32[]{:S(2)}, u32[]{:S(2)}) %collective-permute-start.7) | collective-permute-done | bytes 393248 | tf_op jit(solution)/shard_map/ppermute | solution.py:18
  132.4 0.6 collective-permute-done.9
  133.1 2.6 %collective-permute-start.16 = (bf16[32,3072]{1,0:T(8,128)(2,1)S(1)}, bf16[32,3072]{1,0:T(8,128)(2,1)S(1)}, u32[]{:S(2)}, u32[]{:S(2)}) collective-permute-start(bf16[32,3072]{1,0:T(8,128)(2,1)S(1)} %get-tuple-element.76), channel_id=1, source_target_pairs={{0,48},{16,0},{32,16},{48,32},{1,49},{17,1},{33,17},{49,33},{2,50}... | collective-permute-start | bytes 589832 | tf_op jit(solution)/shard_map/ppermute | solution.py:18
  135.7 3.3 %collective-permute-start.11 = (bf16[64,3072]{1,0:T(8,128)(2,1)S(1)}, bf16[64,3072]{1,0:T(8,128)(2,1)S(1)}, u32[]{:S(2)}, u32[]{:S(2)}) collective-permute-start(bf16[64,3072]{1,0:T(8,128)(2,1)S(1)} %pad_maximum_fusion.5), channel_id=1, source_target_pairs={{0,48},{16,0},{32,16},{48,32},{1,49},{17,1},{33,17},{49,33},{2,50}... | collective-permute-start | bytes 1179656 | tf_op jit(solution)/shard_map/ppermute | solution.py:18
  138.9 2.1 %collective-permute-done.16 = bf16[32,3072]{1,0:T(8,128)(2,1)S(1)} collective-permute-done((bf16[32,3072]{1,0:T(8,128)(2,1)S(1)}, bf16[32,3072]{1,0:T(8,128)(2,1)S(1)}, u32[]{:S(2)}, u32[]{:S(2)}) %collective-permute-start.16) | collective-permute-done | bytes 196640 | tf_op jit(solution)/shard_map/ppermute | solution.py:18
  141.0 3.7 %collective-permute-done.15 = bf16[32,3072]{1,0:T(8,128)(2,1)S(1)} collective-permute-done((bf16[32,3072]{1,0:T(8,128)(2,1)S(1)}, bf16[32,3072]{1,0:T(8,128)(2,1)S(1)}, u32[]{:S(2)}, u32[]{:S(2)}) %collective-permute-start.15) | collective-permute-done | bytes 196640 | tf_op jit(solution)/shard_map/ppermute | solution.py:18
  144.7 0.1 convert_add_fusion.3
  144.9 0.6 collective-permute-start.17
  145.5 3.3 %collective-permute-start.18 = (bf16[16,3072]{1,0:T(8,128)(2,1)S(1)}, bf16[16,3072]{1,0:T(8,128)(2,1)S(1)}, u32[]{:S(2)}, u32[]{:S(2)}) collective-permute-start(bf16[16,3072]{1,0:T(8,128)(2,1)S(1)} %get-tuple-element.96), channel_id=1, source_target_pairs={{0,8},{4,12},{8,0},{12,4},{1,9},{5,13},{9,1},{13,5},{2,10},{6,14},... | collective-permute-start | bytes 294920 | tf_op jit(solution)/shard_map/ppermute | solution.py:18
  148.8 1.2 collective-permute-done.10
  150.1 1.0 collective-permute-start.14
  151.0 1.1 collective-permute-start.13
  152.2 0.4 collective-permute-start.12
  152.5 0.2 collective-permute-done.18
  152.8 4.7 %collective-permute-done.19 = bf16[16,3072]{1,0:T(8,128)(2,1)S(1)} collective-permute-done((bf16[16,3072]{1,0:T(8,128)(2,1)S(1)}, bf16[16,3072]{1,0:T(8,128)(2,1)S(1)}, u32[]{:S(2)}, u32[]{:S(2)}) %collective-permute-start.19) | collective-permute-done | bytes 98336 | tf_op jit(solution)/shard_map/ppermute | solution.py:18
  157.6 0.3 collective-permute-done.13
  157.9 2.9 %collective-permute-done.12 = bf16[64,768]{1,0:T(8,128)(2,1)S(1)} collective-permute-done((bf16[64,768]{1,0:T(8,128)(2,1)S(1)}, bf16[64,768]{1,0:T(8,128)(2,1)S(1)}, u32[]{:S(2)}, u32[]{:S(2)}) %collective-permute-start.12) | collective-permute-done | bytes 98336 | tf_op jit(solution)/shard_map/ppermute | solution.py:18
  160.8 0.1 convert_add_fusion.2
  161.0 0.9 collective-permute-start.20
  161.9 2.4 %collective-permute-start.21 = (bf16[16,3072]{1,0:T(8,128)(2,1)S(1)}, bf16[16,3072]{1,0:T(8,128)(2,1)S(1)}, u32[]{:S(2)}, u32[]{:S(2)}) collective-permute-start(bf16[16,3072]{1,0:T(8,128)(2,1)S(1)} %get-tuple-element.98), channel_id=1, source_target_pairs={{0,8},{4,12},{8,0},{12,4},{1,9},{5,13},{9,1},{13,5},{2,10},{6,14},... | collective-permute-start | bytes 294920 | tf_op jit(solution)/shard_map/ppermute | solution.py:18
  164.3 1.8 %collective-permute-start.22 = (bf16[16,3072]{1,0:T(8,128)(2,1)S(1)}, bf16[16,3072]{1,0:T(8,128)(2,1)S(1)}, u32[]{:S(2)}, u32[]{:S(2)}) collective-permute-start(bf16[16,3072]{1,0:T(8,128)(2,1)S(1)} %get-tuple-element.99), channel_id=1, source_target_pairs={{0,12},{4,0},{8,4},{12,8},{1,13},{5,1},{9,5},{13,9},{2,14},{6,2},{... | collective-permute-start | bytes 294920 | tf_op jit(solution)/shard_map/ppermute | solution.py:18
  166.2 0.9 copy.50
  167.1 0.9 collective-permute-done.21
  168.1 2.0 %collective-permute-done.22 = bf16[16,3072]{1,0:T(8,128)(2,1)S(1)} collective-permute-done((bf16[16,3072]{1,0:T(8,128)(2,1)S(1)}, bf16[16,3072]{1,0:T(8,128)(2,1)S(1)}, u32[]{:S(2)}, u32[]{:S(2)}) %collective-permute-start.22) | collective-permute-done | bytes 98336 | tf_op jit(solution)/shard_map/ppermute | solution.py:18
  170.1 0.9 copy.51
  (72 shorter events, 2.3 us)
Async XLA Ops:
  0.6 29.4 %copy-start.3 = (s32[8]{0:T(128)S(1)}, s32[8]{0:T(128)}, u32[]{:S(2)}) copy-start(s32[8]{0:T(128)} %param.10) | copy-start | bytes 100
  0.6 29.6 %copy-start.2 = (s32[8,16]{1,0:T(8,128)S(1)}, s32[8,16]{1,0:T(8,128)}, u32[]{:S(2)}) copy-start(s32[8,16]{1,0:T(8,128)} %param.11) | copy-start | bytes 1540
  20.7 21.4 %collective-permute-start.2 = (bf16[2,64,3072]{2,1,0:T(8,128)(2,1)S(1)}, bf16[2,64,3072]{2,1,0:T(8,128)(2,1)S(1)}, u32[]{:S(2)}, u32[]{:S(2)}) collective-permute-start(bf16[2,64,3072]{2,1,0:T(8,128)(2,1)S(1)} %all_gather.9), channel_id=1, source_target_pairs={{0,48},{16,0},{32,16},{48,32},{1,49},{17,1},{33,17},{49,33},{2,50}... | collective-permute-start | bytes 2359304 | tf_op jit(solution)/shard_map/ppermute | solution.py:18
  23.6 18.5 %collective-permute-start = (bf16[2,64,3072]{2,1,0:T(8,128)(2,1)S(1)}, bf16[2,64,3072]{2,1,0:T(8,128)(2,1)S(1)}, u32[]{:S(2)}, u32[]{:S(2)}) collective-permute-start(bf16[2,64,3072]{2,1,0:T(8,128)(2,1)S(1)} %all_gather.9), channel_id=1, source_target_pairs={{0,16},{16,32},{32,48},{48,0},{1,17},{17,33},{33,49},{49,1},{2,18}... | collective-permute-start | bytes 2359304 | tf_op jit(solution)/shard_map/ppermute | solution.py:18
  25.3 26.1 %collective-permute-start.3 = (bf16[64,2,768]{2,0,1:T(8,128)(2,1)S(1)}, bf16[64,2,768]{2,0,1:T(8,128)(2,1)S(1)}, u32[]{:S(2)}, u32[]{:S(2)}) collective-permute-start(bf16[64,2,768]{2,0,1:T(8,128)(2,1)S(1)} %copy.59), channel_id=1, source_target_pairs={{0,2},{2,0},{1,3},{3,1},{4,6},{6,4},{5,7},{7,5},{8,10},{10,8},{9,1... | collective-permute-start | bytes 589832 | tf_op jit(solution)/shard_map/ppermute | solution.py:18
  30.7 3.7 %copy-start = (bf16[2,768,3072]{2,1,0:T(8,128)(2,1)S(1)}, bf16[2,768,3072]{2,1,0:T(8,128)(2,1)}, u32[]{:S(2)}) copy-start(bf16[2,768,3072]{2,1,0:T(8,128)(2,1)} %fronts_ref.1) | copy-start | bytes 28311556
  37.9 15.2 %copy-start.1 = (bf16[2,768,3072]{2,1,0:T(8,128)(2,1)}, bf16[2,768,3072]{2,1,0:T(8,128)(2,1)S(1)}, u32[]{:S(2)}) copy-start(bf16[2,768,3072]{2,1,0:T(8,128)(2,1)S(1)} %shard_map.77) | copy-start | bytes 28311556
  42.1 9.2 %collective-permute-start.1 = (bf16[64,3072]{1,0:T(8,128)(2,1)S(1)}, bf16[64,3072]{1,0:T(8,128)(2,1)S(1)}, u32[]{:S(2)}, u32[]{:S(2)}) collective-permute-start(bf16[64,3072]{1,0:T(8,128)(2,1)S(1)} %get-tuple-element.91), channel_id=1, source_target_pairs={{0,16},{16,32},{32,48},{48,0},{1,17},{17,33},{33,49},{49,1},{2,18}... | collective-permute-start | bytes 1179656 | tf_op jit(solution)/shard_map/ppermute | solution.py:18
  42.3 10.8 %collective-permute-start.5 = (bf16[64,3072]{1,0:T(8,128)(2,1)S(1)}, bf16[64,3072]{1,0:T(8,128)(2,1)S(1)}, u32[]{:S(2)}, u32[]{:S(2)}) collective-permute-start(bf16[64,3072]{1,0:T(8,128)(2,1)S(1)} %get-tuple-element.92), channel_id=1, source_target_pairs={{0,48},{16,0},{32,16},{48,32},{1,49},{17,1},{33,17},{49,33},{2,50}... | collective-permute-start | bytes 1179656 | tf_op jit(solution)/shard_map/ppermute | solution.py:18
  52.9 2.2 %collective-permute-start.4 = (bf16[2,64,768]{2,1,0:T(8,128)(2,1)S(1)}, bf16[2,64,768]{2,1,0:T(8,128)(2,1)S(1)}, u32[]{:S(2)}, u32[]{:S(2)}) collective-permute-start(bf16[2,64,768]{2,1,0:T(8,128)(2,1)S(1)} %dynamic-slice_bitcast_fusion.1), channel_id=1, source_target_pairs={{0,1},{1,0},{2,3},{3,2},{4,5},{5,4},{6,7},{7,6},{8,9},{9,8},{10,11... | collective-permute-start | bytes 589832 | tf_op jit(solution)/shard_map/ppermute | solution.py:18
  54.5 1.6 collective-permute-start.6
  88.8 22.9 %all-to-all-start.1 = ((bf16[128,2,768]{2,1,0:T(2,128)(2,1)}), bf16[128,2,768]{2,1,0:T(2,128)(2,1)S(1)}, u32[]{:S(2)}, u32[]{:S(2)}) async-start(bf16[128,2,768]{2,1,0:T(2,128)(2,1)} %pad_maximum_fusion.2), calls=%async_computation.1 | async-start | bytes 786432 | tf_op jit(solution)/shard_map/all_to_all | solution.py:159
  95.2 26.1 %slice-start = ((s8[9437184]{0:T(1024)(128)(4,1)}), s8[1048576]{0:T(1024)(128)(4,1)S(1)}, s32[]{:S(2)}) async-start(s8[9437184]{0:T(1024)(128)(4,1)} %bitcast.114), calls=%async_computation.2 | async-start | bytes 2097152
  112.2 9.1 %slice-start.1 = ((s8[9437184]{0:T(1024)(128)(4,1)}), s8[4194304]{0:T(1024)(128)(4,1)S(1)}, s32[]{:S(2)}) async-start(s8[9437184]{0:T(1024)(128)(4,1)} %bitcast.114), calls=%async_computation.3 | async-start | bytes 8388608
  115.0 6.4 %slice-start.2 = ((s8[9437184]{0:T(1024)(128)(4,1)}), s8[4194304]{0:T(1024)(128)(4,1)S(1)}, s32[]{:S(2)}) async-start(s8[9437184]{0:T(1024)(128)(4,1)} %bitcast.114), calls=%async_computation.4 | async-start | bytes 8388608
  119.2 11.2 %collective-permute-start.8 = (bf16[64,3072]{1,0:T(8,128)(2,1)S(1)}, bf16[64,3072]{1,0:T(8,128)(2,1)S(1)}, u32[]{:S(2)}, u32[]{:S(2)}) collective-permute-start(bf16[64,3072]{1,0:T(8,128)(2,1)S(1)} %pad_maximum_fusion.4), channel_id=1, source_target_pairs={{0,48},{16,0},{32,16},{48,32},{1,49},{17,1},{33,17},{49,33},{2,50}... | collective-permute-start | bytes 1179656 | tf_op jit(solution)/shard_map/ppermute | solution.py:18
  120.4 12.1 %collective-permute-start.7 = (bf16[64,3072]{1,0:T(8,128)(2,1)S(1)}, bf16[64,3072]{1,0:T(8,128)(2,1)S(1)}, u32[]{:S(2)}, u32[]{:S(2)}) collective-permute-start(bf16[64,3072]{1,0:T(8,128)(2,1)S(1)} %slice.181), channel_id=1, source_target_pairs={{0,16},{16,32},{32,48},{48,0},{1,17},{17,33},{33,49},{49,1},{2,18}... | collective-permute-start | bytes 1179656 | tf_op jit(solution)/shard_map/ppermute | solution.py:18
  122.8 10.2 %collective-permute-start.9 = (bf16[64,768]{1,0:T(8,128)(2,1)S(1)}, bf16[64,768]{1,0:T(8,128)(2,1)S(1)}, u32[]{:S(2)}, u32[]{:S(2)}) collective-permute-start(bf16[64,768]{1,0:T(8,128)(2,1)S(1)} %get-tuple-element.42), channel_id=1, source_target_pairs={{0,2},{2,0},{1,3},{3,1},{4,6},{6,4},{5,7},{7,5},{8,10},{10,8},{9,1... | collective-permute-start | bytes 294920 | tf_op jit(solution)/shard_map/ppermute | solution.py:18
  133.1 7.9 %collective-permute-start.16 = (bf16[32,3072]{1,0:T(8,128)(2,1)S(1)}, bf16[32,3072]{1,0:T(8,128)(2,1)S(1)}, u32[]{:S(2)}, u32[]{:S(2)}) collective-permute-start(bf16[32,3072]{1,0:T(8,128)(2,1)S(1)} %get-tuple-element.76), channel_id=1, source_target_pairs={{0,48},{16,0},{32,16},{48,32},{1,49},{17,1},{33,17},{49,33},{2,50}... | collective-permute-start | bytes 589832 | tf_op jit(solution)/shard_map/ppermute | solution.py:18
  135.7 9.0 %collective-permute-start.15 = (bf16[32,3072]{1,0:T(8,128)(2,1)S(1)}, bf16[32,3072]{1,0:T(8,128)(2,1)S(1)}, u32[]{:S(2)}, u32[]{:S(2)}) collective-permute-start(bf16[32,3072]{1,0:T(8,128)(2,1)S(1)} %get-tuple-element.77), channel_id=1, source_target_pairs={{0,16},{16,32},{32,48},{48,0},{1,17},{17,33},{33,49},{49,1},{2,18}... | collective-permute-start | bytes 589832 | tf_op jit(solution)/shard_map/ppermute | solution.py:18
  135.7 14.3 %collective-permute-start.10 = (bf16[64,3072]{1,0:T(8,128)(2,1)S(1)}, bf16[64,3072]{1,0:T(8,128)(2,1)S(1)}, u32[]{:S(2)}, u32[]{:S(2)}) collective-permute-start(bf16[64,3072]{1,0:T(8,128)(2,1)S(1)} %slice.228), channel_id=1, source_target_pairs={{0,16},{16,32},{32,48},{48,0},{1,17},{17,33},{33,49},{49,1},{2,18}... | collective-permute-start | bytes 1179656 | tf_op jit(solution)/shard_map/ppermute | solution.py:18
  135.7 14.3 %collective-permute-start.11 = (bf16[64,3072]{1,0:T(8,128)(2,1)S(1)}, bf16[64,3072]{1,0:T(8,128)(2,1)S(1)}, u32[]{:S(2)}, u32[]{:S(2)}) collective-permute-start(bf16[64,3072]{1,0:T(8,128)(2,1)S(1)} %pad_maximum_fusion.5), channel_id=1, source_target_pairs={{0,48},{16,0},{32,16},{48,32},{1,49},{17,1},{33,17},{49,33},{2,50}... | collective-permute-start | bytes 1179656 | tf_op jit(solution)/shard_map/ppermute | solution.py:18
  144.9 7.3 %collective-permute-start.17 = (bf16[16,3072]{1,0:T(8,128)(2,1)S(1)}, bf16[16,3072]{1,0:T(8,128)(2,1)S(1)}, u32[]{:S(2)}, u32[]{:S(2)}) collective-permute-start(bf16[16,3072]{1,0:T(8,128)(2,1)S(1)} %slice.316), channel_id=1, source_target_pairs={{0,4},{4,8},{8,12},{12,0},{1,5},{5,9},{9,13},{13,1},{2,6},{6,10},{... | collective-permute-start | bytes 294920 | tf_op jit(solution)/shard_map/ppermute | solution.py:18
  145.5 7.3 %collective-permute-start.18 = (bf16[16,3072]{1,0:T(8,128)(2,1)S(1)}, bf16[16,3072]{1,0:T(8,128)(2,1)S(1)}, u32[]{:S(2)}, u32[]{:S(2)}) collective-permute-start(bf16[16,3072]{1,0:T(8,128)(2,1)S(1)} %get-tuple-element.96), channel_id=1, source_target_pairs={{0,8},{4,12},{8,0},{12,4},{1,9},{5,13},{9,1},{13,5},{2,10},{6,14},... | collective-permute-start | bytes 294920 | tf_op jit(solution)/shard_map/ppermute | solution.py:18
  148.8 8.7 %collective-permute-start.19 = (bf16[16,3072]{1,0:T(8,128)(2,1)S(1)}, bf16[16,3072]{1,0:T(8,128)(2,1)S(1)}, u32[]{:S(2)}, u32[]{:S(2)}) collective-permute-start(bf16[16,3072]{1,0:T(8,128)(2,1)S(1)} %get-tuple-element.97), channel_id=1, source_target_pairs={{0,12},{4,0},{8,4},{12,8},{1,13},{5,1},{9,5},{13,9},{2,14},{6,2},{... | collective-permute-start | bytes 294920 | tf_op jit(solution)/shard_map/ppermute | solution.py:18
  150.1 7.5 %collective-permute-start.14 = (bf16[32,3072]{1,0:T(8,128)(2,1)S(1)}, bf16[32,3072]{1,0:T(8,128)(2,1)S(1)}, u32[]{:S(2)}, u32[]{:S(2)}) collective-permute-start(bf16[32,3072]{1,0:T(8,128)(2,1)S(1)} %get-tuple-element.80), channel_id=1, source_target_pairs={{0,48},{16,0},{32,16},{48,32},{1,49},{17,1},{33,17},{49,33},{2,50}... | collective-permute-start | bytes 589832 | tf_op jit(solution)/shard_map/ppermute | solution.py:18
  151.0 6.9 %collective-permute-start.13 = (bf16[32,3072]{1,0:T(8,128)(2,1)S(1)}, bf16[32,3072]{1,0:T(8,128)(2,1)S(1)}, u32[]{:S(2)}, u32[]{:S(2)}) collective-permute-start(bf16[32,3072]{1,0:T(8,128)(2,1)S(1)} %get-tuple-element.81), channel_id=1, source_target_pairs={{0,16},{16,32},{32,48},{48,0},{1,17},{17,33},{33,49},{49,1},{2,18}... | collective-permute-start | bytes 589832 | tf_op jit(solution)/shard_map/ppermute | solution.py:18
  152.2 8.7 %collective-permute-start.12 = (bf16[64,768]{1,0:T(8,128)(2,1)S(1)}, bf16[64,768]{1,0:T(8,128)(2,1)S(1)}, u32[]{:S(2)}, u32[]{:S(2)}) collective-permute-start(bf16[64,768]{1,0:T(8,128)(2,1)S(1)} %get-tuple-element.50), channel_id=1, source_target_pairs={{0,2},{2,0},{1,3},{3,1},{4,6},{6,4},{5,7},{7,5},{8,10},{10,8},{9,1... | collective-permute-start | bytes 294920 | tf_op jit(solution)/shard_map/ppermute | solution.py:18
  161.0 6.1 %collective-permute-start.20 = (bf16[16,3072]{1,0:T(8,128)(2,1)S(1)}, bf16[16,3072]{1,0:T(8,128)(2,1)S(1)}, u32[]{:S(2)}, u32[]{:S(2)}) collective-permute-start(bf16[16,3072]{1,0:T(8,128)(2,1)S(1)} %slice.315), channel_id=1, source_target_pairs={{0,4},{4,8},{8,12},{12,0},{1,5},{5,9},{9,13},{13,1},{2,6},{6,10},{... | collective-permute-start | bytes 294920 | tf_op jit(solution)/shard_map/ppermute | solution.py:18
  161.9 6.2 %collective-permute-start.21 = (bf16[16,3072]{1,0:T(8,128)(2,1)S(1)}, bf16[16,3072]{1,0:T(8,128)(2,1)S(1)}, u32[]{:S(2)}, u32[]{:S(2)}) collective-permute-start(bf16[16,3072]{1,0:T(8,128)(2,1)S(1)} %get-tuple-element.98), channel_id=1, source_target_pairs={{0,8},{4,12},{8,0},{12,4},{1,9},{5,13},{9,1},{13,5},{2,10},{6,14},... | collective-permute-start | bytes 294920 | tf_op jit(solution)/shard_map/ppermute | solution.py:18
  164.3 5.8 %collective-permute-start.22 = (bf16[16,3072]{1,0:T(8,128)(2,1)S(1)}, bf16[16,3072]{1,0:T(8,128)(2,1)S(1)}, u32[]{:S(2)}, u32[]{:S(2)}) collective-permute-start(bf16[16,3072]{1,0:T(8,128)(2,1)S(1)} %get-tuple-element.99), channel_id=1, source_target_pairs={{0,12},{4,0},{8,4},{12,8},{1,13},{5,1},{9,5},{13,9},{2,14},{6,2},{... | collective-permute-start | bytes 294920 | tf_op jit(solution)/shard_map/ppermute | solution.py:18

commit v9 on v8

--- a/solution.py
+++ b/solution.py
@@ -179,22 +179,17 @@
     ordered[1], _ = lax.optimization_barrier((ordered[1], pieces_0))
     product_1 = multiplied(1)
     pieces_1 = first_pieces(product_1)
-    away = [jnp.where(first, half[1], half[0]).astype(BF16) for half in halves]
-    away[0], _ = lax.optimization_barrier((away[0], pieces_0))
-    received_0 = shift(away[0], "h", 1)
-    near_0, product_1, pieces_1, received_0 = lax.optimization_barrier((near_0, product_1, pieces_1, received_0))
+    away = jnp.stack([jnp.where(first, half[1], half[0]).astype(BF16) for half in halves])
+    away, _ = lax.optimization_barrier((away, pieces_0))
+    received = shift(away, "h", 1)
+    near_0, product_1, pieces_1, received = lax.optimization_barrier((near_0, product_1, pieces_1, received))
     far_0 = second_step(second_pieces(product_0, near_0))
     near_1 = first_step(pieces_1)
     total_0 = last_step(product_0, near_0, far_0)
     passed_1 = second_pieces(product_1, near_1)
     far_1 = second_step(passed_1)
-    away[1], _ = lax.optimization_barrier((away[1], passed_1))
-    received_1 = shift(away[1], "h", 1)
-    received_1, far_1 = lax.optimization_barrier((received_1, far_1))
-    slabs = [
-        jnp.where(first, half[0], half[1]) + received.astype(F32)
-        for half, received in zip(halves, (received_0, received_1))
-    ]
+    received, _ = lax.optimization_barrier((received, far_1))
+    slabs = [jnp.where(first, half[0], half[1]) + received[f].astype(F32) for f, half in enumerate(halves)]
     sampled = jnp.stack([total.astype(BF16) for total in slabs], axis=1)
     total_1 = last_step(product_1, near_1, far_1)
     outs = [total_0.astype(BF16), total_1.astype(BF16)]

time: 172 us -> 172 us (level)
  waiting for transfers between devices: 53.8 us -> 58.9 us
  starting transfers between devices: 38.5 us -> 34.6 us
    ppermute x23 -> x22, waiting for transfers between devices: 37.7 us -> 42.8 us  [shift(): return lax.ppermute(value, axis, [(i, (i + by) % n) for i in range(n)])]
    ppermute x23 -> x22, starting transfers between devices: 32.1 us -> 28.2 us  [shift(): return lax.ppermute(value, axis, [(i, (i + by) % n) for i in range(n)])]
  transfers between devices with their start and end apart: 24 -> 23, of which waited for: 16 -> 16; matrix products, arithmetic and copies ran while one was open for 5% -> 5% of each run, Pallas kernels for 2% -> 2%
where the time goes in v9:
time: 172 us; the launch traced here: 171 us
  waiting for transfers between devices  58.9 us (34%)
  blocking collectives  50.5 us (29%)
  starting transfers between devices  34.6 us (20%)
  local copies, waits for them, and re-layouts  10.1 us (6%)
  matrix products  8.46 us (5%)
  other arithmetic  4 us (2%)
  Pallas kernels  3.47 us (2%)
    ppermute x22, waiting for transfers between devices, shift(): return lax.ppermute(value, axis, [(i, (i + by) % n) for i in range(n)])  42.8 us
    all_to_all x1, blocking collectives, shards(): lax.all_to_all(outgoing, spread, split_axis=0, concat_axis=0, tiled=True)  29.4 us
    ppermute x22, starting transfers between devices, shift(): return lax.ppermute(value, axis, [(i, (i + by) % n) for i in range(n)])  28.2 us
    all_gather x1, blocking collectives, shards(): columns = lax.all_gather(mine, 'z', axis=1, tiled=True)  18.6 us
    all_to_all x1, waiting for transfers between devices, shards(): lax.all_to_all(extension, spread, split_axis=0, concat_axis=0, tiled=True)  16.1 us
    all_to_all x1, starting transfers between devices, shards(): lax.all_to_all(extension, spread, split_axis=0, concat_axis=0, tiled=True)  6.41 us
    unnamed x16, local copies, waits for them, and re-layouts  5.47 us
    dot_general x2, matrix products, multiplied(): jnp.einsum('sm,mk->sk', ordered[f], masked[f], preferred_element_type=F32)  5.33 us
  transfers between devices with their start and end apart: 23, of which 16 were waited for; matrix products, arithmetic and copies ran while one was open for 5% of the time, Pallas kernels for 2%

profile of v9, /device:TPU:32, one launch (start us, length us, event | category | flops | bytes accessed | tf_op | source)
XLA Modules:
  0.0 171.2 jit_solution(16153573739814951679)
XLA Ops:
  0.7 1.4 fusion.56
  2.1 18.6 %all_gather.9 = bf16[2,64,3072]{2,1,0:T(8,128)(2,1)S(1)} all-gather(bf16[2,16,3072]{2,1,0:T(8,128)(2,1)S(1)} %pad_maximum_fusion.6), channel_id=1, replica_groups=mesh['group'=4,'x'=4,'z'=4,'h'=2,'c'=2] {'z'}, dimensions={1}, use_global_device_ids=true | all-gather | bytes 983040 | tf_op jit(solution)/shard_map/all_gather | solution.py:133
  20.7 2.8 %collective-permute-start.2 = (bf16[2,64,3072]{2,1,0:T(8,128)(2,1)S(1)}, bf16[2,64,3072]{2,1,0:T(8,128)(2,1)S(1)}, u32[]{:S(2)}, u32[]{:S(2)}) collective-permute-start(bf16[2,64,3072]{2,1,0:T(8,128)(2,1)S(1)} %all_gather.9), channel_id=1, source_target_pairs={{0,48},{16,0},{32,16},{48,32},{1,49},{17,1},{33,17},{49,33},{2,50}... | collective-permute-start | bytes 2359304 | tf_op jit(solution)/shard_map/ppermute | solution.py:18
  23.6 0.7 dynamic_slice.37.sizes_ref
  24.3 0.9 copy.66
  25.3 4.7 %collective-permute-start.3 = (bf16[64,2,768]{2,0,1:T(8,128)(2,1)S(1)}, bf16[64,2,768]{2,0,1:T(8,128)(2,1)S(1)}, u32[]{:S(2)}, u32[]{:S(2)}) collective-permute-start(bf16[64,2,768]{2,0,1:T(8,128)(2,1)S(1)} %copy.66), channel_id=1, source_target_pairs={{0,2},{2,0},{1,3},{3,1},{4,6},{6,4},{5,7},{7,5},{8,10},{10,8},{9,1... | collective-permute-start | bytes 589832 | tf_op jit(solution)/shard_map/ppermute | solution.py:18
  30.1 0.1 eq.36
  30.2 0.1 copy.52
  30.3 0.1 eq.40
  30.5 0.1 and_convert_fusion
  30.7 3.7 %copy-done = bf16[2,768,3072]{2,1,0:T(8,128)(2,1)S(1)} copy-done((bf16[2,768,3072]{2,1,0:T(8,128)(2,1)S(1)}, bf16[2,768,3072]{2,1,0:T(8,128)(2,1)}, u32[]{:S(2)}) %copy-start) | copy-done | bytes 9437208
  34.4 3.5 %shard_map.77 = bf16[2,768,3072]{2,1,0:T(8,128)(2,1)S(1)} custom-call(s32[2]{0:T(128)S(1)} %dynamic_slice.37.sizes_ref, s32[2]{0:T(128)S(1)} %pad_add_fusion.origin_ref, bf16[2,768,3072]{2,1,0:T(8,128)(2,1)S(1)} %copy-done), custom_call_target="tpu_custom_call" | custom-call | tf_op jit(solution)/shard_map/pallas_call | solution.py:53
  37.9 4.1 %collective-permute-done = bf16[2,64,3072]{2,1,0:T(8,128)(2,1)S(1)} collective-permute-done((bf16[2,64,3072]{2,1,0:T(8,128)(2,1)S(1)}, bf16[2,64,3072]{2,1,0:T(8,128)(2,1)S(1)}, u32[]{:S(2)}, u32[]{:S(2)}) %collective-permute-start) | collective-permute-done | bytes 786464 | tf_op jit(solution)/shard_map/ppermute | solution.py:18
  42.3 3.3 %collective-permute-start.5 = (bf16[64,3072]{1,0:T(8,128)(2,1)S(1)}, bf16[64,3072]{1,0:T(8,128)(2,1)S(1)}, u32[]{:S(2)}, u32[]{:S(2)}) collective-permute-start(bf16[64,3072]{1,0:T(8,128)(2,1)S(1)} %get-tuple-element.88), channel_id=1, source_target_pairs={{0,48},{16,0},{32,16},{48,32},{1,49},{17,1},{33,17},{49,33},{2,50}... | collective-permute-start | bytes 1179656 | tf_op jit(solution)/shard_map/ppermute | solution.py:18
  45.5 5.7 %collective-permute-done.1 = bf16[64,3072]{1,0:T(8,128)(2,1)S(1)} collective-permute-done((bf16[64,3072]{1,0:T(8,128)(2,1)S(1)}, bf16[64,3072]{1,0:T(8,128)(2,1)S(1)}, u32[]{:S(2)}, u32[]{:S(2)}) %collective-permute-start.1) | collective-permute-done | bytes 393248 | tf_op jit(solution)/shard_map/ppermute | solution.py:18
  51.3 0.1 pad_maximum_fusion
  51.4 1.5 fusion.16
  53.1 1.5 fusion.13
  54.5 0.6 collective-permute-start.6
  55.3 0.9 collective-permute-done.6
  56.4 0.4 copy.55
  56.8 29.4 %all_to_all.10 = bf16[128,2,768]{2,1,0:T(2,128)(2,1)S(1)} all-to-all(bf16[128,2,768]{2,1,0:T(2,128)(2,1)S(1)} %copy.55), channel_id=1, replica_groups=mesh['group'=4,'x'=4,'z'=4,'h'=2,'c'=2] {'h','group','x','z'}, dimensions={0} | all-to-all | bytes 786432 | tf_op jit(solution)/shard_map/all_to_all | solution.py:153
  86.2 0.2 add_convert_fusion.6
  86.5 0.2 convolution_convert_fusion
  86.8 1.3 pad_maximum_fusion.2
  88.0 6.4 %all-to-all-start.1 = ((bf16[128,2,768]{2,1,0:T(2,128)(2,1)}), bf16[128,2,768]{2,1,0:T(2,128)(2,1)S(1)}, u32[]{:S(2)}, u32[]{:S(2)}) async-start(bf16[128,2,768]{2,1,0:T(2,128)(2,1)} %pad_maximum_fusion.2), calls=%async_computation.1 | async-start | bytes 786432 | tf_op jit(solution)/shard_map/all_to_all | solution.py:159
  94.4 0.3 fusion.25
  94.9 16.1 %all-to-all-done.1 = bf16[128,2,768]{2,1,0:T(2,128)(2,1)S(1)} async-done(((bf16[128,2,768]{2,1,0:T(2,128)(2,1)}), bf16[128,2,768]{2,1,0:T(2,128)(2,1)S(1)}, u32[]{:S(2)}, u32[]{:S(2)}) %all-to-all-start.1) | async-done | bytes 393248 | tf_op jit(solution)/shard_map/all_to_all | solution.py:159
  111.1 0.2 fusion.30
  111.2 0.2 fusion.27
  111.5 2.5 %all-gather = bf16[4,128,768]{2,1,0:T(8,128)(2,1)S(1)} all-gather(bf16[2,128,768]{2,1,0:T(8,128)(2,1)S(1)} %pad_maximum_fusion.3), channel_id=2, replica_groups=mesh['group'=4,'x'=4,'z'=4,'h'=2,'c'=2] {'c'}, dimensions={0}, use_global_device_ids=true | all-gather | bytes 1179648 | tf_op jit(solution)/shard_map/all_gather | solution.py:168
  114.0 0.2 fusion.19
  114.2 3.9 %fusion.5 = bf16[256,3072]{1,0:T(8,128)(2,1)S(1)} fusion(bf16[256,768]{1,0:T(8,128)(2,1)S(1)} %bitcast.111, bf16[2,768,3072]{2,1,0:T(8,128)(2,1)} %copy-done.1), kind=kOutput, calls=%fused_computation.7 | convolution fusion | flops 1208745984 | bytes 6684672 | tf_op jit(solution)/shard_map/sm,mk->sk/dot_general | solution.py:172
  118.2 0.2 fusion.18
  118.4 1.2 collective-permute-start.8
  119.6 0.9 collective-permute-start.7
  120.5 1.4 fusion.4
  122.1 1.1 collective-permute-start.9
  123.3 6.4 %collective-permute-done.8 = bf16[64,3072]{1,0:T(8,128)(2,1)S(1)} collective-permute-done((bf16[64,3072]{1,0:T(8,128)(2,1)S(1)}, bf16[64,3072]{1,0:T(8,128)(2,1)S(1)}, u32[]{:S(2)}, u32[]{:S(2)}) %collective-permute-start.8) | collective-permute-done | bytes 393248 | tf_op jit(solution)/shard_map/ppermute | solution.py:18
  129.7 2.0 %collective-permute-done.7 = bf16[64,3072]{1,0:T(8,128)(2,1)S(1)} collective-permute-done((bf16[64,3072]{1,0:T(8,128)(2,1)S(1)}, bf16[64,3072]{1,0:T(8,128)(2,1)S(1)}, u32[]{:S(2)}, u32[]{:S(2)}) %collective-permute-start.7) | collective-permute-done | bytes 393248 | tf_op jit(solution)/shard_map/ppermute | solution.py:18
  131.7 4.2 %collective-permute-done.9 = bf16[2,64,768]{2,1,0:T(8,128)(2,1)S(1)} collective-permute-done((bf16[2,64,768]{2,1,0:T(8,128)(2,1)S(1)}, bf16[2,64,768]{2,1,0:T(8,128)(2,1)S(1)}, u32[]{:S(2)}, u32[]{:S(2)}) %collective-permute-start.9) | collective-permute-done | bytes 196640 | tf_op jit(solution)/shard_map/ppermute | solution.py:18
  136.0 3.2 %collective-permute-start.15 = (bf16[32,3072]{1,0:T(8,128)(2,1)S(1)}, bf16[32,3072]{1,0:T(8,128)(2,1)S(1)}, u32[]{:S(2)}, u32[]{:S(2)}) collective-permute-start(bf16[32,3072]{1,0:T(8,128)(2,1)S(1)} %get-tuple-element.72), channel_id=1, source_target_pairs={{0,48},{16,0},{32,16},{48,32},{1,49},{17,1},{33,17},{49,33},{2,50}... | collective-permute-start | bytes 589832 | tf_op jit(solution)/shard_map/ppermute | solution.py:18
  139.2 3.3 %collective-permute-start.11 = (bf16[64,3072]{1,0:T(8,128)(2,1)S(1)}, bf16[64,3072]{1,0:T(8,128)(2,1)S(1)}, u32[]{:S(2)}, u32[]{:S(2)}) collective-permute-start(bf16[64,3072]{1,0:T(8,128)(2,1)S(1)} %pad_maximum_fusion.5), channel_id=1, source_target_pairs={{0,48},{16,0},{32,16},{48,32},{1,49},{17,1},{33,17},{49,33},{2,50}... | collective-permute-start | bytes 1179656 | tf_op jit(solution)/shard_map/ppermute | solution.py:18
  142.5 1.7 collective-permute-done.15
  144.2 4.1 %collective-permute-done.14 = bf16[32,3072]{1,0:T(8,128)(2,1)S(1)} collective-permute-done((bf16[32,3072]{1,0:T(8,128)(2,1)S(1)}, bf16[32,3072]{1,0:T(8,128)(2,1)S(1)}, u32[]{:S(2)}, u32[]{:S(2)}) %collective-permute-start.14) | collective-permute-done | bytes 196640 | tf_op jit(solution)/shard_map/ppermute | solution.py:18
  148.2 0.1 convert_add_fusion.3
  148.4 1.0 collective-permute-start.16
  149.4 0.8 collective-permute-start.17
  150.2 0.9 collective-permute-start.18
  151.1 3.4 %collective-permute-done.10 = bf16[64,3072]{1,0:T(8,128)(2,1)S(1)} collective-permute-done((bf16[64,3072]{1,0:T(8,128)(2,1)S(1)}, bf16[64,3072]{1,0:T(8,128)(2,1)S(1)}, u32[]{:S(2)}, u32[]{:S(2)}) %collective-permute-start.10) | collective-permute-done | bytes 393248 | tf_op jit(solution)/shard_map/ppermute | solution.py:18
  154.5 0.1 add_convert_fusion.4
  154.6 0.4 collective-permute-start.13
  154.9 1.8 %collective-permute-start.12 = (bf16[32,3072]{1,0:T(8,128)(2,1)S(1)}, bf16[32,3072]{1,0:T(8,128)(2,1)S(1)}, u32[]{:S(2)}, u32[]{:S(2)}) collective-permute-start(bf16[32,3072]{1,0:T(8,128)(2,1)S(1)} %get-tuple-element.77), channel_id=1, source_target_pairs={{0,16},{16,32},{32,48},{48,0},{1,17},{17,33},{33,49},{49,1},{2,18}... | collective-permute-start | bytes 589832 | tf_op jit(solution)/shard_map/ppermute | solution.py:18
  156.8 3.5 %collective-permute-done.13 = bf16[32,3072]{1,0:T(8,128)(2,1)S(1)} collective-permute-done((bf16[32,3072]{1,0:T(8,128)(2,1)S(1)}, bf16[32,3072]{1,0:T(8,128)(2,1)S(1)}, u32[]{:S(2)}, u32[]{:S(2)}) %collective-permute-start.13) | collective-permute-done | bytes 196640 | tf_op jit(solution)/shard_map/ppermute | solution.py:18
  160.3 1.5 collective-permute-done.12
  161.8 0.1 convert_add_fusion.2
  162.1 0.6 collective-permute-start.19
  162.6 1.1 collective-permute-start.20
  163.7 0.5 collective-permute-start.21
  164.2 0.9 copy.57
  165.1 1.7 collective-permute-done.19
  166.8 1.5 collective-permute-done.20
  168.2 2.0 %collective-permute-done.21 = bf16[16,3072]{1,0:T(8,128)(2,1)S(1)} collective-permute-done((bf16[16,3072]{1,0:T(8,128)(2,1)S(1)}, bf16[16,3072]{1,0:T(8,128)(2,1)S(1)}, u32[]{:S(2)}, u32[]{:S(2)}) %collective-permute-start.21) | collective-permute-done | bytes 98336 | tf_op jit(solution)/shard_map/ppermute | solution.py:18
  170.3 0.9 copy.58
  (70 shorter events, 2.1 us)
Async XLA Ops:
  0.6 29.4 %copy-start.3 = (s32[8]{0:T(128)S(1)}, s32[8]{0:T(128)}, u32[]{:S(2)}) copy-start(s32[8]{0:T(128)} %param.10) | copy-start | bytes 100
  0.6 29.6 %copy-start.2 = (s32[8,16]{1,0:T(8,128)S(1)}, s32[8,16]{1,0:T(8,128)}, u32[]{:S(2)}) copy-start(s32[8,16]{1,0:T(8,128)} %param.11) | copy-start | bytes 1540
  20.7 21.4 %collective-permute-start.2 = (bf16[2,64,3072]{2,1,0:T(8,128)(2,1)S(1)}, bf16[2,64,3072]{2,1,0:T(8,128)(2,1)S(1)}, u32[]{:S(2)}, u32[]{:S(2)}) collective-permute-start(bf16[2,64,3072]{2,1,0:T(8,128)(2,1)S(1)} %all_gather.9), channel_id=1, source_target_pairs={{0,48},{16,0},{32,16},{48,32},{1,49},{17,1},{33,17},{49,33},{2,50}... | collective-permute-start | bytes 2359304 | tf_op jit(solution)/shard_map/ppermute | solution.py:18
  23.6 18.5 %collective-permute-start = (bf16[2,64,3072]{2,1,0:T(8,128)(2,1)S(1)}, bf16[2,64,3072]{2,1,0:T(8,128)(2,1)S(1)}, u32[]{:S(2)}, u32[]{:S(2)}) collective-permute-start(bf16[2,64,3072]{2,1,0:T(8,128)(2,1)S(1)} %all_gather.9), channel_id=1, source_target_pairs={{0,16},{16,32},{32,48},{48,0},{1,17},{17,33},{33,49},{49,1},{2,18}... | collective-permute-start | bytes 2359304 | tf_op jit(solution)/shard_map/ppermute | solution.py:18
  25.3 26.1 %collective-permute-start.3 = (bf16[64,2,768]{2,0,1:T(8,128)(2,1)S(1)}, bf16[64,2,768]{2,0,1:T(8,128)(2,1)S(1)}, u32[]{:S(2)}, u32[]{:S(2)}) collective-permute-start(bf16[64,2,768]{2,0,1:T(8,128)(2,1)S(1)} %copy.66), channel_id=1, source_target_pairs={{0,2},{2,0},{1,3},{3,1},{4,6},{6,4},{5,7},{7,5},{8,10},{10,8},{9,1... | collective-permute-start | bytes 589832 | tf_op jit(solution)/shard_map/ppermute | solution.py:18
  30.7 3.7 %copy-start = (bf16[2,768,3072]{2,1,0:T(8,128)(2,1)S(1)}, bf16[2,768,3072]{2,1,0:T(8,128)(2,1)}, u32[]{:S(2)}) copy-start(bf16[2,768,3072]{2,1,0:T(8,128)(2,1)} %fronts_ref.1) | copy-start | bytes 28311556
  37.9 15.2 %copy-start.1 = (bf16[2,768,3072]{2,1,0:T(8,128)(2,1)}, bf16[2,768,3072]{2,1,0:T(8,128)(2,1)S(1)}, u32[]{:S(2)}) copy-start(bf16[2,768,3072]{2,1,0:T(8,128)(2,1)S(1)} %shard_map.77) | copy-start | bytes 28311556
  42.1 9.2 %collective-permute-start.1 = (bf16[64,3072]{1,0:T(8,128)(2,1)S(1)}, bf16[64,3072]{1,0:T(8,128)(2,1)S(1)}, u32[]{:S(2)}, u32[]{:S(2)}) collective-permute-start(bf16[64,3072]{1,0:T(8,128)(2,1)S(1)} %get-tuple-element.87), channel_id=1, source_target_pairs={{0,16},{16,32},{32,48},{48,0},{1,17},{17,33},{33,49},{49,1},{2,18}... | collective-permute-start | bytes 1179656 | tf_op jit(solution)/shard_map/ppermute | solution.py:18
  42.3 10.8 %collective-permute-start.5 = (bf16[64,3072]{1,0:T(8,128)(2,1)S(1)}, bf16[64,3072]{1,0:T(8,128)(2,1)S(1)}, u32[]{:S(2)}, u32[]{:S(2)}) collective-permute-start(bf16[64,3072]{1,0:T(8,128)(2,1)S(1)} %get-tuple-element.88), channel_id=1, source_target_pairs={{0,48},{16,0},{32,16},{48,32},{1,49},{17,1},{33,17},{49,33},{2,50}... | collective-permute-start | bytes 1179656 | tf_op jit(solution)/shard_map/ppermute | solution.py:18
  52.9 2.2 %collective-permute-start.4 = (bf16[2,64,768]{2,1,0:T(8,128)(2,1)S(1)}, bf16[2,64,768]{2,1,0:T(8,128)(2,1)S(1)}, u32[]{:S(2)}, u32[]{:S(2)}) collective-permute-start(bf16[2,64,768]{2,1,0:T(8,128)(2,1)S(1)} %dynamic-slice_bitcast_fusion.1), channel_id=1, source_target_pairs={{0,1},{1,0},{2,3},{3,2},{4,5},{5,4},{6,7},{7,6},{8,9},{9,8},{10,11... | collective-permute-start | bytes 589832 | tf_op jit(solution)/shard_map/ppermute | solution.py:18
  54.5 1.6 collective-permute-start.6
  88.0 22.9 %all-to-all-start.1 = ((bf16[128,2,768]{2,1,0:T(2,128)(2,1)}), bf16[128,2,768]{2,1,0:T(2,128)(2,1)S(1)}, u32[]{:S(2)}, u32[]{:S(2)}) async-start(bf16[128,2,768]{2,1,0:T(2,128)(2,1)} %pad_maximum_fusion.2), calls=%async_computation.1 | async-start | bytes 786432 | tf_op jit(solution)/shard_map/all_to_all | solution.py:159
  94.4 26.1 %slice-start = ((s8[9437184]{0:T(1024)(128)(4,1)}), s8[1048576]{0:T(1024)(128)(4,1)S(1)}, s32[]{:S(2)}) async-start(s8[9437184]{0:T(1024)(128)(4,1)} %bitcast.96), calls=%async_computation.2 | async-start | bytes 2097152
  111.5 9.0 %slice-start.1 = ((s8[9437184]{0:T(1024)(128)(4,1)}), s8[4194304]{0:T(1024)(128)(4,1)S(1)}, s32[]{:S(2)}) async-start(s8[9437184]{0:T(1024)(128)(4,1)} %bitcast.96), calls=%async_computation.3 | async-start | bytes 8388608
  114.2 6.3 %slice-start.2 = ((s8[9437184]{0:T(1024)(128)(4,1)}), s8[4194304]{0:T(1024)(128)(4,1)S(1)}, s32[]{:S(2)}) async-start(s8[9437184]{0:T(1024)(128)(4,1)} %bitcast.96), calls=%async_computation.4 | async-start | bytes 8388608
  118.4 11.2 %collective-permute-start.8 = (bf16[64,3072]{1,0:T(8,128)(2,1)S(1)}, bf16[64,3072]{1,0:T(8,128)(2,1)S(1)}, u32[]{:S(2)}, u32[]{:S(2)}) collective-permute-start(bf16[64,3072]{1,0:T(8,128)(2,1)S(1)} %pad_maximum_fusion.4), channel_id=1, source_target_pairs={{0,48},{16,0},{32,16},{48,32},{1,49},{17,1},{33,17},{49,33},{2,50}... | collective-permute-start | bytes 1179656 | tf_op jit(solution)/shard_map/ppermute | solution.py:18
  119.6 12.1 %collective-permute-start.7 = (bf16[64,3072]{1,0:T(8,128)(2,1)S(1)}, bf16[64,3072]{1,0:T(8,128)(2,1)S(1)}, u32[]{:S(2)}, u32[]{:S(2)}) collective-permute-start(bf16[64,3072]{1,0:T(8,128)(2,1)S(1)} %slice.187), channel_id=1, source_target_pairs={{0,16},{16,32},{32,48},{48,0},{1,17},{17,33},{33,49},{49,1},{2,18}... | collective-permute-start | bytes 1179656 | tf_op jit(solution)/shard_map/ppermute | solution.py:18
  122.1 13.8 %collective-permute-start.9 = (bf16[2,64,768]{2,1,0:T(8,128)(2,1)S(1)}, bf16[2,64,768]{2,1,0:T(8,128)(2,1)S(1)}, u32[]{:S(2)}, u32[]{:S(2)}) collective-permute-start(bf16[2,64,768]{2,1,0:T(8,128)(2,1)S(1)} %pad_maximum_fusion.7), channel_id=1, source_target_pairs={{0,2},{2,0},{1,3},{3,1},{4,6},{6,4},{5,7},{7,5},{8,10},{10,8},{9,1... | collective-permute-start | bytes 589832 | tf_op jit(solution)/shard_map/ppermute | solution.py:18
  136.0 8.1 %collective-permute-start.15 = (bf16[32,3072]{1,0:T(8,128)(2,1)S(1)}, bf16[32,3072]{1,0:T(8,128)(2,1)S(1)}, u32[]{:S(2)}, u32[]{:S(2)}) collective-permute-start(bf16[32,3072]{1,0:T(8,128)(2,1)S(1)} %get-tuple-element.72), channel_id=1, source_target_pairs={{0,48},{16,0},{32,16},{48,32},{1,49},{17,1},{33,17},{49,33},{2,50}... | collective-permute-start | bytes 589832 | tf_op jit(solution)/shard_map/ppermute | solution.py:18
  139.2 9.0 %collective-permute-start.14 = (bf16[32,3072]{1,0:T(8,128)(2,1)S(1)}, bf16[32,3072]{1,0:T(8,128)(2,1)S(1)}, u32[]{:S(2)}, u32[]{:S(2)}) collective-permute-start(bf16[32,3072]{1,0:T(8,128)(2,1)S(1)} %get-tuple-element.73), channel_id=1, source_target_pairs={{0,16},{16,32},{32,48},{48,0},{1,17},{17,33},{33,49},{49,1},{2,18}... | collective-permute-start | bytes 589832 | tf_op jit(solution)/shard_map/ppermute | solution.py:18
  139.2 15.3 %collective-permute-start.10 = (bf16[64,3072]{1,0:T(8,128)(2,1)S(1)}, bf16[64,3072]{1,0:T(8,128)(2,1)S(1)}, u32[]{:S(2)}, u32[]{:S(2)}) collective-permute-start(bf16[64,3072]{1,0:T(8,128)(2,1)S(1)} %slice.236), channel_id=1, source_target_pairs={{0,16},{16,32},{32,48},{48,0},{1,17},{17,33},{33,49},{49,1},{2,18}... | collective-permute-start | bytes 1179656 | tf_op jit(solution)/shard_map/ppermute | solution.py:18
  139.2 15.3 %collective-permute-start.11 = (bf16[64,3072]{1,0:T(8,128)(2,1)S(1)}, bf16[64,3072]{1,0:T(8,128)(2,1)S(1)}, u32[]{:S(2)}, u32[]{:S(2)}) collective-permute-start(bf16[64,3072]{1,0:T(8,128)(2,1)S(1)} %pad_maximum_fusion.5), channel_id=1, source_target_pairs={{0,48},{16,0},{32,16},{48,32},{1,49},{17,1},{33,17},{49,33},{2,50}... | collective-permute-start | bytes 1179656 | tf_op jit(solution)/shard_map/ppermute | solution.py:18
  148.4 8.3 %collective-permute-start.16 = (bf16[16,3072]{1,0:T(8,128)(2,1)S(1)}, bf16[16,3072]{1,0:T(8,128)(2,1)S(1)}, u32[]{:S(2)}, u32[]{:S(2)}) collective-permute-start(bf16[16,3072]{1,0:T(8,128)(2,1)S(1)} %slice.318), channel_id=1, source_target_pairs={{0,4},{4,8},{8,12},{12,0},{1,5},{5,9},{9,13},{13,1},{2,6},{6,10},{... | collective-permute-start | bytes 294920 | tf_op jit(solution)/shard_map/ppermute | solution.py:18
  149.4 7.3 %collective-permute-start.17 = (bf16[16,3072]{1,0:T(8,128)(2,1)S(1)}, bf16[16,3072]{1,0:T(8,128)(2,1)S(1)}, u32[]{:S(2)}, u32[]{:S(2)}) collective-permute-start(bf16[16,3072]{1,0:T(8,128)(2,1)S(1)} %get-tuple-element.94), channel_id=1, source_target_pairs={{0,8},{4,12},{8,0},{12,4},{1,9},{5,13},{9,1},{13,5},{2,10},{6,14},... | collective-permute-start | bytes 294920 | tf_op jit(solution)/shard_map/ppermute | solution.py:18
  150.2 6.6 %collective-permute-start.18 = (bf16[16,3072]{1,0:T(8,128)(2,1)S(1)}, bf16[16,3072]{1,0:T(8,128)(2,1)S(1)}, u32[]{:S(2)}, u32[]{:S(2)}) collective-permute-start(bf16[16,3072]{1,0:T(8,128)(2,1)S(1)} %get-tuple-element.95), channel_id=1, source_target_pairs={{0,12},{4,0},{8,4},{12,8},{1,13},{5,1},{9,5},{13,9},{2,14},{6,2},{... | collective-permute-start | bytes 294920 | tf_op jit(solution)/shard_map/ppermute | solution.py:18
  154.6 5.7 %collective-permute-start.13 = (bf16[32,3072]{1,0:T(8,128)(2,1)S(1)}, bf16[32,3072]{1,0:T(8,128)(2,1)S(1)}, u32[]{:S(2)}, u32[]{:S(2)}) collective-permute-start(bf16[32,3072]{1,0:T(8,128)(2,1)S(1)} %get-tuple-element.76), channel_id=1, source_target_pairs={{0,48},{16,0},{32,16},{48,32},{1,49},{17,1},{33,17},{49,33},{2,50}... | collective-permute-start | bytes 589832 | tf_op jit(solution)/shard_map/ppermute | solution.py:18
  154.9 6.9 %collective-permute-start.12 = (bf16[32,3072]{1,0:T(8,128)(2,1)S(1)}, bf16[32,3072]{1,0:T(8,128)(2,1)S(1)}, u32[]{:S(2)}, u32[]{:S(2)}) collective-permute-start(bf16[32,3072]{1,0:T(8,128)(2,1)S(1)} %get-tuple-element.77), channel_id=1, source_target_pairs={{0,16},{16,32},{32,48},{48,0},{1,17},{17,33},{33,49},{49,1},{2,18}... | collective-permute-start | bytes 589832 | tf_op jit(solution)/shard_map/ppermute | solution.py:18
  162.1 4.7 %collective-permute-start.19 = (bf16[16,3072]{1,0:T(8,128)(2,1)S(1)}, bf16[16,3072]{1,0:T(8,128)(2,1)S(1)}, u32[]{:S(2)}, u32[]{:S(2)}) collective-permute-start(bf16[16,3072]{1,0:T(8,128)(2,1)S(1)} %slice.317), channel_id=1, source_target_pairs={{0,4},{4,8},{8,12},{12,0},{1,5},{5,9},{9,13},{13,1},{2,6},{6,10},{... | collective-permute-start | bytes 294920 | tf_op jit(solution)/shard_map/ppermute | solution.py:18
  162.6 5.6 %collective-permute-start.20 = (bf16[16,3072]{1,0:T(8,128)(2,1)S(1)}, bf16[16,3072]{1,0:T(8,128)(2,1)S(1)}, u32[]{:S(2)}, u32[]{:S(2)}) collective-permute-start(bf16[16,3072]{1,0:T(8,128)(2,1)S(1)} %get-tuple-element.96), channel_id=1, source_target_pairs={{0,8},{4,12},{8,0},{12,4},{1,9},{5,13},{9,1},{13,5},{2,10},{6,14},... | collective-permute-start | bytes 294920 | tf_op jit(solution)/shard_map/ppermute | solution.py:18
  163.7 6.6 %collective-permute-start.21 = (bf16[16,3072]{1,0:T(8,128)(2,1)S(1)}, bf16[16,3072]{1,0:T(8,128)(2,1)S(1)}, u32[]{:S(2)}, u32[]{:S(2)}) collective-permute-start(bf16[16,3072]{1,0:T(8,128)(2,1)S(1)} %get-tuple-element.97), channel_id=1, source_target_pairs={{0,12},{4,0},{8,4},{12,8},{1,13},{5,1},{9,5},{13,9},{2,14},{6,2},{... | collective-permute-start | bytes 294920 | tf_op jit(solution)/shard_map/ppermute | solution.py:18

commit v10 on v9

--- a/solution.py
+++ b/solution.py
@@ -176,12 +176,12 @@
     product_0, *halves = lax.optimization_barrier((product_0, *halves))
     pieces_0 = first_pieces(product_0)
     near_0 = first_step(pieces_0)
-    ordered[1], _ = lax.optimization_barrier((ordered[1], pieces_0))
-    product_1 = multiplied(1)
-    pieces_1 = first_pieces(product_1)
     away = jnp.stack([jnp.where(first, half[1], half[0]).astype(BF16) for half in halves])
     away, _ = lax.optimization_barrier((away, pieces_0))
     received = shift(away, "h", 1)
+    ordered[1], _ = lax.optimization_barrier((ordered[1], (pieces_0, away)))
+    product_1 = multiplied(1)
+    pieces_1 = first_pieces(product_1)
     near_0, product_1, pieces_1, received = lax.optimization_barrier((near_0, product_1, pieces_1, received))
     far_0 = second_step(second_pieces(product_0, near_0))
     near_1 = first_step(pieces_1)

time: 172 us -> 170 us (0.988)
  transfers between devices with their start and end apart: 23 -> 23, of which waited for: 16 -> 15; matrix products, arithmetic and copies ran while one was open for 5% -> 5% of each run, Pallas kernels for 2% -> 2%
where the time goes in v10:
time: 170 us
  waiting for transfers between devices  57.5 us (34%)
  blocking collectives  50.4 us (30%)
  starting transfers between devices  34.5 us (20%)
  local copies, waits for them, and re-layouts  10.1 us (6%)
  matrix products  8.48 us (5%)
  other arithmetic  4.02 us (2%)
  Pallas kernels  3.47 us (2%)
    ppermute x22, waiting for transfers between devices, shift(): return lax.ppermute(value, axis, [(i, (i + by) % n) for i in range(n)])  41.5 us
    all_to_all x1, blocking collectives, shards(): lax.all_to_all(outgoing, spread, split_axis=0, concat_axis=0, tiled=True)  29.4 us
    ppermute x22, starting transfers between devices, shift(): return lax.ppermute(value, axis, [(i, (i + by) % n) for i in range(n)])  28.1 us
    all_gather x1, blocking collectives, shards(): columns = lax.all_gather(mine, 'z', axis=1, tiled=True)  18.6 us
    all_to_all x1, waiting for transfers between devices, shards(): lax.all_to_all(extension, spread, split_axis=0, concat_axis=0, tiled=True)  16.1 us
    all_to_all x1, starting transfers between devices, shards(): lax.all_to_all(extension, spread, split_axis=0, concat_axis=0, tiled=True)  6.41 us
    unnamed x16, local copies, waits for them, and re-layouts  5.47 us
    dot_general x2, matrix products, multiplied(): jnp.einsum('sm,mk->sk', ordered[f], masked[f], preferred_element_type=F32)  5.35 us
  transfers between devices with their start and end apart: 23, of which 15 were waited for; matrix products, arithmetic and copies ran while one was open for 5% of the time, Pallas kernels for 2%

profile of v10, /device:TPU:32, one launch (start us, length us, event | category | flops | bytes accessed | tf_op | source)
XLA Modules:
  0.0 169.7 jit_solution(16854691480162510238)
XLA Ops:
  0.7 1.4 fusion.56
  2.1 18.6 %all_gather.9 = bf16[2,64,3072]{2,1,0:T(8,128)(2,1)S(1)} all-gather(bf16[2,16,3072]{2,1,0:T(8,128)(2,1)S(1)} %pad_maximum_fusion.6), channel_id=1, replica_groups=mesh['group'=4,'x'=4,'z'=4,'h'=2,'c'=2] {'z'}, dimensions={1}, use_global_device_ids=true | all-gather | bytes 983040 | tf_op jit(solution)/shard_map/all_gather | solution.py:133
  20.7 2.8 %collective-permute-start.2 = (bf16[2,64,3072]{2,1,0:T(8,128)(2,1)S(1)}, bf16[2,64,3072]{2,1,0:T(8,128)(2,1)S(1)}, u32[]{:S(2)}, u32[]{:S(2)}) collective-permute-start(bf16[2,64,3072]{2,1,0:T(8,128)(2,1)S(1)} %all_gather.9), channel_id=1, source_target_pairs={{0,48},{16,0},{32,16},{48,32},{1,49},{17,1},{33,17},{49,33},{2,50}... | collective-permute-start | bytes 2359304 | tf_op jit(solution)/shard_map/ppermute | solution.py:18
  23.6 0.7 dynamic_slice.37.sizes_ref
  24.3 0.9 copy.66
  25.3 4.7 %collective-permute-start.3 = (bf16[64,2,768]{2,0,1:T(8,128)(2,1)S(1)}, bf16[64,2,768]{2,0,1:T(8,128)(2,1)S(1)}, u32[]{:S(2)}, u32[]{:S(2)}) collective-permute-start(bf16[64,2,768]{2,0,1:T(8,128)(2,1)S(1)} %copy.66), channel_id=1, source_target_pairs={{0,2},{2,0},{1,3},{3,1},{4,6},{6,4},{5,7},{7,5},{8,10},{10,8},{9,1... | collective-permute-start | bytes 589832 | tf_op jit(solution)/shard_map/ppermute | solution.py:18
  30.1 0.1 eq.36
  30.2 0.1 copy.52
  30.3 0.1 eq.40
  30.5 0.1 and_convert_fusion
  30.7 3.7 %copy-done = bf16[2,768,3072]{2,1,0:T(8,128)(2,1)S(1)} copy-done((bf16[2,768,3072]{2,1,0:T(8,128)(2,1)S(1)}, bf16[2,768,3072]{2,1,0:T(8,128)(2,1)}, u32[]{:S(2)}) %copy-start) | copy-done | bytes 9437208
  34.4 3.5 %shard_map.77 = bf16[2,768,3072]{2,1,0:T(8,128)(2,1)S(1)} custom-call(s32[2]{0:T(128)S(1)} %dynamic_slice.37.sizes_ref, s32[2]{0:T(128)S(1)} %pad_add_fusion.origin_ref, bf16[2,768,3072]{2,1,0:T(8,128)(2,1)S(1)} %copy-done), custom_call_target="tpu_custom_call" | custom-call | tf_op jit(solution)/shard_map/pallas_call | solution.py:53
  37.9 4.1 %collective-permute-done = bf16[2,64,3072]{2,1,0:T(8,128)(2,1)S(1)} collective-permute-done((bf16[2,64,3072]{2,1,0:T(8,128)(2,1)S(1)}, bf16[2,64,3072]{2,1,0:T(8,128)(2,1)S(1)}, u32[]{:S(2)}, u32[]{:S(2)}) %collective-permute-start) | collective-permute-done | bytes 786464 | tf_op jit(solution)/shard_map/ppermute | solution.py:18
  42.3 3.3 %collective-permute-start.5 = (bf16[64,3072]{1,0:T(8,128)(2,1)S(1)}, bf16[64,3072]{1,0:T(8,128)(2,1)S(1)}, u32[]{:S(2)}, u32[]{:S(2)}) collective-permute-start(bf16[64,3072]{1,0:T(8,128)(2,1)S(1)} %get-tuple-element.88), channel_id=1, source_target_pairs={{0,48},{16,0},{32,16},{48,32},{1,49},{17,1},{33,17},{49,33},{2,50}... | collective-permute-start | bytes 1179656 | tf_op jit(solution)/shard_map/ppermute | solution.py:18
  45.5 5.7 %collective-permute-done.1 = bf16[64,3072]{1,0:T(8,128)(2,1)S(1)} collective-permute-done((bf16[64,3072]{1,0:T(8,128)(2,1)S(1)}, bf16[64,3072]{1,0:T(8,128)(2,1)S(1)}, u32[]{:S(2)}, u32[]{:S(2)}) %collective-permute-start.1) | collective-permute-done | bytes 393248 | tf_op jit(solution)/shard_map/ppermute | solution.py:18
  51.3 0.1 pad_maximum_fusion
  51.4 1.5 fusion.16
  53.1 1.5 fusion.13
  54.5 0.6 collective-permute-start.6
  55.3 0.9 collective-permute-done.6
  56.4 0.4 copy.55
  56.8 29.4 %all_to_all.10 = bf16[128,2,768]{2,1,0:T(2,128)(2,1)S(1)} all-to-all(bf16[128,2,768]{2,1,0:T(2,128)(2,1)S(1)} %copy.55), channel_id=1, replica_groups=mesh['group'=4,'x'=4,'z'=4,'h'=2,'c'=2] {'h','group','x','z'}, dimensions={0} | all-to-all | bytes 786432 | tf_op jit(solution)/shard_map/all_to_all | solution.py:153
  86.2 0.2 add_convert_fusion.6
  86.5 0.2 convolution_convert_fusion
  86.8 1.3 pad_maximum_fusion.2
  88.0 6.4 %all-to-all-start.1 = ((bf16[128,2,768]{2,1,0:T(2,128)(2,1)}), bf16[128,2,768]{2,1,0:T(2,128)(2,1)S(1)}, u32[]{:S(2)}, u32[]{:S(2)}) async-start(bf16[128,2,768]{2,1,0:T(2,128)(2,1)} %pad_maximum_fusion.2), calls=%async_computation.1 | async-start | bytes 786432 | tf_op jit(solution)/shard_map/all_to_all | solution.py:159
  94.4 0.3 fusion.25
  94.9 16.1 %all-to-all-done.1 = bf16[128,2,768]{2,1,0:T(2,128)(2,1)S(1)} async-done(((bf16[128,2,768]{2,1,0:T(2,128)(2,1)}), bf16[128,2,768]{2,1,0:T(2,128)(2,1)S(1)}, u32[]{:S(2)}, u32[]{:S(2)}) %all-to-all-start.1) | async-done | bytes 393248 | tf_op jit(solution)/shard_map/all_to_all | solution.py:159
  111.1 0.2 fusion.30
  111.2 0.2 fusion.27
  111.5 2.4 %all-gather = bf16[4,128,768]{2,1,0:T(8,128)(2,1)S(1)} all-gather(bf16[2,128,768]{2,1,0:T(8,128)(2,1)S(1)} %pad_maximum_fusion.3), channel_id=2, replica_groups=mesh['group'=4,'x'=4,'z'=4,'h'=2,'c'=2] {'c'}, dimensions={0}, use_global_device_ids=true | all-gather | bytes 1179648 | tf_op jit(solution)/shard_map/all_gather | solution.py:168
  113.9 0.2 fusion.19
  114.1 3.9 %fusion.5 = bf16[256,3072]{1,0:T(8,128)(2,1)S(1)} fusion(bf16[256,768]{1,0:T(8,128)(2,1)S(1)} %bitcast.111, bf16[2,768,3072]{2,1,0:T(8,128)(2,1)} %copy-done.1), kind=kOutput, calls=%fused_computation.7 | convolution fusion | flops 1208745984 | bytes 6684672 | tf_op jit(solution)/shard_map/sm,mk->sk/dot_general | solution.py:172
  118.1 0.2 fusion.18
  118.3 1.2 collective-permute-start.8
  119.5 0.9 collective-permute-start.7
  120.5 1.1 collective-permute-start.9
  121.6 1.4 fusion.4
  123.1 6.4 %collective-permute-done.8 = bf16[64,3072]{1,0:T(8,128)(2,1)S(1)} collective-permute-done((bf16[64,3072]{1,0:T(8,128)(2,1)S(1)}, bf16[64,3072]{1,0:T(8,128)(2,1)S(1)}, u32[]{:S(2)}, u32[]{:S(2)}) %collective-permute-start.8) | collective-permute-done | bytes 393248 | tf_op jit(solution)/shard_map/ppermute | solution.py:18
  129.5 2.0 %collective-permute-done.7 = bf16[64,3072]{1,0:T(8,128)(2,1)S(1)} collective-permute-done((bf16[64,3072]{1,0:T(8,128)(2,1)S(1)}, bf16[64,3072]{1,0:T(8,128)(2,1)S(1)}, u32[]{:S(2)}, u32[]{:S(2)}) %collective-permute-start.7) | collective-permute-done | bytes 393248 | tf_op jit(solution)/shard_map/ppermute | solution.py:18
  131.5 2.7 %collective-permute-done.9 = bf16[2,64,768]{2,1,0:T(8,128)(2,1)S(1)} collective-permute-done((bf16[2,64,768]{2,1,0:T(8,128)(2,1)S(1)}, bf16[2,64,768]{2,1,0:T(8,128)(2,1)S(1)}, u32[]{:S(2)}, u32[]{:S(2)}) %collective-permute-start.9) | collective-permute-done | bytes 196640 | tf_op jit(solution)/shard_map/ppermute | solution.py:18
  134.3 0.1 add_convert_fusion.2
  134.4 3.2 %collective-permute-start.15 = (bf16[32,3072]{1,0:T(8,128)(2,1)S(1)}, bf16[32,3072]{1,0:T(8,128)(2,1)S(1)}, u32[]{:S(2)}, u32[]{:S(2)}) collective-permute-start(bf16[32,3072]{1,0:T(8,128)(2,1)S(1)} %get-tuple-element.72), channel_id=1, source_target_pairs={{0,48},{16,0},{32,16},{48,32},{1,49},{17,1},{33,17},{49,33},{2,50}... | collective-permute-start | bytes 589832 | tf_op jit(solution)/shard_map/ppermute | solution.py:18
  137.5 3.3 %collective-permute-start.11 = (bf16[64,3072]{1,0:T(8,128)(2,1)S(1)}, bf16[64,3072]{1,0:T(8,128)(2,1)S(1)}, u32[]{:S(2)}, u32[]{:S(2)}) collective-permute-start(bf16[64,3072]{1,0:T(8,128)(2,1)S(1)} %pad_maximum_fusion.5), channel_id=1, source_target_pairs={{0,48},{16,0},{32,16},{48,32},{1,49},{17,1},{33,17},{49,33},{2,50}... | collective-permute-start | bytes 1179656 | tf_op jit(solution)/shard_map/ppermute | solution.py:18
  140.8 1.8 %collective-permute-done.15 = bf16[32,3072]{1,0:T(8,128)(2,1)S(1)} collective-permute-done((bf16[32,3072]{1,0:T(8,128)(2,1)S(1)}, bf16[32,3072]{1,0:T(8,128)(2,1)S(1)}, u32[]{:S(2)}, u32[]{:S(2)}) %collective-permute-start.15) | collective-permute-done | bytes 196640 | tf_op jit(solution)/shard_map/ppermute | solution.py:18
  142.6 4.0 %collective-permute-done.14 = bf16[32,3072]{1,0:T(8,128)(2,1)S(1)} collective-permute-done((bf16[32,3072]{1,0:T(8,128)(2,1)S(1)}, bf16[32,3072]{1,0:T(8,128)(2,1)S(1)}, u32[]{:S(2)}, u32[]{:S(2)}) %collective-permute-start.14) | collective-permute-done | bytes 196640 | tf_op jit(solution)/shard_map/ppermute | solution.py:18
  146.6 0.1 convert_add_fusion.3
  146.8 0.9 collective-permute-start.16
  147.7 0.8 collective-permute-start.17
  148.6 0.9 collective-permute-start.18
  149.4 3.5 %collective-permute-done.10 = bf16[64,3072]{1,0:T(8,128)(2,1)S(1)} collective-permute-done((bf16[64,3072]{1,0:T(8,128)(2,1)S(1)}, bf16[64,3072]{1,0:T(8,128)(2,1)S(1)}, u32[]{:S(2)}, u32[]{:S(2)}) %collective-permute-start.10) | collective-permute-done | bytes 393248 | tf_op jit(solution)/shard_map/ppermute | solution.py:18
  153.0 0.4 collective-permute-start.13
  153.4 1.8 %collective-permute-start.12 = (bf16[32,3072]{1,0:T(8,128)(2,1)S(1)}, bf16[32,3072]{1,0:T(8,128)(2,1)S(1)}, u32[]{:S(2)}, u32[]{:S(2)}) collective-permute-start(bf16[32,3072]{1,0:T(8,128)(2,1)S(1)} %get-tuple-element.77), channel_id=1, source_target_pairs={{0,16},{16,32},{32,48},{48,0},{1,17},{17,33},{33,49},{49,1},{2,18}... | collective-permute-start | bytes 589832 | tf_op jit(solution)/shard_map/ppermute | solution.py:18
  155.2 3.6 %collective-permute-done.13 = bf16[32,3072]{1,0:T(8,128)(2,1)S(1)} collective-permute-done((bf16[32,3072]{1,0:T(8,128)(2,1)S(1)}, bf16[32,3072]{1,0:T(8,128)(2,1)S(1)}, u32[]{:S(2)}, u32[]{:S(2)}) %collective-permute-start.13) | collective-permute-done | bytes 196640 | tf_op jit(solution)/shard_map/ppermute | solution.py:18
  158.7 1.5 collective-permute-done.12
  160.2 0.1 convert_add_fusion.2
  160.5 0.5 collective-permute-start.19
  161.0 1.1 collective-permute-start.20
  162.1 0.6 collective-permute-start.21
  162.6 0.9 copy.57
  163.5 1.7 collective-permute-done.19
  165.2 1.4 collective-permute-done.20
  166.6 2.1 %collective-permute-done.21 = bf16[16,3072]{1,0:T(8,128)(2,1)S(1)} collective-permute-done((bf16[16,3072]{1,0:T(8,128)(2,1)S(1)}, bf16[16,3072]{1,0:T(8,128)(2,1)S(1)}, u32[]{:S(2)}, u32[]{:S(2)}) %collective-permute-start.21) | collective-permute-done | bytes 98336 | tf_op jit(solution)/shard_map/ppermute | solution.py:18
  168.8 0.9 copy.58
  (70 shorter events, 2.0 us)
Async XLA Ops:
  0.6 29.4 %copy-start.3 = (s32[8]{0:T(128)S(1)}, s32[8]{0:T(128)}, u32[]{:S(2)}) copy-start(s32[8]{0:T(128)} %param.10) | copy-start | bytes 100
  0.6 29.6 %copy-start.2 = (s32[8,16]{1,0:T(8,128)S(1)}, s32[8,16]{1,0:T(8,128)}, u32[]{:S(2)}) copy-start(s32[8,16]{1,0:T(8,128)} %param.11) | copy-start | bytes 1540
  20.7 21.4 %collective-permute-start.2 = (bf16[2,64,3072]{2,1,0:T(8,128)(2,1)S(1)}, bf16[2,64,3072]{2,1,0:T(8,128)(2,1)S(1)}, u32[]{:S(2)}, u32[]{:S(2)}) collective-permute-start(bf16[2,64,3072]{2,1,0:T(8,128)(2,1)S(1)} %all_gather.9), channel_id=1, source_target_pairs={{0,48},{16,0},{32,16},{48,32},{1,49},{17,1},{33,17},{49,33},{2,50}... | collective-permute-start | bytes 2359304 | tf_op jit(solution)/shard_map/ppermute | solution.py:18
  23.6 18.5 %collective-permute-start = (bf16[2,64,3072]{2,1,0:T(8,128)(2,1)S(1)}, bf16[2,64,3072]{2,1,0:T(8,128)(2,1)S(1)}, u32[]{:S(2)}, u32[]{:S(2)}) collective-permute-start(bf16[2,64,3072]{2,1,0:T(8,128)(2,1)S(1)} %all_gather.9), channel_id=1, source_target_pairs={{0,16},{16,32},{32,48},{48,0},{1,17},{17,33},{33,49},{49,1},{2,18}... | collective-permute-start | bytes 2359304 | tf_op jit(solution)/shard_map/ppermute | solution.py:18
  25.3 26.1 %collective-permute-start.3 = (bf16[64,2,768]{2,0,1:T(8,128)(2,1)S(1)}, bf16[64,2,768]{2,0,1:T(8,128)(2,1)S(1)}, u32[]{:S(2)}, u32[]{:S(2)}) collective-permute-start(bf16[64,2,768]{2,0,1:T(8,128)(2,1)S(1)} %copy.66), channel_id=1, source_target_pairs={{0,2},{2,0},{1,3},{3,1},{4,6},{6,4},{5,7},{7,5},{8,10},{10,8},{9,1... | collective-permute-start | bytes 589832 | tf_op jit(solution)/shard_map/ppermute | solution.py:18
  30.7 3.7 %copy-start = (bf16[2,768,3072]{2,1,0:T(8,128)(2,1)S(1)}, bf16[2,768,3072]{2,1,0:T(8,128)(2,1)}, u32[]{:S(2)}) copy-start(bf16[2,768,3072]{2,1,0:T(8,128)(2,1)} %fronts_ref.1) | copy-start | bytes 28311556
  37.9 15.2 %copy-start.1 = (bf16[2,768,3072]{2,1,0:T(8,128)(2,1)}, bf16[2,768,3072]{2,1,0:T(8,128)(2,1)S(1)}, u32[]{:S(2)}) copy-start(bf16[2,768,3072]{2,1,0:T(8,128)(2,1)S(1)} %shard_map.77) | copy-start | bytes 28311556
  42.1 9.2 %collective-permute-start.1 = (bf16[64,3072]{1,0:T(8,128)(2,1)S(1)}, bf16[64,3072]{1,0:T(8,128)(2,1)S(1)}, u32[]{:S(2)}, u32[]{:S(2)}) collective-permute-start(bf16[64,3072]{1,0:T(8,128)(2,1)S(1)} %get-tuple-element.87), channel_id=1, source_target_pairs={{0,16},{16,32},{32,48},{48,0},{1,17},{17,33},{33,49},{49,1},{2,18}... | collective-permute-start | bytes 1179656 | tf_op jit(solution)/shard_map/ppermute | solution.py:18
  42.3 10.8 %collective-permute-start.5 = (bf16[64,3072]{1,0:T(8,128)(2,1)S(1)}, bf16[64,3072]{1,0:T(8,128)(2,1)S(1)}, u32[]{:S(2)}, u32[]{:S(2)}) collective-permute-start(bf16[64,3072]{1,0:T(8,128)(2,1)S(1)} %get-tuple-element.88), channel_id=1, source_target_pairs={{0,48},{16,0},{32,16},{48,32},{1,49},{17,1},{33,17},{49,33},{2,50}... | collective-permute-start | bytes 1179656 | tf_op jit(solution)/shard_map/ppermute | solution.py:18
  52.9 2.2 %collective-permute-start.4 = (bf16[2,64,768]{2,1,0:T(8,128)(2,1)S(1)}, bf16[2,64,768]{2,1,0:T(8,128)(2,1)S(1)}, u32[]{:S(2)}, u32[]{:S(2)}) collective-permute-start(bf16[2,64,768]{2,1,0:T(8,128)(2,1)S(1)} %dynamic-slice_bitcast_fusion.1), channel_id=1, source_target_pairs={{0,1},{1,0},{2,3},{3,2},{4,5},{5,4},{6,7},{7,6},{8,9},{9,8},{10,11... | collective-permute-start | bytes 589832 | tf_op jit(solution)/shard_map/ppermute | solution.py:18
  54.5 1.6 collective-permute-start.6
  88.0 22.9 %all-to-all-start.1 = ((bf16[128,2,768]{2,1,0:T(2,128)(2,1)}), bf16[128,2,768]{2,1,0:T(2,128)(2,1)S(1)}, u32[]{:S(2)}, u32[]{:S(2)}) async-start(bf16[128,2,768]{2,1,0:T(2,128)(2,1)} %pad_maximum_fusion.2), calls=%async_computation.1 | async-start | bytes 786432 | tf_op jit(solution)/shard_map/all_to_all | solution.py:159
  94.8 26.8 %slice-start = ((s8[9437184]{0:T(1024)(128)(4,1)}), s8[1048576]{0:T(1024)(128)(4,1)S(1)}, s32[]{:S(2)}) async-start(s8[9437184]{0:T(1024)(128)(4,1)} %bitcast.96), calls=%async_computation.2 | async-start | bytes 2097152
  113.8 7.7 %slice-start.1 = ((s8[9437184]{0:T(1024)(128)(4,1)}), s8[4194304]{0:T(1024)(128)(4,1)S(1)}, s32[]{:S(2)}) async-start(s8[9437184]{0:T(1024)(128)(4,1)} %bitcast.96), calls=%async_computation.3 | async-start | bytes 8388608
  114.1 7.5 %slice-start.2 = ((s8[9437184]{0:T(1024)(128)(4,1)}), s8[4194304]{0:T(1024)(128)(4,1)S(1)}, s32[]{:S(2)}) async-start(s8[9437184]{0:T(1024)(128)(4,1)} %bitcast.96), calls=%async_computation.4 | async-start | bytes 8388608
  118.3 11.2 %collective-permute-start.8 = (bf16[64,3072]{1,0:T(8,128)(2,1)S(1)}, bf16[64,3072]{1,0:T(8,128)(2,1)S(1)}, u32[]{:S(2)}, u32[]{:S(2)}) collective-permute-start(bf16[64,3072]{1,0:T(8,128)(2,1)S(1)} %pad_maximum_fusion.4), channel_id=1, source_target_pairs={{0,48},{16,0},{32,16},{48,32},{1,49},{17,1},{33,17},{49,33},{2,50}... | collective-permute-start | bytes 1179656 | tf_op jit(solution)/shard_map/ppermute | solution.py:18
  119.5 12.1 %collective-permute-start.7 = (bf16[64,3072]{1,0:T(8,128)(2,1)S(1)}, bf16[64,3072]{1,0:T(8,128)(2,1)S(1)}, u32[]{:S(2)}, u32[]{:S(2)}) collective-permute-start(bf16[64,3072]{1,0:T(8,128)(2,1)S(1)} %slice.187), channel_id=1, source_target_pairs={{0,16},{16,32},{32,48},{48,0},{1,17},{17,33},{33,49},{49,1},{2,18}... | collective-permute-start | bytes 1179656 | tf_op jit(solution)/shard_map/ppermute | solution.py:18
  120.5 13.8 %collective-permute-start.9 = (bf16[2,64,768]{2,1,0:T(8,128)(2,1)S(1)}, bf16[2,64,768]{2,1,0:T(8,128)(2,1)S(1)}, u32[]{:S(2)}, u32[]{:S(2)}) collective-permute-start(bf16[2,64,768]{2,1,0:T(8,128)(2,1)S(1)} %pad_maximum_fusion.7), channel_id=1, source_target_pairs={{0,2},{2,0},{1,3},{3,1},{4,6},{6,4},{5,7},{7,5},{8,10},{10,8},{9,1... | collective-permute-start | bytes 589832 | tf_op jit(solution)/shard_map/ppermute | solution.py:18
  134.4 8.2 %collective-permute-start.15 = (bf16[32,3072]{1,0:T(8,128)(2,1)S(1)}, bf16[32,3072]{1,0:T(8,128)(2,1)S(1)}, u32[]{:S(2)}, u32[]{:S(2)}) collective-permute-start(bf16[32,3072]{1,0:T(8,128)(2,1)S(1)} %get-tuple-element.72), channel_id=1, source_target_pairs={{0,48},{16,0},{32,16},{48,32},{1,49},{17,1},{33,17},{49,33},{2,50}... | collective-permute-start | bytes 589832 | tf_op jit(solution)/shard_map/ppermute | solution.py:18
  137.5 9.0 %collective-permute-start.14 = (bf16[32,3072]{1,0:T(8,128)(2,1)S(1)}, bf16[32,3072]{1,0:T(8,128)(2,1)S(1)}, u32[]{:S(2)}, u32[]{:S(2)}) collective-permute-start(bf16[32,3072]{1,0:T(8,128)(2,1)S(1)} %get-tuple-element.73), channel_id=1, source_target_pairs={{0,16},{16,32},{32,48},{48,0},{1,17},{17,33},{33,49},{49,1},{2,18}... | collective-permute-start | bytes 589832 | tf_op jit(solution)/shard_map/ppermute | solution.py:18
  137.5 15.4 %collective-permute-start.10 = (bf16[64,3072]{1,0:T(8,128)(2,1)S(1)}, bf16[64,3072]{1,0:T(8,128)(2,1)S(1)}, u32[]{:S(2)}, u32[]{:S(2)}) collective-permute-start(bf16[64,3072]{1,0:T(8,128)(2,1)S(1)} %slice.236), channel_id=1, source_target_pairs={{0,16},{16,32},{32,48},{48,0},{1,17},{17,33},{33,49},{49,1},{2,18}... | collective-permute-start | bytes 1179656 | tf_op jit(solution)/shard_map/ppermute | solution.py:18
  137.5 15.4 %collective-permute-start.11 = (bf16[64,3072]{1,0:T(8,128)(2,1)S(1)}, bf16[64,3072]{1,0:T(8,128)(2,1)S(1)}, u32[]{:S(2)}, u32[]{:S(2)}) collective-permute-start(bf16[64,3072]{1,0:T(8,128)(2,1)S(1)} %pad_maximum_fusion.5), channel_id=1, source_target_pairs={{0,48},{16,0},{32,16},{48,32},{1,49},{17,1},{33,17},{49,33},{2,50}... | collective-permute-start | bytes 1179656 | tf_op jit(solution)/shard_map/ppermute | solution.py:18
  146.8 8.4 %collective-permute-start.16 = (bf16[16,3072]{1,0:T(8,128)(2,1)S(1)}, bf16[16,3072]{1,0:T(8,128)(2,1)S(1)}, u32[]{:S(2)}, u32[]{:S(2)}) collective-permute-start(bf16[16,3072]{1,0:T(8,128)(2,1)S(1)} %slice.318), channel_id=1, source_target_pairs={{0,4},{4,8},{8,12},{12,0},{1,5},{5,9},{9,13},{13,1},{2,6},{6,10},{... | collective-permute-start | bytes 294920 | tf_op jit(solution)/shard_map/ppermute | solution.py:18
  147.7 7.4 %collective-permute-start.17 = (bf16[16,3072]{1,0:T(8,128)(2,1)S(1)}, bf16[16,3072]{1,0:T(8,128)(2,1)S(1)}, u32[]{:S(2)}, u32[]{:S(2)}) collective-permute-start(bf16[16,3072]{1,0:T(8,128)(2,1)S(1)} %get-tuple-element.94), channel_id=1, source_target_pairs={{0,8},{4,12},{8,0},{12,4},{1,9},{5,13},{9,1},{13,5},{2,10},{6,14},... | collective-permute-start | bytes 294920 | tf_op jit(solution)/shard_map/ppermute | solution.py:18
  148.6 6.6 %collective-permute-start.18 = (bf16[16,3072]{1,0:T(8,128)(2,1)S(1)}, bf16[16,3072]{1,0:T(8,128)(2,1)S(1)}, u32[]{:S(2)}, u32[]{:S(2)}) collective-permute-start(bf16[16,3072]{1,0:T(8,128)(2,1)S(1)} %get-tuple-element.95), channel_id=1, source_target_pairs={{0,12},{4,0},{8,4},{12,8},{1,13},{5,1},{9,5},{13,9},{2,14},{6,2},{... | collective-permute-start | bytes 294920 | tf_op jit(solution)/shard_map/ppermute | solution.py:18
  153.0 5.7 %collective-permute-start.13 = (bf16[32,3072]{1,0:T(8,128)(2,1)S(1)}, bf16[32,3072]{1,0:T(8,128)(2,1)S(1)}, u32[]{:S(2)}, u32[]{:S(2)}) collective-permute-start(bf16[32,3072]{1,0:T(8,128)(2,1)S(1)} %get-tuple-element.76), channel_id=1, source_target_pairs={{0,48},{16,0},{32,16},{48,32},{1,49},{17,1},{33,17},{49,33},{2,50}... | collective-permute-start | bytes 589832 | tf_op jit(solution)/shard_map/ppermute | solution.py:18
  153.4 6.9 %collective-permute-start.12 = (bf16[32,3072]{1,0:T(8,128)(2,1)S(1)}, bf16[32,3072]{1,0:T(8,128)(2,1)S(1)}, u32[]{:S(2)}, u32[]{:S(2)}) collective-permute-start(bf16[32,3072]{1,0:T(8,128)(2,1)S(1)} %get-tuple-element.77), channel_id=1, source_target_pairs={{0,16},{16,32},{32,48},{48,0},{1,17},{17,33},{33,49},{49,1},{2,18}... | collective-permute-start | bytes 589832 | tf_op jit(solution)/shard_map/ppermute | solution.py:18
  160.5 4.7 %collective-permute-start.19 = (bf16[16,3072]{1,0:T(8,128)(2,1)S(1)}, bf16[16,3072]{1,0:T(8,128)(2,1)S(1)}, u32[]{:S(2)}, u32[]{:S(2)}) collective-permute-start(bf16[16,3072]{1,0:T(8,128)(2,1)S(1)} %slice.317), channel_id=1, source_target_pairs={{0,4},{4,8},{8,12},{12,0},{1,5},{5,9},{9,13},{13,1},{2,6},{6,10},{... | collective-permute-start | bytes 294920 | tf_op jit(solution)/shard_map/ppermute | solution.py:18
  161.0 5.6 %collective-permute-start.20 = (bf16[16,3072]{1,0:T(8,128)(2,1)S(1)}, bf16[16,3072]{1,0:T(8,128)(2,1)S(1)}, u32[]{:S(2)}, u32[]{:S(2)}) collective-permute-start(bf16[16,3072]{1,0:T(8,128)(2,1)S(1)} %get-tuple-element.96), channel_id=1, source_target_pairs={{0,8},{4,12},{8,0},{12,4},{1,9},{5,13},{9,1},{13,5},{2,10},{6,14},... | collective-permute-start | bytes 294920 | tf_op jit(solution)/shard_map/ppermute | solution.py:18
  162.1 6.7 %collective-permute-start.21 = (bf16[16,3072]{1,0:T(8,128)(2,1)S(1)}, bf16[16,3072]{1,0:T(8,128)(2,1)S(1)}, u32[]{:S(2)}, u32[]{:S(2)}) collective-permute-start(bf16[16,3072]{1,0:T(8,128)(2,1)S(1)} %get-tuple-element.97), channel_id=1, source_target_pairs={{0,12},{4,0},{8,4},{12,8},{1,13},{5,1},{9,5},{13,9},{2,14},{6,2},{... | collective-permute-start | bytes 294920 | tf_op jit(solution)/shard_map/ppermute | solution.py:18
